TPU v7x, 32 devices: a whole 2x2x4 slice. The times are simulated.
32 devices in a mesh: shard: 2 (over x), ctx: 4 (over y, core), tensor: 4 (over z).
Axes of the slice: x: 2, y: 2, z: 4, core: 2. Of those that a mesh axis runs over, the one named last changes fastest.
Arguments:
- block_input: bfloat16 [4096, 1536], P(('shard', 'ctx'), 'tensor'), may hold values from -6 to 6
- gain_input: bfloat16 [1536], P('tensor'), may hold values from 0.5 to 1.5
- proj_main: bfloat16 [1536, 2, 3072], P(('shard', 'ctx'), None, 'tensor'), may hold values from -0.15625 to 0.15625
- proj_state: bfloat16 [1536, 256], P(('shard', 'ctx')), may hold values from -0.15625 to 0.15625
- proj_step: bfloat16 [1536, 48], P(('shard', 'ctx'), 'tensor'), may hold values from -0.15625 to 0.15625
- conv_main: bfloat16 [4, 3072], P(None, 'tensor'), may hold values from -3 to 3
- conv_state: bfloat16 [4, 256], replicated, may hold values from -3 to 3
- step_bias: float32 [48], P('tensor'), may hold values from -4 to -1
- decay_log: float32 [48], P('tensor'), may hold values from -8 to -1
- skip_gain: float32 [48], P('tensor'), may hold values from 0.5 to 1.5
- gain_gate: bfloat16 [3072], P('tensor'), may hold values from 0.5 to 1.5
- proj_out: bfloat16 [1536, 3072], P(('shard', 'ctx'), 'tensor'), may hold values from -0.109375 to 0.109375
- gain_mix: bfloat16 [1536], P('tensor'), may hold values from 0.5 to 1.5
- router_weight: bfloat16 [1536, 16], P(('shard', 'ctx')), may hold values from -0.078125 to 0.078125
- shared_gates: bfloat16 [1536, 2, 1024], P(('shard', 'ctx'), None, 'tensor'), may hold values from -0.15625 to 0.15625
- shared_down: bfloat16 [1536, 1024], P(('shard', 'ctx'), 'tensor'), may hold values from -0.1875 to 0.1875
- expert_gates: bfloat16 [16, 1536, 2, 512], P(('shard', 'ctx'), None, None, 'tensor'), may hold values from -0.15625 to 0.15625
- expert_down: bfloat16 [16, 512, 1536], P(('shard', 'ctx'), 'tensor'), may hold values from -0.5 to 0.5
- segments: int32 [2, 2048], P('shard', 'ctx'), may hold values from 0 to 2, never falling along the last dimension, each value on 1 to 1024 neighbouring positions
- routes: int32 [4096, 6], P(('shard', 'ctx')), may hold values from 0 to 15, all different within a row; in each aligned block of 512 rows (0 to 511, 512 to 1023, ...) at most 384 rows name the same one
- cotangent: bfloat16 [4096, 1536], P(('shard', 'ctx'), 'tensor'), may hold values from -6 to 6
Outputs:
- output: bfloat16 [4096, 1536], P(('shard', 'ctx'), 'tensor')
- grad_input: float32 [4096, 1536], P(('shard', 'ctx'), 'tensor')
- grad_gain_input: float32 [1536], P('tensor')
- grad_proj_main: float32 [1536, 2, 3072], P(('shard', 'ctx'), None, 'tensor')
- grad_proj_state: float32 [1536, 256], P(('shard', 'ctx'))
- grad_proj_step: float32 [1536, 48], P(('shard', 'ctx'), 'tensor')
- grad_conv_main: float32 [4, 3072], P(None, 'tensor')
- grad_conv_state: float32 [4, 256], replicated
- grad_step_bias: float32 [48], P('tensor')
- grad_decay_log: float32 [48], P('tensor')
- grad_skip_gain: float32 [48], P('tensor')
- grad_gain_gate: float32 [3072], P('tensor')
- grad_proj_out: float32 [1536, 3072], P(('shard', 'ctx'), 'tensor')
- grad_gain_mix: float32 [1536], P('tensor')
- grad_router_weight: float32 [1536, 16], P(('shard', 'ctx'))
- grad_shared_gates: float32 [1536, 2, 1024], P(('shard', 'ctx'), None, 'tensor')
- grad_shared_down: float32 [1536, 1024], P(('shard', 'ctx'), 'tensor')
- grad_expert_gates: float32 [16, 1536, 2, 512], P(('shard', 'ctx'), None, None, 'tensor')
- grad_expert_down: float32 [16, 512, 1536], P(('shard', 'ctx'), 'tensor')
Inputs may be any that keep to these rules, and one draw needn't show every extreme that they name: `routes`: each row names 6 different experts; among the rows of one device (512 tokens, aligned blocks) no expert is named more than 384 times. `segments`: along each group the document numbers never fall; each document has at most 1024 tokens.
All inputs are finite; a program needn't handle non-finite values.
Results may differ from a plain program's by a relative error of at most 0.015.
Values may be sent and summed in bfloat16 or wider, within the bound.
A program may use at most 448 MiB of HBM per device.

v0:
```python
from functools import partial

import jax
import jax.numpy as jnp
from jax import lax
from jax.sharding import PartitionSpec as P

D = 1536
CONV = 4
DI = 3072


epsilon = 1e-05
highest = lax.Precision.HIGHEST


def shifted(value, axis, steps):
    count = lax.axis_size(axis)
    leading, last = (max(0, -steps), min(count, count - steps))
    return lax.ppermute(value, axis, [(source, source + steps) for source in range(leading, last)])


def prefix(shard, axis, combine, identity, reverse):
    devices, index = (lax.axis_size(axis), lax.axis_index(axis))
    everything = jax.tree.map(lambda part: lax.all_gather(part, axis), shard)
    start = jax.tree.map(
        lambda part, zero: jnp.broadcast_to(jnp.asarray(zero, part.dtype), part.shape),
        shard,
        identity,
    )

    def lap(k, before):
        at = devices - 1 - k if reverse else k
        reached = at > index if reverse else at < index
        new = combine(before, jax.tree.map(lambda part: part[at], everything))
        return jax.tree.map(lambda a, b: jnp.where(reached, a, b), new, before)

    return lax.fori_loop(0, devices, lap, start)


def dot_rows(left, right):
    return jnp.dot(left, right, preferred_element_type=jnp.float32)


def dot_inner(left, right):
    return lax.dot_general(
        left, right, (((0,), (0,)), ((), ())), preferred_element_type=jnp.float32
    )


def dot_outer(left, right):
    return lax.dot_general(
        left, right, (((1,), (1,)), ((), ())), preferred_element_type=jnp.float32
    )


def silu_grad(value):
    sigmoid_value = jax.nn.sigmoid(value)
    return sigmoid_value * (1.0 + value * (1.0 - sigmoid_value))


def gather_weights(
    proj_main, proj_state, proj_step, proj_out, router_weight, shared_gates, shared_down
):
    return (
        lax.all_gather(proj_main, ("shard", "ctx"), axis=0, tiled=True),
        lax.all_gather(proj_state, ("shard", "ctx"), axis=0, tiled=True),
        lax.all_gather(proj_step, ("shard", "ctx"), axis=0, tiled=True),
        lax.all_gather(proj_out, ("shard", "ctx"), axis=0, tiled=True),
        lax.all_gather(router_weight, ("shard", "ctx"), axis=0, tiled=True),
        lax.all_gather(shared_gates, ("shard", "ctx"), axis=0, tiled=True),
        lax.all_gather(shared_down, ("shard", "ctx"), axis=0, tiled=True),
    )


def gather_features(rows, gain):
    return (
        lax.all_gather(rows, "tensor", axis=1, tiled=True),
        lax.all_gather(gain[None, :], "tensor", axis=1, tiled=True),
    )


def gather_grads(rows):
    return lax.all_gather(rows, "tensor", axis=1, tiled=True)


def head_sums(partial_rows):
    return lax.psum_scatter(partial_rows, "tensor", scatter_dimension=1, tiled=True)


def tensor_sums(values):
    return lax.psum(values, "tensor")


def route_out(rows):
    return lax.all_to_all(rows, ("shard", "ctx"), split_axis=0, concat_axis=0, tiled=True)


def route_back(rows):
    return lax.all_to_all(rows, ("shard", "ctx"), split_axis=0, concat_axis=0, tiled=True)


def chain_join(earlier, later):
    return (earlier[0] * later[0], later[0][:, None, None] * earlier[1] + later[1])


def norm_forward(full_rows, gain_row):
    values = full_rows.astype(jnp.float32)
    scale = lax.rsqrt(jnp.mean(values * values, axis=-1, keepdims=True) + epsilon)
    normed = values * scale
    return (normed, scale, (normed * gain_row.astype(jnp.float32)).astype(jnp.bfloat16))


def norm_backward(summed, normed_full, scale, gain, column, quarter):
    normed_part = lax.dynamic_slice_in_dim(normed_full, column, quarter, 1)
    gain_grad = jnp.sum(summed * normed_part, axis=0)
    weighted = summed * gain.astype(jnp.float32)[None, :]
    cross = tensor_sums(jnp.sum(weighted * normed_part, axis=1))
    return (scale * (weighted - normed_part * (cross / D)[:, None]), gain_grad)


def conv_act(rows_ext, weights, same_doc):
    count = rows_ext.shape[0] - (CONV - 1)
    total = jnp.zeros((count, rows_ext.shape[1]), jnp.float32)
    for offset in range(CONV):
        total = total + jnp.where(
            same_doc[offset][:, None], rows_ext[offset : offset + count] * weights[offset], 0.0
        )
    return jax.nn.silu(total)


def end_terms(keys_state, scaled, running, at_end, link):
    toward_end = jnp.exp(running[-1:, :] - running) * at_end[:, None]
    state_local = jnp.einsum("th,thp,tn->hpn", toward_end, scaled, keys_state, precision=highest)
    through = jnp.exp(running[-1]) * link[-1]
    return (state_local, through)


def mixer_scan(
    signal, keys_state, query_state, step_size, decay_rate, state_in, allowed, at_end, link
):
    running = jnp.cumsum(step_size * decay_rate[None, :], axis=0)
    scaled = signal * step_size[:, :, None]
    scores = jnp.where(allowed, jnp.dot(query_state, keys_state.T, precision=highest), 0.0)

    def one_head(columns):
        running_col, scaled_col = columns
        spread = jnp.where(allowed, running_col[:, None] - running_col[None, :], 0.0)
        return jnp.dot(jnp.exp(spread) * scores, scaled_col, precision=highest)

    inner = lax.map(one_head, (running.T, scaled.transpose(1, 0, 2))).transpose(1, 0, 2)
    weight = jnp.exp(running) * link[:, None]
    carried = (
        jnp.einsum("tn,hpn->thp", query_state, state_in, precision=highest) * weight[:, :, None]
    )
    state_local, through = end_terms(keys_state, scaled, running, at_end, link)
    return (inner + carried, through[:, None, None] * state_in + state_local)


def local(
    block_input,
    gain_input,
    proj_main,
    proj_state,
    proj_step,
    conv_main,
    conv_state,
    step_bias,
    decay_log,
    skip_gain,
    gain_gate,
    proj_out,
    gain_mix,
    router_weight,
    shared_gates,
    shared_down,
    expert_gates,
    expert_down,
    segments,
    routes,
    cotangent,
):
    tokens_here = block_input.shape[0]
    quarter = block_input.shape[1]
    heads_here = step_bias.shape[0]
    inner_here = conv_main.shape[1]
    state_width = conv_state.shape[1] // 2
    head_width = inner_here // heads_here
    top_count = routes.shape[1]
    local_experts = expert_gates.shape[0]
    senders = lax.axis_size(("shard", "ctx"))
    experts_all = local_experts * senders
    capacity = 2 * tokens_here * top_count // experts_all
    column = lax.axis_index("tensor") * quarter
    leader = lax.axis_index("tensor") == 0
    gates_local, down_local = (expert_gates, expert_down)
    slot_low = jnp.int32(0)
    hidden_width = gates_local.shape[3]
    main_full, state_full, step_full, out_full, router_full, shared_gates_full, shared_down_full = (
        gather_weights(
            proj_main, proj_state, proj_step, proj_out, router_weight, shared_gates, shared_down
        )
    )
    input_full, gain_row = gather_features(block_input, gain_input)
    normed_one, scale_one, mixed_one = norm_forward(input_full, gain_row)
    main_flat = main_full.reshape(D, -1)
    main_value = dot_rows(mixed_one, main_flat).reshape(tokens_here, 2, inner_here)
    state_value = dot_rows(mixed_one, state_full)
    step_raw = dot_rows(mixed_one, step_full)
    gate_z = main_value[:, 0]
    conv_rows = jnp.concatenate([main_value[:, 1], state_value], axis=1)
    seg_row = segments[0]
    halo_rows, halo_segments = shifted(
        (conv_rows[tokens_here - CONV + 1 :], seg_row[tokens_here - CONV + 1 :]), "ctx", 1
    )
    rows_ext = jnp.concatenate([halo_rows, conv_rows], axis=0)
    segments_ext = jnp.concatenate([halo_segments, seg_row], axis=0)
    same_doc = jnp.stack(
        [segments_ext[offset : offset + tokens_here] == seg_row for offset in range(CONV)]
    )
    conv_weights = jnp.concatenate([conv_main, conv_state], axis=1).astype(jnp.float32)
    convolved, conv_pull = jax.vjp(partial(conv_act, same_doc=same_doc), rows_ext, conv_weights)
    activated = convolved.astype(jnp.bfloat16)
    signal_f = (
        activated[:, :inner_here].astype(jnp.float32).reshape(tokens_here, heads_here, head_width)
    )
    keys_f = activated[:, inner_here : inner_here + state_width].astype(jnp.float32)
    query_f = activated[:, inner_here + state_width :].astype(jnp.float32)
    step_sum = step_raw + step_bias[None, :]
    step_size = jax.nn.softplus(step_sum)
    decay_rate = -jnp.exp(decay_log)
    link = (seg_row == halo_segments[-1]).astype(jnp.float32)
    at_end = (seg_row == seg_row[-1]).astype(jnp.float32)
    positions = jnp.arange(tokens_here)
    allowed = (positions[:, None] >= positions[None, :]) & (seg_row[:, None] == seg_row[None, :])
    running = jnp.cumsum(step_size * decay_rate[None, :], axis=0)
    state_local, through = end_terms(
        keys_f, signal_f * step_size[:, :, None], running, at_end, link
    )
    identity = (jnp.ones_like(through), jnp.zeros_like(state_local))
    through_in, state_in = prefix((through, state_local), "ctx", chain_join, identity, False)
    scan_fn = partial(mixer_scan, allowed=allowed, at_end=at_end, link=link)
    scan_pair, scan_pull = jax.vjp(
        scan_fn, signal_f, keys_f, query_f, step_size, decay_rate, state_in
    )
    mixed_heads = scan_pair[0] + skip_gain[None, :, None] * signal_f
    mixer_flat = mixed_heads.reshape(tokens_here, inner_here)
    gate_act = jax.nn.silu(gate_z)
    gated = mixer_flat * gate_act
    gated_total = tensor_sums(jnp.sum(gated * gated, axis=1))
    gated_scale = lax.rsqrt(gated_total / DI + epsilon)
    gain_gate_f = gain_gate.astype(jnp.float32)
    gated_out = (gated * gated_scale[:, None] * gain_gate_f[None, :]).astype(jnp.bfloat16)
    mixer_sum = head_sums(dot_outer(gated_out, out_full))
    residual = (block_input.astype(jnp.float32) + mixer_sum).astype(jnp.bfloat16)
    middle_full, gain_mid = gather_features(residual, gain_mix)
    normed_two, scale_two, mixed_two = norm_forward(middle_full, gain_mid)
    logits = dot_rows(mixed_two, router_full)
    gates = jax.nn.softmax(jnp.take_along_axis(logits, routes, axis=1), axis=1)
    shared_value = dot_rows(mixed_two, shared_gates_full.reshape(D, -1)).reshape(tokens_here, 2, -1)
    shared_hidden = (jax.nn.silu(shared_value[:, 0]) * shared_value[:, 1]).astype(jnp.bfloat16)
    shared_part = dot_outer(shared_hidden, shared_down_full)
    flat_routes = routes.reshape(-1)
    expert_ids = jnp.arange(experts_all, dtype=jnp.int32)
    hits = (flat_routes[:, None] == expert_ids[None, :]).astype(jnp.int32)
    ranks = jnp.sum((jnp.cumsum(hits, axis=0) - 1) * hits, axis=1)
    rank_grid = ranks.reshape(tokens_here, top_count)
    owned = ((rank_grid >= slot_low) & (rank_grid < slot_low + capacity)).astype(jnp.float32)
    local_rank = jnp.clip(rank_grid, 0, capacity - 1)
    dispatch = (
        jnp.zeros((experts_all, capacity, D), jnp.bfloat16)
        .at[flat_routes, ranks]
        .set(jnp.repeat(mixed_two, top_count, axis=0))
    )
    arrived = route_out(dispatch.reshape(-1, D)).reshape(senders, local_experts, capacity, D)
    gates_flat = gates_local.reshape(local_experts, D, -1)
    expert_value = jnp.einsum(
        "secd,edf->secf", arrived, gates_flat, preferred_element_type=jnp.float32
    ).reshape(senders, local_experts, capacity, 2, hidden_width)
    expert_first = expert_value[:, :, :, 0]
    expert_second = expert_value[:, :, :, 1]
    expert_hidden = (jax.nn.silu(expert_first) * expert_second).astype(jnp.bfloat16)
    expert_part = jnp.einsum(
        "secf,efd->secd", expert_hidden, down_local, preferred_element_type=jnp.float32
    )
    returned = route_back(expert_part.reshape(-1, D)).reshape(experts_all, capacity, D)
    picked = returned[routes, local_rank] * owned[:, :, None]
    routed_part = jnp.sum(gates[:, :, None] * picked, axis=1)
    block_sum = head_sums(routed_part + shared_part)
    output = (residual.astype(jnp.float32) + block_sum).astype(jnp.bfloat16)
    cot_full = gather_grads(cotangent)
    cot_float = cot_full.astype(jnp.float32)
    grad_shared_down = dot_inner(cot_full, shared_hidden)
    shared_hidden_grad = dot_rows(cot_full, shared_down_full)
    shared_first = shared_value[:, 0]
    shared_second = shared_value[:, 1]
    shared_value_grad = (
        jnp.stack(
            [
                shared_hidden_grad * shared_second * silu_grad(shared_first),
                shared_hidden_grad * jax.nn.silu(shared_first),
            ],
            axis=1,
        )
        .astype(jnp.bfloat16)
        .reshape(tokens_here, -1)
    )
    grad_shared_gates = dot_inner(mixed_two, shared_value_grad).reshape(shared_gates_full.shape)
    mixed_two_grad = dot_outer(shared_value_grad, shared_gates_full.reshape(D, -1))
    gate_grad = tensor_sums(jnp.sum(picked * cot_float[:, None, :], axis=2))
    chosen_grad = gates * (gate_grad - jnp.sum(gates * gate_grad, axis=1, keepdims=True))
    route_hits = (routes[:, :, None] == expert_ids[None, None, :]).astype(jnp.float32)
    logits_grad = jnp.sum(chosen_grad[:, :, None] * route_hits, axis=1).astype(jnp.bfloat16)
    grad_router = dot_inner(mixed_two, logits_grad)
    router_back = dot_outer(logits_grad, router_full)
    spread_grad = (gates[:, :, None] * cot_float[:, None, :]).astype(jnp.bfloat16)
    grad_dispatch = (
        jnp.zeros((experts_all, capacity, D), jnp.bfloat16)
        .at[flat_routes, ranks]
        .set(spread_grad.reshape(-1, D))
    )
    arrived_grad = route_out(grad_dispatch.reshape(-1, D)).reshape(
        senders, local_experts, capacity, D
    )
    grad_down_here = jnp.einsum(
        "secf,secd->efd", expert_hidden, arrived_grad, preferred_element_type=jnp.float32
    )
    hidden_grad = jnp.einsum(
        "secd,efd->secf", arrived_grad, down_local, preferred_element_type=jnp.float32
    )
    value_grad = (
        jnp.stack(
            [
                hidden_grad * expert_second * silu_grad(expert_first),
                hidden_grad * jax.nn.silu(expert_first),
            ],
            axis=3,
        )
        .astype(jnp.bfloat16)
        .reshape(senders, local_experts, capacity, -1)
    )
    grad_gates_here = jnp.einsum(
        "secd,secf->edf", arrived, value_grad, preferred_element_type=jnp.float32
    ).reshape(gates_local.shape)
    arrived_back = jnp.einsum(
        "secf,edf->secd", value_grad, gates_flat, preferred_element_type=jnp.float32
    )
    returned_grad = route_back(arrived_back.reshape(-1, D)).reshape(experts_all, capacity, D)
    expert_input_grad = jnp.sum(returned_grad[routes, local_rank] * owned[:, :, None], axis=1)
    grad_expert_gates, grad_expert_down = (grad_gates_here, grad_down_here)
    mixed_two_grad = mixed_two_grad + expert_input_grad + jnp.where(leader, router_back, 0.0)
    mixed_two_sum = head_sums(mixed_two_grad)
    residual_norm_grad, grad_gain_mix = norm_backward(
        mixed_two_sum, normed_two, scale_two, gain_mix, column, quarter
    )
    residual_grad = cotangent.astype(jnp.float32) + residual_norm_grad
    mixer_grad_full = gather_grads(residual_grad.astype(jnp.bfloat16))
    grad_proj_out = dot_inner(mixer_grad_full, gated_out)
    gated_out_grad = dot_rows(mixer_grad_full, out_full)
    weighted = gated_out_grad * gain_gate_f[None, :]
    grad_gain_gate = jnp.sum(gated_out_grad * gated * gated_scale[:, None], axis=0)
    cross = tensor_sums(jnp.sum(weighted * gated, axis=1))
    cube = gated_scale * gated_scale * gated_scale
    gated_grad = gated_scale[:, None] * weighted - gated * (cube * cross / DI)[:, None]
    heads_grad = (gated_grad * gate_act).reshape(tokens_here, heads_here, head_width)
    gate_z_grad = gated_grad * mixer_flat * silu_grad(gate_z)
    grad_skip = jnp.sum(heads_grad * signal_f, axis=(0, 2))
    direct = jnp.einsum(
        "thp,tn,th->hpn", heads_grad, query_f, jnp.exp(running) * link[:, None], precision=highest
    )
    through_out, state_out_grad = prefix((through, direct), "ctx", chain_join, identity, True)
    signal_grad, keys_grad, query_grad, step_grad, rate_grad, state_in_grad = scan_pull(
        (heads_grad, state_out_grad)
    )
    signal_grad = signal_grad + skip_gain[None, :, None] * heads_grad
    state_grads = tensor_sums(jnp.concatenate([keys_grad, query_grad], axis=1))
    act_grad = jnp.concatenate([signal_grad.reshape(tokens_here, -1), state_grads], axis=1)
    rows_ext_grad, conv_weights_grad = conv_pull(act_grad)
    halo_grad = shifted(rows_ext_grad[: CONV - 1], "ctx", -1)
    rows_grad = rows_ext_grad[CONV - 1 :] + jnp.pad(
        halo_grad, ((tokens_here - CONV + 1, 0), (0, 0))
    )
    step_raw_grad = step_grad * jax.nn.sigmoid(step_sum)
    grad_step_bias = jnp.sum(step_raw_grad, axis=0)
    grad_decay_log = rate_grad * decay_rate
    main_grad = (
        jnp.stack([gate_z_grad, rows_grad[:, :inner_here]], axis=1)
        .astype(jnp.bfloat16)
        .reshape(tokens_here, -1)
    )
    state_value_grad = rows_grad[:, inner_here:].astype(jnp.bfloat16)
    step_low = step_raw_grad.astype(jnp.bfloat16)
    grad_proj_main = dot_inner(mixed_one, main_grad).reshape(main_full.shape)
    grad_proj_state = dot_inner(mixed_one, state_value_grad)
    grad_proj_step = dot_inner(mixed_one, step_low)
    mixed_one_grad = (
        dot_outer(main_grad, main_flat)
        + dot_outer(step_low, step_full)
        + jnp.where(leader, dot_outer(state_value_grad, state_full), 0.0)
    )
    mixed_one_sum = head_sums(mixed_one_grad)
    input_norm_grad, grad_gain_input = norm_backward(
        mixed_one_sum, normed_one, scale_one, gain_input, column, quarter
    )
    grad_input = residual_grad + input_norm_grad
    summed = (
        lax.psum_scatter(
            grad_proj_main.astype(jnp.bfloat16), ("shard", "ctx"), scatter_dimension=0, tiled=True
        ).astype(jnp.float32),
        lax.psum_scatter(
            grad_proj_state.astype(jnp.bfloat16), ("shard", "ctx"), scatter_dimension=0, tiled=True
        ).astype(jnp.float32),
        lax.psum_scatter(
            grad_proj_step.astype(jnp.bfloat16), ("shard", "ctx"), scatter_dimension=0, tiled=True
        ).astype(jnp.float32),
        lax.psum_scatter(
            grad_proj_out.astype(jnp.bfloat16), ("shard", "ctx"), scatter_dimension=0, tiled=True
        ).astype(jnp.float32),
        lax.psum_scatter(
            grad_router.astype(jnp.bfloat16), ("shard", "ctx"), scatter_dimension=0, tiled=True
        ).astype(jnp.float32),
        lax.psum_scatter(
            grad_shared_gates.astype(jnp.bfloat16),
            ("shard", "ctx"),
            scatter_dimension=0,
            tiled=True,
        ).astype(jnp.float32),
        lax.psum_scatter(
            grad_shared_down.astype(jnp.bfloat16), ("shard", "ctx"), scatter_dimension=0, tiled=True
        ).astype(jnp.float32),
    )
    small = lax.psum(
        (
            grad_gain_input,
            conv_weights_grad,
            grad_step_bias,
            grad_decay_log,
            grad_skip,
            grad_gain_gate,
            grad_gain_mix,
        ),
        ("shard", "ctx"),
    )
    conv_summed = small[1]
    return (
        output,
        grad_input,
        small[0],
        summed[0],
        summed[1],
        summed[2],
        conv_summed[:, :inner_here],
        conv_summed[:, inner_here:],
        small[2],
        small[3],
        small[4],
        small[5],
        summed[3],
        small[6],
        summed[4],
        summed[5],
        summed[6],
        grad_expert_gates,
        grad_expert_down,
    )


def solution(mesh):
    return jax.shard_map(
        local,
        mesh=mesh,
        in_specs=(
            P(("shard", "ctx"), "tensor"),
            P("tensor"),
            P(("shard", "ctx"), None, "tensor"),
            P(("shard", "ctx"), None),
            P(("shard", "ctx"), "tensor"),
            P(None, "tensor"),
            P(),
            P("tensor"),
            P("tensor"),
            P("tensor"),
            P("tensor"),
            P(("shard", "ctx"), "tensor"),
            P("tensor"),
            P(("shard", "ctx"), None),
            P(("shard", "ctx"), None, "tensor"),
            P(("shard", "ctx"), "tensor"),
            P(("shard", "ctx"), None, None, "tensor"),
            P(("shard", "ctx"), "tensor", None),
            P("shard", "ctx"),
            P(("shard", "ctx"), None),
            P(("shard", "ctx"), "tensor"),
        ),
        out_specs=(
            P(("shard", "ctx"), "tensor"),
            P(("shard", "ctx"), "tensor"),
            P("tensor"),
            P(("shard", "ctx"), None, "tensor"),
            P(("shard", "ctx"), None),
            P(("shard", "ctx"), "tensor"),
            P(None, "tensor"),
            P(),
            P("tensor"),
            P("tensor"),
            P("tensor"),
            P("tensor"),
            P(("shard", "ctx"), "tensor"),
            P("tensor"),
            P(("shard", "ctx"), None),
            P(("shard", "ctx"), None, "tensor"),
            P(("shard", "ctx"), "tensor"),
            P(("shard", "ctx"), None, None, "tensor"),
            P(("shard", "ctx"), "tensor", None),
        ),
        check_vma=False,
    )
```

profile of v0, /device:TPU:0, one launch (start us, length us, event | category | flops | bytes accessed | tf_op | source)
XLA Modules:
  0.0 2734.6 jit_solution(16933484615114304580)
XLA Ops:
  58.0 32.0 %all-gather.21.cloned.1.call-done = bf16[1536,2,768]{2,0,1:T(8,128)(2,1)} async-done(((bf16[192,2,768]{2,0,1:T(8,128)(2,1)}), bf16[1536,2,768]{2,0,1:T(8,128)(2,1)}) %all-gather.21.cloned.1.call-update) | async-done | bytes 4718608 | tf_op jit(solution)/shard_map/all_gather | solution.py:66
  132.9 56.6 %while.65 = (s32[]{:T(128)}, f32[12,512,64]{1,2,0:T(8,128)}, f32[12,512,512]{2,1,0:T(8,128)}, f32[12,512,512]{2,1,0:T(8,128)}, f32[12,512]{1,0:T(8,128)S(1)}, /*...) while((s32[]{:T(128)}, f32[12,512,64]{1,2,0:T(8,128)}, ...), condition=%wide.region_4.5_spmd.clone, body=%wide.region_3.4_spmd.clone.sunk | while | flops 204472320 | bytes 4609133 | solution.py:151
  225.4 58.3 %reduce-scatter.18.cloned.1.call-done = f32[512,384]{1,0:T(8,128)} async-done(((f32[512,1536]{1,0:T(8,128)}), f32[512,384]{1,0:T(8,128)}) %reduce-scatter.18.cloned.1.call-update) | async-done | bytes 786448 | tf_op jit(solution)/shard_map/reduce_scatter | solution.py:88
  348.5 26.1 scatter_custom_fusion
  381.3 209.0 %all-gather.8 = bf16[8,192,16]{1,2,0:T(8,128)(2,1)S(1)} all-gather(bf16[1,192,16]{1,2,0:T(8,128)(2,1)S(1)} %bitcast.490), channel_id=1, replica_groups=mesh['shard'=2,'ctx'=4,'tensor'=4] {'shard','ctx'}, dimensions={0}, use_global_device_ids=true | all-gather | bytes 55296 | tf_op jit(solution)/shard_map/all_gather | solution.py:70
  624.8 24.9 gather_fusion.2
  650.5 40.1 %scatter_custom_fusion.1 = bf16[6144,1536]{1,0:T(8,128)(2,1)} fusion(s32[3072]{0:T(1024)S(1)} %broadcast_select_fusion, f32[3072,1536]{1,0:T(8,128)} %mul.729, bf16[]{:T(256)} %constant.234.clone.1, f32[3072]{0:T(1024)S(1)} %mul.726), kind=kCustom, calls=%fused_computation.67 | custom fusion | flops 9437184 | bytes 37761024
  712.6 189.6 %all-to-all-done.2 = bf16[8,768,1536]{2,1,0:T(8,128)(2,1)} async-done(((bf16[8,768,1536]{2,1,0:T(8,128)(2,1)}), bf16[8,768,1536]{2,1,0:T(8,128)(2,1)}, u32[]{:S(2)}, u32[]{:S(2)}) %all-to-all-start.2) | async-done | bytes 18874400 | tf_op jit(solution)/shard_map/all_to_all | solution.py:96
  933.8 28.4 %copy.390 = f32[8,2,384,1536]{3,2,1,0:T(8,128)} copy(f32[8,2,384,1536]{3,2,0,1:T(8,128)} %convolution_bitcast_fusion.3) | data formatting | bytes 75497472 | tf_op jit(solution)/shard_map/secf,edf->secd/transpose | solution.py:345
  984.4 28.4 %copy.378 = f32[8,2,384,1536]{3,2,1,0:T(8,128)} copy(f32[8,2,384,1536]{3,2,0,1:T(8,128)} %convolution_bitcast_fusion.2) | data formatting | bytes 75497472 | tf_op jit(solution)/shard_map/secf,efd->secd/transpose | solution.py:283
  1012.9 364.6 %all-to-all-done.3 = f32[8,768,1536]{2,1,0:T(8,128)} async-done(((f32[8,768,1536]{2,1,0:T(8,128)}), f32[8,768,1536]{2,1,0:T(8,128)}, u32[]{:S(2)}, u32[]{:S(2)}) %all-to-all-start.3) | async-done | bytes 37748768 | tf_op jit(solution)/shard_map/all_to_all | solution.py:100
  1387.2 417.8 %all_gather.70 = bf16[1536,256]{1,0:T(8,128)(2,1)S(1)} all-gather(bf16[192,256]{1,0:T(8,128)(2,1)S(1)} %copy-done.75), channel_id=1, replica_groups=mesh['shard'=2,'ctx'=4,'tensor'=4] {'shard','ctx'}, dimensions={0}, use_global_device_ids=true | all-gather | bytes 884736 | tf_op jit(solution)/shard_map/all_gather | solution.py:72
  1814.0 67.9 %gather_fusion.1 = f32[3072,1536]{1,0:T(8,128)} fusion(f32[16,384,1536]{2,1,0:T(8,128)} %bitcast.64, s32[3072]{0:T(1024)S(1)} %reshape.594), kind=kCustom, calls=%fused_computation.1 | custom fusion | bytes 37773312 | tf_op jit(solution)/shard_map/gather | solution.py:349
  1903.1 68.0 %gather_fusion = f32[3072,1536]{1,0:T(8,128)} fusion(f32[16,384,1536]{2,1,0:T(8,128)} %bitcast.43, s32[3072]{0:T(1024)S(1)} %reshape.594), kind=kCustom, calls=%fused_computation | custom fusion | bytes 37773312 | tf_op jit(solution)/shard_map/gather | solution.py:287
  1992.5 28.6 %multiply_reduce_fusion = (f32[512,6]{1,0:T(8,128)S(1)}, f32[512,1536]{1,0:T(8,128)}, f32[512,1536]{1,0:T(8,128)}) fusion(f32[512,6,1536]{2,1,0:T(8,128)} %reshape.597, f32[512,1536]{1,0:T(8,128)} %convert_element_type.193, f32[512,6]{1,0:T(8,128)S(1)} %copy-done.49, f32[512,6]{1,0:T(8,128)S(1)} %copy-done.42, f32[512,6,1536]{2,1,0:T(8,128)} %reshape.603), kind=kLoop, calls=%fused_computation.55 | loop fusion | flops 31454208 | bytes 47222784 | tf_op jit(solution)/shard_map/reduce_sum | solution.py:310
  2043.8 57.0 %reduce-scatter.22.cloned.1.call-done = f32[512,384]{1,0:T(8,128)} async-done(((f32[512,1536]{1,0:T(8,128)}), f32[512,384]{1,0:T(8,128)}) %reduce-scatter.22.cloned.1.call-update) | async-done | bytes 786448 | tf_op jit(solution)/shard_map/reduce_scatter | solution.py:88
  2115.3 35.5 %all-gather.31.cloned.1.call-done = bf16[512,1536]{1,0:T(8,128)(2,1)} async-done(((bf16[512,384]{1,0:T(8,128)(2,1)}), bf16[512,1536]{1,0:T(8,128)(2,1)}) %all-gather.31.cloned.1.call-update) | async-done | bytes 1572880 | tf_op jit(solution)/shard_map/all_gather | solution.py:84
  2177.7 69.1 %while.68 = (s32[]{:T(128)}, f32[512,512]{1,0:T(8,128)S(1)}, f32[12,512]{1,0:T(8,128)S(1)}, f32[12,512,64]{1,2,0:T(8,128)}, f32[12,512,512]{2,1,0:T(8,128)}, /*i...) while((s32[]{:T(128)}, f32[512,512]{1,0:T(8,128)S(1)}, ...), condition=%wide.region_35.36_spmd.clone, body=%wide.region_32.35_spmd.clone.sunk | while | flops 405536768 | bytes 8017566 | solution.py:151
  2345.4 38.4 %reduce-scatter.32.cloned.1.call-done = bf16[192,2,256]{2,0,1:T(8,128)(2,1)} async-done(((bf16[1536,2,256]{2,0,1:T(8,128)(2,1)}), bf16[192,2,256]{2,0,1:T(8,128)(2,1)}) %reduce-scatter.32.cloned.1.call-update) | async-done | bytes 196624 | tf_op jit(solution)/shard_map/reduce_scatter | solution.py:422
  2422.0 60.9 %reduce-scatter.20.cloned.1.call-done = f32[512,384]{1,0:T(8,128)} async-done(((f32[512,1536]{1,0:T(8,128)}), f32[512,384]{1,0:T(8,128)}) %reduce-scatter.20.cloned.1.call-update) | async-done | bytes 786448 | tf_op jit(solution)/shard_map/reduce_scatter | solution.py:88
  2485.1 34.7 %reduce-scatter.34.cloned.1.call-done = bf16[192,12]{1,0:T(8,128)(2,1)} async-done(((bf16[1536,12]{1,0:T(8,128)(2,1)}), bf16[192,12]{1,0:T(8,128)(2,1)}) %reduce-scatter.34.cloned.1.call-update) | async-done | bytes 4624
  2521.3 44.2 %reduce-scatter.30.cloned.1.call-done = bf16[192,768]{1,0:T(8,128)(2,1)} async-done(((bf16[1536,768]{1,0:T(8,128)(2,1)}), bf16[192,768]{1,0:T(8,128)(2,1)}) %reduce-scatter.30.cloned.1.call-update) | async-done | bytes 294928 | tf_op jit(solution)/shard_map/reduce_scatter | solution.py:416
  2567.3 37.2 %reduce-scatter.28.cloned.1.call-done = bf16[192,256]{1,0:T(8,128)(2,1)} async-done(((bf16[1536,256]{1,0:T(8,128)(2,1)}), bf16[192,256]{1,0:T(8,128)(2,1)}) %reduce-scatter.28.cloned.1.call-update) | async-done | bytes 98320 | tf_op jit(solution)/shard_map/reduce_scatter | solution.py:410
  2606.2 61.0 %reduce-scatter.24.cloned.1.call-done = f32[512,384]{1,0:T(8,128)} async-done(((f32[512,1536]{1,0:T(8,128)}), f32[512,384]{1,0:T(8,128)}) %reduce-scatter.24.cloned.1.call-update) | async-done | bytes 786448 | tf_op jit(solution)/shard_map/reduce_scatter | solution.py:88
  (654 shorter events, 780.1 us)
Async XLA Ops:
  8.0 81.9 %all-gather.21.cloned.1.call-start = ((), (), s32[]{:S(2)}) async-start(), calls=%async_computation.16 | async-start | bytes 5308416 | tf_op jit(solution)/shard_map/all_gather | solution.py:66
  10.0 179.5 %all-gather.33.cloned.1.call-start = ((), (), s32[]{:S(2)}) async-start(), calls=%async_computation.31 | async-start | bytes 1966080 | tf_op jit(solution)/shard_map/all_gather | solution.py:25
  114.9 105.0 %all-gather.23.cloned.1.call-start = ((), (), s32[]{:S(2)}) async-start(), calls=%async_computation.17 | async-start | bytes 2654208 | tf_op jit(solution)/shard_map/all_gather | solution.py:69
  115.5 168.1 %reduce-scatter.18.cloned.1.call-start = ((), (), s32[]{:S(2)}) async-start(), calls=%async_computation.18 | async-start | bytes 3932160 | tf_op jit(solution)/shard_map/reduce_scatter | solution.py:88
  225.3 97.7 %all-gather.25.cloned.1.call-start = ((), (), s32[]{:S(2)}) async-start(), calls=%async_computation.19 | async-start | bytes 1966080 | tf_op jit(solution)/shard_map/all_gather | solution.py:78
  374.6 316.0 %all-to-all-start = ((bf16[8,768,1536]{2,1,0:T(8,128)(2,1)}), bf16[8,768,1536]{2,1,0:T(8,128)(2,1)}, u32[]{:S(2)}, u32[]{:S(2)}) async-start(bf16[8,768,1536]{2,1,0:T(8,128)(2,1)} %bitcast.440), calls=%async_computation.1 | async-start | bytes 37748736 | tf_op jit(solution)/shard_map/all_to_all | solution.py:96
  380.5 211.2 %all-gather.29.cloned.1.call-start = ((), (), s32[]{:S(2)}) async-start(), calls=%async_computation.22 | async-start | bytes 1966080 | tf_op jit(solution)/shard_map/all_gather | solution.py:84
  690.6 211.5 %all-to-all-start.2 = ((bf16[8,768,1536]{2,1,0:T(8,128)(2,1)}), bf16[8,768,1536]{2,1,0:T(8,128)(2,1)}, u32[]{:S(2)}, u32[]{:S(2)}) async-start(bf16[8,768,1536]{2,1,0:T(8,128)(2,1)} %bitcast.441), calls=%async_computation.4 | async-start | bytes 37748736 | tf_op jit(solution)/shard_map/all_to_all | solution.py:96
  962.2 415.3 %all-to-all-start.3 = ((f32[8,768,1536]{2,1,0:T(8,128)}), f32[8,768,1536]{2,1,0:T(8,128)}, u32[]{:S(2)}, u32[]{:S(2)}) async-start(f32[8,768,1536]{2,1,0:T(8,128)} %bitcast.439), calls=%async_computation.5 | async-start | bytes 75497472 | tf_op jit(solution)/shard_map/all_to_all | solution.py:100
  1377.5 525.7 %all-to-all-start.1 = ((f32[8,768,1536]{2,1,0:T(8,128)}), f32[8,768,1536]{2,1,0:T(8,128)}, u32[]{:S(2)}, u32[]{:S(2)}) async-start(f32[8,768,1536]{2,1,0:T(8,128)} %bitcast.438), calls=%async_computation.2 | async-start | bytes 75497472 | tf_op jit(solution)/shard_map/all_to_all | solution.py:100
  1385.1 422.0 %all-gather.27.cloned.1.call-start = ((), (), s32[]{:S(2)}) async-start(), calls=%async_computation.20 | async-start | bytes 1769472 | tf_op jit(solution)/shard_map/all_gather | solution.py:71
  1385.9 714.9 %reduce-scatter.22.cloned.1.call-start = ((), (), s32[]{:S(2)}) async-start(), calls=%async_computation.23 | async-start | bytes 3932160 | tf_op jit(solution)/shard_map/reduce_scatter | solution.py:88
  2043.1 107.7 %all-gather.31.cloned.1.call-start = ((), (), s32[]{:S(2)}) async-start(), calls=%async_computation.24 | async-start | bytes 1966080 | tf_op jit(solution)/shard_map/all_gather | solution.py:84
  2115.2 137.9 %all-gather.35.cloned.1.call-start = ((), (), s32[]{:S(2)}) async-start(), calls=%async_computation.32 | async-start | bytes 1966080 | tf_op jit(solution)/shard_map/all_gather | solution.py:25
  2176.2 135.4 %all-reduce.14.cloned.1.call-start = ((), (), s32[]{:S(2)}) async-start(), calls=%async_computation.25 | async-start | bytes 1048576 | tf_op jit(solution)/shard_map/psum | solution.py:92
  2267.2 76.4 %reduce-scatter.38.cloned.1.call-start = ((), (), s32[]{:S(2)}) async-start(), calls=%async_computation.35 | async-start | bytes 884736
  2272.8 111.0 %reduce-scatter.32.cloned.1.call-start = ((), (), s32[]{:S(2)}) async-start(), calls=%async_computation.30 | async-start | bytes 1769472 | tf_op jit(solution)/shard_map/reduce_scatter | solution.py:422
  2276.0 144.5 %reduce-scatter.36.cloned.1.call-start = ((), (), s32[]{:S(2)}) async-start(), calls=%async_computation.34 | async-start | bytes 442368
  2277.4 205.6 %reduce-scatter.20.cloned.1.call-start = ((), (), s32[]{:S(2)}) async-start(), calls=%async_computation.21 | async-start | bytes 3932160 | tf_op jit(solution)/shard_map/reduce_scatter | solution.py:88
  2282.3 237.5 %reduce-scatter.34.cloned.1.call-start = ((), (), s32[]{:S(2)}) async-start(), calls=%async_computation.33 | async-start | bytes 442368
  2298.7 266.8 %reduce-scatter.30.cloned.1.call-start = ((), (), s32[]{:S(2)}) async-start(), calls=%async_computation.29 | async-start | bytes 2654208 | tf_op jit(solution)/shard_map/reduce_scatter | solution.py:416
  2303.1 301.5 %reduce-scatter.28.cloned.1.call-start = ((), (), s32[]{:S(2)}) async-start(), calls=%async_computation.28 | async-start | bytes 884736 | tf_op jit(solution)/shard_map/reduce_scatter | solution.py:410
  2322.2 344.9 %reduce-scatter.24.cloned.1.call-start = ((), (), s32[]{:S(2)}) async-start(), calls=%async_computation.26 | async-start | bytes 3932160 | tf_op jit(solution)/shard_map/reduce_scatter | solution.py:88
  2330.5 394.4 %reduce-scatter.26.cloned.1.call-start = ((), (), s32[]{:S(2)}) async-start(), calls=%async_computation.27 | async-start | bytes 5308416 | tf_op jit(solution)/shard_map/reduce_scatter | solution.py:407
  (132 other events, 5293.0 us)
Sparse Core Ops, SparseCore 0:
  9.7 39.7 all-gather.18
  52.0 37.9 all-gather.20
  115.0 21.7 all-gather.32
  138.5 29.0 all-gather.22
  225.4 58.1 reduce-scatter.17
  285.7 37.2 all-gather.24
  382.9 36.4 all-gather.28
  1388.4 38.1 all-gather.26
  2043.3 57.4 reduce-scatter.21
  2115.4 35.4 all-gather.30
  2176.3 17.9 all-gather.34
  2267.4 36.5 all-reduce.13
  2307.1 34.9 reduce-scatter.37
  2345.3 38.4 reduce-scatter.31
  2386.7 33.8 reduce-scatter.35
  2422.7 60.2 reduce-scatter.19
  2485.9 33.8 reduce-scatter.33
  2523.0 42.4 reduce-scatter.29
  2569.6 34.9 reduce-scatter.27
  2606.8 60.2 reduce-scatter.23
  2670.9 53.8 reduce-scatter.25
where the time goes:
time: 2740 us; the launch traced here: 2730 us
  waiting for transfers between devices  1060 us (39%)
  blocking collectives  762 us (28%)
  local copies, waits for them, and re-layouts  418 us (15%)
  matrix products  268 us (10%)
  other arithmetic  174 us (6%)
  starting transfers between devices  34.4 us (1%)
    all_gather x1, blocking collectives, gather_weights(): lax.all_gather(shared_down, ('shard', 'ctx'), axis=0, tiled=True)  418 us
    all_to_all x2, waiting for transfers between devices, route_back(): lax.all_to_all(rows, ('shard', 'ctx'), split_axis=0, concat_axis=0, tiled...  365 us
    reduce_scatter x4, waiting for transfers between devices, head_sums(): lax.psum_scatter(partial_rows, 'tensor', scatter_dimension=1, tiled=True)  237 us
    all_gather x1, blocking collectives, gather_weights(): lax.all_gather(router_weight, ('shard', 'ctx'), axis=0, tiled=True)  209 us
    all_to_all x2, waiting for transfers between devices, route_out(): lax.all_to_all(rows, ('shard', 'ctx'), split_axis=0, concat_axis=0, tiled...  190 us
    dot_general x36, matrix products, one_head(): return jnp.dot(jnp.exp(spread) * scores, scaled_col, precision=highest)  102 us
    gather x2, local copies, waits for them, and re-layouts, local(): picked = returned[routes, local_rank] * owned[:, :, None]  89.3 us
    gather x2, local copies, waits for them, and re-layouts, local(): returned_grad[routes, local_rank] * owned[:, :, None]  89.2 us
  transfers between devices with their start and end apart: 28, of which 18 were waited for; matrix products, arithmetic and copies ran while one was open for 20% of the time, Pallas kernels for 0%

commit v1 on v0

v1 whole, which is shorter than its diff:
```python
from functools import partial

import jax
import jax.numpy as jnp
from jax import lax
from jax.experimental import pallas as pl
from jax.experimental.pallas import tpu as pltpu
from jax.sharding import PartitionSpec as P

CONV = 4
HALO = 16
LANES = 128
LANES = 128
LANES = 128


epsilon = 1e-05
highest = lax.Precision.HIGHEST
ROWS = ("shard", "ctx")
EVERY = ("shard", "ctx", "tensor")
f32 = jnp.float32
bf16 = jnp.bfloat16
BIG = pltpu.CompilerParams(vmem_limit_bytes=56 << 20)


def cost(micros):
    return pl.CostEstimate(flops=micros * 900_000_000, transcendentals=0, bytes_accessed=1 << 20)
BIG = pltpu.CompilerParams(vmem_limit_bytes=56 << 20)


def cost(micros):
    return pl.CostEstimate(flops=micros * 900_000_000, transcendentals=0, bytes_accessed=1 << 20)
BIG = pltpu.CompilerParams(vmem_limit_bytes=56 << 20)


def cost(micros):
    return pl.CostEstimate(flops=micros * 900_000_000, transcendentals=0, bytes_accessed=1 << 20)


def shifted(value, axis, steps):
    count = lax.axis_size(axis)
    leading, last = (max(0, -steps), min(count, count - steps))
    return lax.ppermute(value, axis, [(source, source + steps) for source in range(leading, last)])


def dot_rows(left, right, precision=None):
    return jnp.dot(left, right, preferred_element_type=f32, precision=precision)


def dot_inner(left, right):
    return lax.dot_general(left, right, (((0,), (0,)), ((), ())), preferred_element_type=f32)


def dot_outer(left, right):
    return lax.dot_general(left, right, (((1,), (1,)), ((), ())), preferred_element_type=f32)


def sigmoid(value):
    return 1.0 / (1.0 + jnp.exp(-value))


def gather_rows(value):
    return lax.all_gather(value, ROWS, axis=0, tiled=True)


def scatter_rows(value):
    return lax.psum_scatter(value, ROWS, scatter_dimension=0, tiled=True)


def exchange(blocks):
    return lax.all_to_all(blocks, "tensor", split_axis=0, concat_axis=0, tiled=True)


def spread(block):
    count = lax.axis_size("tensor")
    return exchange(jnp.broadcast_to(block[None], (count,) + block.shape))


def spread_small(block):
    count, index = lax.axis_size("tensor"), lax.axis_index("tensor")
    width = block.shape[1]
    full = jnp.zeros((block.shape[0], count * width), block.dtype)
    for away in range(count):
        moved = block if away == 0 else lax.ppermute(
            block, "tensor", [(i, (i + away) % count) for i in range(count)]
        )
        origin = lax.rem(index - away + count, count)
        full = lax.dynamic_update_slice_in_dim(full, moved, origin * width, 1)
    return full


def halves(value):
    high = value.astype(bf16)
    return high, (value - high.astype(f32)).astype(bf16)


def chain(through, state, reverse):
    count = lax.axis_size("ctx")
    width = state.shape[0] // through.shape[0]
    packed = (through, state.astype(bf16))
    passed, total = None, None
    for away in range(1, count):
        far_through, far_state = jax.tree.map(
            lambda part: shifted(part, "ctx", -away if reverse else away), packed
        )
        far_state = far_state.astype(f32)
        if total is None:
            total, passed = far_state, far_through
        else:
            total = total + jnp.repeat(passed, width)[:, None] * far_state
            passed = passed * far_through
    return total


def row_iota(shape):
    return lax.broadcasted_iota(jnp.int32, shape, 0)


def col_iota(shape):
    return lax.broadcasted_iota(jnp.int32, shape, 1)


def expander(lanes, width, per):
    low = row_iota((lanes, width)) * per
    at = col_iota((lanes, width))
    return ((at >= low) & (at < low + per)).astype(f32)


def head_fold(width, lanes, per):
    low = col_iota((width, lanes)) * per
    at = row_iota((width, lanes))
    return ((at >= low) & (at < low + per)).astype(f32)


def fold_heads(value, folds):
    high, low = halves(value)
    return dot_rows(high, folds) + dot_rows(low, folds)


def conv_pre(value_ref, column, taps_ref, taps_column, same_ref, tokens):
    rows = value_ref[:, pl.ds(column, LANES)]
    total = None
    for offset in range(CONV):
        first = HALO - CONV + 1 + offset
        term = rows[first : first + tokens] * (
            same_ref[offset] * taps_ref[offset : offset + 1, pl.ds(taps_column, LANES)]
        )
        total = term if total is None else total + term
    return rows, total


def enter_kernel(mixed_ref, w_ref, taps_ref, same_ref, bias_ref, decay_ref, end_ref,
                 value_ref, act_ref, scaled_ref, step_ref, run_ref, run_exp_ref,
                 state_ref, *, inner, nstate, per):
    tokens = act_ref.shape[0]
    width = w_ref.shape[1]
    tile = 384

    def matmul(i, _):
        columns = pl.ds(pl.multiple_of(i * tile, LANES), tile)
        value_ref[:, columns] = dot_rows(mixed_ref[...], w_ref[:, columns])
        return 0

    lax.fori_loop(0, width // tile, matmul, 0)

    def conv(i, _):
        at = pl.multiple_of(i * LANES, LANES)
        _, total = conv_pre(value_ref, inner + at, taps_ref, at, same_ref, tokens)
        act_ref[:, pl.ds(at, LANES)] = (total * sigmoid(total)).astype(bf16)
        return 0

    lax.fori_loop(0, (inner + 2 * nstate) // LANES, conv, 0)
    raw = value_ref[HALO:, 2 * inner + 2 * nstate :] + bias_ref[...]
    step = jnp.maximum(raw, 0.0) + jnp.log1p(jnp.exp(-jnp.abs(raw)))
    log_decay = step * -jnp.exp(decay_ref[...])
    tri = (row_iota((tokens, tokens)) >= col_iota((tokens, tokens))).astype(f32)
    running = dot_rows(tri, log_decay, highest)
    step_ref[...] = step
    run_ref[...] = running
    grow = expander(LANES, inner, per)
    run_exp_ref[...] = dot_rows(running, grow, highest)
    signal = act_ref[:, :inner].astype(f32)
    scaled_ref[...] = (signal * dot_rows(step, grow, highest)).astype(bf16)
    toward = step * jnp.exp(running[tokens - 1 :] - running) * end_ref[...]
    pushed = (signal * dot_rows(toward, grow, highest)).astype(bf16)
    state_ref[...] = dot_inner(pushed, act_ref[:, inner : inner + nstate])


def enter(mixed_ext, main_w, taps, same, bias, decay, at_end, inner, nstate, per):
    ext = mixed_ext.shape[0]
    tokens = ext - HALO
    shape = jax.ShapeDtypeStruct
    return pl.pallas_call(
        partial(enter_kernel, inner=inner, nstate=nstate, per=per),
        out_shape=[
            shape((ext, main_w.shape[1]), f32), shape((tokens, inner + 2 * nstate), bf16),
            shape((tokens, inner), bf16), shape((tokens, LANES), f32), shape((tokens, LANES), f32),
            shape((tokens, inner), f32), shape((inner, nstate), f32),
        ],
        compiler_params=BIG,
        cost_estimate=cost(8),
        name="enter",
    )(mixed_ext, main_w, taps, same, bias, decay, at_end)


def masked_scores(query, keys, seg_col_ref, seg_row_ref, start, stop):
    shape = (stop - start, stop)
    allowed = (row_iota(shape) + start >= col_iota(shape)) & (
        seg_col_ref[start:stop, :1] == seg_row_ref[:, :stop]
    )
    return jnp.where(allowed, dot_outer(query[start:stop], keys[:stop]), 0.0)


def intra_kernel(act_ref, scaled_ref, run_t_ref, run_exp_ref, seg_col_ref, seg_row_ref,
                 inner_ref, scores_ref, *, inner, nstate, per, block):
    tokens = act_ref.shape[0]
    keys = act_ref[:, inner : inner + nstate]
    query = act_ref[:, inner + nstate :]
    for start in range(0, tokens, block):
        stop = start + block
        scores_ref[start:stop, :stop] = masked_scores(
            query, keys, seg_col_ref, seg_row_ref, start, stop
        )

    def pair(i, _):
        columns = pl.ds(pl.multiple_of(i * LANES, LANES), LANES)
        scaled = scaled_ref[:, columns]
        lane = col_iota(scaled.shape)
        run = run_exp_ref[:, columns]
        for start in range(0, tokens, block):
            stop = start + block
            total = None
            for h in range(LANES // per):
                mine = (lane >= h * per) & (lane < (h + 1) * per)
                vals = jnp.where(mine, scaled, jnp.zeros_like(scaled))[:stop]
                row = run_t_ref[i * (LANES // per) + h, :, :stop]
                decay = jnp.exp(jnp.minimum(run[start:stop, h * per : h * per + 1] - row, 0.0))
                weight = (decay * scores_ref[start:stop, :stop]).astype(bf16)
                term = dot_rows(weight, vals)
                total = term if total is None else total + term
            inner_ref[start:stop, columns] = total
        return 0

    lax.fori_loop(0, inner // LANES, pair, 0)


def intra(act, scaled, run_t, run_exp, seg_col, seg_row, inner, nstate, per):
    tokens = act.shape[0]
    return pl.pallas_call(
        partial(intra_kernel, inner=inner, nstate=nstate, per=per, block=128),
        out_shape=jax.ShapeDtypeStruct((tokens, inner), f32),
        scratch_shapes=[pltpu.VMEM((tokens, tokens), f32)],
        compiler_params=BIG,
        cost_estimate=cost(10),
        name="intra",
    )(act, scaled, run_t, run_exp, seg_col, seg_row)


def leave_kernel(act_ref, inner_ref, z_ref, state_ref, run_exp_ref, link_ref, skip_ref, gain_ref,
                 w_ref, mixer_ref, part_ref, *, inner, nstate):
    depth = w_ref.shape[0]
    tokens = act_ref.shape[0]
    query = act_ref[:, inner + nstate :]
    carried = dot_outer(query, state_ref[...].astype(bf16)) * (
        jnp.exp(run_exp_ref[...]) * link_ref[...]
    )
    mixer = inner_ref[...] + carried + skip_ref[...] * act_ref[:, :inner].astype(f32)
    mixer_ref[...] = mixer
    z = z_ref[HALO:, :]
    gated = mixer * (z * sigmoid(z))
    high, low = halves(jnp.sum(gated * gated, axis=1, keepdims=True))
    lane = col_iota((tokens, LANES))
    part_ref[:, depth:] = jnp.where(lane == 0, high, jnp.where(lane == 1, low, jnp.zeros_like(low)))
    lifted = (gated * gain_ref[...]).astype(bf16)
    part_ref[:, :depth] = dot_outer(lifted, w_ref[...]).astype(bf16)


def leave(act, within, value, state, run_exp, link, skip, gain, mid_w, inner, nstate):
    tokens = act.shape[0]
    depth = mid_w.shape[0]
    full = lambda a: pl.BlockSpec(a.shape, lambda i: (0,) * a.ndim)
    columns = lambda a: pl.BlockSpec((a.shape[0], inner), lambda i: (0, 0))
    return pl.pallas_call(
        partial(leave_kernel, inner=inner, nstate=nstate),
        grid=(1,),
        in_specs=[full(act), full(within), columns(value), full(state), full(run_exp), full(link),
                  full(skip), full(gain), columns(mid_w)],
        out_specs=[pl.BlockSpec((tokens, inner), lambda i: (0, 0)),
                   pl.BlockSpec((tokens, depth + LANES), lambda i: (0, 0))],
        out_shape=[jax.ShapeDtypeStruct((tokens, inner), f32),
                   jax.ShapeDtypeStruct((tokens, depth + LANES), bf16)],
        compiler_params=BIG,
        cost_estimate=cost(8),
        name="leave",
    )(act, within, value, state, run_exp, link, skip, gain, mid_w)


def back_kernel(dout_ref, w_ref, mixer_ref, z_ref, act_ref, run_exp_ref, link_ref, gain_ref,
                stat_ref, heads_ref, zgrad_ref, gated_ref, direct_ref, sums_ref,
                *, inner, nstate, di_all):
    scale = stat_ref[:, 0:1]
    cross = stat_ref[:, 1:2]
    mixer = mixer_ref[...]
    z = z_ref[HALO:, :]
    sig = sigmoid(z)
    act = z * sig
    gated = mixer * act
    grad = dot_rows(dout_ref[...], w_ref[...])
    gated_ref[...] = (gated * scale * gain_ref[...]).astype(bf16)
    sums_ref[0:1, :] = jnp.sum(grad * gated * scale, axis=0, keepdims=True)
    gated_grad = scale * (grad * gain_ref[...]) - gated * (scale * scale * scale * cross / di_all)
    zgrad_ref[...] = (gated_grad * mixer * (sig * (1.0 + z * (1.0 - sig)))).astype(bf16)
    heads = gated_grad * act
    heads_ref[...] = heads
    sums_ref[1:2, :] = jnp.sum(heads * act_ref[:, :inner].astype(f32), axis=0, keepdims=True)
    sums_ref[2:, :] = jnp.zeros((6, inner), f32)
    carried = (heads * (jnp.exp(run_exp_ref[...]) * link_ref[...])).astype(bf16)
    direct_ref[...] = dot_inner(carried, act_ref[:, inner + nstate :])


def back(dout, mid_w, mixer, value, act, run_exp, link, gain, stats, inner, nstate, di_all):
    tokens = act.shape[0]
    full = lambda a: pl.BlockSpec(a.shape, lambda i: (0,) * a.ndim)
    columns = lambda a: pl.BlockSpec((a.shape[0], inner), lambda i: (0, 0))
    shape = jax.ShapeDtypeStruct
    outs = [shape((tokens, inner), f32), shape((tokens, inner), bf16), shape((tokens, inner), bf16),
            shape((inner, nstate), f32), shape((8, inner), f32)]
    return pl.pallas_call(
        partial(back_kernel, inner=inner, nstate=nstate, di_all=di_all),
        grid=(1,),
        in_specs=[pl.BlockSpec((tokens, mid_w.shape[0]), lambda i: (0, 0)), columns(mid_w),
                  full(mixer), columns(value), full(act), full(run_exp), full(link),
                  full(gain), full(stats)],
        out_specs=[full(o) for o in outs],
        out_shape=outs,
        compiler_params=BIG,
        cost_estimate=cost(8),
        name="back",
    )(dout, mid_w, mixer, value, act, run_exp, link, gain, stats)


def intra_back_kernel(heads_ref, act_ref, scaled_ref, run_t_ref, run_exp_ref, seg_col_ref,
                      seg_row_ref, dscaled_ref, dstate_ref, drun_ref, scores_ref, dscores_ref,
                      rows_ref, *, inner, nstate, per, block):
    tokens = act_ref.shape[0]
    keys = act_ref[:, inner : inner + nstate]
    query = act_ref[:, inner + nstate :]
    for start in range(0, tokens, block):
        stop = start + block
        scores_ref[start:stop, :stop] = masked_scores(
            query, keys, seg_col_ref, seg_row_ref, start, stop
        )
    dscores_ref[...] = jnp.zeros_like(dscores_ref)
    drun_ref[...] = jnp.zeros_like(drun_ref)

    def pair(i, _):
        columns = pl.ds(pl.multiple_of(i * LANES, LANES), LANES)
        scaled = scaled_ref[:, columns]
        heads = heads_ref[:, columns].astype(bf16)
        lane = col_iota(scaled.shape)
        run = run_exp_ref[:, columns]
        dscaled_ref[:, columns] = jnp.zeros((tokens, LANES), f32)
        for h in range(LANES // per):
            head = i * (LANES // per) + h
            mine = (lane >= h * per) & (lane < (h + 1) * per)
            vals = jnp.where(mine, scaled, jnp.zeros_like(scaled))
            grads = jnp.where(mine, heads, jnp.zeros_like(heads))
            pick = (col_iota((block, LANES)) == head).astype(bf16)
            for start in range(0, tokens, block):
                stop = start + block
                row = run_t_ref[head, :, :stop]
                decay = jnp.exp(jnp.minimum(run[start:stop, h * per : h * per + 1] - row, 0.0))
                weight = decay * scores_ref[start:stop, :stop]
                dweight = dot_outer(grads[start:stop], vals[:stop])
                dscores_ref[start:stop, :stop] += dweight * decay
                flow = (dweight * weight).astype(bf16)
                dscaled_ref[:stop, columns] += dot_inner(weight.astype(bf16), grads[start:stop])
                picks = jnp.broadcast_to(pick[:1], (stop, LANES))
                drun_ref[start:stop, :] += dot_rows(flow, picks)
                drun_ref[:stop, :] -= dot_inner(flow, pick)
        return 0

    lax.fori_loop(0, inner // LANES, pair, 0)
    dkeys = jnp.zeros((tokens, nstate), f32)
    dstate_ref[:, :nstate] = dkeys
    for start in range(0, tokens, block):
        stop = start + block
        shape = (block, stop)
        allowed = (row_iota(shape) + start >= col_iota(shape)) & (
            seg_col_ref[start:stop, :1] == seg_row_ref[:, :stop]
        )
        grad = jnp.where(allowed, dscores_ref[start:stop, :stop], 0.0).astype(bf16)
        dstate_ref[start:stop, nstate:] = dot_rows(grad, keys[:stop])
        dstate_ref[:stop, :nstate] += dot_inner(grad, query[start:stop])


def intra_back(heads, act, scaled, run_t, run_exp, seg_col, seg_row, inner, nstate, per):
    tokens = act.shape[0]
    shape = jax.ShapeDtypeStruct
    return pl.pallas_call(
        partial(intra_back_kernel, inner=inner, nstate=nstate, per=per, block=128),
        out_shape=[shape((tokens, inner), f32), shape((tokens, 2 * nstate), f32),
                   shape((tokens, LANES), f32)],
        scratch_shapes=[pltpu.VMEM((tokens, tokens), f32), pltpu.VMEM((tokens, tokens), f32),
                        pltpu.VMEM((8, LANES), f32)],
        compiler_params=BIG,
        cost_estimate=cost(20),
        name="intra_back",
    )(heads, act, scaled, run_t, run_exp, seg_col, seg_row)


def exit_kernel(heads_ref, act_ref, scaled_ref, step_ref, run_ref, run_exp_ref, link_ref,
                end_ref, value_ref, taps_ref, same_ref, bias_ref, decay_ref, skip_ref,
                mixer_ref, inner_ref, dscaled_ref, dstate_ref, drun_ref, in_ref, out_ref,
                through_ref, zgrad_ref,
                grad_ref, dtaps_ref, small_ref, pad_ref, *, inner, nstate, per):
    tokens = act_ref.shape[0]
    keys = act_ref[:, inner : inner + nstate]
    signal = act_ref[:, :inner].astype(f32)
    grow = expander(LANES, inner, per)
    folds = head_fold(inner, LANES, per).astype(bf16)
    step = step_ref[...]
    running = run_ref[...]
    state_grad = out_ref[...]
    heads = heads_ref[...]
    weight = jnp.exp(run_exp_ref[...]) * link_ref[...]
    carried = mixer_ref[...] - inner_ref[...] - skip_ref[...] * signal
    lifted = (heads * weight).astype(bf16)
    dquery = dot_rows(lifted, in_ref[...].astype(bf16)) + dstate_ref[:, nstate:]
    toward = jnp.exp(running[tokens - 1 :] - running) * end_ref[...]
    toward_exp = dot_rows(toward, grow, highest)
    step_exp = dot_rows(step, grow, highest)
    leaving = dot_outer(keys, state_grad.astype(bf16)) * toward_exp
    pushed = (signal * step_exp * toward_exp).astype(bf16)
    dkeys = dot_rows(pushed, state_grad.astype(bf16)) + dstate_ref[:, :nstate]
    dscaled = dscaled_ref[...] + leaving
    tri = (row_iota((tokens, tokens)) <= col_iota((tokens, tokens))).astype(f32)
    strict = (row_iota((tokens, tokens)) > col_iota((tokens, tokens))).astype(f32)
    kept = jnp.sum(in_ref[...] * state_grad, axis=1, keepdims=True)
    kept = jnp.sum(head_fold(inner, LANES, per) * kept, axis=0, keepdims=True) * through_ref[...]
    back_sum = drun_ref[...] + fold_heads(heads * carried, folds)
    front_sum = fold_heads(signal * step_exp * leaving, folds)
    dlog = dot_rows(tri, back_sum, highest) + dot_rows(strict, front_sum, highest) + kept
    rate = -jnp.exp(decay_ref[...])
    dstep = dlog * rate + fold_heads(dscaled * signal, folds)
    raw = value_ref[HALO:, 2 * inner + 2 * nstate :] + bias_ref[...]
    draw = dstep * sigmoid(raw)
    small_ref[0:1, :] = jnp.sum(draw, axis=0, keepdims=True)
    small_ref[1:2, :] = jnp.sum(dlog * step, axis=0, keepdims=True) * rate
    small_ref[2:, :] = jnp.zeros((6, LANES), f32)
    ext = tokens + HALO
    grad_ref[:HALO, :inner] = jnp.zeros((HALO, inner), bf16)
    grad_ref[HALO:, :inner] = zgrad_ref[...]
    grad_ref[:HALO, 2 * inner + 2 * nstate :] = jnp.zeros((HALO, LANES), bf16)
    used = col_iota((tokens, LANES)) < inner // per
    grad_ref[HALO:, 2 * inner + 2 * nstate :] = jnp.where(used, draw, 0.0).astype(bf16)
    pad_ref[:, :inner] = dscaled * step_exp + skip_ref[...] * heads
    pad_ref[:, inner : inner + nstate] = dkeys
    pad_ref[:, inner + nstate :] = dquery

    def conv(i, _):
        at = pl.multiple_of(i * LANES, LANES)
        rows, total = conv_pre(value_ref, inner + at, taps_ref, at, same_ref, tokens)
        sig = sigmoid(total)
        dpre = pad_ref[:, pl.ds(at, LANES)] * (sig * (1.0 + total * (1.0 - sig)))
        drows = None
        for offset in range(CONV):
            first = HALO - CONV + 1 + offset
            kept = dpre * same_ref[offset]
            dtaps_ref[offset : offset + 1, pl.ds(at, LANES)] = jnp.sum(
                kept * rows[first : first + tokens], axis=0, keepdims=True
            )
            term = kept * taps_ref[offset : offset + 1, pl.ds(at, LANES)]
            term = jnp.concatenate(
                [jnp.zeros((first, LANES), f32), term,
                 jnp.zeros((ext - first - tokens, LANES), f32)][: 3 if ext > first + tokens else 2],
                axis=0,
            )
            drows = term if drows is None else drows + term
        grad_ref[:, pl.ds(inner + at, LANES)] = drows.astype(bf16)
        return 0

    lax.fori_loop(0, (inner + 2 * nstate) // LANES, conv, 0)


def exits(args, inner, nstate, per):
    tokens = args[1].shape[0]
    wide = args[8].shape[1]
    shape = jax.ShapeDtypeStruct
    return pl.pallas_call(
        partial(exit_kernel, inner=inner, nstate=nstate, per=per),
        out_shape=[shape((tokens + HALO, wide), bf16), shape((CONV, inner + 2 * nstate), f32),
                   shape((8, LANES), f32)],
        scratch_shapes=[pltpu.VMEM((tokens, inner + 2 * nstate), f32)],
        compiler_params=BIG,
        cost_estimate=cost(15),
        name="exits",
    )(*args)


def experts_kernel(mix_ref, cot_ref, gate_ref, w_ref, out_in, dmix_in,
                   out_ref, dmix_ref, dgate_ref, dw_ref, down_ref, hidden_ref, dval_ref, *, tile):
    @pl.when(pl.program_id(0) == 0)
    def _():
        out_ref[...] = out_in[...]
        dmix_ref[...] = dmix_in[...]

    rows, depth = mix_ref.shape
    wide = w_ref.shape[3]
    hid = wide // 2
    chunks = depth // wide
    for p in range(2):
        for c in range(chunks):
            down_ref[p * hid : (p + 1) * hid, c * wide : (c + 1) * wide] = (
                w_ref[0, p, depth + c * hid : depth + (c + 1) * hid, :]
            )
    down = down_ref[...]

    def part(i, _):
        at = pl.ds(pl.multiple_of(i * tile, tile), tile)
        mix = mix_ref[at, :]
        dh_raw = dot_outer(cot_ref[at, :], down)
        dmix = None
        for p in range(2):
            gate = gate_ref[0, at, p : p + 1]
            value = dot_rows(mix, w_ref[0, p, :depth, :])
            first, second = value[:, :hid], value[:, hid:]
            sig = sigmoid(first)
            act = first * sig
            hidden = (act * second).astype(bf16).astype(f32)
            raw = dh_raw[:, p * hid : (p + 1) * hid]
            dgate_ref[0, at, p : p + 1] = jnp.sum(hidden * raw, axis=1, keepdims=True)
            dh = gate * raw
            dval_ref[p, at, :hid] = (dh * second * (sig * (1.0 + first * (1.0 - sig)))).astype(bf16)
            dval_ref[p, at, hid:] = (dh * act).astype(bf16)
            hidden_ref[at, p * hid : (p + 1) * hid] = (gate * hidden).astype(bf16)
            term = dot_outer(dval_ref[p, at, :], w_ref[0, p, :depth, :])
            dmix = term if dmix is None else dmix + term
        out_ref[at, :] += dot_rows(hidden_ref[at, :], down)
        dmix_ref[at, :] += dmix
        return 0

    lax.fori_loop(0, rows // tile, part, 0)
    for c in range(chunks):
        grad = dot_inner(hidden_ref[...], cot_ref[:, c * wide : (c + 1) * wide]).astype(bf16)
        for p in range(2):
            dw_ref[0, p, depth + c * hid : depth + (c + 1) * hid, :] = grad[p * hid : (p + 1) * hid]
    for p in range(2):
        dw_ref[0, p, :depth, :] = dot_inner(mix_ref[...], dval_ref[p]).astype(bf16)


def experts(mix, cot, gate, weights, out, dmix):
    pairs, _, deep, wide = weights.shape
    rows, depth = mix.shape
    whole = lambda shape: pl.BlockSpec(shape, lambda i: (0,) * len(shape))
    each = lambda shape: pl.BlockSpec((1,) + shape, lambda i: (i,) + (0,) * len(shape))
    return pl.pallas_call(
        partial(experts_kernel, tile=min(256, rows)),
        grid=(pairs,),
        in_specs=[
            whole((rows, depth)), pl.BlockSpec((rows, depth), lambda i: (0, 0)), each((rows, 2)),
            each((2, deep, wide)), whole((rows, depth)), whole((rows, depth)),
        ],
        out_specs=[
            whole((rows, depth)), whole((rows, depth)), each((rows, 2)), each((2, deep, wide)),
        ],
        out_shape=[
            jax.ShapeDtypeStruct((rows, depth), f32), jax.ShapeDtypeStruct((rows, depth), f32),
            jax.ShapeDtypeStruct((pairs, rows, 2), f32),
            jax.ShapeDtypeStruct(weights.shape, bf16),
        ],
        scratch_shapes=[
            pltpu.VMEM((wide, depth), bf16), pltpu.VMEM((rows, wide), bf16),
            pltpu.VMEM((2, rows, wide), bf16),
        ],
        compiler_params=BIG,
        cost_estimate=cost(6 * pairs),
        name="experts",
    )(mix, cot, gate, weights, out, dmix)


def pack_experts(gates, down):
    count, depth, wide = gates.shape
    hid = wide // 2
    down = down.reshape(count, hid, depth // wide, wide).transpose(0, 2, 1, 3)
    return jnp.concatenate([gates, down.reshape(count, -1, wide)], axis=1)


def unpack_experts(packed):
    count, deep, wide = packed.shape
    hid = wide // 2
    depth = deep * 2 // 3
    down = packed[:, depth:].reshape(count, depth // wide, hid, wide).transpose(0, 2, 1, 3)
    return packed[:, :depth], down.reshape(count, hid, depth)


def local(
    block_input, gain_input, proj_main, proj_state, proj_step, conv_main, conv_state, step_bias,
    decay_log, skip_gain, gain_gate, proj_out, gain_mix, router_weight, shared_gates, shared_down,
    expert_gates, expert_down, segments, routes, cotangent,
):
    tokens, quarter = block_input.shape
    heads = step_bias.shape[0]
    inner = conv_main.shape[1]
    nstate = conv_state.shape[1] // 2
    per = inner // heads
    tensors = lax.axis_size("tensor")
    zi = lax.axis_index("tensor")
    senders = lax.axis_size(ROWS)
    depth = quarter * tensors
    di_all = inner * tensors
    own = tokens // tensors
    column = zi * quarter
    row0 = zi * own
    wrows = proj_main.shape[0]
    hid = expert_gates.shape[3]
    local_experts = expert_gates.shape[0]
    experts_all = local_experts * senders
    shared_here = shared_down.shape[1]
    router_pad = -experts_all % LANES

    main_w = gather_rows(
        jnp.concatenate(
            [proj_main[:, 0], proj_main[:, 1], proj_state,
             jnp.pad(proj_step, ((0, 0), (0, LANES - heads)))], axis=1
        )
    )
    shared_pair = shared_gates.reshape(wrows, 2, 2, shared_here // 2).transpose(0, 2, 1, 3)
    mid_w = gather_rows(
        jnp.concatenate(
            [proj_out, shared_pair.reshape(wrows, -1), shared_down,
             jnp.pad(router_weight, ((0, 0), (0, router_pad)))], axis=1
        )
    )
    expert_w = gather_rows(
        pack_experts(expert_gates.reshape(local_experts, depth, 2 * hid), expert_down)[None]
    )
    at_down = inner + 2 * shared_here
    at_router = at_down + shared_here
    router_full = mid_w[:, at_router : at_router + experts_all]
    shared_w = pack_experts(
        jnp.stack([mid_w[:, inner : inner + shared_here], mid_w[:, inner + shared_here : at_down]]),
        mid_w[:, at_down:at_router].T.reshape(2, shared_here // 2, depth),
    )[None]

    seg_row = segments[0]
    last = jnp.concatenate(
        [block_input[tokens - CONV + 1 :],
         jnp.pad(seg_row[None, tokens - CONV + 1 :].astype(bf16), ((0, 0), (0, quarter - CONV + 1)))], axis=0
    )
    halo = shifted(last, "ctx", 1)
    halo_seg = halo[CONV - 1, : CONV - 1].astype(jnp.int32)
    extra = jnp.concatenate(
        [jnp.zeros((HALO - CONV + 1, quarter), bf16), halo[: CONV - 1], gain_input[None],
         gain_mix[None], jnp.zeros((14, quarter), bf16)], axis=0
    )
    wide = lambda got: got.transpose(1, 0, 2).reshape(got.shape[1], depth)
    got = spread(block_input)
    cotangent, got = lax.optimization_barrier((cotangent, got))
    got = wide(got)
    got_extra = spread_small(extra)
    cot_full = wide(spread(cotangent))
    gain_row = got_extra[HALO].astype(f32)
    gain_mid = got_extra[HALO + 1].astype(f32)
    x_ext = jnp.concatenate([got_extra[:HALO], got], axis=0).astype(f32)
    scale_ext = lax.rsqrt(jnp.mean(x_ext * x_ext, axis=-1, keepdims=True) + epsilon)
    normed_ext = x_ext * scale_ext
    mixed_ext = (normed_ext * gain_row).astype(bf16)

    segments_ext = jnp.concatenate([halo_seg, seg_row], axis=0)
    same = jnp.stack(
        [segments_ext[offset : offset + tokens] == seg_row for offset in range(CONV)]
    ).astype(f32)
    same = jnp.broadcast_to(same[:, :, None], (CONV, tokens, LANES))
    taps = jnp.concatenate([conv_main, conv_state], axis=1).astype(f32)
    lanes = lambda v: jnp.pad(v, (0, LANES - heads))[None]
    bias = lanes(step_bias)
    decay = lanes(decay_log)
    skip = jnp.repeat(skip_gain, per)[None]
    link = (seg_row == halo_seg[-1]).astype(f32)[:, None]
    at_end = (seg_row == seg_row[-1]).astype(f32)[:, None]
    seg_col = seg_row[:, None]
    seg_line = seg_row[None]
    value, act, scaled, step, running, run_exp, state_local = enter(
        mixed_ext, main_w, taps, same, bias, decay, at_end, inner, nstate, per
    )
    run_t = running[:, :heads].T[:, None, :]
    through_row = jnp.exp(running[-1]) * link[-1]
    through = through_row[:heads]
    state_in = chain(through, state_local, False)
    within = intra(act, scaled, run_t, run_exp, seg_col, seg_line, inner, nstate, per)
    gain_gate_f = gain_gate.astype(f32)[None, :]
    mixer, part = leave(
        act, within, value, state_in, run_exp, link, skip, gain_gate_f, mid_w, inner, nstate
    )
    part, cot_full = lax.optimization_barrier((part, cot_full))
    parts = jnp.sum(exchange(part.reshape(tensors, own, -1)).astype(f32), axis=0)
    scale_own = lax.rsqrt((parts[:, depth] + parts[:, depth + 1]) / di_all + epsilon)
    input_own = lax.dynamic_slice_in_dim(x_ext, row0 + HALO, own, 0)
    residual_own = (input_own + parts[:, :depth] * scale_own[:, None]).astype(bf16)
    scale_cols = jnp.pad(jnp.stack(halves(scale_own), axis=1), ((0, 0), (0, LANES - 2)))
    middle = spread(jnp.concatenate([residual_own, scale_cols], axis=1)).reshape(tokens, -1)
    residual = middle[:, :depth]
    gated_scale = middle[:, depth].astype(f32) + middle[:, depth + 1].astype(f32)

    res_f = residual.astype(f32)
    scale_two = lax.rsqrt(jnp.mean(res_f * res_f, axis=-1, keepdims=True) + epsilon)
    mixed_two = (res_f * scale_two * gain_mid).astype(bf16)
    logits = dot_rows(mixed_two, router_full)
    expert_ids = jnp.arange(experts_all, dtype=jnp.int32)
    chosen = jnp.any(routes[:, :, None] == expert_ids[None, None, :], axis=1)
    top = jnp.max(jnp.where(chosen, logits, -jnp.inf), axis=1, keepdims=True)
    weight = jnp.where(chosen, jnp.exp(jnp.where(chosen, logits - top, 0.0)), 0.0)
    gates = weight / jnp.sum(weight, axis=1, keepdims=True)
    zero = jnp.zeros((tokens, depth), f32)
    ones = jnp.ones((1, tokens, 2), f32)
    out_part, dmix_part, _, shared_grad = experts(mixed_two, cot_full, ones, shared_w, zero, zero)
    gate_pairs = gates.reshape(tokens, senders, local_experts).transpose(1, 0, 2)
    out_part, dmix_part, dgate, expert_grad = experts(
        mixed_two, cot_full, gate_pairs, expert_w, out_part, dmix_part
    )
    deep = expert_grad.shape[2]
    expert_rows = scatter_rows(expert_grad.reshape(-1, 2 * hid)).reshape(local_experts, deep, 2 * hid)

    dgate = dgate.transpose(1, 0, 2).reshape(tokens, experts_all)
    router_grad = lambda moved: (
        gates * (moved - jnp.sum(gates * moved, axis=1, keepdims=True))
    ).astype(bf16)
    dmix_part = (dmix_part + dot_outer(router_grad(dgate), router_full)).astype(bf16)
    marks = jnp.concatenate(halves(dgate), axis=1)
    mark_pad = -marks.shape[1] % LANES
    moved = exchange(
        jnp.concatenate([dmix_part, jnp.pad(marks, ((0, 0), (0, mark_pad)))], axis=1)
        .reshape(tensors, own, -1)
    )
    moved = jnp.sum(moved.astype(f32), axis=0)
    dmix = moved[:, :depth]
    dgate_own = moved[:, depth : depth + experts_all] + moved[:, depth + experts_all : depth + 2 * experts_all]
    res_own = residual_own.astype(f32)
    scale_mid = lax.rsqrt(jnp.mean(res_own * res_own, axis=-1, keepdims=True) + epsilon)
    normed_mid = res_own * scale_mid
    grad_gain_mix = jnp.sum(dmix * normed_mid, axis=0)
    lifted_mid = dmix * gain_mid
    cross_mid = jnp.mean(lifted_mid * normed_mid, axis=1, keepdims=True)
    cot_own = lax.dynamic_slice_in_dim(cot_full, row0, own, 0).astype(f32)
    dres_own = (cot_own + scale_mid * (lifted_mid - normed_mid * cross_mid)).astype(bf16)
    cross_own = jnp.sum(dres_own.astype(f32) * parts[:, :depth], axis=1, keepdims=True)
    notes = jnp.concatenate(halves(cross_own) + halves(dgate_own), axis=1)
    dres_all = spread(
        jnp.concatenate([dres_own, jnp.pad(notes, ((0, 0), (0, -notes.shape[1] % LANES)))], axis=1)
    ).reshape(tokens, -1)
    dmixer = dres_all[:, :depth]
    cross = dres_all[:, depth].astype(f32) + dres_all[:, depth + 1].astype(f32)
    first = depth + 2
    dgate_all = (dres_all[:, first : first + experts_all].astype(f32)
                 + dres_all[:, first + experts_all : first + 2 * experts_all].astype(f32))

    stats = jnp.stack([gated_scale, cross], axis=1)
    heads_grad, z_grad, gated_out, direct, sums = back(
        dres_all, mid_w, mixer, value, act, run_exp, link, gain_gate_f, stats, inner, nstate, di_all
    )
    state_grad = chain(through, direct, True)
    dscaled, dstate, drun = intra_back(
        heads_grad, act, scaled, run_t, run_exp, seg_col, seg_line, inner, nstate, per
    )
    value_grad, dtaps, small_sums = exits(
        (heads_grad, act, scaled, step, running, run_exp, link, at_end, value, taps, same, bias,
         decay, skip, mixer, within, dscaled, dstate, drun, state_in, state_grad,
         through_row[None], z_grad),
        inner, nstate, per,
    )
    first = 2 * inner
    last = first + 2 * nstate
    halo_back = shifted(value_grad[:HALO], "ctx", -1)
    mixed_grad = dot_outer(value_grad[HALO:], main_w)
    mixed_grad = mixed_grad.at[tokens - HALO :].add(dot_outer(halo_back, main_w))
    normed_one = normed_ext[HALO:]
    scale_one = scale_ext[HALO:]
    grad_gain_part = jnp.sum(mixed_grad * normed_one, axis=0)
    cross_part = jnp.concatenate(
        halves(jnp.sum(mixed_grad * gain_row * normed_one, axis=1, keepdims=True)), axis=1
    )
    cross_part = jnp.pad(cross_part, ((0, 0), (0, LANES - 2)))
    blocks = mixed_grad.astype(bf16).reshape(tokens, tensors, quarter).transpose(1, 0, 2)
    summed = jnp.sum(
        exchange(
            jnp.concatenate(
                [blocks, jnp.broadcast_to(cross_part[None], (tensors,) + cross_part.shape)], axis=2
            )
        ).astype(f32), axis=0,
    )
    normed_slice = lax.dynamic_slice_in_dim(normed_one, column, quarter, 1)
    cross_one = (summed[:, quarter] + summed[:, quarter + 1])[:, None]
    grad_input = (
        lax.dynamic_slice_in_dim(dmixer, column, quarter, 1).astype(f32)
        + scale_one * (summed[:, :quarter] * gain_input.astype(f32)[None, :]
                       - normed_slice * (cross_one / depth))
    )
    out_blocks = out_part.astype(bf16).reshape(tokens, tensors, quarter).transpose(1, 0, 2)
    block_sum = jnp.sum(exchange(out_blocks).astype(f32), axis=0)
    output = (
        lax.dynamic_slice_in_dim(residual, column, quarter, 1).astype(f32) + block_sum
    ).astype(bf16)

    state_all = jnp.sum(spread(value_grad[:, first:last]).astype(f32), axis=0).astype(bf16)
    grad_main = dot_inner(
        mixed_ext, jnp.concatenate([value_grad[:, :first], state_all, value_grad[:, last:]], axis=1)
    )
    grad_proj_out = dot_inner(dmixer, gated_out)
    grad_router = jnp.pad(dot_inner(mixed_two, router_grad(dgate_all)), ((0, 0), (0, router_pad)))
    shared_up, shared_dn = unpack_experts(shared_grad[0])
    mid_local = jnp.concatenate(
        [shared_up[0], shared_up[1], shared_dn.reshape(shared_here, depth).T,
         grad_proj_out.astype(bf16), grad_router.astype(bf16)], axis=1
    )
    mid_local, expert_rows = lax.optimization_barrier((mid_local, expert_rows))
    mid_grad = scatter_rows(mid_local)
    main_local, mid_grad = lax.optimization_barrier((grad_main.astype(bf16), mid_grad))
    mid_grad = mid_grad.astype(f32)
    main_grad = scatter_rows(main_local).astype(f32)
    gates_rows, down_rows = unpack_experts(expert_rows)
    shared_rows = mid_grad[:, : 2 * shared_here].reshape(wrows, 2, 2, shared_here // 2)
    gains, conv_state_grad = lax.psum(
        (jnp.stack([grad_gain_part, grad_gain_mix]), dtaps[:, inner:]), EVERY
    )
    small = lax.psum((dtaps[:, :inner], small_sums[:2], sums[:2]), ROWS)
    gains = lax.dynamic_slice_in_dim(gains, column, quarter, 1)
    return (
        output,
        grad_input,
        gains[0],
        jnp.stack([main_grad[:, :inner], main_grad[:, inner:first]], axis=1),
        main_grad[:, first:last],
        main_grad[:, last : last + heads],
        small[0],
        conv_state_grad,
        small[1][0, :heads],
        small[1][1, :heads],
        jnp.sum(small[2][1].reshape(heads, per), axis=1),
        small[2][0],
        mid_grad[:, 3 * shared_here : at_router],
        gains[1],
        mid_grad[:, at_router : at_router + experts_all],
        shared_rows.transpose(0, 2, 1, 3).reshape(wrows, 2, shared_here),
        mid_grad[:, 2 * shared_here : 3 * shared_here],
        gates_rows.reshape(expert_gates.shape).astype(f32),
        down_rows.astype(f32),
    )


def solution(mesh):
    return jax.shard_map(
        local,
        mesh=mesh,
        in_specs=(
            P(ROWS, "tensor"),
            P("tensor"),
            P(ROWS, None, "tensor"),
            P(ROWS, None),
            P(ROWS, "tensor"),
            P(None, "tensor"),
            P(),
            P("tensor"),
            P("tensor"),
            P("tensor"),
            P("tensor"),
            P(ROWS, "tensor"),
            P("tensor"),
            P(ROWS, None),
            P(ROWS, None, "tensor"),
            P(ROWS, "tensor"),
            P(ROWS, None, None, "tensor"),
            P(ROWS, "tensor", None),
            P("shard", "ctx"),
            P(ROWS, None),
            P(ROWS, "tensor"),
        ),
        out_specs=(
            P(ROWS, "tensor"),
            P(ROWS, "tensor"),
            P("tensor"),
            P(ROWS, None, "tensor"),
            P(ROWS, None),
            P(ROWS, "tensor"),
            P(None, "tensor"),
            P(),
            P("tensor"),
            P("tensor"),
            P("tensor"),
            P("tensor"),
            P(ROWS, "tensor"),
            P("tensor"),
            P(ROWS, None),
            P(ROWS, None, "tensor"),
            P(ROWS, "tensor"),
            P(ROWS, None, None, "tensor"),
            P(ROWS, "tensor", None),
        ),
        check_vma=False,
    )
```

time: 2740 us -> 715 us (0.26)
  waiting for transfers between devices: 1060 us -> 230 us
  blocking collectives: 762 us -> 63.5 us
  local copies, waits for them, and re-layouts: 418 us -> 109 us
  matrix products: 268 us -> 29.7 us
  Pallas kernels: 0 us -> 142 us
  other arithmetic: 174 us -> 53.1 us
  starting transfers between devices: 34.4 us -> 63.9 us
    all_gather x7 -> x0, blocking collectives: 679 us -> none  [the longest x1 418 us: gather_weights(): lax.all_gather(shared_down, ('shard', 'ctx'), axis=0, tiled=True)]
    reduce_scatter x8 -> x2, waiting for transfers between devices: 374 us -> 0.01 us  [scatter_rows(): return lax.psum_scatter(value, ROWS, scatter_dimension=0, tiled=True)]
    all_to_all x4 -> x9, waiting for transfers between devices: 554 us -> 227 us  [exchange(): lax.all_to_all(blocks, 'tensor', split_axis=0, concat_axis=0, tiled=True)]
    dot_general x58 -> x1, matrix products: 224 us -> 3.02 us  [dot_rows(): return jnp.dot(left, right, preferred_element_type=f32, precision=precision)]
    gather x9 -> x0, local copies, waits for them, and re-layouts: 204 us -> none  [the longest x2 89.3 us: local(): picked = returned[routes, local_rank] * owned[:, :, None]]
    pallas_call x0 -> x8, Pallas kernels: none -> 142 us  [the longest x2 61.9 us: experts(): pl.pallas_call(partial(experts_kernel, tile=min(256, rows)), grid=(pairs,...]
    all_gather x9 -> x3, waiting for transfers between devices: 86.7 us -> 0.01 us  [gather_rows(): return lax.all_gather(value, ROWS, axis=0, tiled=True)]
    transpose x2 -> x5, local copies, waits for them, and re-layouts: 56.8 us -> 5.8 us  [the longest x2 3.32 us: pack_experts(): down = down.reshape(count, hid, depth // wide, wide).transpose(0, 2, 1, 3)]
  transfers between devices with their start and end apart: 28 -> 30, of which waited for: 18 -> 10; matrix products, arithmetic and copies ran while one was open for 20% -> 24% of each run, Pallas kernels for 0% -> 13%
where the time goes in v1:
time: 715 us; the launch traced here: 707 us
  waiting for transfers between devices  230 us (32%)
  Pallas kernels  142 us (20%)
  local copies, waits for them, and re-layouts  109 us (15%)
  starting transfers between devices  63.9 us (9%)
  blocking collectives  63.5 us (9%)
  other arithmetic  53.1 us (7%)
  matrix products  29.7 us (4%)
  between operations  16.4 us (2%)
    all_to_all x9, waiting for transfers between devices, exchange(): lax.all_to_all(blocks, 'tensor', split_axis=0, concat_axis=0, tiled=True)  227 us
    pallas_call x2, Pallas kernels, experts(): pl.pallas_call(partial(experts_kernel, tile=min(256, rows)), grid=(pairs,...  61.9 us
    all_to_all x9, starting transfers between devices, exchange(): lax.all_to_all(blocks, 'tensor', split_axis=0, concat_axis=0, tiled=True)  40.7 us
    psum x1, blocking collectives, local(): lax.psum((jnp.stack([grad_gain_part, grad_gain_mix]), dtaps[:, inner:]),...  39.4 us
    psum x1, blocking collectives, local(): small = lax.psum((dtaps[:, :inner], small_sums[:2], sums[:2]), ROWS)  24.2 us
    unnamed x100, local copies, waits for them, and re-layouts  23.6 us
    pallas_call x1, Pallas kernels, exits(): pl.pallas_call(partial(exit_kernel, inner=inner, nstate=nstate, per=per),...  21.7 us
    pallas_call x1, Pallas kernels, enter(): pl.pallas_call(partial(enter_kernel, inner=inner, nstate=nstate, per=per)...  20.3 us
  transfers between devices with their start and end apart: 30, of which 10 were waited for; matrix products, arithmetic and copies ran while one was open for 24% of the time, Pallas kernels for 13%

profile of v1, /device:TPU:0, one launch (start us, length us, event | category | flops | bytes accessed | tf_op | source)
XLA Modules:
  0.0 707.4 jit_solution(12490602347079049393)
XLA Ops:
  20.1 6.5 all-to-all-start
  36.6 28.5 %all-to-all-done = bf16[4,512,384]{2,1,0:T(8,128)(2,1)S(1)} async-done(((bf16[4,512,384]{2,1,0:T(8,128)(2,1)}), bf16[4,512,384]{2,1,0:T(8,128)(2,1)S(1)}, u32[]{:S(2)}, u32[]{:S(2)}) %all-to-all-start) | async-done | bytes 1572896 | tf_op jit(solution)/shard_map/all_to_all | solution.py:71
  79.3 27.7 %all-to-all-done.1 = bf16[4,512,384]{2,1,0:T(8,128)(2,1)} async-done(((bf16[4,512,384]{2,1,0:T(8,128)(2,1)}), bf16[4,512,384]{2,1,0:T(8,128)(2,1)}, u32[]{:S(2)}, u32[]{:S(2)}) %all-to-all-start.1) | async-done | bytes 1572896 | tf_op jit(solution)/shard_map/all_to_all | solution.py:71
  111.0 20.3 %enter.1 = (f32[528,1920]{1,0:T(8,128)}, bf16[512,1024]{1,0:T(8,128)(2,1)}, bf16[512,768]{1,0:T(8,128)(2,1)}, f32[512,128]{1,0:T(8,128)}, f32[512,128]{1,0:T(8,1...) custom-call(bf16[528,1536]{1,0:T(8,128)(2,1)} %get-tuple-element.252.mixed_ref, ...), custom_call_target="tpu_custom_call" | custom-call | flops 7200000000 | bytes 1048576 | tf_op jit(solution)/shard_map/enter/pallas_call | solution.py:193
  143.5 6.5 intra.1.inner_ref
  151.4 7.2 %leave.1 = (f32[512,768]{1,0:T(8,128)}, bf16[512,1664]{1,0:T(8,128)(2,1)}) custom-call(bf16[512,1024]{1,0:T(8,128)(2,1)} %get-tuple-element.67.act_ref, f32[512,768]{1,0:T(8,128)} %intra.1.inner_ref, f32[528,1920]{1,0:T(8,128)} %get-tuple-element.71.z_ref.value_ref, f32[768,128]{1,0:T(8,128)} %multiply_add_fusion.1.state_ref.in_ref, ...), custom_call_target="tpu_custom_call" | custom-call | flops 7200000000 | bytes 1048576 | tf_op jit(solution)/shard_map/leave/pallas_call | solution.py:283
  164.7 37.9 %all-to-all-done.2 = bf16[4,128,1664]{2,1,0:T(8,128)(2,1)S(1)} async-done(((bf16[4,128,1664]{2,1,0:T(8,128)(2,1)}), bf16[4,128,1664]{2,1,0:T(8,128)(2,1)S(1)}, u32[]{:S(2)}, u32[]{:S(2)}) %all-to-all-start.2) | async-done | bytes 1703968 | tf_op jit(solution)/shard_map/all_to_all | solution.py:71
  223.9 26.8 %all-to-all-done.3 = bf16[4,128,1664]{2,1,0:T(8,128)(2,1)S(1)} async-done(((bf16[4,128,1664]{2,1,0:T(8,128)(2,1)}), bf16[4,128,1664]{2,1,0:T(8,128)(2,1)S(1)}, u32[]{:S(2)}, u32[]{:S(2)}) %all-to-all-start.3) | async-done | bytes 1703968 | tf_op jit(solution)/shard_map/all_to_all | solution.py:71
  266.1 11.8 %experts.2 = (f32[512,1536]{1,0:T(8,128)}, f32[512,1536]{1,0:T(8,128)}, f32[1,512,2]{2,1,0:T(8,128)}, bf16[1,2,2304,256]{3,2,1,0:T(8,128)(2,1)}) custom-call(bf16[512,1536]{1,0:T(8,128)(2,1)} %copy-done, bf16[512,1536]{1,0:T(8,128)(2,1)} %bitcast.143, f32[1,512,2]{2,1,0:T(8,128)} %broadcast_in_dim.149.gate_ref, ...), custom_call_target="tpu_custom_call" | custom-call | flops 5400000000 | bytes 1048576 | tf_op jit(solution)/shard_map/experts/pallas_call | solution.py:557
  277.9 50.0 %experts.3 = (f32[512,1536]{1,0:T(8,128)}, f32[512,1536]{1,0:T(8,128)}, f32[8,512,2]{2,1,0:T(8,128)}, bf16[8,2,2304,256]{3,2,1,0:T(8,128)(2,1)}) custom-call(bf16[512,1536]{1,0:T(8,128)(2,1)} %copy-done, bf16[512,1536]{1,0:T(8,128)(2,1)} %bitcast.144, f32[8,512,2]{2,1,0:T(8,128)} %bitcast.151, bf16[8,2,2304,256]{3,2,1,0:T(8,128)(2,1)} %bitcast.162, ...), custom_call_target="tpu_custom_call" | custom-call | flops 43200000000 | bytes 1048576 | tf_op jit(solution)/shard_map/experts/pallas_call | solution.py:557
  335.4 4.7 all-to-all-start.5
  340.1 38.6 %all-to-all-done.5 = bf16[4,128,1664]{2,1,0:T(8,128)(2,1)} async-done(((bf16[4,128,1664]{2,1,0:T(8,128)(2,1)}), bf16[4,128,1664]{2,1,0:T(8,128)(2,1)}, u32[]{:S(2)}, u32[]{:S(2)}) %all-to-all-start.5) | async-done | bytes 1703968 | tf_op jit(solution)/shard_map/all_to_all | solution.py:71
  406.2 24.4 %all-to-all-done.6 = bf16[4,128,1664]{2,1,0:T(8,128)(2,1)} async-done(((bf16[4,128,1664]{2,1,0:T(8,128)(2,1)}), bf16[4,128,1664]{2,1,0:T(8,128)(2,1)}, u32[]{:S(2)}, u32[]{:S(2)}) %all-to-all-start.6) | async-done | bytes 1703968 | tf_op jit(solution)/shard_map/all_to_all | solution.py:71
  438.9 8.3 %back.1 = (f32[512,768]{1,0:T(8,128)}, bf16[512,768]{1,0:T(8,128)(2,1)}, bf16[512,768]{1,0:T(8,128)(2,1)}, f32[768,128]{1,0:T(8,128)}, f32[8,768]{1,0:T(8,128)}) custom-call(bf16[512,1664]{1,0:T(8,128)(2,1)} %bitcast.33.dout_ref, bf16[1536,1664]{1,0:T(8,128)(2,1)} %all-gather.7.cloned.1.call-done.w_ref, f32[512,768]{1,0:T(8,128)} %get-tuple-element.82.mixer_ref, ...), custom_call_target="tpu_custom_call" | custom-call | flops 7200000000 | bytes 1048576 | tf_op jit(solution)/shard_map/back/pallas_call | solution.py:328
  452.5 7.7 %copy.278 = bf16[1536,1664]{1,0:T(8,128)(2,1)} copy(bf16[1536,1664]{0,1:T(8,128)(2,1)} %pad_dynamic-update-slice_fusion) | data formatting | bytes 10223616
  470.4 16.2 %intra_back.1 = (f32[512,768]{1,0:T(8,128)}, f32[512,256]{1,0:T(8,128)}, f32[512,128]{1,0:T(8,128)}) custom-call(f32[512,768]{1,0:T(8,128)} %get-tuple-element.83.heads_ref, bf16[512,1024]{1,0:T(8,128)(2,1)} %get-tuple-element.67.act_ref, bf16[512,768]{1,0:T(8,128)(2,1)} %get-tuple-element.68.scaled_ref, f32[12,1,512]{2,1,0:T(1,128)} %broadcast_in_dim.69.run_t_ref, ...), custom_call_target="tpu_custom_call" | custom-call | flops 17999998976 | bytes 1048576 | tf_op jit(solution)/shard_map/intra_back/pallas_call | solution.py:400
  487.6 21.7 %exits.1 = (bf16[528,1920]{1,0:T(8,128)(2,1)}, f32[4,1024]{1,0:T(4,128)}, f32[8,128]{1,0:T(8,128)}) custom-call(f32[512,768]{1,0:T(8,128)} %get-tuple-element.83.heads_ref, bf16[512,1024]{1,0:T(8,128)(2,1)} %get-tuple-element.67.act_ref, bf16[512,768]{1,0:T(8,128)(2,1)} %get-tuple-element.68.scaled_ref, f32[512,128]{1,0:T(8,128)} %get-tuple-element.84.step_ref, ...), custom_call_target="tpu_custom_call" | custom-call | flops 13500000256 | bytes 1048576 | tf_op jit(solution)/shard_map/exits/pallas_call | solution.py:490
  511.3 4.6 all-to-all-start.8
  519.6 23.6 %all-to-all-done.8 = bf16[4,528,256]{2,1,0:T(8,128)(2,1)S(1)} async-done(((bf16[4,528,256]{2,1,0:T(8,128)(2,1)}), bf16[4,528,256]{2,1,0:T(8,128)(2,1)S(1)}, u32[]{:S(2)}, u32[]{:S(2)}) %all-to-all-start.8) | async-done | bytes 1081376 | tf_op jit(solution)/shard_map/all_to_all | solution.py:71
  543.5 8.8 %convolution_convert_fusion = bf16[1536,1920]{1,0:T(8,128)(2,1)} fusion(bf16[528,1536]{1,0:T(8,128)(2,1)} %get-tuple-element.252.mixed_ref, bf16[528,128]{1,0:T(8,128)(2,1)S(1)} %slice.286, bf16[528,256]{1,0:T(8,128)(2,1)S(1)} %reduce_sum.176, bf16[528,1536]{1,0:T(8,128)(2,1)} %slice.284), kind=kOutput, calls=%fused_computation | convolution fusion | flops 3123302400 | bytes 9547776 | tf_op jit(solution)/shard_map/dot_general | solution.py:51
  564.3 6.9 fusion.12
  579.8 19.7 %all-to-all-done.4 = bf16[4,512,384]{2,1,0:T(8,128)(2,1)S(1)} async-done(((bf16[4,512,384]{2,1,0:T(8,128)(2,1)}), bf16[4,512,384]{2,1,0:T(8,128)(2,1)S(1)}, u32[]{:S(2)}, u32[]{:S(2)}) %all-to-all-start.4) | async-done | bytes 1572896 | tf_op jit(solution)/shard_map/all_to_all | solution.py:71
  608.2 24.2 %all-reduce.11 = (f32[4,768]{1,0:T(4,128)}, f32[2,128]{1,0:T(2,128)S(1)}, f32[2,768]{1,0:T(2,128)S(1)}) all-reduce(f32[4,768]{1,0:T(4,128)S(1)} %slice.296, f32[2,128]{1,0:T(2,128)S(1)} %slice.298, f32[2,768]{1,0:T(2,128)S(1)} %slice.301), channel_id=1, replica_groups=mesh['shard'=2,'ctx'=4,'tensor'=4] {'shard','ctx'}, use_global_device_ids=true, to_apply=%region_22.23 | all-reduce | flops 4864 | bytes 38912 | tf_op jit(solution)/shard_map/psum | solution.py:826
  634.2 39.4 %all-reduce.10 = (f32[2,1536]{1,0:T(2,128)S(1)}, f32[4,256]{1,0:T(4,128)}) all-reduce(f32[2,1536]{1,0:T(2,128)S(1)} %pad_maximum_fusion.6, f32[4,256]{1,0:T(4,128)S(1)} %slice.297), channel_id=1, replica_groups=mesh['shard'=2,'ctx'=4,'tensor'=4] {'shard','ctx','tensor'}, use_global_device_ids=true, to_apply=%region_16.17 | all-reduce | flops 4096 | bytes 32768 | tf_op jit(solution)/shard_map/psum | solution.py:823
  (346 shorter events, 219.0 us)
Async XLA Ops:
  7.2 102.5 %all-gather.5.cloned.1.call-start = ((), (), s32[]{:S(2)}) async-start(), calls=%async_computation.12 | async-start | bytes 6635520 | tf_op jit(solution)/shard_map/all_gather | solution.py:63
  11.5 139.9 %all-gather.7.cloned.1.call-start = ((), (), s32[]{:S(2)}) async-start(), calls=%async_computation.13 | async-start | bytes 5750784 | tf_op jit(solution)/shard_map/all_gather | solution.py:63
  12.7 265.2 %all-gather.9.cloned.1.call-start = ((), (), s32[]{:S(2)}) async-start(), calls=%async_computation.16 | async-start | bytes 21233664 | tf_op jit(solution)/shard_map/all_gather | solution.py:63
  20.1 45.0 %all-to-all-start = ((bf16[4,512,384]{2,1,0:T(8,128)(2,1)}), bf16[4,512,384]{2,1,0:T(8,128)(2,1)S(1)}, u32[]{:S(2)}, u32[]{:S(2)}) async-start(bf16[4,512,384]{2,1,0:T(8,128)(2,1)} %broadcast_in_dim.65), calls=%async_computation | async-start | bytes 3145728 | tf_op jit(solution)/shard_map/all_to_all | solution.py:71
  31.8 44.2 %collective-permute-start.3 = (bf16[32,384]{1,0:T(8,128)(2,1)S(1)}, bf16[32,384]{1,0:T(8,128)(2,1)S(1)}, u32[]{:S(2)}, u32[]{:S(2)}) collective-permute-start(bf16[32,384]{1,0:T(8,128)(2,1)S(1)} %concatenate.61), channel_id=1, source_target_pairs={{0,3},{1,0},{2,1},{3,2},{4,7},{5,4},{6,5},{7,6},{8,11},{9,8},{10,9... | collective-permute-start | bytes 73736 | tf_op jit(solution)/shard_map/ppermute | solution.py:84
  35.5 40.5 %collective-permute-start.2 = (bf16[32,384]{1,0:T(8,128)(2,1)S(1)}, bf16[32,384]{1,0:T(8,128)(2,1)S(1)}, u32[]{:S(2)}, u32[]{:S(2)}) collective-permute-start(bf16[32,384]{1,0:T(8,128)(2,1)S(1)} %concatenate.61), channel_id=1, source_target_pairs={{0,2},{1,3},{2,0},{3,1},{4,6},{5,7},{6,4},{7,5},{8,10},{9,11},{10,... | collective-permute-start | bytes 73736 | tf_op jit(solution)/shard_map/ppermute | solution.py:84
  35.5 40.4 %collective-permute-start.1 = (bf16[32,384]{1,0:T(8,128)(2,1)S(1)}, bf16[32,384]{1,0:T(8,128)(2,1)S(1)}, u32[]{:S(2)}, u32[]{:S(2)}) collective-permute-start(bf16[32,384]{1,0:T(8,128)(2,1)S(1)} %concatenate.61), channel_id=1, source_target_pairs={{0,1},{1,2},{2,3},{3,0},{4,5},{5,6},{6,7},{7,4},{8,9},{9,10},{10,1... | collective-permute-start | bytes 73736 | tf_op jit(solution)/shard_map/ppermute | solution.py:84
  66.4 40.6 %all-to-all-start.1 = ((bf16[4,512,384]{2,1,0:T(8,128)(2,1)}), bf16[4,512,384]{2,1,0:T(8,128)(2,1)}, u32[]{:S(2)}, u32[]{:S(2)}) async-start(bf16[4,512,384]{2,1,0:T(8,128)(2,1)} %broadcast_in_dim.144), calls=%async_computation.1 | async-start | bytes 3145728 | tf_op jit(solution)/shard_map/all_to_all | solution.py:71
  132.0 18.2 %collective-permute-start.7 = (f32[12]{0:T(128)S(1)}, f32[12]{0:T(128)S(1)}, u32[]{:S(2)}, u32[]{:S(2)}) collective-permute-start(f32[12]{0:T(128)S(1)} %slice_bitcast_fusion.10), channel_id=1, source_target_pairs={{0,8},{4,12},{1,9},{5,13},{2,10},{6,14},{3,11},{7,15},{16,24},{20,... | collective-permute-start | bytes 152 | tf_op jit(solution)/shard_map/ppermute | solution.py:43
  135.5 14.6 %collective-permute-start.5 = (f32[12]{0:T(128)S(1)}, f32[12]{0:T(128)S(1)}, u32[]{:S(2)}, u32[]{:S(2)}) collective-permute-start(f32[12]{0:T(128)S(1)} %slice_bitcast_fusion.10), channel_id=1, source_target_pairs={{0,4},{4,8},{8,12},{1,5},{5,9},{9,13},{2,6},{6,10},{10,14},{3,7},{... | collective-permute-start | bytes 152 | tf_op jit(solution)/shard_map/ppermute | solution.py:43
  137.8 12.6 %collective-permute-start.8 = (bf16[768,128]{1,0:T(8,128)(2,1)S(1)}, bf16[768,128]{1,0:T(8,128)(2,1)S(1)}, u32[]{:S(2)}, u32[]{:S(2)}) collective-permute-start(bf16[768,128]{1,0:T(8,128)(2,1)S(1)} %convert_element_type.320), channel_id=1, source_target_pairs={{0,12},{1,13},{2,14},{3,15},{16,28},{17,29},{18,30},{19,31}} | collective-permute-start | bytes 589832 | tf_op jit(solution)/shard_map/ppermute | solution.py:43
  158.6 44.0 %all-to-all-start.2 = ((bf16[4,128,1664]{2,1,0:T(8,128)(2,1)}), bf16[4,128,1664]{2,1,0:T(8,128)(2,1)S(1)}, u32[]{:S(2)}, u32[]{:S(2)}) async-start(bf16[4,128,1664]{2,1,0:T(8,128)(2,1)} %bitcast.153), calls=%async_computation.2 | async-start | bytes 3407872 | tf_op jit(solution)/shard_map/all_to_all | solution.py:71
  207.8 43.0 %all-to-all-start.3 = ((bf16[4,128,1664]{2,1,0:T(8,128)(2,1)}), bf16[4,128,1664]{2,1,0:T(8,128)(2,1)S(1)}, u32[]{:S(2)}, u32[]{:S(2)}) async-start(bf16[4,128,1664]{2,1,0:T(8,128)(2,1)} %broadcast_in_dim.145), calls=%async_computation.3 | async-start | bytes 3407872 | tf_op jit(solution)/shard_map/all_to_all | solution.py:71
  211.5 241.0 %reduce-scatter.6.cloned.1.call-start = ((), (), s32[]{:S(2)}) async-start(), calls=%async_computation.14 | async-start | bytes 21233664 | tf_op jit(solution)/shard_map/reduce_scatter | solution.py:67
  335.4 43.4 %all-to-all-start.5 = ((bf16[4,128,1664]{2,1,0:T(8,128)(2,1)}), bf16[4,128,1664]{2,1,0:T(8,128)(2,1)}, u32[]{:S(2)}, u32[]{:S(2)}) async-start(bf16[4,128,1664]{2,1,0:T(8,128)(2,1)} %bitcast.126), calls=%async_computation.5 | async-start | bytes 3407872 | tf_op jit(solution)/shard_map/all_to_all | solution.py:71
  386.8 43.8 %all-to-all-start.6 = ((bf16[4,128,1664]{2,1,0:T(8,128)(2,1)}), bf16[4,128,1664]{2,1,0:T(8,128)(2,1)}, u32[]{:S(2)}, u32[]{:S(2)}) async-start(bf16[4,128,1664]{2,1,0:T(8,128)(2,1)} %broadcast_in_dim.152), calls=%async_computation.6 | async-start | bytes 3407872 | tf_op jit(solution)/shard_map/all_to_all | solution.py:71
  391.2 161.1 %reduce-scatter.10.cloned.1.call-start = ((), (), s32[]{:S(2)}) async-start(), calls=%async_computation.17 | async-start | bytes 5750784
  466.5 20.1 %collective-permute-start.13 = (bf16[768,128]{1,0:T(8,128)(2,1)S(1)}, bf16[768,128]{1,0:T(8,128)(2,1)S(1)}, u32[]{:S(2)}, u32[]{:S(2)}) collective-permute-start(bf16[768,128]{1,0:T(8,128)(2,1)S(1)} %convert_element_type.357), channel_id=1, source_target_pairs={{12,0},{13,1},{14,2},{15,3},{28,16},{29,17},{30,18},{31,19}} | collective-permute-start | bytes 589832 | tf_op jit(solution)/shard_map/ppermute | solution.py:43
  467.8 18.8 %collective-permute-start.11 = (bf16[768,128]{1,0:T(8,128)(2,1)S(1)}, bf16[768,128]{1,0:T(8,128)(2,1)S(1)}, u32[]{:S(2)}, u32[]{:S(2)}) collective-permute-start(bf16[768,128]{1,0:T(8,128)(2,1)S(1)} %convert_element_type.357), channel_id=1, source_target_pairs={{8,0},{12,4},{9,1},{13,5},{10,2},{14,6},{11,3},{15,7},{24,16},{28,... | collective-permute-start | bytes 589832 | tf_op jit(solution)/shard_map/ppermute | solution.py:43
  469.1 17.5 %collective-permute-start.9 = (bf16[768,128]{1,0:T(8,128)(2,1)S(1)}, bf16[768,128]{1,0:T(8,128)(2,1)S(1)}, u32[]{:S(2)}, u32[]{:S(2)}) collective-permute-start(bf16[768,128]{1,0:T(8,128)(2,1)S(1)} %convert_element_type.357), channel_id=1, source_target_pairs={{4,0},{8,4},{12,8},{5,1},{9,5},{13,9},{6,2},{10,6},{14,10},{7,3},{... | collective-permute-start | bytes 589832 | tf_op jit(solution)/shard_map/ppermute | solution.py:43
  511.3 31.9 %all-to-all-start.8 = ((bf16[4,528,256]{2,1,0:T(8,128)(2,1)}), bf16[4,528,256]{2,1,0:T(8,128)(2,1)S(1)}, u32[]{:S(2)}, u32[]{:S(2)}) async-start(bf16[4,528,256]{2,1,0:T(8,128)(2,1)} %broadcast_in_dim.156), calls=%async_computation.8 | async-start | bytes 2162688 | tf_op jit(solution)/shard_map/all_to_all | solution.py:71
  515.9 177.7 %reduce-scatter.8.cloned.1.call-start = ((), (), s32[]{:S(2)}) async-start(), calls=%async_computation.15 | async-start | bytes 6635520 | tf_op jit(solution)/shard_map/reduce_scatter | solution.py:67
  558.0 41.4 %all-to-all-start.4 = ((bf16[4,512,384]{2,1,0:T(8,128)(2,1)}), bf16[4,512,384]{2,1,0:T(8,128)(2,1)S(1)}, u32[]{:S(2)}, u32[]{:S(2)}) async-start(bf16[4,512,384]{2,1,0:T(8,128)(2,1)} %bitcast.128), calls=%async_computation.4 | async-start | bytes 3145728 | tf_op jit(solution)/shard_map/all_to_all | solution.py:71
  599.4 74.8 %all-to-all-start.7 = ((bf16[4,512,512]{2,1,0:T(8,128)(2,1)}), bf16[4,512,512]{2,1,0:T(8,128)(2,1)}, u32[]{:S(2)}, u32[]{:S(2)}) async-start(bf16[4,512,512]{2,1,0:T(8,128)(2,1)} %pad_maximum_fusion.1), calls=%async_computation.7 | async-start | bytes 4194304 | tf_op jit(solution)/shard_map/all_to_all | solution.py:71
  (49 other events, 482.4 us)
Sparse Core Ops, SparseCore 0:
  11.7 46.5 all-gather.4
  60.7 40.5 all-gather.6
  103.2 100.0 all-gather.8
  328.1 124.2 reduce-scatter.5
  460.4 55.8 reduce-scatter.9
  554.8 60.1 reduce-scatter.7

commit v2 on v1

v2 whole, which is shorter than its diff:
```python
from functools import partial

import jax
import jax.numpy as jnp
from jax import lax
from jax.experimental import pallas as pl
from jax.experimental.pallas import tpu as pltpu
from jax.sharding import PartitionSpec as P

CONV = 4
HALO = 16
LANES = 128
LANES = 128
LANES = 128


epsilon = 1e-05
highest = lax.Precision.HIGHEST
CTX = ("cy", "core")
CHIPS = ("shard", "cy")
ROWS = ("shard", "cy", "core")
f32 = jnp.float32
MESH = pl.DeviceIdType.MESH
bf16 = jnp.bfloat16
BIG = pltpu.CompilerParams(vmem_limit_bytes=56 << 20)


def cost(micros):
    return pl.CostEstimate(flops=micros * 900_000_000, transcendentals=0, bytes_accessed=1 << 20)
BIG = pltpu.CompilerParams(vmem_limit_bytes=56 << 20)


def cost(micros):
    return pl.CostEstimate(flops=micros * 900_000_000, transcendentals=0, bytes_accessed=1 << 20)
BIG = pltpu.CompilerParams(vmem_limit_bytes=56 << 20)


def cost(micros):
    return pl.CostEstimate(flops=micros * 900_000_000, transcendentals=0, bytes_accessed=1 << 20)


def shifted(value, axis, steps):
    count = lax.axis_size(axis)
    leading, last = (max(0, -steps), min(count, count - steps))
    return lax.ppermute(value, axis, [(source, source + steps) for source in range(leading, last)])


def dot_rows(left, right, precision=None):
    return jnp.dot(left, right, preferred_element_type=f32, precision=precision)


def dot_inner(left, right):
    return lax.dot_general(left, right, (((0,), (0,)), ((), ())), preferred_element_type=f32)


def dot_outer(left, right):
    return lax.dot_general(left, right, (((1,), (1,)), ((), ())), preferred_element_type=f32)


def sigmoid(value):
    return 1.0 / (1.0 + jnp.exp(-value))


def gather_rows(value):
    return lax.all_gather(value, ROWS, axis=0, tiled=True)


def scatter_rows(value):
    return lax.psum_scatter(value, ROWS, scatter_dimension=0, tiled=True)


def scatter_chips(value):
    axes = CHIPS if lax.axis_size("core") == 2 else ROWS
    return lax.psum_scatter(value, axes, scatter_dimension=0, tiled=True)


def exchange(blocks):
    return lax.all_to_all(blocks, "tensor", split_axis=0, concat_axis=0, tiled=True)


def spread(block):
    count = lax.axis_size("tensor")
    return exchange(jnp.broadcast_to(block[None], (count,) + block.shape))


def spread_small(block):
    count, index = lax.axis_size("tensor"), lax.axis_index("tensor")
    width = block.shape[1]
    full = jnp.zeros((block.shape[0], count * width), block.dtype)
    for away in range(count):
        moved = block if away == 0 else lax.ppermute(
            block, "tensor", [(i, (i + away) % count) for i in range(count)]
        )
        origin = lax.rem(index - away + count, count)
        full = lax.dynamic_update_slice_in_dim(full, moved, origin * width, 1)
    return full


def halves(value):
    high = value.astype(bf16)
    return high, (value - high.astype(f32)).astype(bf16)


def far_states(packed, reverse):
    count = lax.axis_size(CTX)
    return jnp.stack([
        shifted(packed, CTX, -away if reverse else away) for away in range(1, count)
    ])


def row_iota(shape):
    return lax.broadcasted_iota(jnp.int32, shape, 0)


def col_iota(shape):
    return lax.broadcasted_iota(jnp.int32, shape, 1)


def expander(lanes, width, per):
    low = row_iota((lanes, width)) * per
    at = col_iota((lanes, width))
    return ((at >= low) & (at < low + per)).astype(f32)


def head_fold(width, lanes, per):
    low = col_iota((width, lanes)) * per
    at = row_iota((width, lanes))
    return ((at >= low) & (at < low + per)).astype(f32)


def pack_state(state, through):
    high, low = halves(through)
    row = row_iota((16, LANES))
    tail = jnp.where(row == 0, high.astype(f32), jnp.where(row == 1, low.astype(f32), 0.0))
    return jnp.concatenate([state, tail], axis=0).astype(bf16)


def join_states(far_ref, inner, per):
    spread_heads = head_fold(inner, LANES, per)
    total = None
    for k in reversed(range(far_ref.shape[0])):
        state = far_ref[k, :inner, :].astype(f32)
        if total is not None:
            through = far_ref[k, inner : inner + 16, :].astype(f32)
            through = through[0:1] + through[1:2]
            state = state + jnp.sum(spread_heads * through, axis=1, keepdims=True) * total
        total = state
    return total


def thirds(value):
    high = value.astype(bf16)
    rest = value - high.astype(f32)
    middle = rest.astype(bf16)
    return high, middle, (rest - middle.astype(f32)).astype(bf16)


def spread_lanes(value, grow):
    ones = grow.astype(bf16)
    return sum(dot_rows(part, ones) for part in thirds(value))


def left_sums(zero_one, value):
    return sum(dot_rows(zero_one, part) for part in thirds(value))


def fold_heads(value, folds):
    high, low = halves(value)
    return dot_rows(high, folds) + dot_rows(low, folds)


def conv_pre(value_ref, column, taps_ref, taps_column, same_ref, tokens):
    rows = value_ref[:, pl.ds(column, LANES)]
    total = None
    for offset in range(CONV):
        first = HALO - CONV + 1 + offset
        term = rows[first : first + tokens] * (
            same_ref[offset] * taps_ref[offset : offset + 1, pl.ds(taps_column, LANES)]
        )
        total = term if total is None else total + term
    return rows, total


def enter_kernel(mixed_ref, w_ref, taps_ref, same_ref, bias_ref, decay_ref, end_ref, link_ref,
                 value_ref, act_ref, scaled_ref, step_ref, run_ref, run_exp_ref,
                 state_ref, *, inner, nstate, per):
    tokens = act_ref.shape[0]
    width = 2 * inner + 2 * nstate + LANES
    tile = 384

    def matmul(i, _):
        columns = pl.ds(pl.multiple_of(i * tile, LANES), tile)
        value_ref[:, columns] = dot_rows(mixed_ref[...], w_ref[:, columns])
        return 0

    lax.fori_loop(0, width // tile, matmul, 0)

    def conv(i, _):
        at = pl.multiple_of(i * LANES, LANES)
        _, total = conv_pre(value_ref, inner + at, taps_ref, at, same_ref, tokens)
        act_ref[:, pl.ds(at, LANES)] = (total * sigmoid(total)).astype(bf16)
        return 0

    lax.fori_loop(0, (inner + 2 * nstate) // LANES, conv, 0)
    raw = value_ref[HALO:, 2 * inner + 2 * nstate :] + bias_ref[...]
    step = jnp.maximum(raw, 0.0) + jnp.log1p(jnp.exp(-jnp.abs(raw)))
    log_decay = step * -jnp.exp(decay_ref[...])
    tri = (row_iota((tokens, tokens)) >= col_iota((tokens, tokens))).astype(bf16)
    running = left_sums(tri, log_decay)
    step_ref[...] = step
    run_ref[...] = running
    grow = expander(LANES, inner, per)
    run_exp_ref[...] = spread_lanes(running, grow)
    signal = act_ref[:, :inner].astype(f32)
    scaled_ref[...] = (signal * spread_lanes(step, grow)).astype(bf16)
    toward = step * jnp.exp(running[tokens - 1 :] - running) * end_ref[...]
    pushed = (signal * spread_lanes(toward, grow)).astype(bf16)
    through = jnp.exp(running[tokens - 1 :]) * link_ref[tokens - 1 :]
    state_ref[...] = pack_state(dot_inner(pushed, act_ref[:, inner : inner + nstate]), through)


def whole(a):
    return pl.BlockSpec(a.shape, lambda i: (0,) * len(a.shape))


def columns(a, width, at=0):
    assert at % width == 0
    return pl.BlockSpec((a.shape[0], width), lambda i: (0, at // width))


def enter(mixed_ext, weights, taps, same, bias, decay, at_end, link, inner, nstate, per):
    ext = mixed_ext.shape[0]
    tokens = ext - HALO
    wide = 2 * inner + 2 * nstate + LANES
    shape = jax.ShapeDtypeStruct
    outs = [
        shape((ext, wide), f32), shape((tokens, inner + 2 * nstate), bf16),
        shape((tokens, inner), bf16), shape((tokens, LANES), f32), shape((tokens, LANES), f32),
        shape((tokens, inner), f32), shape((inner + 16, nstate), bf16),
    ]
    return pl.pallas_call(
        partial(enter_kernel, inner=inner, nstate=nstate, per=per),
        grid=(1,),
        in_specs=[whole(mixed_ext), columns(weights, wide)]
        + [whole(a) for a in (taps, same, bias, decay, at_end, link)],
        out_specs=[whole(o) for o in outs],
        out_shape=outs,
        compiler_params=BIG,
        cost_estimate=cost(8),
        name="enter",
    )(mixed_ext, weights, taps, same, bias, decay, at_end, link)


def masked_scores(query, keys, seg_col_ref, seg_row_ref, start, stop):
    shape = (stop - start, stop)
    allowed = (row_iota(shape) + start >= col_iota(shape)) & (
        seg_col_ref[start:stop, :1] == seg_row_ref[:, :stop]
    )
    return jnp.where(allowed, dot_outer(query[start:stop], keys[:stop]), 0.0)


def intra_kernel(act_ref, scaled_ref, run_t_ref, run_exp_ref, seg_col_ref, seg_row_ref,
                 inner_ref, scores_ref, *, inner, nstate, per, block):
    tokens = act_ref.shape[0]
    keys = act_ref[:, inner : inner + nstate]
    query = act_ref[:, inner + nstate :]
    for start in range(0, tokens, block):
        stop = start + block
        scores_ref[start:stop, :stop] = masked_scores(
            query, keys, seg_col_ref, seg_row_ref, start, stop
        )

    def pair(i, _):
        columns = pl.ds(pl.multiple_of(i * LANES, LANES), LANES)
        scaled = scaled_ref[:, columns]
        lane = col_iota(scaled.shape)
        run = run_exp_ref[:, columns]
        for start in range(0, tokens, block):
            stop = start + block
            total = None
            for h in range(LANES // per):
                mine = (lane >= h * per) & (lane < (h + 1) * per)
                vals = jnp.where(mine, scaled, jnp.zeros_like(scaled))[:stop]
                row = run_t_ref[i * (LANES // per) + h, :, :stop]
                decay = jnp.exp(jnp.minimum(run[start:stop, h * per : h * per + 1] - row, 0.0))
                weight = (decay * scores_ref[start:stop, :stop]).astype(bf16)
                term = dot_rows(weight, vals)
                total = term if total is None else total + term
            inner_ref[start:stop, columns] = total
        return 0

    lax.fori_loop(0, inner // LANES, pair, 0)


def intra(act, scaled, run_t, run_exp, seg_col, seg_row, inner, nstate, per):
    tokens = act.shape[0]
    return pl.pallas_call(
        partial(intra_kernel, inner=inner, nstate=nstate, per=per, block=128),
        out_shape=jax.ShapeDtypeStruct((tokens, inner), f32),
        scratch_shapes=[pltpu.VMEM((tokens, tokens), f32)],
        compiler_params=BIG,
        cost_estimate=cost(10),
        name="intra",
    )(act, scaled, run_t, run_exp, seg_col, seg_row)


def leave_kernel(act_ref, inner_ref, z_ref, far_ref, run_exp_ref, link_ref, skip_ref, gain_ref,
                 wa_ref, wb_ref, mixer_ref, part_ref, square_ref, state_ref, *, inner, nstate, per):
    query = act_ref[:, inner + nstate :]
    state = join_states(far_ref, inner, per)
    state_ref[...] = state
    carried = dot_outer(query, state.astype(bf16)) * (
        jnp.exp(run_exp_ref[...]) * link_ref[...]
    )
    mixer = inner_ref[...] + carried + skip_ref[...] * act_ref[:, :inner].astype(f32)
    mixer_ref[...] = mixer
    z = z_ref[HALO:, :]
    gated = mixer * (z * sigmoid(z))
    square_ref[...] = row_sums(gated * gated)
    lifted = (gated * gain_ref[...]).astype(bf16)
    half = inner // 2
    part_ref[...] = (
        dot_outer(lifted[:, :half], wa_ref[...]) + dot_outer(lifted[:, half:], wb_ref[...])
    ).astype(bf16)


def row_sums(value):
    folded = value[:, :LANES]
    for at in range(LANES, value.shape[1], LANES):
        folded = folded + value[:, at : at + LANES]
    ones = jnp.ones((8, LANES), bf16)
    high, low = halves(folded)
    return dot_outer(ones, high) + dot_outer(ones, low)


def as_column(row):
    n = row.shape[1]
    eye = row_iota((n, n)) == col_iota((n, n))
    return jnp.sum(jnp.where(eye, row, 0.0), axis=1, keepdims=True)


def leave(act, within, value, far, run_exp, link, skip, gain, weights, inner, nstate, per):
    tokens = act.shape[0]
    depth = weights.shape[0]
    half = inner // 2
    first = 2 * inner + 2 * nstate + LANES
    outs = [jax.ShapeDtypeStruct((tokens, inner), f32), jax.ShapeDtypeStruct((tokens, depth), bf16),
            jax.ShapeDtypeStruct((8, tokens), f32), jax.ShapeDtypeStruct((inner, nstate), f32)]
    return pl.pallas_call(
        partial(leave_kernel, inner=inner, nstate=nstate, per=per),
        grid=(1,),
        in_specs=[whole(act), whole(within), columns(value, inner), whole(far), whole(run_exp),
                  whole(link), whole(skip), whole(gain), columns(weights, half, first),
                  columns(weights, half, first + half)],
        out_specs=[whole(o) for o in outs],
        out_shape=outs,
        compiler_params=BIG,
        cost_estimate=cost(8),
        name="leave",
    )(act, within, value, far, run_exp, link, skip, gain, weights, weights)


def tensor_barrier(me, n):
    barrier = pltpu.get_barrier_semaphore()
    for d in range(1, n):
        pl.semaphore_signal(
            barrier, inc=1, device_id={"tensor": lax.rem(me + d, n)}, device_id_type=MESH
        )
    pl.semaphore_wait(barrier, n - 1)


def push(source, target, sems, slot, peer):
    send, receive = sems
    return pltpu.make_async_remote_copy(
        src_ref=source, dst_ref=target, send_sem=send.at[slot], recv_sem=receive.at[slot],
        device_id={"tensor": peer}, device_id_type=MESH,
    )


def residual_kernel(part_ref, square_ref, x_ref, res_ref, stat_ref, own_ref,
                    inbox, square_box, res_box, stat_box, *sems, di_all, n):
    me = lax.axis_index("tensor")
    rows, depth = part_ref.shape
    own = rows // n
    groups = [(sems[2 * i], sems[2 * i + 1]) for i in range(4)]
    mine = pl.ds(pl.multiple_of(me * own, own), own)
    tensor_barrier(me, n)
    first, second = [], []
    for d in range(1, n):
        peer = lax.rem(me + d, n)
        theirs = pl.ds(pl.multiple_of(peer * own, own), own)
        first.append(push(part_ref.at[theirs], inbox.at[d - 1], groups[0], d - 1, peer))
        first.append(push(square_ref.at[:, theirs], square_box.at[d - 1], groups[1], d - 1, peer))
    for copy in first:
        copy.start()
    total = part_ref[mine, :].astype(f32)
    square = square_ref[:, mine]
    for copy in first:
        copy.wait_recv()
    for d in range(1, n):
        total = total + inbox[d - 1].astype(f32)
        square = square + square_box[d - 1]
    own_ref[...] = total
    scale = lax.rsqrt(square / di_all + epsilon)
    stat_box[:, mine] = scale
    res_box[mine, :] = (x_ref[mine, :].astype(f32) + total * as_column(scale[:1])).astype(bf16)
    for d in range(1, n):
        peer = lax.rem(me + d, n)
        second.append(push(res_box.at[mine], res_box.at[mine], groups[2], d - 1, peer))
        second.append(push(stat_box.at[:, mine], stat_box.at[:, mine], groups[3], d - 1, peer))
    for copy in second:
        copy.start()
    for copy in first:
        copy.wait_send()
    for copy in second:
        copy.wait()
    res_ref[...] = res_box[...]
    stat_ref[...] = stat_box[...]


def pairs(count, n):
    return [pltpu.SemaphoreType.DMA((n - 1,))] * (2 * count)


def residual_step(part, square, x, di_all):
    n = lax.axis_size("tensor")
    tokens, depth = part.shape
    own = tokens // n
    shape = jax.ShapeDtypeStruct
    return pl.pallas_call(
        partial(residual_kernel, di_all=di_all, n=n),
        in_specs=[pl.BlockSpec(memory_space=pltpu.VMEM)] * 3,
        out_specs=[pl.BlockSpec(memory_space=pltpu.VMEM)] * 3,
        out_shape=[shape((tokens, depth), bf16), shape((8, tokens), f32), shape((own, depth), f32)],
        scratch_shapes=[
            pltpu.VMEM((n - 1, own, depth), bf16), pltpu.VMEM((n - 1, 8, own), f32),
            pltpu.VMEM((tokens, depth), bf16), pltpu.VMEM((8, tokens), f32),
        ] + pairs(4, n),
        compiler_params=pltpu.CompilerParams(
            vmem_limit_bytes=40 << 20, collective_id=1, has_side_effects=True
        ),
        cost_estimate=cost(60),
        name="residual_step",
    )(part, square, x)


def turn_kernel(dmix_ref, dgate_ref, res_ref, cot_ref, own_ref, gain_ref,
                dres_ref, notes_ref, gains_ref,
                inbox, gate_box, dres_box, notes_box, *sems, n):
    me = lax.axis_index("tensor")
    rows, depth = dmix_ref.shape
    own = rows // n
    groups = [(sems[2 * i], sems[2 * i + 1]) for i in range(4)]
    mine = pl.ds(pl.multiple_of(me * own, own), own)
    tensor_barrier(me, n)
    first, second = [], []
    for d in range(1, n):
        peer = lax.rem(me + d, n)
        theirs = pl.ds(pl.multiple_of(peer * own, own), own)
        first.append(push(dmix_ref.at[theirs], inbox.at[d - 1], groups[0], d - 1, peer))
        first.append(push(dgate_ref.at[theirs], gate_box.at[d - 1], groups[1], d - 1, peer))
    for copy in first:
        copy.start()
    res = res_ref[mine, :].astype(f32)
    scale = lax.rsqrt(jnp.mean(res * res, axis=1, keepdims=True) + epsilon)
    normed = res * scale
    dmix = dmix_ref[mine, :].astype(f32)
    dgate = dgate_ref[mine, :]
    for copy in first:
        copy.wait_recv()
    for d in range(1, n):
        dmix = dmix + inbox[d - 1].astype(f32)
        dgate = dgate + gate_box[d - 1]
    gains_ref[...] = jnp.broadcast_to(jnp.sum(dmix * normed, axis=0, keepdims=True), gains_ref.shape)
    lifted = dmix * gain_ref[...]
    inside = jnp.mean(lifted * normed, axis=1, keepdims=True)
    dres = (cot_ref[mine, :].astype(f32) + scale * (lifted - normed * inside)).astype(bf16)
    cross = jnp.sum(dres.astype(f32) * own_ref[...], axis=1, keepdims=True)
    dres_box[mine, :] = dres
    notes_box[mine, :] = jnp.where(col_iota(dgate.shape) == LANES - 1, cross, dgate)
    for d in range(1, n):
        peer = lax.rem(me + d, n)
        second.append(push(dres_box.at[mine], dres_box.at[mine], groups[2], d - 1, peer))
        second.append(push(notes_box.at[mine], notes_box.at[mine], groups[3], d - 1, peer))
    for copy in second:
        copy.start()
    for copy in first:
        copy.wait_send()
    for copy in second:
        copy.wait()
    dres_ref[...] = dres_box[...]
    notes_ref[...] = notes_box[...]


def turn_step(dmix, dgate, residual, cot, own_part, gain):
    n = lax.axis_size("tensor")
    tokens, depth = dmix.shape
    own = tokens // n
    shape = jax.ShapeDtypeStruct
    return pl.pallas_call(
        partial(turn_kernel, n=n),
        in_specs=[pl.BlockSpec(memory_space=pltpu.VMEM)] * 6,
        out_specs=[pl.BlockSpec(memory_space=pltpu.VMEM)] * 3,
        out_shape=[shape((tokens, depth), bf16), shape((tokens, LANES), f32),
                   shape((8, depth), f32)],
        scratch_shapes=[
            pltpu.VMEM((n - 1, own, depth), bf16), pltpu.VMEM((n - 1, own, LANES), f32),
            pltpu.VMEM((tokens, depth), bf16), pltpu.VMEM((tokens, LANES), f32),
        ] + pairs(4, n),
        compiler_params=pltpu.CompilerParams(
            vmem_limit_bytes=40 << 20, collective_id=2, has_side_effects=True
        ),
        cost_estimate=cost(60),
        name="turn_step",
    )(dmix, dgate, residual, cot, own_part, gain)


def finish_kernel(grad_ref, halo_ref, w_ref, x_ref, dres_ref, gain_ref, mid_ref, state_ref,
                  out_ref, gains_ref, state_out_ref,
                  outbox, inbox, cross_box, cross_in, gains_box, gains_in, state_in, *sems, n):
    me = lax.axis_index("tensor")
    rows, depth = x_ref.shape
    quarter = depth // n
    groups = [(sems[2 * i], sems[2 * i + 1]) for i in range(4)]
    tensor_barrier(me, n)
    x = x_ref[...].astype(f32)
    scale = lax.rsqrt(jnp.mean(x * x, axis=1, keepdims=True) + epsilon)
    copies = []
    for d in range(1, n):
        peer = lax.rem(me + d, n)
        copies.append(push(state_ref, state_in.at[d - 1], groups[3], d - 1, peer))
        copies[-1].start()
    cross = jnp.zeros((8, rows), f32)
    kept = None
    for d in tuple(range(1, n)) + (0,):
        peer = lax.rem(me + d, n)
        theirs = pl.ds(pl.multiple_of(peer * quarter, LANES), quarter)
        w = w_ref[theirs, :]
        block = dot_outer(grad_ref[HALO:, :], w)
        tail = dot_outer(halo_ref[...], w)
        block = jnp.concatenate([block[: rows - HALO], block[rows - HALO :] + tail], axis=0)
        normed = x_ref[:, theirs].astype(f32) * scale
        cross = cross + row_sums(block * normed * gain_ref[:, theirs])
        gains = jnp.where(
            row_iota((8, quarter)) == 0, jnp.sum(block * normed, axis=0, keepdims=True),
            mid_ref[:, theirs],
        )
        if d == 0:
            kept, kept_gains, kept_normed = block, gains, normed
            continue
        gains_box[d - 1] = gains
        outbox[d - 1] = block.astype(bf16)
        copies.append(push(outbox.at[d - 1], inbox.at[d - 1], groups[0], d - 1, peer))
        copies[-1].start()
        copies.append(push(gains_box.at[d - 1], gains_in.at[d - 1], groups[1], d - 1, peer))
        copies[-1].start()
    cross_box[...] = cross
    for d in range(1, n):
        copies.append(
            push(cross_box, cross_in.at[d - 1], groups[2], d - 1, lax.rem(me + d, n))
        )
        copies[-1].start()
    for copy in copies:
        copy.wait()
    state = state_ref[...]
    for d in range(1, n):
        kept = kept + inbox[d - 1].astype(f32)
        kept_gains = kept_gains + gains_in[d - 1]
        cross = cross + cross_in[d - 1]
        state = state + state_in[d - 1]
    gains_ref[...] = kept_gains
    state_out_ref[...] = state
    here = pl.ds(pl.multiple_of(me * quarter, LANES), quarter)
    inside = jnp.concatenate(
        [as_column(cross[:1, at : at + LANES]) for at in range(0, rows, LANES)], axis=0
    ) / depth
    out_ref[...] = dres_ref[:, here].astype(f32) + scale * (
        kept * gain_ref[:, here] - kept_normed * inside
    )


def finish_step(value_grad, halo, weights, x, dres, gain, gains_mid, state):
    n = lax.axis_size("tensor")
    tokens, depth = x.shape
    quarter = depth // n
    shape = jax.ShapeDtypeStruct
    outs = [shape((tokens, quarter), f32), shape((8, quarter), f32), shape(state.shape, f32)]
    args = (value_grad, halo, weights, x, dres, gain, gains_mid, state)
    return pl.pallas_call(
        partial(finish_kernel, n=n),
        grid=(1,),
        in_specs=[whole(a) if a is not weights else columns(a, value_grad.shape[1]) for a in args],
        out_specs=[whole(o) for o in outs],
        out_shape=outs,
        scratch_shapes=[
            pltpu.VMEM((n - 1, tokens, quarter), bf16), pltpu.VMEM((n - 1, tokens, quarter), bf16),
            pltpu.VMEM((8, tokens), f32), pltpu.VMEM((n - 1, 8, tokens), f32),
            pltpu.VMEM((n - 1, 8, quarter), f32), pltpu.VMEM((n - 1, 8, quarter), f32),
            pltpu.VMEM((n - 1,) + state.shape, f32),
        ] + pairs(4, n),
        compiler_params=pltpu.CompilerParams(
            vmem_limit_bytes=56 << 20, collective_id=3, has_side_effects=True
        ),
        cost_estimate=cost(45),
        name="finish_step",
    )(*args)


def back_kernel(dout_ref, wa_ref, wb_ref, mixer_ref, z_ref, act_ref, run_exp_ref, link_ref, gain_ref,
                stat_ref, through_ref, heads_ref, zgrad_ref, gated_ref, direct_ref, sums_ref,
                *, inner, nstate, di_all):
    scale = stat_ref[:, 0:1]
    cross = stat_ref[:, 1:2]
    mixer = mixer_ref[...]
    z = z_ref[HALO:, :]
    sig = sigmoid(z)
    act = z * sig
    gated = mixer * act
    dout = dout_ref[...]
    grad = jnp.concatenate([dot_rows(dout, wa_ref[...]), dot_rows(dout, wb_ref[...])], axis=1)
    gated_ref[...] = (gated * scale * gain_ref[...]).astype(bf16)
    sums_ref[0:1, :] = jnp.sum(grad * gated * scale, axis=0, keepdims=True)
    gated_grad = scale * (grad * gain_ref[...]) - gated * (scale * scale * scale * cross / di_all)
    zgrad_ref[...] = (gated_grad * mixer * (sig * (1.0 + z * (1.0 - sig)))).astype(bf16)
    heads = gated_grad * act
    heads_ref[...] = heads
    sums_ref[1:2, :] = jnp.sum(heads * act_ref[:, :inner].astype(f32), axis=0, keepdims=True)
    sums_ref[2:, :] = jnp.zeros((6, inner), f32)
    carried = (heads * (jnp.exp(run_exp_ref[...]) * link_ref[...])).astype(bf16)
    direct_ref[:inner, :] = dot_inner(carried, act_ref[:, inner + nstate :]).astype(bf16)
    direct_ref[inner:, :] = through_ref[...]


def back(dout, weights, mixer, value, act, run_exp, link, gain, stats, through, inner, nstate, di_all):
    tokens = act.shape[0]
    half = inner // 2
    first = 2 * inner + 2 * nstate + LANES
    shape = jax.ShapeDtypeStruct
    outs = [shape((tokens, inner), f32), shape((tokens, inner), bf16), shape((tokens, inner), bf16),
            shape((inner + 16, nstate), bf16), shape((8, inner), f32)]
    return pl.pallas_call(
        partial(back_kernel, inner=inner, nstate=nstate, di_all=di_all),
        grid=(1,),
        in_specs=[whole(dout), columns(weights, half, first), columns(weights, half, first + half),
                  whole(mixer), columns(value, inner), whole(act), whole(run_exp), whole(link),
                  whole(gain), whole(stats), whole(through)],
        out_specs=[whole(o) for o in outs],
        out_shape=outs,
        compiler_params=BIG,
        cost_estimate=cost(8),
        name="back",
    )(dout, weights, weights, mixer, value, act, run_exp, link, gain, stats, through)


def intra_back_kernel(heads_ref, act_ref, scaled_ref, run_t_ref, run_exp_ref, seg_col_ref,
                      seg_row_ref, dscaled_ref, dstate_ref, drun_ref, scores_ref, dscores_ref,
                      rows_ref, *, inner, nstate, per, block):
    tokens = act_ref.shape[0]
    keys = act_ref[:, inner : inner + nstate]
    query = act_ref[:, inner + nstate :]
    for start in range(0, tokens, block):
        stop = start + block
        scores_ref[start:stop, :stop] = masked_scores(
            query, keys, seg_col_ref, seg_row_ref, start, stop
        )
    dscores_ref[...] = jnp.zeros_like(dscores_ref)
    drun_ref[...] = jnp.zeros_like(drun_ref)

    def pair(i, _):
        columns = pl.ds(pl.multiple_of(i * LANES, LANES), LANES)
        scaled = scaled_ref[:, columns]
        heads = heads_ref[:, columns].astype(bf16)
        lane = col_iota(scaled.shape)
        run = run_exp_ref[:, columns]
        dscaled_ref[:, columns] = jnp.zeros((tokens, LANES), f32)
        for h in range(LANES // per):
            head = i * (LANES // per) + h
            mine = (lane >= h * per) & (lane < (h + 1) * per)
            vals = jnp.where(mine, scaled, jnp.zeros_like(scaled))
            grads = jnp.where(mine, heads, jnp.zeros_like(heads))
            pick = (col_iota((block, LANES)) == head).astype(bf16)
            for start in range(0, tokens, block):
                stop = start + block
                row = run_t_ref[head, :, :stop]
                decay = jnp.exp(jnp.minimum(run[start:stop, h * per : h * per + 1] - row, 0.0))
                weight = decay * scores_ref[start:stop, :stop]
                dweight = dot_outer(grads[start:stop], vals[:stop])
                dscores_ref[start:stop, :stop] += dweight * decay
                flow = (dweight * weight).astype(bf16)
                dscaled_ref[:stop, columns] += dot_inner(weight.astype(bf16), grads[start:stop])
                picks = jnp.broadcast_to(pick[:1], (stop, LANES))
                drun_ref[start:stop, :] += dot_rows(flow, picks)
                drun_ref[:stop, :] -= dot_inner(flow, pick)
        return 0

    lax.fori_loop(0, inner // LANES, pair, 0)
    dkeys = jnp.zeros((tokens, nstate), f32)
    dstate_ref[:, :nstate] = dkeys
    for start in range(0, tokens, block):
        stop = start + block
        shape = (block, stop)
        allowed = (row_iota(shape) + start >= col_iota(shape)) & (
            seg_col_ref[start:stop, :1] == seg_row_ref[:, :stop]
        )
        grad = jnp.where(allowed, dscores_ref[start:stop, :stop], 0.0).astype(bf16)
        dstate_ref[start:stop, nstate:] = dot_rows(grad, keys[:stop])
        dstate_ref[:stop, :nstate] += dot_inner(grad, query[start:stop])


def intra_back(heads, act, scaled, run_t, run_exp, seg_col, seg_row, inner, nstate, per):
    tokens = act.shape[0]
    shape = jax.ShapeDtypeStruct
    return pl.pallas_call(
        partial(intra_back_kernel, inner=inner, nstate=nstate, per=per, block=128),
        out_shape=[shape((tokens, inner), f32), shape((tokens, 2 * nstate), f32),
                   shape((tokens, LANES), f32)],
        scratch_shapes=[pltpu.VMEM((tokens, tokens), f32), pltpu.VMEM((tokens, tokens), f32),
                        pltpu.VMEM((8, LANES), f32)],
        compiler_params=BIG,
        cost_estimate=cost(20),
        name="intra_back",
    )(heads, act, scaled, run_t, run_exp, seg_col, seg_row)


def conv_back(value_ref, column, taps_ref, same_ref, dact, at, dtaps_ref, tokens):
    ext = tokens + HALO
    rows, total = conv_pre(value_ref, column, taps_ref, at, same_ref, tokens)
    sig = sigmoid(total)
    dpre = dact * (sig * (1.0 + total * (1.0 - sig)))
    drows = None
    for offset in range(CONV):
        first = HALO - CONV + 1 + offset
        kept = dpre * same_ref[offset]
        dtaps_ref[offset : offset + 1, pl.ds(at, LANES)] = jnp.sum(
            kept * rows[first : first + tokens], axis=0, keepdims=True
        )
        term = kept * taps_ref[offset : offset + 1, pl.ds(at, LANES)]
        after = ext - first - tokens
        pieces = [jnp.zeros((first, LANES), f32), term]
        if after:
            pieces.append(jnp.zeros((after, LANES), f32))
        term = jnp.concatenate(pieces, axis=0)
        drows = term if drows is None else drows + term
    return drows


def state_back_kernel(heads_ref, act_ref, step_ref, run_ref, run_exp_ref, link_ref, end_ref,
                      value_ref, taps_ref, same_ref, dstate_ref, in_ref, far_ref,
                      rows_ref, dtaps_ref, leaving_ref, kept_ref, dact_ref, *, inner, nstate, per):
    tokens = act_ref.shape[0]
    keys = act_ref[:, inner : inner + nstate]
    signal = act_ref[:, :inner].astype(f32)
    grow = expander(LANES, inner, per)
    running = run_ref[...]
    state_grad = join_states(far_ref, inner, per)
    lifted = (heads_ref[...] * (jnp.exp(run_exp_ref[...]) * link_ref[...])).astype(bf16)
    dact_ref[:, nstate:] = dot_rows(lifted, in_ref[...].astype(bf16)) + dstate_ref[:, nstate:]
    toward = jnp.exp(running[tokens - 1 :] - running) * end_ref[...]
    toward_exp = spread_lanes(toward, grow)
    pushed = (signal * spread_lanes(step_ref[...] * toward, grow)).astype(bf16)
    leaving_ref[...] = dot_outer(keys, state_grad.astype(bf16)) * toward_exp
    dact_ref[:, :nstate] = dot_rows(pushed, state_grad.astype(bf16)) + dstate_ref[:, :nstate]
    kept = jnp.sum(in_ref[...] * state_grad, axis=1, keepdims=True)
    kept = jnp.sum(head_fold(inner, LANES, per) * kept, axis=0, keepdims=True)
    kept = kept * jnp.exp(running[tokens - 1 :]) * link_ref[tokens - 1 :]
    kept_ref[...] = jnp.broadcast_to(kept, kept_ref.shape)

    def conv(i, _):
        at = pl.multiple_of(i * LANES, LANES)
        drows = conv_back(value_ref, at, taps_ref, same_ref, dact_ref[:, pl.ds(at, LANES)], at,
                          dtaps_ref, tokens)
        rows_ref[:, pl.ds(at, LANES)] = drows.astype(bf16)
        return 0

    lax.fori_loop(0, 2 * nstate // LANES, conv, 0)


def state_back(heads, act, step, running, run_exp, link, at_end, value, taps, same, dstate, state_in,
               far, inner, nstate, per):
    tokens = act.shape[0]
    shape = jax.ShapeDtypeStruct
    outs = [shape((tokens + HALO, 2 * nstate), bf16), shape((CONV, 2 * nstate), f32),
            shape((tokens, inner), f32), shape((8, LANES), f32)]
    args = (heads, act, step, running, run_exp, link, at_end, value, taps, same, dstate, state_in, far)
    specs = [whole(a) for a in args]
    specs[7] = columns(value, 2 * nstate, 2 * inner)
    specs[8] = columns(taps, 2 * nstate, inner)
    return pl.pallas_call(
        partial(state_back_kernel, inner=inner, nstate=nstate, per=per),
        grid=(1,),
        in_specs=specs,
        out_specs=[whole(o) for o in outs],
        out_shape=outs,
        scratch_shapes=[pltpu.VMEM((tokens, 2 * nstate), f32)],
        compiler_params=BIG,
        cost_estimate=cost(6),
        name="state_back",
    )(*args)


def signal_back_kernel(heads_ref, act_ref, step_ref, value_ref, raw_ref, taps_ref, same_ref, bias_ref,
                       decay_ref, skip_ref, mixer_ref, inner_ref, dscaled_ref, drun_ref, leaving_ref,
                       kept_ref, zgrad_ref, state_ref,
                       grad_ref, dtaps_ref, small_ref, dact_ref, *, inner, nstate, per):
    tokens = act_ref.shape[0]
    signal = act_ref[:, :inner].astype(f32)
    grow = expander(LANES, inner, per)
    folds = head_fold(inner, LANES, per).astype(bf16)
    step = step_ref[...]
    heads = heads_ref[...]
    leaving = leaving_ref[...]
    step_exp = spread_lanes(step, grow)
    dscaled = dscaled_ref[...] + leaving
    dact_ref[...] = dscaled * step_exp + skip_ref[...] * heads

    def conv(i, _):
        at = pl.multiple_of(i * LANES, LANES)
        drows = conv_back(value_ref, at, taps_ref, same_ref, dact_ref[:, pl.ds(at, LANES)], at,
                          dtaps_ref, tokens)
        grad_ref[:, pl.ds(inner + at, LANES)] = drows.astype(bf16)
        return 0

    lax.fori_loop(0, inner // LANES, conv, 0)
    carried = mixer_ref[...] - inner_ref[...] - skip_ref[...] * signal
    tri = (row_iota((tokens, tokens)) <= col_iota((tokens, tokens))).astype(bf16)
    strict = (row_iota((tokens, tokens)) > col_iota((tokens, tokens))).astype(bf16)
    back_sum = drun_ref[...] + fold_heads(heads * carried, folds)
    front_sum = fold_heads(signal * step_exp * leaving, folds)
    dlog = left_sums(tri, back_sum) + left_sums(strict, front_sum) + kept_ref[0:1, :]
    rate = -jnp.exp(decay_ref[...])
    dstep = dlog * rate + fold_heads(dscaled * signal, folds)
    draw = dstep * sigmoid(raw_ref[HALO:, :] + bias_ref[...])
    small_ref[0:1, :] = jnp.sum(draw, axis=0, keepdims=True)
    small_ref[1:2, :] = jnp.sum(dlog * step, axis=0, keepdims=True) * rate
    small_ref[2:, :] = jnp.zeros((6, LANES), f32)
    state_at = 2 * inner
    step_at = state_at + 2 * nstate
    grad_ref[:HALO, :inner] = jnp.zeros((HALO, inner), bf16)
    grad_ref[HALO:, :inner] = zgrad_ref[...]
    grad_ref[:, state_at:step_at] = state_ref[...]
    grad_ref[:HALO, step_at:] = jnp.zeros((HALO, LANES), bf16)
    used = col_iota((tokens, LANES)) < inner // per
    grad_ref[HALO:, step_at:] = jnp.where(used, draw, 0.0).astype(bf16)


def signal_back(heads, act, step, value, taps, same, bias, decay, skip, mixer, within, dscaled, drun,
                leaving, kept, z_grad, state_rows, inner, nstate, per):
    tokens = act.shape[0]
    wide = value.shape[1]
    shape = jax.ShapeDtypeStruct
    outs = [shape((tokens + HALO, wide), bf16), shape((CONV, inner), f32), shape((8, LANES), f32)]
    args = (heads, act, step, value, value, taps, same, bias, decay, skip, mixer, within, dscaled, drun,
            leaving, kept, z_grad, state_rows)
    specs = [whole(a) for a in args]
    specs[3] = columns(value, inner, inner)
    specs[4] = columns(value, LANES, wide - LANES)
    specs[5] = columns(taps, inner)
    return pl.pallas_call(
        partial(signal_back_kernel, inner=inner, nstate=nstate, per=per),
        grid=(1,),
        in_specs=specs,
        out_specs=[whole(o) for o in outs],
        out_shape=outs,
        scratch_shapes=[pltpu.VMEM((tokens, inner), f32)],
        compiler_params=BIG,
        cost_estimate=cost(12),
        name="signal_back",
    )(*args)


def swiglu(first, second):
    sig = sigmoid(first)
    act = first * sig
    return act, sig * (1.0 + first * (1.0 - sig)), (act * second).astype(bf16)


def shared_kernel(res_ref, cot_ref, gain_ref, router_ref, chosen_ref, w_ref,
                  out_ref, dmix_ref, mix_ref, gates_ref, dw_ref, first_ref, down_ref, hidden_ref,
                  dval_ref, *, tile):
    rows, depth = res_ref.shape
    wrows = w_ref.shape[1] // 3
    wide = w_ref.shape[2]
    hid = wide // 2
    for p in range(2):
        first_ref[p] = w_ref[:, p * wrows : (p + 1) * wrows, :].reshape(depth, wide)
    down_ref[...] = w_ref[:, 2 * wrows :, :].reshape(depth, wide)

    def part(i, _):
        at = pl.ds(pl.multiple_of(i * tile, tile), tile)
        res = res_ref[at, :].astype(f32)
        scale = lax.rsqrt(jnp.mean(res * res, axis=1, keepdims=True) + epsilon)
        mix_ref[at, :] = (res * scale * gain_ref[...]).astype(bf16)
        mix = mix_ref[at, :]
        chosen = chosen_ref[at, :] > 0.0
        logits = dot_rows(mix, router_ref[...])
        top = jnp.max(jnp.where(chosen, logits, -1e30), axis=1, keepdims=True)
        weight = jnp.where(chosen, jnp.exp(jnp.where(chosen, logits - top, 0.0)), 0.0)
        gates_ref[at, :] = weight / jnp.sum(weight, axis=1, keepdims=True)
        raw = dot_rows(cot_ref[at, :], down_ref[...])
        dmix = None
        for p in range(2):
            value = dot_rows(mix, first_ref[p])
            act, slope, hidden = swiglu(value[:, :hid], value[:, hid:])
            here = pl.ds(p * hid, hid)
            dh = raw[:, p * hid : (p + 1) * hid]
            dval_ref[p, at, :hid] = (dh * value[:, hid:] * slope).astype(bf16)
            dval_ref[p, at, hid:] = (dh * act).astype(bf16)
            hidden_ref[at, here] = hidden
            term = dot_outer(dval_ref[p, at, :], first_ref[p])
            dmix = term if dmix is None else dmix + term
        out_ref[at, :] = dot_outer(hidden_ref[at, :], down_ref[...])
        dmix_ref[at, :] = dmix
        return 0

    lax.fori_loop(0, rows // tile, part, 0)
    for p in range(2):
        dw_ref[:, p * wrows : (p + 1) * wrows, :] = (
            dot_inner(mix_ref[...], dval_ref[p]).astype(bf16).reshape(-1, wrows, wide)
        )
    dw_ref[:, 2 * wrows :, :] = (
        dot_inner(cot_ref[...], hidden_ref[...]).astype(bf16).reshape(-1, wrows, wide)
    )


def shared_expert(residual, cot, gain, weights, router_at, chosen, experts_w):
    rows, depth = residual.shape
    senders, deep, wide = experts_w.shape
    part = 3 * (depth // senders)
    own = deep - part
    assert own % part == 0
    shape = jax.ShapeDtypeStruct
    block = pl.BlockSpec((senders, part, wide), lambda i: (0, own // part, 0))
    grads = shape((senders, part, wide), bf16)
    outs = [shape((rows, depth), f32), shape((rows, depth), f32), shape((rows, depth), bf16),
            shape((rows, LANES), f32)]
    return pl.pallas_call(
        partial(shared_kernel, tile=min(256, rows)),
        grid=(1,),
        in_specs=[whole(residual), whole(cot), whole(gain), columns(weights, LANES, router_at),
                  whole(chosen), block],
        out_specs=[whole(o) for o in outs + [grads]],
        out_shape=outs + [grads],
        scratch_shapes=[
            pltpu.VMEM((2, depth, wide), bf16), pltpu.VMEM((depth, wide), bf16),
            pltpu.VMEM((rows, wide), bf16), pltpu.VMEM((2, rows, wide), bf16),
        ],
        compiler_params=BIG,
        cost_estimate=cost(10),
        name="shared_expert",
    )(residual, cot, gain, weights, chosen, experts_w)


def experts_kernel(mix_ref, cot_ref, gates_ref, router_ref, w_ref, out_in, dmix_in, ds_ref,
                   out_ref, dmix_ref, dgate_ref, dw_ref,
                   total_ref, grads_ref, down_ref, hidden_ref, dval_ref, grad_ref, load_sem,
                   *remote, tile, senders, core):
    step = pl.program_id(0)
    last = step == pl.num_programs(0) - 1
    rows, depth = mix_ref.shape
    wide = w_ref.shape[2]
    hid = wide // 2
    chunks = depth // wide
    deep = depth + depth // 2
    if core == 2:
        inbox, shared_box, send, receive, shared_send, shared_receive = remote
        me = lax.axis_index("core")
        other = 1 - me
        slot = lax.rem(step + me, 2)

        def to_sibling(source, target, send_sem, recv_sem):
            return pltpu.make_async_remote_copy(
                src_ref=source, dst_ref=target, send_sem=send_sem, recv_sem=recv_sem,
                device_id={"core": other}, device_id_type=MESH,
            )

        shared_copy = to_sibling(ds_ref.at[other], shared_box, shared_send, shared_receive)
        pair_copy = lambda k: to_sibling(grad_ref.at[1], inbox.at[k], send.at[k], receive.at[k])
    else:
        slot = 0

    @pl.when(step == 0)
    def _():
        loads = [pltpu.make_async_copy(out_in, total_ref, load_sem.at[0]),
                 pltpu.make_async_copy(dmix_in, grads_ref, load_sem.at[1])]
        for copy in loads:
            copy.start()
        dgate_ref[...] = jnp.zeros_like(dgate_ref)
        if core == 2:
            barrier = pltpu.get_barrier_semaphore()
            pl.semaphore_signal(barrier, inc=1, device_id={"core": other}, device_id_type=MESH)
            pl.semaphore_wait(barrier, 1)
            shared_copy.start()
        for copy in loads:
            copy.wait()

    if core == 2:
        @pl.when((step >= 2) & (step < senders) & (slot == 1))
        def _():
            pair_copy((step - 2) // 2).wait_send()

    @pl.when(step < senders)
    def _():
        pair_grads(
            step, slot, mix_ref, cot_ref, gates_ref, w_ref, dgate_ref, total_ref, grads_ref, down_ref,
            hidden_ref, dval_ref, grad_ref, tile
        )

    if core == 2:
        @pl.when((step < senders) & (slot == 1))
        def _():
            pair_copy(step // 2).start()

        @pl.when((step >= 1) & (slot == 1))
        def _():
            at = (step - 1) // 2

            @pl.when(step <= 2)
            def _():
                shared_copy.wait()

            pair_copy(at).wait_recv()
            dw_ref[0, : 3 * depth, :] = grad_ref[0] + inbox[at]
            dw_ref[0, 3 * depth :, :] = ds_ref[me, at] + shared_box[at]

        @pl.when(last)
        def _():
            pair_copy(senders // 2 - 1).wait_send()
    else:
        dw_ref[0, : 3 * depth, :] = grad_ref[0]
        dw_ref[0, 3 * depth :, :] = ds_ref[0, step]

    @pl.when(last)
    def _():
        gates = gates_ref[...]
        dgate = dgate_ref[...]
        inside = jnp.sum(gates * dgate, axis=1, keepdims=True)
        dlogits = (gates * (dgate - inside)).astype(bf16)
        dmix_ref[...] = (grads_ref[...] + dot_outer(dlogits, router_ref[...])).astype(bf16)
        out_ref[...] = total_ref[...].astype(bf16)


def pair_grads(step, slot, mix_ref, cot_ref, gates_ref, w_ref, dgate_ref, total_ref, grads_ref,
               down_ref, hidden_ref, dval_ref, grad_ref, tile):
    rows, depth = mix_ref.shape
    wide = w_ref.shape[2]
    hid = wide // 2
    chunks = depth // wide
    deep = depth + depth // 2
    for p in range(2):
        for c in range(chunks):
            down_ref[p * hid : (p + 1) * hid, c * wide : (c + 1) * wide] = (
                w_ref[0, p * deep + depth + c * hid : p * deep + depth + (c + 1) * hid, :]
            )
    down = down_ref[...]

    def part(i, _):
        at = pl.ds(pl.multiple_of(i * tile, tile), tile)
        mix = mix_ref[at, :]
        raw = dot_outer(cot_ref[at, :], down)
        gates = gates_ref[at, :]
        lane = col_iota(gates.shape)
        dmix, noted = None, jnp.zeros_like(gates)
        for p in range(2):
            here = lane == 2 * step + p
            gate = jnp.sum(jnp.where(here, gates, 0.0), axis=1, keepdims=True)
            weights = w_ref[0, p * deep : p * deep + depth, :]
            value = dot_rows(mix, weights)
            act, slope, hidden = swiglu(value[:, :hid], value[:, hid:])
            hidden = hidden.astype(f32)
            dh = raw[:, p * hid : (p + 1) * hid]
            noted = noted + jnp.where(here, jnp.sum(hidden * dh, axis=1, keepdims=True), 0.0)
            dh = gate * dh
            dval_ref[p, at, :hid] = (dh * value[:, hid:] * slope).astype(bf16)
            dval_ref[p, at, hid:] = (dh * act).astype(bf16)
            hidden_ref[at, p * hid : (p + 1) * hid] = (gate * hidden).astype(bf16)
            term = dot_outer(dval_ref[p, at, :], weights)
            dmix = term if dmix is None else dmix + term
        dgate_ref[at, :] += noted
        total_ref[at, :] += dot_rows(hidden_ref[at, :], down)
        grads_ref[at, :] += dmix
        return 0

    lax.fori_loop(0, rows // tile, part, 0)
    for c in range(chunks):
        grad = dot_inner(hidden_ref[...], cot_ref[:, c * wide : (c + 1) * wide]).astype(bf16)
        for p in range(2):
            first = p * deep + depth + c * hid
            grad_ref[slot, first : first + hid, :] = grad[p * hid : (p + 1) * hid]
    for p in range(2):
        grad_ref[slot, p * deep : p * deep + depth, :] = (
            dot_inner(mix_ref[...], dval_ref[p]).astype(bf16)
        )


def experts(mix, cot, gates, weights, router_at, experts_w, out, dmix, ds):
    senders, deep, wide = experts_w.shape
    rows, depth = mix.shape
    core = lax.axis_size("core")
    kept = senders // core
    part = deep - 3 * depth
    ds = ds.reshape(kept, core, part, wide).transpose(1, 0, 2, 3)
    shape = jax.ShapeDtypeStruct
    once = lambda a: pl.BlockSpec(
        a.shape, lambda i: (0,) * a.ndim, pipeline_mode=pl.Buffered(1)
    )
    outs = [shape((rows, depth), bf16), shape((rows, depth), bf16), shape((rows, LANES), f32)]
    if core == 2:
        steps = senders + 1
        kept_map = lambda i: (jnp.maximum(i - 1, 0) // 2, 0, 0)
        remote = [
            pltpu.VMEM((kept, 3 * depth, wide), bf16), pltpu.VMEM((kept, part, wide), bf16),
            pltpu.SemaphoreType.DMA((kept,)), pltpu.SemaphoreType.DMA((kept,)),
            pltpu.SemaphoreType.DMA, pltpu.SemaphoreType.DMA,
        ]
        params = pltpu.CompilerParams(
            vmem_limit_bytes=60 << 20, collective_id=4, has_side_effects=True
        )
    else:
        steps, remote, params = senders, [], pltpu.CompilerParams(vmem_limit_bytes=60 << 20)
        kept_map = lambda i: (i, 0, 0)
    return pl.pallas_call(
        partial(experts_kernel, tile=min(256, rows), senders=senders, core=core),
        grid=(steps,),
        in_specs=[once(mix), once(cot), once(gates),
                  pl.BlockSpec((depth, LANES), lambda i: (0, router_at // LANES)),
                  pl.BlockSpec((1, 3 * depth, wide), lambda i: (jnp.minimum(i, senders - 1), 0, 0)),
                  pl.BlockSpec(memory_space=pl.ANY), pl.BlockSpec(memory_space=pl.ANY), once(ds)],
        out_specs=[whole(o) for o in outs] + [pl.BlockSpec((1, deep, wide), kept_map)],
        out_shape=outs + [shape((kept, deep, wide), bf16)],
        scratch_shapes=[
            pltpu.VMEM((rows, depth), f32), pltpu.VMEM((rows, depth), f32),
            pltpu.VMEM((wide, depth), bf16), pltpu.VMEM((rows, wide), bf16),
            pltpu.VMEM((2, rows, wide), bf16), pltpu.VMEM((core, 3 * depth, wide), bf16),
            pltpu.SemaphoreType.DMA((2,)),
        ] + remote,
        compiler_params=params,
        cost_estimate=cost(6 * senders),
        name="experts",
    )(mix, cot, gates, weights, experts_w, out, dmix, ds)


def local(
    block_input, gain_input, proj_main, proj_state, proj_step, conv_main, conv_state, step_bias,
    decay_log, skip_gain, gain_gate, proj_out, gain_mix, router_weight, shared_gates, shared_down,
    expert_gates, expert_down, segments, routes, cotangent,
):
    tokens, quarter = block_input.shape
    heads = step_bias.shape[0]
    inner = conv_main.shape[1]
    nstate = conv_state.shape[1] // 2
    per = inner // heads
    tensors = lax.axis_size("tensor")
    zi = lax.axis_index("tensor")
    senders = lax.axis_size(ROWS)
    depth = quarter * tensors
    di_all = inner * tensors
    own = tokens // tensors
    column = zi * quarter
    row0 = zi * own
    wrows = proj_main.shape[0]
    hid = expert_gates.shape[3]
    local_experts = expert_gates.shape[0]
    experts_all = local_experts * senders
    shared_here = shared_down.shape[1]
    router_pad = -experts_all % LANES

    main_wide = 2 * inner + 2 * nstate + LANES
    router_at = main_wide + inner
    weights = gather_rows(
        jnp.concatenate(
            [proj_main[:, 0], proj_main[:, 1], proj_state,
             jnp.pad(proj_step, ((0, 0), (0, LANES - heads))), proj_out,
             jnp.pad(router_weight, ((0, 0), (0, router_pad)))], axis=1
        )
    )
    pair_down = expert_down.reshape(local_experts, hid, depth // (2 * hid), 2 * hid)
    pair = jnp.concatenate(
        [expert_gates.reshape(local_experts, depth, 2 * hid),
         pair_down.transpose(0, 2, 1, 3).reshape(local_experts, -1, 2 * hid)], axis=1
    )
    shared_pair = shared_gates.reshape(wrows, 2, 2, shared_here // 2).transpose(2, 0, 1, 3)
    packed = jnp.concatenate(
        [pair.reshape(-1, 2 * hid), shared_pair.reshape(-1, shared_here), shared_down], axis=0
    )
    experts_w = gather_rows(packed[None])

    seg_row = segments[0]
    last = jnp.concatenate(
        [block_input[tokens - CONV + 1 :],
         jnp.pad(seg_row[None, tokens - CONV + 1 :].astype(bf16), ((0, 0), (0, quarter - CONV + 1)))], axis=0
    )
    halo = shifted(last, CTX, 1)
    halo_seg = halo[CONV - 1, : CONV - 1].astype(jnp.int32)
    extra = jnp.concatenate(
        [jnp.zeros((HALO - CONV + 1, quarter), bf16), halo[: CONV - 1], gain_input[None],
         gain_mix[None], jnp.zeros((14, quarter), bf16)], axis=0
    )
    wide = lambda got: got.transpose(1, 0, 2).reshape(got.shape[1], depth)
    got = spread(block_input)
    cotangent, got = lax.optimization_barrier((cotangent, got))
    got = wide(got)
    got_extra = spread_small(extra)
    cot_raw = spread(cotangent)
    gain_row = got_extra[HALO].astype(f32)
    gain_mid = got_extra[HALO + 1].astype(f32)
    x_ext = jnp.concatenate([got_extra[:HALO], got], axis=0).astype(f32)
    scale_ext = lax.rsqrt(jnp.mean(x_ext * x_ext, axis=-1, keepdims=True) + epsilon)
    normed_ext = x_ext * scale_ext
    mixed_ext = (normed_ext * gain_row).astype(bf16)

    segments_ext = jnp.concatenate([halo_seg, seg_row], axis=0)
    same = jnp.stack(
        [segments_ext[offset : offset + tokens] == seg_row for offset in range(CONV)]
    ).astype(f32)
    same = jnp.broadcast_to(same[:, :, None], (CONV, tokens, LANES))
    taps = jnp.concatenate([conv_main, conv_state], axis=1).astype(f32)
    lanes = lambda v: jnp.pad(v, (0, LANES - heads))[None]
    bias = lanes(step_bias)
    decay = lanes(decay_log)
    skip = jnp.repeat(skip_gain, per)[None]
    link = (seg_row == halo_seg[-1]).astype(f32)[:, None]
    at_end = (seg_row == seg_row[-1]).astype(f32)[:, None]
    seg_col = seg_row[:, None]
    seg_line = seg_row[None]
    value, act, scaled, step, running, run_exp, state_local = enter(
        mixed_ext, weights, taps, same, bias, decay, at_end, link, inner, nstate, per
    )
    run_t = running[:, :heads].T[:, None, :]
    far_in = far_states(state_local, False)
    within = intra(act, scaled, run_t, run_exp, seg_col, seg_line, inner, nstate, per)
    gain_gate_f = gain_gate.astype(f32)[None, :]
    mixer, part, square, state_in = leave(
        act, within, value, far_in, run_exp, link, skip, gain_gate_f, weights, inner, nstate, per
    )
    part, cot_raw = lax.optimization_barrier((part, cot_raw))
    cot_full = wide(cot_raw)
    residual, scale_rows, own_part = residual_step(part, square, got, di_all)

    gain_mid = gain_mid[None]
    chosen = jnp.any(
        routes[:, :, None] == jnp.arange(LANES, dtype=jnp.int32)[None, None, :], axis=1
    ).astype(f32)
    out_part, dmix_part, mixed_two, gates, shared_grad = shared_expert(
        residual, cot_full, gain_mid, weights, router_at, chosen, experts_w
    )
    out_part, dmix_part, dgate, dw = experts(
        mixed_two, cot_full, gates, weights, router_at, experts_w, out_part, dmix_part, shared_grad
    )
    expert_rows = scatter_chips(dw.reshape(-1, 2 * hid))
    dmixer, notes, gains_mid = turn_step(
        dmix_part, dgate, residual, cot_full, own_part, gain_mid
    )

    stats = jnp.stack([scale_rows[0], notes[:, LANES - 1]], axis=1)
    heads_grad, z_grad, gated_out, direct, sums = back(
        dmixer, weights, mixer, value, act, run_exp, link, gain_gate_f, stats, state_local[inner:],
        inner, nstate, di_all
    )
    out_part, dmixer = lax.optimization_barrier((out_part, dmixer))
    out_blocks = out_part.reshape(tokens, tensors, quarter).transpose(1, 0, 2)
    out_raw = exchange(out_blocks)
    far_out = far_states(direct, True)
    dscaled, dstate, drun = intra_back(
        heads_grad, act, scaled, run_t, run_exp, seg_col, seg_line, inner, nstate, per
    )
    state_rows, state_taps, leaving, kept = state_back(
        heads_grad, act, step, running, run_exp, link, at_end, value, taps, same, dstate, state_in,
        far_out, inner, nstate, per
    )
    state_rows, out_raw = lax.optimization_barrier((state_rows, out_raw))
    state_raw = spread(state_rows)
    value_grad, dtaps, small_sums = signal_back(
        heads_grad, act, step, value, taps, same, bias, decay, skip, mixer, within, dscaled, drun,
        leaving, kept, z_grad, state_rows, inner, nstate, per
    )
    first = 2 * inner
    last = first + 2 * nstate
    halo_back = shifted(value_grad[:HALO], CTX, -1)
    state_taps = jnp.pad(state_taps, ((0, 8 - CONV), (0, 0)))
    grad_input, gains, state_taps = finish_step(
        value_grad, halo_back, weights, got, dmixer, gain_row[None], gains_mid, state_taps
    )
    block_sum = jnp.sum(out_raw.astype(f32), axis=0)
    output = (
        lax.dynamic_slice_in_dim(residual, column, quarter, 1).astype(f32) + block_sum
    ).astype(bf16)

    grad_main = dot_inner(mixed_ext, value_grad)
    grad_state = dot_inner(mixed_ext, jnp.sum(state_raw.astype(f32), axis=0).astype(bf16))
    grad_proj_out = dot_inner(dmixer, gated_out)
    moved = jnp.where(col_iota(notes.shape) < experts_all, notes, 0.0)
    dlogits = (gates * (moved - jnp.sum(gates * moved, axis=1, keepdims=True))).astype(bf16)
    grad_router = dot_inner(mixed_two, dlogits)
    main_local = jnp.concatenate(
        [grad_main[:, :first].astype(bf16), grad_state.astype(bf16),
         grad_main[:, last:].astype(bf16), grad_proj_out.astype(bf16), grad_router.astype(bf16)], axis=1
    )
    main_local, expert_rows = lax.optimization_barrier((main_local, expert_rows))
    main_grad = scatter_rows(main_local).astype(f32)
    pair_rows = expert_rows[: local_experts * 3 * depth // 2].reshape(local_experts, -1, 2 * hid)
    down_rows = pair_rows[:, depth:].reshape(local_experts, depth // (2 * hid), hid, 2 * hid)
    shared_rows = expert_rows[local_experts * 3 * depth // 2 :]
    shared_up = shared_rows[: 2 * wrows].reshape(2, wrows, 2, shared_here // 2)
    small = lax.psum((dtaps, small_sums[:2], sums[:2], gains[:2], state_taps[:CONV]), ROWS)
    return (
        output,
        grad_input,
        small[3][0],
        jnp.stack([main_grad[:, :inner], main_grad[:, inner:first]], axis=1),
        main_grad[:, first:last],
        main_grad[:, last : last + heads],
        small[0],
        small[4],
        small[1][0, :heads],
        small[1][1, :heads],
        jnp.sum(small[2][1].reshape(heads, per), axis=1),
        small[2][0],
        main_grad[:, main_wide:router_at],
        small[3][1],
        main_grad[:, router_at : router_at + experts_all],
        shared_up.transpose(1, 2, 0, 3).reshape(wrows, 2, shared_here).astype(f32),
        shared_rows[2 * wrows :].astype(f32),
        pair_rows[:, :depth].reshape(expert_gates.shape).astype(f32),
        down_rows.transpose(0, 2, 1, 3).reshape(expert_down.shape).astype(f32),
    )


def solution(mesh):
    shard, ctx, tensor = (mesh.shape[name] for name in ("shard", "ctx", "tensor"))
    core = 2 if shard * ctx == 8 else 1
    split = jax.sharding.Mesh(
        mesh.devices.reshape(shard, ctx // core, core, tensor), ("shard", "cy", "core", "tensor")
    )
    return jax.shard_map(
        local,
        mesh=split,
        in_specs=(
            P(ROWS, "tensor"),
            P("tensor"),
            P(ROWS, None, "tensor"),
            P(ROWS, None),
            P(ROWS, "tensor"),
            P(None, "tensor"),
            P(),
            P("tensor"),
            P("tensor"),
            P("tensor"),
            P("tensor"),
            P(ROWS, "tensor"),
            P("tensor"),
            P(ROWS, None),
            P(ROWS, None, "tensor"),
            P(ROWS, "tensor"),
            P(ROWS, None, None, "tensor"),
            P(ROWS, "tensor", None),
            P("shard", CTX),
            P(ROWS, None),
            P(ROWS, "tensor"),
        ),
        out_specs=(
            P(ROWS, "tensor"),
            P(ROWS, "tensor"),
            P("tensor"),
            P(ROWS, None, "tensor"),
            P(ROWS, None),
            P(ROWS, "tensor"),
            P(None, "tensor"),
            P(),
            P("tensor"),
            P("tensor"),
            P("tensor"),
            P("tensor"),
            P(ROWS, "tensor"),
            P("tensor"),
            P(ROWS, None),
            P(ROWS, None, "tensor"),
            P(ROWS, "tensor"),
            P(ROWS, None, None, "tensor"),
            P(ROWS, "tensor", None),
        ),
        check_vma=False,
    )
```

time: 715 us -> 597 us (0.83)
  Pallas kernels: 142 us -> 346 us
  waiting for transfers between devices: 230 us -> 45.4 us
  local copies, waits for them, and re-layouts: 109 us -> 66.7 us
  blocking collectives: 63.5 us -> 27.6 us
  other arithmetic: 53.1 us -> 22.1 us
  matrix products: 29.7 us -> 14.7 us
  starting transfers between devices: 63.9 us -> 50.2 us
    all_to_all x9 -> x4, waiting for transfers between devices: 227 us -> 12 us  [exchange(): lax.all_to_all(blocks, 'tensor', split_axis=0, concat_axis=0, tiled=True)]
    pallas_call x4 -> x8, Pallas kernels: 90.7 us -> 298 us  [the longest x1 82.5 us: turn_step(): pl.pallas_call(partial(turn_kernel, n=n), in_specs=[pl.BlockSpec(memory_s...]
    psum x2 -> x1, blocking collectives: 63.5 us -> 27.6 us  [local(): lax.psum((dtaps, small_sums[:2], sums[:2], gains[:2], state_taps[:CONV]),...]
    ppermute x3, waiting for transfers between devices: 0.01 us -> 25.6 us  [spread_small(): lax.ppermute(block, 'tensor', [(i, (i + away) % count) for i in range(cou...]
    dot_general x4 -> x0, matrix products: 15 us -> none  [the longest x3 11.9 us: dot_outer(): lax.dot_general(left, right, (((1,), (1,)), ((), ())), preferred_element_...]
    reduce_sum x11 -> x2, other arithmetic: 13.5 us -> 2.38 us  [the longest x1 2.17 us: local(): jnp.sum(state_raw.astype(f32), axis=0).astype(bf16)]
    all_to_all x9 -> x4, starting transfers between devices: 40.7 us -> 30 us  [exchange(): lax.all_to_all(blocks, 'tensor', split_axis=0, concat_axis=0, tiled=True)]
    slice x21 -> x13, local copies, waits for them, and re-layouts: 18.1 us -> 10 us  [the longest x1 2.29 us: local(): proj_main[:, 1]]
  transfers between devices with their start and end apart: 30 -> 19, of which waited for: 10 -> 4; matrix products, arithmetic and copies ran while one was open for 24% -> 13% of each run, Pallas kernels for 13% -> 47%
where the time goes in v2:
time: 597 us; the launch traced here: 588 us
  Pallas kernels  346 us (58%)
  local copies, waits for them, and re-layouts  66.7 us (11%)
  starting transfers between devices  50.2 us (8%)
  waiting for transfers between devices  45.4 us (8%)
  blocking collectives  27.6 us (5%)
  other arithmetic  22.1 us (4%)
  between operations  15.1 us (3%)
  matrix products  14.7 us (2%)
    pallas_call x1, Pallas kernels, turn_step(): pl.pallas_call(partial(turn_kernel, n=n), in_specs=[pl.BlockSpec(memory_s...  82.5 us
    pallas_call x1, Pallas kernels, residual_step(): pl.pallas_call(partial(residual_kernel, di_all=di_all, n=n), in_specs=[pl...  63.1 us
    pallas_call x1, Pallas kernels, experts(): pl.pallas_call(partial(experts_kernel, tile=min(256, rows), senders=sende...  58.5 us
    pallas_call x1, Pallas kernels, finish_step(): pl.pallas_call(partial(finish_kernel, n=n), grid=(1,), in_specs=[whole(a)...  51 us
    all_to_all x4, starting transfers between devices, exchange(): lax.all_to_all(blocks, 'tensor', split_axis=0, concat_axis=0, tiled=True)  30 us
    psum x1, blocking collectives, local(): lax.psum((dtaps, small_sums[:2], sums[:2], gains[:2], state_taps[:CONV]),...  27.6 us
    ppermute x3, waiting for transfers between devices, spread_small(): lax.ppermute(block, 'tensor', [(i, (i + away) % count) for i in range(cou...  25.6 us
    unnamed x112, local copies, waits for them, and re-layouts  24.8 us
  transfers between devices with their start and end apart: 19, of which 4 were waited for; matrix products, arithmetic and copies ran while one was open for 13% of the time, Pallas kernels for 47%

profile of v2, /device:TPU:0, one launch (start us, length us, event | category | flops | bytes accessed | tf_op | source)
XLA Modules:
  0.0 587.8 jit_solution(9282093729494758221)
XLA Ops:
  22.8 5.8 all-to-all-start
  42.5 17.2 %collective-permute-done.1 = bf16[32,384]{1,0:T(8,128)(2,1)S(1)} collective-permute-done((bf16[32,384]{1,0:T(8,128)(2,1)S(1)}, bf16[32,384]{1,0:T(8,128)(2,1)S(1)}, u32[]{:S(2)}, u32[]{:S(2)}) %collective-permute-start.1) | collective-permute-done | bytes 24608 | tf_op jit(solution)/shard_map/ppermute | solution.py:91
  59.7 8.4 %collective-permute-done.2 = bf16[32,384]{1,0:T(8,128)(2,1)S(1)} collective-permute-done((bf16[32,384]{1,0:T(8,128)(2,1)S(1)}, bf16[32,384]{1,0:T(8,128)(2,1)S(1)}, u32[]{:S(2)}, u32[]{:S(2)}) %collective-permute-start.2) | collective-permute-done | bytes 24608 | tf_op jit(solution)/shard_map/ppermute | solution.py:91
  71.6 4.3 all-to-all-start.1
  79.3 17.3 %enter.1 = (f32[528,1920]{1,0:T(8,128)}, bf16[512,1024]{1,0:T(8,128)(2,1)}, bf16[512,768]{1,0:T(8,128)(2,1)}, f32[512,128]{1,0:T(8,128)}, f32[512,128]{1,0:T(8,1...) custom-call(bf16[528,1536]{1,0:T(8,128)(2,1)} %fusion.3.mixed_ref, ...), custom_call_target="tpu_custom_call" | custom-call | flops 7200000000 | bytes 1048576 | tf_op jit(solution)/shard_map/enter/pallas_call | solution.py:241
  104.7 6.5 %intra.1.inner_ref = f32[512,768]{1,0:T(8,128)} custom-call(bf16[512,1024]{1,0:T(8,128)(2,1)} %get-tuple-element.74.act_ref, bf16[512,768]{1,0:T(8,128)(2,1)} %get-tuple-element.75.scaled_ref, f32[12,1,512]{2,1,0:T(1,128)} %broadcast_in_dim.82.run_t_ref, f32[512,768]{1,0:T(8,128)} %get-tuple-element.77.run_exp_ref, s32[512,1]{1,0:T(8,128)} %copy-done.24, ...), custom_call_target="tpu_custom_call" | custom-call | flops 8999999488 | bytes 1048576 | tf_op jit(solution)/shard_map/intra/pallas_call | solution.py:297
  111.2 7.7 %collective-permute-done.6 = bf16[784,128]{1,0:T(8,128)(2,1)S(1)} collective-permute-done((bf16[784,128]{1,0:T(8,128)(2,1)}, bf16[784,128]{1,0:T(8,128)(2,1)S(1)}, u32[]{:S(2)}, u32[]{:S(2)}) %collective-permute-start.6) | collective-permute-done | bytes 200736 | tf_op jit(solution)/shard_map/ppermute | solution.py:45
  119.8 7.9 %leave.1 = (f32[512,768]{1,0:T(8,128)}, bf16[512,1536]{1,0:T(8,128)(2,1)}, f32[8,512]{1,0:T(8,128)}, f32[768,128]{1,0:T(8,128)}) custom-call(bf16[512,1024]{1,0:T(8,128)(2,1)} %get-tuple-element.74.act_ref, f32[512,768]{1,0:T(8,128)} %intra.1.inner_ref, f32[528,1920]{1,0:T(8,128)} %get-tuple-element.78.z_ref.value_ref.raw_ref, ...), custom_call_target="tpu_custom_call" | custom-call | flops 7200000000 | bytes 1048576 | tf_op jit(solution)/shard_map/leave/pallas_call | solution.py:349
  127.7 3.3 copy.166
  131.0 63.1 %residual_step.1 = (bf16[512,1536]{1,0:T(8,128)(2,1)S(1)}, f32[8,512]{1,0:T(8,128)S(1)}, f32[128,1536]{1,0:T(8,128)S(1)}) custom-call(bf16[512,1536]{1,0:T(8,128)(2,1)S(1)} %copy-done.7, f32[8,512]{1,0:T(8,128)S(1)} %copy-done.8, bf16[512,1536]{1,0:T(8,128)(2,1)S(1)} %bitcast.89), custom_call_target="tpu_custom_call" | custom-call | flops 54000001024 | bytes 1048576 | tf_op jit(solution)/shard_map/residual_step/pallas_call | solution.py:430
  196.2 11.2 %shared_expert.1 = (f32[512,1536]{1,0:T(8,128)}, f32[512,1536]{1,0:T(8,128)}, bf16[512,1536]{1,0:T(8,128)(2,1)}, f32[512,128]{1,0:T(8,128)}, bf16[8,576,256]{2,1,0:T(8,128)(2,1)}) custom-call(bf16[512,1536]{1,0:T(8,128)(2,1)} %copy-done.4, bf16[512,1536]{1,0:T(8,128)(2,1)} %bitcast.91, f32[1,1536]{1,0:T(1,128)} %get-tuple-element.238.gain_ref, ...), custom_call_target="tpu_custom_call" | custom-call | flops 8999999488 | bytes 1048576 | tf_op jit(solution)/shard_map/shared_expert/pallas_call | solution.py:936
  210.6 58.5 %experts.1 = (bf16[512,1536]{1,0:T(8,128)(2,1)}, bf16[512,1536]{1,0:T(8,128)(2,1)}, f32[512,128]{1,0:T(8,128)}, bf16[4,5184,256]{2,1,0:T(8,128)(2,1)}) custom-call(bf16[512,1536]{1,0:T(8,128)(2,1)} %get-tuple-element.86.mix_ref, bf16[512,1536]{1,0:T(8,128)(2,1)} %bitcast.92, f32[512,128]{1,0:T(8,128)} %get-tuple-element.87.gates_ref, ...), custom_call_target="tpu_custom_call" | custom-call | flops 43200000000 | bytes 1048576 | tf_op jit(solution)/shard_map/experts/pallas_call | solution.py:1121
  274.9 82.5 %turn_step.1 = (bf16[512,1536]{1,0:T(8,128)(2,1)S(1)}, f32[512,128]{1,0:T(8,128)S(1)}, f32[8,1536]{1,0:T(8,128)S(1)}) custom-call(bf16[512,1536]{1,0:T(8,128)(2,1)S(1)} %copy-done.9, f32[512,128]{1,0:T(8,128)S(1)} %copy-done.12, bf16[512,1536]{1,0:T(8,128)(2,1)S(1)} %copy-done.5, bf16[512,1536]{1,0:T(8,128)(2,1)S(1)} %bitcast.93, ...), custom_call_target="tpu_custom_call" | custom-call | flops 54000001024 | bytes 1048576 | tf_op jit(solution)/shard_map/turn_step/pallas_call | solution.py:500
  360.2 9.0 %back.1 = (f32[512,768]{1,0:T(8,128)}, bf16[512,768]{1,0:T(8,128)(2,1)}, bf16[512,768]{1,0:T(8,128)(2,1)}, bf16[784,128]{1,0:T(8,128)(2,1)}, f32[8,768]{1,0:T(8,128)}) custom-call(bf16[512,1536]{1,0:T(8,128)(2,1)} %copy-done.1, bf16[1536,2816]{1,0:T(8,128)(2,1)} %all-gather.4.cloned.1.call-done.w_ref.wa_ref.wb_ref.router_ref, ...), custom_call_target="tpu_custom_call" | custom-call | flops 7200000000 | bytes 1048576 | tf_op jit(solution)/shard_map/back/pallas_call | solution.py:641
  374.4 15.6 %all-to-all-start.2 = ((bf16[4,512,384]{2,1,0:T(8,128)(2,1)}), bf16[4,512,384]{2,1,0:T(8,128)(2,1)S(1)}, u32[]{:S(2)}, u32[]{:S(2)}) async-start(bf16[4,512,384]{2,1,0:T(8,128)(2,1)} %bitcast.99), calls=%async_computation.2 | async-start | bytes 3145728 | tf_op jit(solution)/shard_map/all_to_all | solution.py:78
  390.0 15.4 %intra_back.1 = (f32[512,768]{1,0:T(8,128)}, f32[512,256]{1,0:T(8,128)}, f32[512,128]{1,0:T(8,128)}) custom-call(f32[512,768]{1,0:T(8,128)} %get-tuple-element.98.heads_ref, bf16[512,1024]{1,0:T(8,128)(2,1)} %get-tuple-element.74.act_ref, bf16[512,768]{1,0:T(8,128)(2,1)} %get-tuple-element.75.scaled_ref, f32[12,1,512]{2,1,0:T(1,128)} %broadcast_in_dim.82.run_t_ref, ...), custom_call_target="tpu_custom_call" | custom-call | flops 17999998976 | bytes 1048576 | tf_op jit(solution)/shard_map/intra_back/pallas_call | solution.py:713
  407.6 8.7 %state_back.1 = (bf16[528,256]{1,0:T(8,128)(2,1)}, f32[4,256]{1,0:T(4,128)}, f32[512,768]{1,0:T(8,128)}, f32[8,128]{1,0:T(8,128)}) custom-call(f32[512,768]{1,0:T(8,128)} %get-tuple-element.98.heads_ref, bf16[512,1024]{1,0:T(8,128)(2,1)} %get-tuple-element.74.act_ref, f32[512,128]{1,0:T(8,128)} %get-tuple-element.99.step_ref, ...), custom_call_target="tpu_custom_call" | custom-call | flops 5400000000 | bytes 1048576 | tf_op jit(solution)/shard_map/state_back/pallas_call | solution.py:788
  416.3 12.0 %all-to-all-done.2 = bf16[4,512,384]{2,1,0:T(8,128)(2,1)S(1)} async-done(((bf16[4,512,384]{2,1,0:T(8,128)(2,1)}), bf16[4,512,384]{2,1,0:T(8,128)(2,1)S(1)}, u32[]{:S(2)}, u32[]{:S(2)}) %all-to-all-start.2) | async-done | bytes 1572896 | tf_op jit(solution)/shard_map/all_to_all | solution.py:78
  430.3 4.3 all-to-all-start.3
  434.6 15.1 %signal_back.1 = (bf16[528,1920]{1,0:T(8,128)(2,1)}, f32[4,768]{1,0:T(4,128)}, f32[8,128]{1,0:T(8,128)}) custom-call(f32[512,768]{1,0:T(8,128)} %get-tuple-element.98.heads_ref, bf16[512,1024]{1,0:T(8,128)(2,1)} %get-tuple-element.74.act_ref, f32[512,128]{1,0:T(8,128)} %get-tuple-element.99.step_ref, f32[528,1920]{1,0:T(8,128)} %get-tuple-element.78.z_ref.value_ref.raw_ref, ...), custom_call_target="tpu_custom_call" | custom-call | flops 10800000000 | bytes 1048576 | tf_op jit(solution)/shard_map/signal_back/pallas_call | solution.py:858
  449.7 6.9 %convolution_convert_fusion = bf16[1536,1920]{1,0:T(8,128)(2,1)S(1)} fusion(bf16[528,1536]{1,0:T(8,128)(2,1)S(1)} %copy-done.18, bf16[528,1920]{1,0:T(8,128)(2,1)} %get-tuple-element.113.grad_ref), kind=kOutput, calls=%fused_computation | convolution fusion | flops 3117219840 | bytes 9547776 | tf_op jit(solution)/shard_map/dot_general | solution.py:53
  463.9 3.4 fusion.4
  479.7 51.0 %finish_step.1 = (f32[512,384]{1,0:T(8,128)}, f32[8,384]{1,0:T(8,128)}, f32[8,256]{1,0:T(8,128)}) custom-call(bf16[528,1920]{1,0:T(8,128)(2,1)} %get-tuple-element.113.grad_ref, bf16[16,1920]{1,0:T(8,128)(2,1)} %copy-done.47, bf16[1536,2816]{1,0:T(8,128)(2,1)} %all-gather.4.cloned.1.call-done.w_ref.wa_ref.wb_ref.router_ref, bf16[512,1536]{1,0:T(8,128)(2,1)} %bitcast.90, ...), custom_call_target="tpu_custom_call" | custom-call | flops 40499998720 | bytes 1048576 | tf_op jit(solution)/shard_map/finish_step/pallas_call | solution.py:589
  532.1 27.6 %all-reduce.6 = (f32[2,384]{1,0:T(2,128)S(1)}, f32[4,768]{1,0:T(4,128)}, f32[4,256]{1,0:T(4,128)}, f32[2,128]{1,0:T(2,128)S(1)}, f32[2,768]{1,0:T(2,128)S(1)}) all-reduce(f32[2,384]{1,0:T(2,128)S(1)} %slice.154, f32[4,768]{1,0:T(4,128)S(1)} %copy-done.34, ...), channel_id=1, replica_groups=mesh['shard'=2,'cy'=2,'core'=2,'tensor'=4] {'shard','cy','core'}, use_global_device_ids=true, to_apply=%region_3.4 | all-reduce | flops 6656 | bytes 53248 | tf_op jit(solution)/shard_map/psum | solution.py:1304
  (244 shorter events, 110.2 us)
Async XLA Ops:
  7.2 70.8 %all-gather.4.cloned.1.call-start = ((), (), s32[]{:S(2)}) async-start(), calls=%async_computation.6 | async-start | bytes 9732096 | tf_op jit(solution)/shard_map/all_gather | solution.py:65
  11.6 184.6 %all-gather.6.cloned.1.call-start = ((), (), s32[]{:S(2)}) async-start(), calls=%async_computation.9 | async-start | bytes 23887872 | tf_op jit(solution)/shard_map/all_gather | solution.py:65
  19.1 14.2 %collective-permute-start = (bf16[4,384]{1,0:T(4,128)(2,1)S(1)}, bf16[4,384]{1,0:T(4,128)(2,1)S(1)}, u32[]{:S(2)}, u32[]{:S(2)}) collective-permute-start(bf16[4,384]{1,0:T(4,128)(2,1)S(1)} %fusion.13), channel_id=1, source_target_pairs={{0,4},{4,8},{8,12},{1,5},{5,9},{9,13},{2,6},{6,10},{10,14},{3,7},{... | collective-permute-start | bytes 9224 | tf_op jit(solution)/shard_map/ppermute | solution.py:45
  22.8 46.0 %all-to-all-start = ((bf16[4,512,384]{2,1,0:T(8,128)(2,1)}), bf16[4,512,384]{2,1,0:T(8,128)(2,1)S(1)}, u32[]{:S(2)}, u32[]{:S(2)}) async-start(bf16[4,512,384]{2,1,0:T(8,128)(2,1)} %broadcast_in_dim.78), calls=%async_computation | async-start | bytes 3145728 | tf_op jit(solution)/shard_map/all_to_all | solution.py:78
  31.2 37.8 %copy-start.24 = (s32[512,1]{1,0:T(8,128)}, s32[512,1]{1,0:T(8,128)S(1)}, u32[]{:S(2)}) copy-start(s32[512,1]{1,0:T(8,128)S(1)} %copy.137.seg_col_ref) | copy-start | bytes 6148
  33.6 26.1 %collective-permute-start.1 = (bf16[32,384]{1,0:T(8,128)(2,1)S(1)}, bf16[32,384]{1,0:T(8,128)(2,1)S(1)}, u32[]{:S(2)}, u32[]{:S(2)}) collective-permute-start(bf16[32,384]{1,0:T(8,128)(2,1)S(1)} %concatenate.32), channel_id=1, source_target_pairs={{0,1},{1,2},{2,3},{3,0},{4,5},{5,6},{6,7},{7,4},{8,9},{9,10},{10,1... | collective-permute-start | bytes 73736 | tf_op jit(solution)/shard_map/ppermute | solution.py:91
  35.7 32.5 %collective-permute-start.2 = (bf16[32,384]{1,0:T(8,128)(2,1)S(1)}, bf16[32,384]{1,0:T(8,128)(2,1)S(1)}, u32[]{:S(2)}, u32[]{:S(2)}) collective-permute-start(bf16[32,384]{1,0:T(8,128)(2,1)S(1)} %concatenate.32), channel_id=1, source_target_pairs={{0,2},{1,3},{2,0},{3,1},{4,6},{5,7},{6,4},{7,5},{8,10},{9,11},{10,... | collective-permute-start | bytes 73736 | tf_op jit(solution)/shard_map/ppermute | solution.py:91
  38.0 30.1 %collective-permute-start.3 = (bf16[32,384]{1,0:T(8,128)(2,1)S(1)}, bf16[32,384]{1,0:T(8,128)(2,1)S(1)}, u32[]{:S(2)}, u32[]{:S(2)}) collective-permute-start(bf16[32,384]{1,0:T(8,128)(2,1)S(1)} %concatenate.32), channel_id=1, source_target_pairs={{0,3},{1,0},{2,1},{3,2},{4,7},{5,4},{6,5},{7,6},{8,11},{9,8},{10,9... | collective-permute-start | bytes 73736 | tf_op jit(solution)/shard_map/ppermute | solution.py:91
  69.0 62.0 %copy-start = (bf16[4,64,8,384]{3,2,0,1:T(8,128)(2,1)}, bf16[4,64,8,384]{3,2,0,1:T(8,128)(2,1)S(1)}, u32[]{:S(2)}) copy-start(bf16[4,64,8,384]{3,2,0,1:T(8,128)(2,1)S(1)} %copy.165) | copy-start | bytes 4718596
  71.6 56.1 %all-to-all-start.1 = ((bf16[4,512,384]{2,1,0:T(8,128)(2,1)}), bf16[4,512,384]{2,1,0:T(8,128)(2,1)}, u32[]{:S(2)}, u32[]{:S(2)}) async-start(bf16[4,512,384]{2,1,0:T(8,128)(2,1)} %broadcast_in_dim.86), calls=%async_computation.1 | async-start | bytes 3145728 | tf_op jit(solution)/shard_map/all_to_all | solution.py:78
  75.9 397.6 %reduce-scatter.3.cloned.1.call-start = ((), (), s32[]{:S(2)}) async-start(), calls=%async_computation.7 | async-start | bytes 13271040 | tf_op jit(solution)/shard_map/reduce_scatter | solution.py:74
  96.6 14.6 %collective-permute-start.4 = (bf16[784,128]{1,0:T(8,128)(2,1)}, bf16[784,128]{1,0:T(8,128)(2,1)S(1)}, u32[]{:S(2)}, u32[]{:S(2)}) collective-permute-start(bf16[784,128]{1,0:T(8,128)(2,1)} %get-tuple-element.79), channel_id=1, source_target_pairs={{0,4},{4,8},{8,12},{1,5},{5,9},{9,13},{2,6},{6,10},{10,14},{3,7},{... | collective-permute-start | bytes 602120 | tf_op jit(solution)/shard_map/ppermute | solution.py:45
  99.2 12.1 %collective-permute-start.5 = (bf16[784,128]{1,0:T(8,128)(2,1)}, bf16[784,128]{1,0:T(8,128)(2,1)S(1)}, u32[]{:S(2)}, u32[]{:S(2)}) collective-permute-start(bf16[784,128]{1,0:T(8,128)(2,1)} %get-tuple-element.79), channel_id=1, source_target_pairs={{0,8},{4,12},{1,9},{5,13},{2,10},{6,14},{3,11},{7,15},{16,24},{20,... | collective-permute-start | bytes 602120 | tf_op jit(solution)/shard_map/ppermute | solution.py:45
  101.2 17.7 %collective-permute-start.6 = (bf16[784,128]{1,0:T(8,128)(2,1)}, bf16[784,128]{1,0:T(8,128)(2,1)S(1)}, u32[]{:S(2)}, u32[]{:S(2)}) collective-permute-start(bf16[784,128]{1,0:T(8,128)(2,1)} %get-tuple-element.79), channel_id=1, source_target_pairs={{0,12},{1,13},{2,14},{3,15},{16,28},{17,29},{18,30},{19,31}} | collective-permute-start | bytes 602120 | tf_op jit(solution)/shard_map/ppermute | solution.py:45
  274.9 84.4 %copy-start.23 = (f32[512,1]{1,0:T(8,128)S(1)}, f32[512,1]{1,0:T(8,128)}, u32[]{:S(2)}) copy-start(f32[512,1]{1,0:T(8,128)} %copy.147) | copy-start | bytes 6148
  369.2 36.4 %collective-permute-start.7 = (bf16[784,128]{1,0:T(8,128)(2,1)}, bf16[784,128]{1,0:T(8,128)(2,1)}, u32[]{:S(2)}, u32[]{:S(2)}) collective-permute-start(bf16[784,128]{1,0:T(8,128)(2,1)} %get-tuple-element.102), channel_id=1, source_target_pairs={{4,0},{8,4},{12,8},{5,1},{9,5},{13,9},{6,2},{10,6},{14,10},{7,3},{... | collective-permute-start | bytes 602120 | tf_op jit(solution)/shard_map/ppermute | solution.py:45
  370.4 35.1 %collective-permute-start.8 = (bf16[784,128]{1,0:T(8,128)(2,1)}, bf16[784,128]{1,0:T(8,128)(2,1)}, u32[]{:S(2)}, u32[]{:S(2)}) collective-permute-start(bf16[784,128]{1,0:T(8,128)(2,1)} %get-tuple-element.102), channel_id=1, source_target_pairs={{8,0},{12,4},{9,1},{13,5},{10,2},{14,6},{11,3},{15,7},{24,16},{28,... | collective-permute-start | bytes 602120 | tf_op jit(solution)/shard_map/ppermute | solution.py:45
  371.8 33.8 %collective-permute-start.9 = (bf16[784,128]{1,0:T(8,128)(2,1)}, bf16[784,128]{1,0:T(8,128)(2,1)}, u32[]{:S(2)}, u32[]{:S(2)}) collective-permute-start(bf16[784,128]{1,0:T(8,128)(2,1)} %get-tuple-element.102), channel_id=1, source_target_pairs={{12,0},{13,1},{14,2},{15,3},{28,16},{29,17},{30,18},{31,19}} | collective-permute-start | bytes 602120 | tf_op jit(solution)/shard_map/ppermute | solution.py:45
  374.4 53.9 %all-to-all-start.2 = ((bf16[4,512,384]{2,1,0:T(8,128)(2,1)}), bf16[4,512,384]{2,1,0:T(8,128)(2,1)S(1)}, u32[]{:S(2)}, u32[]{:S(2)}) async-start(bf16[4,512,384]{2,1,0:T(8,128)(2,1)} %bitcast.99), calls=%async_computation.2 | async-start | bytes 3145728 | tf_op jit(solution)/shard_map/all_to_all | solution.py:78
  430.3 31.5 %all-to-all-start.3 = ((bf16[4,528,256]{2,1,0:T(8,128)(2,1)}), bf16[4,528,256]{2,1,0:T(8,128)(2,1)}, u32[]{:S(2)}, u32[]{:S(2)}) async-start(bf16[4,528,256]{2,1,0:T(8,128)(2,1)} %broadcast_in_dim.88), calls=%async_computation.3 | async-start | bytes 2162688 | tf_op jit(solution)/shard_map/all_to_all | solution.py:78
  434.5 139.0 %reduce-scatter.5.cloned.1.call-start = ((), (), s32[]{:S(2)}) async-start(), calls=%async_computation.8 | async-start | bytes 9732096 | tf_op jit(solution)/shard_map/reduce_scatter | solution.py:69
  475.7 3.3 collective-permute-start.10
  479.7 52.4 %copy-start.34 = (f32[4,768]{1,0:T(4,128)S(1)}, f32[4,768]{1,0:T(4,128)}, u32[]{:S(2)}) copy-start(f32[4,768]{1,0:T(4,128)} %get-tuple-element.122) | copy-start | bytes 36868
  479.7 82.4 %copy-start.16 = (bf16[5184,256]{1,0:T(8,128)(2,1)S(1)}, bf16[5184,256]{1,0:T(8,128)(2,1)}, u32[]{:S(2)}) copy-start(bf16[5184,256]{1,0:T(8,128)(2,1)} %reduce-scatter.3.cloned.1.call-done) | copy-start | bytes 7962628
  (43 other events, 172.7 us)
Sparse Core Ops, SparseCore 0:
  11.7 58.2 all-gather.3
  72.4 117.2 all-gather.5
  269.3 119.3 reduce-scatter.2
  473.7 75.8 reduce-scatter.4

commit v3 on v2

--- a/solution.py
+++ b/solution.py
@@ -22,17 +22,17 @@
 f32 = jnp.float32
 MESH = pl.DeviceIdType.MESH
 bf16 = jnp.bfloat16
-BIG = pltpu.CompilerParams(vmem_limit_bytes=56 << 20)
+BIG = pltpu.CompilerParams(vmem_limit_bytes=60 << 20)
 
 
 def cost(micros):
     return pl.CostEstimate(flops=micros * 900_000_000, transcendentals=0, bytes_accessed=1 << 20)
-BIG = pltpu.CompilerParams(vmem_limit_bytes=56 << 20)
+BIG = pltpu.CompilerParams(vmem_limit_bytes=60 << 20)
 
 
 def cost(micros):
     return pl.CostEstimate(flops=micros * 900_000_000, transcendentals=0, bytes_accessed=1 << 20)
-BIG = pltpu.CompilerParams(vmem_limit_bytes=56 << 20)
+BIG = pltpu.CompilerParams(vmem_limit_bytes=60 << 20)
 
 
 def cost(micros):
@@ -181,7 +181,7 @@
     return rows, total
 
 
-def enter_kernel(mixed_ref, w_ref, taps_ref, same_ref, bias_ref, decay_ref, end_ref, link_ref,
+def enter_part(mixed_ref, w_ref, taps_ref, same_ref, bias_ref, decay_ref, end_ref, link_ref,
                  value_ref, act_ref, scaled_ref, step_ref, run_ref, run_exp_ref,
                  state_ref, *, inner, nstate, per):
     tokens = act_ref.shape[0]
@@ -228,29 +228,6 @@
     return pl.BlockSpec((a.shape[0], width), lambda i: (0, at // width))
 
 
-def enter(mixed_ext, weights, taps, same, bias, decay, at_end, link, inner, nstate, per):
-    ext = mixed_ext.shape[0]
-    tokens = ext - HALO
-    wide = 2 * inner + 2 * nstate + LANES
-    shape = jax.ShapeDtypeStruct
-    outs = [
-        shape((ext, wide), f32), shape((tokens, inner + 2 * nstate), bf16),
-        shape((tokens, inner), bf16), shape((tokens, LANES), f32), shape((tokens, LANES), f32),
-        shape((tokens, inner), f32), shape((inner + 16, nstate), bf16),
-    ]
-    return pl.pallas_call(
-        partial(enter_kernel, inner=inner, nstate=nstate, per=per),
-        grid=(1,),
-        in_specs=[whole(mixed_ext), columns(weights, wide)]
-        + [whole(a) for a in (taps, same, bias, decay, at_end, link)],
-        out_specs=[whole(o) for o in outs],
-        out_shape=outs,
-        compiler_params=BIG,
-        cost_estimate=cost(8),
-        name="enter",
-    )(mixed_ext, weights, taps, same, bias, decay, at_end, link)
-
-
 def masked_scores(query, keys, seg_col_ref, seg_row_ref, start, stop):
     shape = (stop - start, stop)
     allowed = (row_iota(shape) + start >= col_iota(shape)) & (
@@ -259,7 +236,7 @@
     return jnp.where(allowed, dot_outer(query[start:stop], keys[:stop]), 0.0)
 
 
-def intra_kernel(act_ref, scaled_ref, run_t_ref, run_exp_ref, seg_col_ref, seg_row_ref,
+def intra_part(act_ref, scaled_ref, run_t_ref, run_exp_ref, seg_col_ref, seg_row_ref,
                  inner_ref, scores_ref, *, inner, nstate, per, block):
     tokens = act_ref.shape[0]
     keys = act_ref[:, inner : inner + nstate]
@@ -292,38 +269,6 @@
     lax.fori_loop(0, inner // LANES, pair, 0)
 
 
-def intra(act, scaled, run_t, run_exp, seg_col, seg_row, inner, nstate, per):
-    tokens = act.shape[0]
-    return pl.pallas_call(
-        partial(intra_kernel, inner=inner, nstate=nstate, per=per, block=128),
-        out_shape=jax.ShapeDtypeStruct((tokens, inner), f32),
-        scratch_shapes=[pltpu.VMEM((tokens, tokens), f32)],
-        compiler_params=BIG,
-        cost_estimate=cost(10),
-        name="intra",
-    )(act, scaled, run_t, run_exp, seg_col, seg_row)
-
-
-def leave_kernel(act_ref, inner_ref, z_ref, far_ref, run_exp_ref, link_ref, skip_ref, gain_ref,
-                 wa_ref, wb_ref, mixer_ref, part_ref, square_ref, state_ref, *, inner, nstate, per):
-    query = act_ref[:, inner + nstate :]
-    state = join_states(far_ref, inner, per)
-    state_ref[...] = state
-    carried = dot_outer(query, state.astype(bf16)) * (
-        jnp.exp(run_exp_ref[...]) * link_ref[...]
-    )
-    mixer = inner_ref[...] + carried + skip_ref[...] * act_ref[:, :inner].astype(f32)
-    mixer_ref[...] = mixer
-    z = z_ref[HALO:, :]
-    gated = mixer * (z * sigmoid(z))
-    square_ref[...] = row_sums(gated * gated)
-    lifted = (gated * gain_ref[...]).astype(bf16)
-    half = inner // 2
-    part_ref[...] = (
-        dot_outer(lifted[:, :half], wa_ref[...]) + dot_outer(lifted[:, half:], wb_ref[...])
-    ).astype(bf16)
-
-
 def row_sums(value):
     folded = value[:, :LANES]
     for at in range(LANES, value.shape[1], LANES):
@@ -339,27 +284,6 @@
     return jnp.sum(jnp.where(eye, row, 0.0), axis=1, keepdims=True)
 
 
-def leave(act, within, value, far, run_exp, link, skip, gain, weights, inner, nstate, per):
-    tokens = act.shape[0]
-    depth = weights.shape[0]
-    half = inner // 2
-    first = 2 * inner + 2 * nstate + LANES
-    outs = [jax.ShapeDtypeStruct((tokens, inner), f32), jax.ShapeDtypeStruct((tokens, depth), bf16),
-            jax.ShapeDtypeStruct((8, tokens), f32), jax.ShapeDtypeStruct((inner, nstate), f32)]
-    return pl.pallas_call(
-        partial(leave_kernel, inner=inner, nstate=nstate, per=per),
-        grid=(1,),
-        in_specs=[whole(act), whole(within), columns(value, inner), whole(far), whole(run_exp),
-                  whole(link), whole(skip), whole(gain), columns(weights, half, first),
-                  columns(weights, half, first + half)],
-        out_specs=[whole(o) for o in outs],
-        out_shape=outs,
-        compiler_params=BIG,
-        cost_estimate=cost(8),
-        name="leave",
-    )(act, within, value, far, run_exp, link, skip, gain, weights, weights)
-
-
 def tensor_barrier(me, n):
     barrier = pltpu.get_barrier_semaphore()
     for d in range(1, n):
@@ -373,46 +297,337 @@
     send, receive = sems
     return pltpu.make_async_remote_copy(
         src_ref=source, dst_ref=target, send_sem=send.at[slot], recv_sem=receive.at[slot],
-        device_id={"tensor": peer}, device_id_type=MESH,
-    )
-
-
-def residual_kernel(part_ref, square_ref, x_ref, res_ref, stat_ref, own_ref,
-                    inbox, square_box, res_box, stat_box, *sems, di_all, n):
+        device_id=peer if isinstance(peer, dict) else {"tensor": peer}, device_id_type=MESH,
+    )
+
+
+def ctx_place():
+    core = lax.axis_size("core")
+    return lax.axis_index("cy") * core + lax.axis_index("core"), lax.axis_size("cy") * core
+
+
+def ctx_peer(place):
+    core = lax.axis_size("core")
+    return {"cy": place // core, "core": lax.rem(place, core)}
+
+
+def front_barrier(me, n):
+    barrier = pltpu.get_barrier_semaphore()
+    place, count = ctx_place()
+    for d in range(1, n):
+        pl.semaphore_signal(
+            barrier, inc=1, device_id={"tensor": lax.rem(me + d, n)}, device_id_type=MESH
+        )
+    for d in range(1, count):
+        pl.semaphore_signal(
+            barrier, inc=1, device_id=ctx_peer(lax.rem(place + d, count)), device_id_type=MESH
+        )
+    pl.semaphore_wait(barrier, n - 1 + count - 1)
+
+
+class StatePush:
+    def __init__(self, source, far_ref, sems, reverse):
+        place, count = ctx_place()
+        sign = -1 if reverse else 1
+        self.copies = []
+        for d in range(1, count):
+            to, origin = place + sign * d, place - sign * d
+            copy = push(source, far_ref.at[d - 1], sems, d - 1,
+                        ctx_peer(lax.rem(to + count, count)))
+            self.copies.append((copy, (to >= 0) & (to < count), (origin >= 0) & (origin < count)))
+
+    def start(self):
+        for copy, sends, _ in self.copies:
+            pl.when(sends)(copy.start)
+
+    def wait_recv(self):
+        for copy, _, gets in self.copies:
+            pl.when(gets)(copy.wait_recv)
+
+    def wait_send(self):
+        for copy, sends, _ in self.copies:
+            pl.when(sends)(copy.wait_send)
+
+
+class LineReduce:
+    def __init__(self, me, n, blocks, right, left, sems):
+        self.me, self.n, self.blocks, self.right, self.left = me, n, blocks, right, left
+        self.right_sems, self.left_sems = sems
+        self.keep = lambda d: jnp.minimum(jnp.maximum(d, 0), n - 1)
+
+    def rightward(self, d):
+        return push(self.blocks(d), self.right.at[d], self.right_sems, d,
+                    jnp.minimum(self.me + 1, self.n - 1))
+
+    def leftward(self, d):
+        return push(self.blocks(d), self.left.at[d], self.left_sems, d, jnp.maximum(self.me - 1, 0))
+
+    def step(self, t):
+        me, n = self.me, self.n
+        ways = []
+        if t < n:
+            ways.append((n - 1 - t + me, me >= 1, lambda d: d > me, t >= me, self.rightward, self.right))
+            ways.append((t - (n - 1 - me), me <= n - 2, lambda d: d < me, t >= n - 1 - me,
+                         self.leftward, self.left))
+        for d, gets, passes, ready, copy_of, box in ways:
+            at = self.keep(d)
+            copy = copy_of(at)
+
+            @pl.when(gets & ready)
+            def _():
+                copy.wait_recv()
+
+            @pl.when(gets & ready & passes(d))
+            def _():
+                view = self.blocks(at)
+                view[...] = view[...] + box[at]
+
+            @pl.when(ready & passes(d))
+            def _():
+                copy.start()
+
+    def total(self):
+        me, n = self.me, self.n
+        value = self.blocks(me)[...].astype(f32)
+        value = value + jnp.where(me >= 1, self.right[me].astype(f32), 0.0)
+        return value + jnp.where(me <= n - 2, self.left[me].astype(f32), 0.0)
+
+    def wait_send(self):
+        for d in range(self.n):
+            pl.when(self.me < d)(self.rightward(d).wait_send)
+            pl.when(self.me > d)(self.leftward(d).wait_send)
+
+
+class LineGather:
+    def __init__(self, me, n, blocks, sems):
+        self.me, self.n, self.blocks = me, n, blocks
+        self.right_sems, self.left_sems = sems
+
+    def rightward(self, d):
+        return push(self.blocks(d), self.blocks(d), self.right_sems, d,
+                    jnp.minimum(self.me + 1, self.n - 1))
+
+    def leftward(self, d):
+        return push(self.blocks(d), self.blocks(d), self.left_sems, d, jnp.maximum(self.me - 1, 0))
+
+    def step(self, t):
+        me, n = self.me, self.n
+        from_left, from_right = me - t, me + t
+        right = self.rightward(jnp.maximum(from_left, 0))
+        left = self.leftward(jnp.minimum(from_right, n - 1))
+        if t > 0:
+            pl.when(from_left >= 0)(right.wait_recv)
+        pl.when((from_left >= 0) & (me <= n - 2))(right.start)
+        if t > 0:
+            pl.when(from_right <= n - 1)(left.wait_recv)
+        pl.when((from_right <= n - 1) & (me >= 1))(left.start)
+
+    def wait_send(self):
+        for d in range(self.n):
+            pl.when((self.me >= d) & (self.me <= self.n - 2))(self.rightward(d).wait_send)
+            pl.when((self.me <= d) & (self.me >= 1))(self.leftward(d).wait_send)
+
+
+def line_sems(n):
+    return [pltpu.SemaphoreType.DMA((n,))] * 4
+
+
+def line_groups(sems):
+    return (sems[0], sems[1]), (sems[2], sems[3])
+
+
+def line_barrier(me, n):
+    barrier = pltpu.get_barrier_semaphore()
+    for d in range(1, n):
+        pl.semaphore_signal(
+            barrier, inc=1, device_id={"tensor": lax.rem(me + d, n)}, device_id_type=MESH
+        )
+    return barrier
+
+
+def intake_kernel(x_ref, gains_ref, mixed_ref, mixed_t_ref, full_ref, gain_out,
+                  x_box, gains_box, halo_box, *sems, n):
     me = lax.axis_index("tensor")
-    rows, depth = part_ref.shape
+    place, count = ctx_place()
+    rows, quarter = x_ref.shape
+    column = lambda d: pl.ds(pl.multiple_of(d * quarter, LANES), quarter)
+    gain_sems, halo_sems = (sems[0], sems[1]), (sems[2], sems[3])
+    halo_box[...] = jnp.zeros_like(halo_box)
+    x_box[:, column(me)] = x_ref[...]
+    gains_box[:, column(me)] = gains_ref[...]
+    barrier = line_barrier(me, n)
+    for away in (1, count - 1):
+        for z in range(n):
+            pl.semaphore_signal(
+                barrier, inc=1, device_id={**ctx_peer(lax.rem(place + away, count)), "tensor": z},
+                device_id_type=MESH,
+            )
+    pl.semaphore_wait(barrier, n - 1 + 2 * n)
+    x_line = LineGather(me, n, lambda d: x_box.at[:, column(d)], line_groups(sems[4:8]))
+    x_line.step(0)
+    gains = [push(gains_box.at[:, column(me)], gains_box.at[:, column(me)], gain_sems, d - 1,
+                  lax.rem(me + d, n)) for d in range(1, n)]
+    for copy in gains:
+        copy.start()
+    sends, gets = place < count - 1, place > 0
+    halos = []
+    for d in range(n):
+        peer = {**ctx_peer(jnp.minimum(place + 1, count - 1)), "tensor": lax.rem(me + d, n)}
+        halos.append(push(x_ref.at[rows - HALO :], halo_box.at[:, column(me)], halo_sems, d, peer))
+        pl.when(sends)(halos[-1].start)
+    for t in range(1, n):
+        x_line.step(t)
+    for copy in gains:
+        copy.wait_recv()
+    for copy in halos:
+        pl.when(gets)(copy.wait_recv)
+    gain = gains_box[0:1, :].astype(f32)
+    gain_out[...] = gains_box[...].astype(f32)
+
+    def normed(x):
+        x = x.astype(f32)
+        scale = lax.rsqrt(jnp.mean(x * x, axis=1, keepdims=True) + epsilon)
+        return (x * scale * gain).astype(bf16)
+
+    mixed_ref[:HALO, :] = normed(halo_box[...])
+    full_ref[...] = x_box[...]
+    mixed_ref[HALO:, :] = normed(x_box[...])
+    mixed_t_ref[...] = mixed_ref[HALO:, :].T
+    for copy in gains:
+        copy.wait_send()
+    for copy in halos:
+        pl.when(sends)(copy.wait_send)
+    x_line.wait_send()
+
+
+def intake(x, gains):
+    n = lax.axis_size("tensor")
+    rows, quarter = x.shape
+    depth = n * quarter
+    shape = jax.ShapeDtypeStruct
+    dma = pltpu.SemaphoreType.DMA
+    return pl.pallas_call(
+        partial(intake_kernel, n=n),
+        in_specs=[VMEM] * 2,
+        out_specs=[VMEM] * 4,
+        out_shape=[shape((rows + HALO, depth), bf16), shape((depth, rows), bf16),
+                   shape((rows, depth), bf16), shape((16, depth), f32)],
+        scratch_shapes=[
+            pltpu.VMEM((rows, depth), bf16),
+            pltpu.VMEM((16, depth), bf16), pltpu.VMEM((HALO, depth), bf16),
+            dma((n - 1,)), dma((n - 1,)), dma((n,)), dma((n,)),
+        ] + line_sems(n),
+        compiler_params=pltpu.CompilerParams(
+            vmem_limit_bytes=60 << 20, collective_id=7, has_side_effects=True
+        ),
+        cost_estimate=cost(50),
+        name="intake",
+    )(x, gains)
+
+
+def row_columns(row):
+    return jnp.concatenate(
+        [as_column(row[:, at : at + LANES]) for at in range(0, row.shape[1], LANES)], axis=0
+    )
+
+
+def front_kernel(mixed_ref, taps_ref, same_ref, bias_ref, decay_ref, end_ref, link_ref, seg_col_ref,
+                 seg_row_ref, skip_ref, gain_ref, x_ref, cot_ref, w_ref,
+                 value_ref, act_ref, scaled_ref, step_ref, run_ref, run_exp_ref, inner_ref, mixer_ref,
+                 state_ref, packed_ref, res_ref, stat_ref, own_ref, cot_full_ref,
+                 wm_ref, wo_ref, run_t_ref, scores_ref, part_ref, square_ref, lifted_ref, far_ref,
+                 right_box, left_box, square_box, res_box, stat_box, cot_box, local_sem, *sems,
+                 inner, nstate, per, heads, di_all, n):
+    me = lax.axis_index("tensor")
+    rows, depth = x_ref.shape
     own = rows // n
-    groups = [(sems[2 * i], sems[2 * i + 1]) for i in range(4)]
+    groups = [(sems[2 * i], sems[2 * i + 1]) for i in range(3)]
+    block_at = lambda d: pl.ds(pl.multiple_of(d * own, own), own)
     mine = pl.ds(pl.multiple_of(me * own, own), own)
-    tensor_barrier(me, n)
-    first, second = [], []
+    wide = wm_ref.shape[1]
+    loads = [
+        pltpu.make_async_copy(w_ref.at[:, pl.ds(0, wide)], wm_ref, local_sem.at[0]),
+        pltpu.make_async_copy(w_ref.at[:, pl.ds(wide, inner)], wo_ref, local_sem.at[1]),
+    ]
+    for copy in loads:
+        copy.start()
+    far_ref[...] = jnp.zeros_like(far_ref)
+    quarter = cot_ref.shape[1]
+    column = pl.ds(pl.multiple_of(me * quarter, LANES), quarter)
+    cot_box[:, column] = cot_ref[...]
+    front_barrier(me, n)
+    cots = LineGather(
+        me, n, lambda d: cot_box.at[:, pl.ds(pl.multiple_of(d * quarter, LANES), quarter)],
+        line_groups(sems[14:18]),
+    )
+    cots.step(0)
+    loads[0].wait()
+    enter_part(mixed_ref, wm_ref, taps_ref, same_ref, bias_ref, decay_ref, end_ref, link_ref,
+               value_ref, act_ref, scaled_ref, step_ref, run_ref, run_exp_ref, packed_ref,
+               inner=inner, nstate=nstate, per=per)
+    states = StatePush(packed_ref, far_ref, groups[0], False)
+    states.start()
+    cots.step(1)
+    run_t = run_ref[...].T
+    for h in range(heads):
+        run_t_ref[h] = run_t[h : h + 1, :]
+    intra_part(act_ref, scaled_ref, run_t_ref, run_exp_ref, seg_col_ref, seg_row_ref, inner_ref,
+               scores_ref, inner=inner, nstate=nstate, per=per, block=128)
+    cots.step(2)
+    states.wait_recv()
+    state = join_states(far_ref, inner, per)
+    state_ref[...] = state
+    carried = dot_outer(act_ref[:, inner + nstate :], state.astype(bf16)) * (
+        jnp.exp(run_exp_ref[...]) * link_ref[...]
+    )
+    mixer = inner_ref[...] + carried + skip_ref[...] * act_ref[:, :inner].astype(f32)
+    mixer_ref[...] = mixer
+    z = value_ref[HALO:, :inner]
+    gated = mixer * (z * sigmoid(z))
+    square_ref[...] = row_sums(gated * gated)
+    lifted_ref[...] = (gated * gain_ref[...]).astype(bf16)
+    loads[1].wait()
+    for t in range(3, n):
+        cots.step(t)
+    squares, stats = [], []
     for d in range(1, n):
         peer = lax.rem(me + d, n)
-        theirs = pl.ds(pl.multiple_of(peer * own, own), own)
-        first.append(push(part_ref.at[theirs], inbox.at[d - 1], groups[0], d - 1, peer))
-        first.append(push(square_ref.at[:, theirs], square_box.at[d - 1], groups[1], d - 1, peer))
-    for copy in first:
-        copy.start()
-    total = part_ref[mine, :].astype(f32)
+        squares.append(push(square_ref.at[:, block_at(peer)], square_box.at[d - 1], groups[1], d - 1, peer))
+        squares[-1].start()
+    line = LineReduce(me, n, lambda d: part_ref.at[d], right_box, left_box, line_groups(sems[6:10]))
+    for k in range(n):
+        d = jnp.where(2 * me < n, n - 1 - k, k)
+        part_ref[d] = dot_outer(lifted_ref[block_at(d), :], wo_ref[...]).astype(bf16)
+        if k == 0:
+            line.step(0)
+    for t in range(1, n):
+        line.step(t)
+    total = line.total()
     square = square_ref[:, mine]
-    for copy in first:
+    for copy in squares:
         copy.wait_recv()
     for d in range(1, n):
-        total = total + inbox[d - 1].astype(f32)
         square = square + square_box[d - 1]
     own_ref[...] = total
     scale = lax.rsqrt(square / di_all + epsilon)
     stat_box[:, mine] = scale
     res_box[mine, :] = (x_ref[mine, :].astype(f32) + total * as_column(scale[:1])).astype(bf16)
+    gather = LineGather(me, n, lambda d: res_box.at[block_at(d)], line_groups(sems[10:14]))
+    gather.step(0)
     for d in range(1, n):
-        peer = lax.rem(me + d, n)
-        second.append(push(res_box.at[mine], res_box.at[mine], groups[2], d - 1, peer))
-        second.append(push(stat_box.at[:, mine], stat_box.at[:, mine], groups[3], d - 1, peer))
-    for copy in second:
-        copy.start()
-    for copy in first:
+        stats.append(push(stat_box.at[:, mine], stat_box.at[:, mine], groups[2], d - 1,
+                          lax.rem(me + d, n)))
+        stats[-1].start()
+    for t in range(1, n):
+        gather.step(t)
+    cot_full_ref[...] = cot_box[...]
+    states.wait_send()
+    cots.wait_send()
+    line.wait_send()
+    gather.wait_send()
+    for copy in squares:
         copy.wait_send()
-    for copy in second:
+    for copy in stats:
         copy.wait()
     res_ref[...] = res_box[...]
     stat_ref[...] = stat_box[...]
@@ -422,68 +637,101 @@
     return [pltpu.SemaphoreType.DMA((n - 1,))] * (2 * count)
 
 
-def residual_step(part, square, x, di_all):
+VMEM = pl.BlockSpec(memory_space=pltpu.VMEM)
+HBM = pl.BlockSpec(memory_space=pl.ANY)
+
+
+def front(mixed_ext, taps, same, bias, decay, at_end, link, seg_col, seg_row, skip, gain, x, cot, weights,
+          inner, nstate, per, heads, di_all):
     n = lax.axis_size("tensor")
-    tokens, depth = part.shape
+    others = lax.axis_size(CTX) - 1
+    tokens, depth = x.shape
+    ext = tokens + HALO
     own = tokens // n
+    wide = 2 * inner + 2 * nstate + LANES
     shape = jax.ShapeDtypeStruct
+    outs = [
+        shape((ext, wide), f32), shape((tokens, inner + 2 * nstate), bf16),
+        shape((tokens, inner), bf16), shape((tokens, LANES), f32), shape((tokens, LANES), f32),
+        shape((tokens, inner), f32), shape((tokens, inner), f32), shape((tokens, inner), f32),
+        shape((inner, nstate), f32), shape((inner + 16, nstate), bf16),
+        shape((tokens, depth), bf16), shape((8, tokens), f32), shape((own, depth), f32),
+        shape((tokens, depth), bf16),
+    ]
+    dma = pltpu.SemaphoreType.DMA
     return pl.pallas_call(
-        partial(residual_kernel, di_all=di_all, n=n),
-        in_specs=[pl.BlockSpec(memory_space=pltpu.VMEM)] * 3,
-        out_specs=[pl.BlockSpec(memory_space=pltpu.VMEM)] * 3,
-        out_shape=[shape((tokens, depth), bf16), shape((8, tokens), f32), shape((own, depth), f32)],
+        partial(front_kernel, inner=inner, nstate=nstate, per=per, heads=heads, di_all=di_all, n=n),
+        in_specs=[VMEM] * 13 + [HBM],
+        out_specs=[VMEM] * 14,
+        out_shape=outs,
         scratch_shapes=[
-            pltpu.VMEM((n - 1, own, depth), bf16), pltpu.VMEM((n - 1, 8, own), f32),
+            pltpu.VMEM((depth, wide), bf16), pltpu.VMEM((depth, inner), bf16),
+            pltpu.VMEM((heads, 1, tokens), f32), pltpu.VMEM((tokens, tokens), f32),
+            pltpu.VMEM((n, own, depth), bf16), pltpu.VMEM((8, tokens), f32),
+            pltpu.VMEM((tokens, inner), bf16), pltpu.VMEM((others, inner + 16, nstate), bf16),
+            pltpu.VMEM((n, own, depth), bf16), pltpu.VMEM((n, own, depth), bf16),
+            pltpu.VMEM((n - 1, 8, own), f32),
             pltpu.VMEM((tokens, depth), bf16), pltpu.VMEM((8, tokens), f32),
-        ] + pairs(4, n),
+            pltpu.VMEM((tokens, depth), bf16), dma((2,)), dma((others,)), dma((others,)),
+        ] + pairs(2, n) + line_sems(n) * 3,
         compiler_params=pltpu.CompilerParams(
-            vmem_limit_bytes=40 << 20, collective_id=1, has_side_effects=True
+            vmem_limit_bytes=60 << 20, collective_id=1, has_side_effects=True
         ),
-        cost_estimate=cost(60),
-        name="residual_step",
-    )(part, square, x)
-
-
-def turn_kernel(dmix_ref, dgate_ref, res_ref, cot_ref, own_ref, gain_ref,
+        cost_estimate=cost(100),
+        name="front",
+    )(mixed_ext, taps, same, bias, decay, at_end, link, seg_col, seg_row, skip, gain, x, cot, weights)
+
+
+def turn_kernel(dmix_hbm, dgate_ref, res_ref, cot_ref, own_ref, gain_ref,
                 dres_ref, notes_ref, gains_ref,
-                inbox, gate_box, dres_box, notes_box, *sems, n):
+                dmix_ref, right_box, left_box, gate_box, dres_box, notes_box, load_sem, *sems, n):
     me = lax.axis_index("tensor")
-    rows, depth = dmix_ref.shape
+    rows, depth = res_ref.shape
     own = rows // n
-    groups = [(sems[2 * i], sems[2 * i + 1]) for i in range(4)]
-    mine = pl.ds(pl.multiple_of(me * own, own), own)
+    groups = [(sems[2 * i], sems[2 * i + 1]) for i in range(2)]
+    block_at = lambda d: pl.ds(pl.multiple_of(d * own, own), own)
+    mine = block_at(me)
+    load = pltpu.make_async_copy(dmix_hbm, dmix_ref, load_sem)
+    load.start()
     tensor_barrier(me, n)
+    load.wait()
+    line = LineReduce(me, n, lambda d: dmix_ref.at[block_at(d)], right_box, left_box,
+                      line_groups(sems[4:8]))
+    gather = LineGather(me, n, lambda d: dres_box.at[block_at(d)], line_groups(sems[8:12]))
+    line.step(0)
     first, second = [], []
     for d in range(1, n):
         peer = lax.rem(me + d, n)
-        theirs = pl.ds(pl.multiple_of(peer * own, own), own)
-        first.append(push(dmix_ref.at[theirs], inbox.at[d - 1], groups[0], d - 1, peer))
-        first.append(push(dgate_ref.at[theirs], gate_box.at[d - 1], groups[1], d - 1, peer))
-    for copy in first:
-        copy.start()
+        first.append(push(dgate_ref.at[:, block_at(peer)], gate_box.at[d - 1], groups[0], d - 1, peer))
+        first[-1].start()
     res = res_ref[mine, :].astype(f32)
     scale = lax.rsqrt(jnp.mean(res * res, axis=1, keepdims=True) + epsilon)
     normed = res * scale
-    dmix = dmix_ref[mine, :].astype(f32)
-    dgate = dgate_ref[mine, :]
+    for t in range(1, n):
+        line.step(t)
+    dmix = line.total()
+    lifted = dmix * gain_ref[...]
+    inside = jnp.mean(lifted * normed, axis=1, keepdims=True)
+    dres = (cot_ref[mine, :].astype(f32) + scale * (lifted - normed * inside)).astype(bf16)
+    dres_box[mine, :] = dres
+    gather.step(0)
+    gains_ref[...] = jnp.broadcast_to(jnp.sum(dmix * normed, axis=0, keepdims=True), gains_ref.shape)
+    dgate = dgate_ref[:, mine]
     for copy in first:
         copy.wait_recv()
     for d in range(1, n):
-        dmix = dmix + inbox[d - 1].astype(f32)
         dgate = dgate + gate_box[d - 1]
-    gains_ref[...] = jnp.broadcast_to(jnp.sum(dmix * normed, axis=0, keepdims=True), gains_ref.shape)
-    lifted = dmix * gain_ref[...]
-    inside = jnp.mean(lifted * normed, axis=1, keepdims=True)
-    dres = (cot_ref[mine, :].astype(f32) + scale * (lifted - normed * inside)).astype(bf16)
-    cross = jnp.sum(dres.astype(f32) * own_ref[...], axis=1, keepdims=True)
-    dres_box[mine, :] = dres
-    notes_box[mine, :] = jnp.where(col_iota(dgate.shape) == LANES - 1, cross, dgate)
+    gates = dgate.shape[0]
+    notes_box[:gates, mine] = dgate
+    notes_box[gates:, mine] = row_sums(dres.astype(f32) * own_ref[...])
     for d in range(1, n):
         peer = lax.rem(me + d, n)
-        second.append(push(dres_box.at[mine], dres_box.at[mine], groups[2], d - 1, peer))
-        second.append(push(notes_box.at[mine], notes_box.at[mine], groups[3], d - 1, peer))
-    for copy in second:
-        copy.start()
+        second.append(push(notes_box.at[:, mine], notes_box.at[:, mine], groups[1], d - 1, peer))
+        second[-1].start()
+    for t in range(1, n):
+        gather.step(t)
+    line.wait_send()
+    gather.wait_send()
     for copy in first:
         copy.wait_send()
     for copy in second:
@@ -499,125 +747,184 @@
     shape = jax.ShapeDtypeStruct
     return pl.pallas_call(
         partial(turn_kernel, n=n),
-        in_specs=[pl.BlockSpec(memory_space=pltpu.VMEM)] * 6,
-        out_specs=[pl.BlockSpec(memory_space=pltpu.VMEM)] * 3,
-        out_shape=[shape((tokens, depth), bf16), shape((tokens, LANES), f32),
+        in_specs=[HBM] + [VMEM] * 5,
+        out_specs=[VMEM] * 3,
+        out_shape=[shape((tokens, depth), bf16), shape((dgate.shape[0] + 8, tokens), f32),
                    shape((8, depth), f32)],
         scratch_shapes=[
-            pltpu.VMEM((n - 1, own, depth), bf16), pltpu.VMEM((n - 1, own, LANES), f32),
-            pltpu.VMEM((tokens, depth), bf16), pltpu.VMEM((tokens, LANES), f32),
-        ] + pairs(4, n),
+            pltpu.VMEM((tokens, depth), bf16),
+            pltpu.VMEM((n, own, depth), bf16), pltpu.VMEM((n, own, depth), bf16),
+            pltpu.VMEM((n - 1, dgate.shape[0], own), f32),
+            pltpu.VMEM((tokens, depth), bf16), pltpu.VMEM((dgate.shape[0] + 8, tokens), f32),
+            pltpu.SemaphoreType.DMA,
+        ] + pairs(2, n) + line_sems(n) * 2,
         compiler_params=pltpu.CompilerParams(
-            vmem_limit_bytes=40 << 20, collective_id=2, has_side_effects=True
+            vmem_limit_bytes=60 << 20, collective_id=2, has_side_effects=True
         ),
         cost_estimate=cost(60),
         name="turn_step",
     )(dmix, dgate, residual, cot, own_part, gain)
 
 
-def finish_kernel(grad_ref, halo_ref, w_ref, x_ref, dres_ref, gain_ref, mid_ref, state_ref,
-                  out_ref, gains_ref, state_out_ref,
-                  outbox, inbox, cross_box, cross_in, gains_box, gains_in, state_in, *sems, n):
+def in_order(box, me, count):
+    total = None
+    for source in range(count):
+        term = box[lax.rem(me - source + 2 * count - 1, count)].astype(f32)
+        total = term if total is None else total + term
+    return total
+
+
+def row_place():
+    cy, core = lax.axis_size("cy"), lax.axis_size("core")
+    return (lax.axis_index("shard") * cy + lax.axis_index("cy")) * core + lax.axis_index("core")
+
+
+def row_peer(place):
+    cy, core = lax.axis_size("cy"), lax.axis_size("core")
+    return {"shard": place // (cy * core), "cy": lax.rem(place // core, cy), "core": lax.rem(place, core)}
+
+
+def finish_kernel(grad_ref, x_ref, dres_ref, gain_ref, mid_ref, state_ref, early_ref,
+                  w_hbm, pair_hbm,
+                  out_ref, early_out, late_out, gates_out, down_out,
+                  w_ref, pair_ref, blocks_ref, right_box, left_box, cross_box, cross_in, gains_box, gains_in,
+                  state_in, early_in, late_ref, late_in, load_sem, *sems, n, count):
     me = lax.axis_index("tensor")
+    place = row_place()
     rows, depth = x_ref.shape
     quarter = depth // n
-    groups = [(sems[2 * i], sems[2 * i + 1]) for i in range(4)]
-    tensor_barrier(me, n)
+    wide = w_ref.shape[1]
+    groups = [(sems[2 * i], sems[2 * i + 1]) for i in range(3)]
+    row_groups = [(sems[6 + 2 * i], sems[7 + 2 * i]) for i in range(2)]
+    loads = [pltpu.make_async_copy(w_hbm.at[:, pl.ds(0, wide)], w_ref, load_sem.at[0]),
+             pltpu.make_async_copy(pair_hbm, pair_ref, load_sem.at[1])]
+    for copy in loads:
+        copy.start()
+    barrier = line_barrier(me, n)
+    for d in range(1, count):
+        pl.semaphore_signal(barrier, inc=1, device_id=row_peer(lax.rem(place + d, count)),
+                            device_id_type=MESH)
+    pl.semaphore_wait(barrier, n - 1 + count - 1)
+    copies, states, lates = [], [], []
+    for d in range(1, n):
+        states.append(push(state_ref, state_in.at[d - 1], groups[2], d - 1, lax.rem(me + d, n)))
+        states[-1].start()
     x = x_ref[...].astype(f32)
     scale = lax.rsqrt(jnp.mean(x * x, axis=1, keepdims=True) + epsilon)
-    copies = []
-    for d in range(1, n):
-        peer = lax.rem(me + d, n)
-        copies.append(push(state_ref, state_in.at[d - 1], groups[3], d - 1, peer))
-        copies[-1].start()
+    loads[0].wait()
+    line = LineReduce(me, n, lambda d: blocks_ref.at[d], right_box, left_box, line_groups(sems[10:14]))
     cross = jnp.zeros((8, rows), f32)
-    kept = None
-    for d in tuple(range(1, n)) + (0,):
-        peer = lax.rem(me + d, n)
-        theirs = pl.ds(pl.multiple_of(peer * quarter, LANES), quarter)
+    for k in range(n):
+        d = jnp.where(2 * me < n, n - 1 - k, k)
+        theirs = pl.ds(pl.multiple_of(d * quarter, LANES), quarter)
         w = w_ref[theirs, :]
-        block = dot_outer(grad_ref[HALO:, :], w)
-        tail = dot_outer(halo_ref[...], w)
-        block = jnp.concatenate([block[: rows - HALO], block[rows - HALO :] + tail], axis=0)
+        block = dot_outer(grad_ref[...], w)
+        blocks_ref[d] = block.astype(bf16)
+        if k == 0:
+            line.step(0)
         normed = x_ref[:, theirs].astype(f32) * scale
         cross = cross + row_sums(block * normed * gain_ref[:, theirs])
-        gains = jnp.where(
+        gains_box[d] = jnp.where(
             row_iota((8, quarter)) == 0, jnp.sum(block * normed, axis=0, keepdims=True),
             mid_ref[:, theirs],
         )
-        if d == 0:
-            kept, kept_gains, kept_normed = block, gains, normed
-            continue
-        gains_box[d - 1] = gains
-        outbox[d - 1] = block.astype(bf16)
-        copies.append(push(outbox.at[d - 1], inbox.at[d - 1], groups[0], d - 1, peer))
-        copies[-1].start()
-        copies.append(push(gains_box.at[d - 1], gains_in.at[d - 1], groups[1], d - 1, peer))
-        copies[-1].start()
     cross_box[...] = cross
     for d in range(1, n):
-        copies.append(
-            push(cross_box, cross_in.at[d - 1], groups[2], d - 1, lax.rem(me + d, n))
-        )
-        copies[-1].start()
+        peer = lax.rem(me + d, n)
+        copies.append(push(gains_box.at[peer], gains_in.at[d - 1], groups[0], d - 1, peer))
+        copies.append(push(cross_box, cross_in.at[d - 1], groups[1], d - 1, peer))
+    for d in range(1, count):
+        copies.append(push(early_ref, early_in.at[d - 1], row_groups[0], d - 1,
+                           row_peer(lax.rem(place + d, count))))
     for copy in copies:
-        copy.wait()
+        copy.start()
+    if n > 1:
+        line.step(1)
+    loads[1].wait()
+    hid = down_out.shape[1]
+    wides = 2 * hid
+    deep = pair_ref.shape[0] // 2
+    for p in range(2):
+        top = pair_ref[p * deep : p * deep + depth, :].astype(f32)
+        gates_out[p * depth : (p + 1) * depth, 0, :] = top[:, :hid]
+        gates_out[p * depth : (p + 1) * depth, 1, :] = top[:, hid:]
+        for c in range(depth // wides):
+            at = p * deep + depth + c * hid
+            down_out[p, :, c * wides : (c + 1) * wides] = pair_ref[at : at + hid, :].astype(f32)
+    for copy in copies[: 2 * (n - 1)] + states:
+        copy.wait_recv()
+    gains = gains_box[me]
     state = state_ref[...]
     for d in range(1, n):
-        kept = kept + inbox[d - 1].astype(f32)
-        kept_gains = kept_gains + gains_in[d - 1]
+        gains = gains + gains_in[d - 1]
         cross = cross + cross_in[d - 1]
-        state = state + state_in[d - 1]
-    gains_ref[...] = kept_gains
-    state_out_ref[...] = state
+    state_in[n - 1] = state
+    state = in_order(state_in, me, n)
+    late_ref[:, :quarter] = gains
+    late_ref[:, quarter:] = state
+    for d in range(1, count):
+        lates.append(push(late_ref, late_in.at[d - 1], row_groups[1], d - 1,
+                          row_peer(lax.rem(place + d, count))))
+        lates[-1].start()
+    for t in range(2, n):
+        line.step(t)
+    total = line.total()
     here = pl.ds(pl.multiple_of(me * quarter, LANES), quarter)
-    inside = jnp.concatenate(
-        [as_column(cross[:1, at : at + LANES]) for at in range(0, rows, LANES)], axis=0
-    ) / depth
+    inside = row_columns(cross[:1]) / depth
     out_ref[...] = dres_ref[:, here].astype(f32) + scale * (
-        kept * gain_ref[:, here] - kept_normed * inside
-    )
-
-
-def finish_step(value_grad, halo, weights, x, dres, gain, gains_mid, state):
-    n = lax.axis_size("tensor")
+        total * gain_ref[:, here] - x_ref[:, here].astype(f32) * scale * inside
+    )
+    for copy in copies[2 * (n - 1) :] + lates:
+        copy.wait_recv()
+    early_in[count - 1] = early_ref[...]
+    late_in[count - 1] = late_ref[...]
+    early_out[...] = in_order(early_in, place, count)
+    late_out[...] = in_order(late_in, place, count)
+    for copy in copies + states + lates:
+        copy.wait_send()
+    line.wait_send()
+
+
+def finish_step(value_grad, weights, x, dres, gain, gains_mid, state, early, pair_rows, hid):
+    n, count = lax.axis_size("tensor"), lax.axis_size(ROWS)
     tokens, depth = x.shape
     quarter = depth // n
+    wide = value_grad.shape[1]
+    late = quarter + state.shape[1]
     shape = jax.ShapeDtypeStruct
-    outs = [shape((tokens, quarter), f32), shape((8, quarter), f32), shape(state.shape, f32)]
-    args = (value_grad, halo, weights, x, dres, gain, gains_mid, state)
+    dma = pltpu.SemaphoreType.DMA
     return pl.pallas_call(
-        partial(finish_kernel, n=n),
-        grid=(1,),
-        in_specs=[whole(a) if a is not weights else columns(a, value_grad.shape[1]) for a in args],
-        out_specs=[whole(o) for o in outs],
-        out_shape=outs,
+        partial(finish_kernel, n=n, count=count),
+        in_specs=[VMEM] * 7 + [HBM] * 2,
+        out_specs=[VMEM] * 5,
+        out_shape=[shape((tokens, quarter), f32), shape(early.shape, f32), shape((8, late), f32),
+                   shape((2 * depth, 2, hid), f32), shape((2, hid, depth), f32)],
         scratch_shapes=[
-            pltpu.VMEM((n - 1, tokens, quarter), bf16), pltpu.VMEM((n - 1, tokens, quarter), bf16),
+            pltpu.VMEM((depth, wide), bf16), pltpu.VMEM((3 * depth, 2 * hid), bf16),
+            pltpu.VMEM((n, tokens, quarter), bf16),
+            pltpu.VMEM((n, tokens, quarter), bf16), pltpu.VMEM((n, tokens, quarter), bf16),
             pltpu.VMEM((8, tokens), f32), pltpu.VMEM((n - 1, 8, tokens), f32),
-            pltpu.VMEM((n - 1, 8, quarter), f32), pltpu.VMEM((n - 1, 8, quarter), f32),
-            pltpu.VMEM((n - 1,) + state.shape, f32),
-        ] + pairs(4, n),
+            pltpu.VMEM((n, 8, quarter), f32), pltpu.VMEM((n - 1, 8, quarter), f32),
+            pltpu.VMEM((n,) + state.shape, f32), pltpu.VMEM((count,) + early.shape, f32),
+            pltpu.VMEM((8, late), f32), pltpu.VMEM((count, 8, late), f32), dma((2,)),
+        ] + pairs(3, n) + [dma((count - 1,))] * 4 + line_sems(n),
         compiler_params=pltpu.CompilerParams(
-            vmem_limit_bytes=56 << 20, collective_id=3, has_side_effects=True
+            vmem_limit_bytes=60 << 20, collective_id=3, has_side_effects=True
         ),
         cost_estimate=cost(45),
         name="finish_step",
-    )(*args)
-
-
-def back_kernel(dout_ref, wa_ref, wb_ref, mixer_ref, z_ref, act_ref, run_exp_ref, link_ref, gain_ref,
-                stat_ref, through_ref, heads_ref, zgrad_ref, gated_ref, direct_ref, sums_ref,
+    )(value_grad, x, dres, gain, gains_mid, state, early, weights, pair_rows)
+
+
+def back_part(dout_ref, w_ref, mixer_ref, value_ref, act_ref, run_exp_ref, link_ref, gain_ref,
+                scale, cross, through_ref, heads_ref, zgrad_ref, gated_ref, direct_ref, sums_ref,
                 *, inner, nstate, di_all):
-    scale = stat_ref[:, 0:1]
-    cross = stat_ref[:, 1:2]
     mixer = mixer_ref[...]
-    z = z_ref[HALO:, :]
+    z = value_ref[HALO:, :inner]
     sig = sigmoid(z)
     act = z * sig
     gated = mixer * act
-    dout = dout_ref[...]
-    grad = jnp.concatenate([dot_rows(dout, wa_ref[...]), dot_rows(dout, wb_ref[...])], axis=1)
+    grad = dot_rows(dout_ref[...], w_ref[...])
     gated_ref[...] = (gated * scale * gain_ref[...]).astype(bf16)
     sums_ref[0:1, :] = jnp.sum(grad * gated * scale, axis=0, keepdims=True)
     gated_grad = scale * (grad * gain_ref[...]) - gated * (scale * scale * scale * cross / di_all)
@@ -631,30 +938,8 @@
     direct_ref[inner:, :] = through_ref[...]
 
 
-def back(dout, weights, mixer, value, act, run_exp, link, gain, stats, through, inner, nstate, di_all):
-    tokens = act.shape[0]
-    half = inner // 2
-    first = 2 * inner + 2 * nstate + LANES
-    shape = jax.ShapeDtypeStruct
-    outs = [shape((tokens, inner), f32), shape((tokens, inner), bf16), shape((tokens, inner), bf16),
-            shape((inner + 16, nstate), bf16), shape((8, inner), f32)]
-    return pl.pallas_call(
-        partial(back_kernel, inner=inner, nstate=nstate, di_all=di_all),
-        grid=(1,),
-        in_specs=[whole(dout), columns(weights, half, first), columns(weights, half, first + half),
-                  whole(mixer), columns(value, inner), whole(act), whole(run_exp), whole(link),
-                  whole(gain), whole(stats), whole(through)],
-        out_specs=[whole(o) for o in outs],
-        out_shape=outs,
-        compiler_params=BIG,
-        cost_estimate=cost(8),
-        name="back",
-    )(dout, weights, weights, mixer, value, act, run_exp, link, gain, stats, through)
-
-
-def intra_back_kernel(heads_ref, act_ref, scaled_ref, run_t_ref, run_exp_ref, seg_col_ref,
-                      seg_row_ref, dscaled_ref, dstate_ref, drun_ref, scores_ref, dscores_ref,
-                      rows_ref, *, inner, nstate, per, block):
+def intra_back_part(heads_ref, act_ref, scaled_ref, run_t_ref, run_exp_ref, seg_col_ref,
+                      seg_row_ref, dscaled_ref, dstate_ref, drun_ref, scores_ref, dscores_ref, *, inner, nstate, per, block):
     tokens = act_ref.shape[0]
     keys = act_ref[:, inner : inner + nstate]
     query = act_ref[:, inner + nstate :]
@@ -707,21 +992,6 @@
         dstate_ref[:stop, :nstate] += dot_inner(grad, query[start:stop])
 
 
-def intra_back(heads, act, scaled, run_t, run_exp, seg_col, seg_row, inner, nstate, per):
-    tokens = act.shape[0]
-    shape = jax.ShapeDtypeStruct
-    return pl.pallas_call(
-        partial(intra_back_kernel, inner=inner, nstate=nstate, per=per, block=128),
-        out_shape=[shape((tokens, inner), f32), shape((tokens, 2 * nstate), f32),
-                   shape((tokens, LANES), f32)],
-        scratch_shapes=[pltpu.VMEM((tokens, tokens), f32), pltpu.VMEM((tokens, tokens), f32),
-                        pltpu.VMEM((8, LANES), f32)],
-        compiler_params=BIG,
-        cost_estimate=cost(20),
-        name="intra_back",
-    )(heads, act, scaled, run_t, run_exp, seg_col, seg_row)
-
-
 def conv_back(value_ref, column, taps_ref, same_ref, dact, at, dtaps_ref, tokens):
     ext = tokens + HALO
     rows, total = conv_pre(value_ref, column, taps_ref, at, same_ref, tokens)
@@ -744,7 +1014,7 @@
     return drows
 
 
-def state_back_kernel(heads_ref, act_ref, step_ref, run_ref, run_exp_ref, link_ref, end_ref,
+def state_back_part(heads_ref, act_ref, step_ref, run_ref, run_exp_ref, link_ref, end_ref,
                       value_ref, taps_ref, same_ref, dstate_ref, in_ref, far_ref,
                       rows_ref, dtaps_ref, leaving_ref, kept_ref, dact_ref, *, inner, nstate, per):
     tokens = act_ref.shape[0]
@@ -767,41 +1037,18 @@
 
     def conv(i, _):
         at = pl.multiple_of(i * LANES, LANES)
-        drows = conv_back(value_ref, at, taps_ref, same_ref, dact_ref[:, pl.ds(at, LANES)], at,
-                          dtaps_ref, tokens)
+        drows = conv_back(value_ref, 2 * inner + at, taps_ref, same_ref, dact_ref[:, pl.ds(at, LANES)],
+                          inner + at, dtaps_ref, tokens)
         rows_ref[:, pl.ds(at, LANES)] = drows.astype(bf16)
         return 0
 
     lax.fori_loop(0, 2 * nstate // LANES, conv, 0)
 
 
-def state_back(heads, act, step, running, run_exp, link, at_end, value, taps, same, dstate, state_in,
-               far, inner, nstate, per):
-    tokens = act.shape[0]
-    shape = jax.ShapeDtypeStruct
-    outs = [shape((tokens + HALO, 2 * nstate), bf16), shape((CONV, 2 * nstate), f32),
-            shape((tokens, inner), f32), shape((8, LANES), f32)]
-    args = (heads, act, step, running, run_exp, link, at_end, value, taps, same, dstate, state_in, far)
-    specs = [whole(a) for a in args]
-    specs[7] = columns(value, 2 * nstate, 2 * inner)
-    specs[8] = columns(taps, 2 * nstate, inner)
-    return pl.pallas_call(
-        partial(state_back_kernel, inner=inner, nstate=nstate, per=per),
-        grid=(1,),
-        in_specs=specs,
-        out_specs=[whole(o) for o in outs],
-        out_shape=outs,
-        scratch_shapes=[pltpu.VMEM((tokens, 2 * nstate), f32)],
-        compiler_params=BIG,
-        cost_estimate=cost(6),
-        name="state_back",
-    )(*args)
-
-
-def signal_back_kernel(heads_ref, act_ref, step_ref, value_ref, raw_ref, taps_ref, same_ref, bias_ref,
+def signal_back_part(heads_ref, act_ref, step_ref, value_ref, taps_ref, same_ref, bias_ref,
                        decay_ref, skip_ref, mixer_ref, inner_ref, dscaled_ref, drun_ref, leaving_ref,
                        kept_ref, zgrad_ref, state_ref,
-                       grad_ref, dtaps_ref, small_ref, dact_ref, *, inner, nstate, per):
+                       grad_ref, dtaps_ref, small_ref, dact_ref, middle, between, *, inner, nstate, per):
     tokens = act_ref.shape[0]
     signal = act_ref[:, :inner].astype(f32)
     grow = expander(LANES, inner, per)
@@ -815,12 +1062,16 @@
 
     def conv(i, _):
         at = pl.multiple_of(i * LANES, LANES)
-        drows = conv_back(value_ref, at, taps_ref, same_ref, dact_ref[:, pl.ds(at, LANES)], at,
+        drows = conv_back(value_ref, inner + at, taps_ref, same_ref, dact_ref[:, pl.ds(at, LANES)], at,
                           dtaps_ref, tokens)
         grad_ref[:, pl.ds(inner + at, LANES)] = drows.astype(bf16)
         return 0
 
-    lax.fori_loop(0, inner // LANES, conv, 0)
+    half = inner // LANES // 2
+    lax.fori_loop(0, half, conv, 0)
+    middle()
+    lax.fori_loop(half, inner // LANES, conv, 0)
+    between()
     carried = mixer_ref[...] - inner_ref[...] - skip_ref[...] * signal
     tri = (row_iota((tokens, tokens)) <= col_iota((tokens, tokens))).astype(bf16)
     strict = (row_iota((tokens, tokens)) > col_iota((tokens, tokens))).astype(bf16)
@@ -829,7 +1080,7 @@
     dlog = left_sums(tri, back_sum) + left_sums(strict, front_sum) + kept_ref[0:1, :]
     rate = -jnp.exp(decay_ref[...])
     dstep = dlog * rate + fold_heads(dscaled * signal, folds)
-    draw = dstep * sigmoid(raw_ref[HALO:, :] + bias_ref[...])
+    draw = dstep * sigmoid(value_ref[HALO:, 2 * inner + 2 * nstate :] + bias_ref[...])
     small_ref[0:1, :] = jnp.sum(draw, axis=0, keepdims=True)
     small_ref[1:2, :] = jnp.sum(dlog * step, axis=0, keepdims=True) * rate
     small_ref[2:, :] = jnp.zeros((6, LANES), f32)
@@ -843,29 +1094,251 @@
     grad_ref[HALO:, step_at:] = jnp.where(used, draw, 0.0).astype(bf16)
 
 
-def signal_back(heads, act, step, value, taps, same, bias, decay, skip, mixer, within, dscaled, drun,
-                leaving, kept, z_grad, state_rows, inner, nstate, per):
-    tokens = act.shape[0]
-    wide = value.shape[1]
+def rear_kernel(dout_ref, stat_ref, notes_ref, mixer_ref, inner_ref, act_ref, scaled_ref, step_ref,
+                run_ref, run_exp_ref, state_ref, taps_ref, same_ref, bias_ref, decay_ref, skip_ref,
+                gain_ref, end_ref, link_ref, seg_col_ref, seg_row_ref, packed_ref,
+                part_hbm, value_hbm, w_hbm, res_hbm,
+                grad_ref, gated_ref, dtaps_ref, sums_ref, small_ref, state_all_ref, out_ref,
+                value_ref, w_ref, res_ref, run_t_ref, heads_ref, zgrad_ref, direct_ref, dscaled_ref,
+                dstate_ref, drun_ref, scores_ref, dscores_ref, leaving_ref, kept_ref, rows_ref, dact_ref,
+                far_ref, part_ref, right_box, left_box, rows_box, sum_box, ext_ref, state_halo, signal_halo,
+                local_sem, *sems,
+                inner, nstate, per, heads, di_all, n):
+    me = lax.axis_index("tensor")
+    tokens = act_ref.shape[0]
+    quarter = part_ref.shape[1] // n
+    own = tokens // n
+    wide = value_ref.shape[1]
+    groups = [(sems[2 * i], sems[2 * i + 1]) for i in range(4)]
+    column = lambda k: pl.ds(pl.multiple_of(k * quarter, LANES), quarter)
+    loads = [
+        pltpu.make_async_copy(part_hbm, part_ref, local_sem.at[3]),
+        pltpu.make_async_copy(w_hbm.at[:, pl.ds(wide, inner)], w_ref, local_sem.at[0]),
+        pltpu.make_async_copy(value_hbm, value_ref, local_sem.at[1]),
+        pltpu.make_async_copy(res_hbm.at[:, column(me)], res_ref, local_sem.at[2]),
+    ]
+    for copy in loads:
+        copy.start()
+    far_ref[...] = jnp.zeros_like(far_ref)
+    state_halo[...] = jnp.zeros_like(state_halo)
+    signal_halo[...] = jnp.zeros_like(signal_halo)
+    front_barrier(me, n)
+    line = LineReduce(me, n, lambda d: part_ref.at[:, column(d)], right_box, left_box,
+                      line_groups(sems[8:12]))
+    loads[0].wait()
+    line.step(0)
+    for copy in loads[1:]:
+        copy.wait()
+    scale = row_columns(stat_ref[0:1, :])
+    gates = notes_ref.shape[0] - 8
+    cross = row_columns(notes_ref[gates : gates + 1, :])
+    back_part(dout_ref, w_ref, mixer_ref, value_ref, act_ref, run_exp_ref, link_ref, gain_ref,
+              scale, cross, packed_ref, heads_ref, zgrad_ref, gated_ref, direct_ref, sums_ref,
+              inner=inner, nstate=nstate, di_all=di_all)
+    states = StatePush(direct_ref, far_ref, groups[0], True)
+    states.start()
+    line.step(1)
+    run_t = run_ref[...].T
+    for h in range(heads):
+        run_t_ref[h] = run_t[h : h + 1, :]
+    intra_back_part(heads_ref, act_ref, scaled_ref, run_t_ref, run_exp_ref, seg_col_ref, seg_row_ref,
+                    dscaled_ref, dstate_ref, drun_ref, scores_ref, dscores_ref,
+                    inner=inner, nstate=nstate, per=per, block=128)
+    line.step(2)
+    states.wait_recv()
+    state_back_part(heads_ref, act_ref, step_ref, run_ref, run_exp_ref, link_ref, end_ref, value_ref,
+                    taps_ref, same_ref, dstate_ref, state_ref, far_ref, rows_ref, dtaps_ref,
+                    leaving_ref, kept_ref, dact_ref.at[:, pl.ds(0, 2 * nstate)],
+                    inner=inner, nstate=nstate, per=per)
+    body = lambda d: pl.ds(pl.multiple_of(HALO + d * own, 16), own)
+    reduces, gathers = [], []
+    place, count = ctx_place()
+    sends, gets = place > 0, place < count - 1
+    before = ctx_peer(jnp.maximum(place - 1, 0))
+    state_copy = push(rows_ref.at[pl.ds(0, HALO)], state_halo, groups[2], 0, before)
+    signal_copy = push(ext_ref.at[pl.ds(0, HALO), pl.ds(inner, inner)], signal_halo, groups[2], 1, before)
+    pl.when(sends)(state_copy.start)
+
+    def middle():
+        pl.when(gets)(state_copy.wait_recv)
+        rows_ref[tokens:, :] = rows_ref[tokens:, :] + state_halo[...]
+        for d in range(1, n):
+            peer = lax.rem(me + d, n)
+            reduces.append(push(rows_ref.at[body(peer)], rows_box.at[d - 1], groups[1], d - 1, peer))
+            reduces[-1].start()
+
+    def between():
+        pl.when(sends)(signal_copy.start)
+        total = rows_ref[body(me), :].astype(f32)
+        for copy in reduces:
+            copy.wait_recv()
+        for d in range(1, n):
+            total = total + rows_box[d - 1].astype(f32)
+        sum_box[body(me), :] = total.astype(bf16)
+        for d in range(1, n):
+            peer = lax.rem(me + d, n)
+            gathers.append(push(sum_box.at[body(me)], sum_box.at[body(me)], groups[3], d - 1, peer))
+            gathers[-1].start()
+
+    signal_back_part(heads_ref, act_ref, step_ref, value_ref, taps_ref, same_ref, bias_ref, decay_ref,
+                     skip_ref, mixer_ref, inner_ref, dscaled_ref, drun_ref, leaving_ref, kept_ref,
+                     zgrad_ref, rows_ref, ext_ref, dtaps_ref, small_ref, dact_ref, middle, between,
+                     inner=inner, nstate=nstate, per=per)
+    grad_ref[...] = ext_ref[HALO:, :]
+    pl.when(gets)(signal_copy.wait_recv)
+    grad_ref[tokens - HALO :, inner : 2 * inner] = (
+        ext_ref[tokens:, inner : 2 * inner] + signal_halo[...]
+    )
+    for t in range(3, n):
+        line.step(t)
+    out_ref[...] = (line.total() + res_ref[...].astype(f32)).astype(bf16)
+    for copy in gathers:
+        copy.wait_recv()
+    state_all_ref[...] = sum_box[HALO:, :]
+    states.wait_send()
+    line.wait_send()
+    pl.when(sends)(state_copy.wait_send)
+    pl.when(sends)(signal_copy.wait_send)
+    for copy in reduces + gathers:
+        copy.wait_send()
+
+
+def rear(vmem_args, part, value, weights, residual, inner, nstate, per, heads, di_all):
+    n = lax.axis_size("tensor")
+    others = lax.axis_size(CTX) - 1
+    ext, wide = value.shape
+    tokens = ext - HALO
+    depth = residual.shape[1]
+    quarter = depth // n
     shape = jax.ShapeDtypeStruct
-    outs = [shape((tokens + HALO, wide), bf16), shape((CONV, inner), f32), shape((8, LANES), f32)]
-    args = (heads, act, step, value, value, taps, same, bias, decay, skip, mixer, within, dscaled, drun,
-            leaving, kept, z_grad, state_rows)
-    specs = [whole(a) for a in args]
-    specs[3] = columns(value, inner, inner)
-    specs[4] = columns(value, LANES, wide - LANES)
-    specs[5] = columns(taps, inner)
+    outs = [
+        shape((tokens, wide), bf16), shape((tokens, inner), bf16), shape((CONV, inner + 2 * nstate), f32),
+        shape((8, inner), f32), shape((8, LANES), f32), shape((tokens, 2 * nstate), bf16),
+        shape((tokens, quarter), bf16),
+    ]
+    dma = pltpu.SemaphoreType.DMA
     return pl.pallas_call(
-        partial(signal_back_kernel, inner=inner, nstate=nstate, per=per),
-        grid=(1,),
-        in_specs=specs,
-        out_specs=[whole(o) for o in outs],
+        partial(rear_kernel, inner=inner, nstate=nstate, per=per, heads=heads, di_all=di_all, n=n),
+        in_specs=[VMEM] * len(vmem_args) + [HBM] * 4,
+        out_specs=[VMEM] * len(outs),
         out_shape=outs,
-        scratch_shapes=[pltpu.VMEM((tokens, inner), f32)],
-        compiler_params=BIG,
+        scratch_shapes=[
+            pltpu.VMEM((ext, wide), f32), pltpu.VMEM((depth, inner), bf16),
+            pltpu.VMEM((tokens, quarter), bf16), pltpu.VMEM((heads, 1, tokens), f32),
+            pltpu.VMEM((tokens, inner), f32), pltpu.VMEM((tokens, inner), bf16),
+            pltpu.VMEM((inner + 16, nstate), bf16), pltpu.VMEM((tokens, inner), f32),
+            pltpu.VMEM((tokens, 2 * nstate), f32), pltpu.VMEM((tokens, LANES), f32),
+            pltpu.VMEM((tokens, tokens), f32), pltpu.VMEM((tokens, tokens), f32),
+            pltpu.VMEM((tokens, inner), f32), pltpu.VMEM((8, LANES), f32),
+            pltpu.VMEM((ext, 2 * nstate), bf16), pltpu.VMEM((tokens, inner), f32),
+            pltpu.VMEM((others, inner + 16, nstate), bf16),
+            pltpu.VMEM((tokens, depth), bf16),
+            pltpu.VMEM((n, tokens, quarter), bf16), pltpu.VMEM((n, tokens, quarter), bf16),
+            pltpu.VMEM((n - 1, tokens // n, 2 * nstate), bf16),
+            pltpu.VMEM((ext, 2 * nstate), bf16), pltpu.VMEM((ext, wide), bf16),
+            pltpu.VMEM((HALO, 2 * nstate), bf16), pltpu.VMEM((HALO, inner), bf16),
+            dma((4,)), dma((others,)), dma((others,)), dma((n - 1,)), dma((n - 1,)), dma((2,)), dma((2,)),
+            dma((n - 1,)), dma((n - 1,)),
+        ] + line_sems(n),
+        compiler_params=pltpu.CompilerParams(
+            vmem_limit_bytes=60 << 20, collective_id=5, has_side_effects=True
+        ),
+        cost_estimate=cost(50),
+        name="rear",
+    )(*vmem_args, part, value, weights, residual)
+
+
+def weight_kernel(mixed_ref, value_ref, state_ref, dout_ref, gated_ref, mix_ref, gates_ref, notes_ref,
+                  out_ref, stage_ref, *remote, first, last, inner, core):
+    depth, width = stage_ref.shape
+    wide = value_ref.shape[1]
+    block = depth // 2
+    blocks = depth // block
+    me = lax.axis_index("core") if core == 2 else 0
+    count = remote[0].shape[0] if core == 2 else 0
+    owner = depth // (2 * count) if core == 2 else 0
+    copies = []
+    if core == 2:
+        inbox, send, receive = remote
+        other = 1 - me
+        barrier = pltpu.get_barrier_semaphore()
+        pl.semaphore_signal(barrier, inc=1, device_id={"core": other}, device_id_type=MESH)
+        pl.semaphore_wait(barrier, 1)
+
+    def segment(number, lhs_ref, rhs, at, transposed=True):
+        span = rhs.shape[1]
+
+        def rows(m, _):
+            here = pl.ds(pl.multiple_of(m * block, block), block)
+            if transposed:
+                product = dot_rows(lhs_ref[here, :], rhs[...])
+            else:
+                product = dot_inner(lhs_ref[:, here], rhs[...])
+            stage_ref[here, at : at + span] = product.astype(bf16)
+            return 0
+
+        lax.fori_loop(0, blocks, rows, 0)
+        if core == 2:
+            for j in range(count):
+                theirs = pl.ds(pl.multiple_of((2 * j + other) * owner, 64), owner)
+                copy = pltpu.make_async_remote_copy(
+                    src_ref=stage_ref.at[theirs, pl.ds(at, span)],
+                    dst_ref=inbox.at[j, :, pl.ds(at, span)],
+                    send_sem=send.at[number * count + j], recv_sem=receive.at[number * count + j],
+                    device_id={"core": other}, device_id_type=MESH,
+                )
+                copy.start()
+                copies.append(copy)
+
+    gates = gates_ref[...]
+    kinds = notes_ref.shape[0] - 8
+    moved = jnp.concatenate(
+        [notes_ref[:kinds, :], jnp.zeros((LANES - kinds, gates.shape[0]), f32)], axis=0
+    ).T
+    inside = jnp.sum(gates * moved, axis=1, keepdims=True)
+    segment(0, mix_ref, (gates * (moved - inside)).astype(bf16), wide + inner)
+    segment(1, dout_ref, gated_ref, wide, False)
+    segment(2, mixed_ref, value_ref.at[:, pl.ds(0, inner)], 0)
+    segment(3, mixed_ref, value_ref.at[:, pl.ds(inner, inner)], inner)
+    segment(4, mixed_ref, state_ref, first)
+    segment(5, mixed_ref, value_ref.at[:, pl.ds(last, LANES)], last)
+    if core == 2:
+        for copy in copies:
+            copy.wait_recv()
+        for j in range(count):
+            kept = pl.ds(pl.multiple_of((2 * j + me) * owner, 64), owner)
+            out_ref[j * owner : (j + 1) * owner, :] = stage_ref[kept, :] + inbox[j]
+        for copy in copies:
+            copy.wait_send()
+    else:
+        out_ref[...] = stage_ref[...]
+
+
+def weight_grads(mixed_ext, value_grad, state_all, dout, gated_out, mix, gates, notes, inner, nstate):
+    core = lax.axis_size("core")
+    count = lax.axis_size(CHIPS)
+    depth = mix.shape[0]
+    wide = value_grad.shape[1]
+    width = wide + inner + LANES
+    first = 2 * inner
+    remote, params = [], pltpu.CompilerParams(vmem_limit_bytes=60 << 20)
+    if core == 2:
+        owner = depth // (2 * count)
+        remote = [pltpu.VMEM((count, owner, width), bf16), pltpu.SemaphoreType.DMA((6 * count,)),
+                  pltpu.SemaphoreType.DMA((6 * count,))]
+        params = pltpu.CompilerParams(
+            vmem_limit_bytes=60 << 20, collective_id=6, has_side_effects=True
+        )
+    return pl.pallas_call(
+        partial(weight_kernel, first=first, last=first + 2 * nstate, inner=inner, core=core),
+        in_specs=[VMEM] * 8,
+        out_specs=VMEM,
+        out_shape=jax.ShapeDtypeStruct((depth // core, width), bf16),
+        scratch_shapes=[pltpu.VMEM((depth, width), bf16)] + remote,
+        compiler_params=params,
         cost_estimate=cost(12),
-        name="signal_back",
-    )(*args)
+        name="weight_grads",
+    )(mixed_ext, value_grad, state_all, dout, gated_out, mix, gates, notes)
 
 
 def swiglu(first, second):
@@ -875,7 +1348,7 @@
 
 
 def shared_kernel(res_ref, cot_ref, gain_ref, router_ref, chosen_ref, w_ref,
-                  out_ref, dmix_ref, mix_ref, gates_ref, dw_ref, first_ref, down_ref, hidden_ref,
+                  out_ref, dmix_ref, mix_ref, mix_t_ref, gates_ref, dw_ref, first_ref, down_ref, hidden_ref,
                   dval_ref, *, tile):
     rows, depth = res_ref.shape
     wrows = w_ref.shape[1] // 3
@@ -913,9 +1386,10 @@
         return 0
 
     lax.fori_loop(0, rows // tile, part, 0)
+    mix_t_ref[...] = mix_ref[...].T
     for p in range(2):
         dw_ref[:, p * wrows : (p + 1) * wrows, :] = (
-            dot_inner(mix_ref[...], dval_ref[p]).astype(bf16).reshape(-1, wrows, wide)
+            dot_rows(mix_t_ref[...], dval_ref[p]).astype(bf16).reshape(-1, wrows, wide)
         )
     dw_ref[:, 2 * wrows :, :] = (
         dot_inner(cot_ref[...], hidden_ref[...]).astype(bf16).reshape(-1, wrows, wide)
@@ -932,9 +1406,9 @@
     block = pl.BlockSpec((senders, part, wide), lambda i: (0, own // part, 0))
     grads = shape((senders, part, wide), bf16)
     outs = [shape((rows, depth), f32), shape((rows, depth), f32), shape((rows, depth), bf16),
-            shape((rows, LANES), f32)]
+            shape((depth, rows), bf16), shape((rows, LANES), f32)]
     return pl.pallas_call(
-        partial(shared_kernel, tile=min(256, rows)),
+        partial(shared_kernel, tile=min(512, rows)),
         grid=(1,),
         in_specs=[whole(residual), whole(cot), whole(gain), columns(weights, LANES, router_at),
                   whole(chosen), block],
@@ -950,9 +1424,9 @@
     )(residual, cot, gain, weights, chosen, experts_w)
 
 
-def experts_kernel(mix_ref, cot_ref, gates_ref, router_ref, w_ref, out_in, dmix_in, ds_ref,
-                   out_ref, dmix_ref, dgate_ref, dw_ref,
-                   total_ref, grads_ref, down_ref, hidden_ref, dval_ref, grad_ref, load_sem,
+def experts_kernel(mix_ref, mix_t_ref, cot_ref, gates_ref, router_ref, w_ref, out_in, dmix_in, ds_ref,
+                   out_ref, dmix_ref, dgate_t_ref, dw_ref,
+                   dgate_ref, total_ref, grads_ref, down_ref, hidden_ref, dval_ref, grad_ref, load_sem,
                    *remote, tile, senders, core):
     step = pl.program_id(0)
     last = step == pl.num_programs(0) - 1
@@ -1001,7 +1475,7 @@
     @pl.when(step < senders)
     def _():
         pair_grads(
-            step, slot, mix_ref, cot_ref, gates_ref, w_ref, dgate_ref, total_ref, grads_ref, down_ref,
+            step, slot, mix_ref, mix_t_ref, cot_ref, gates_ref, w_ref, dgate_ref, total_ref, grads_ref, down_ref,
             hidden_ref, dval_ref, grad_ref, tile
         )
 
@@ -1037,9 +1511,10 @@
         dlogits = (gates * (dgate - inside)).astype(bf16)
         dmix_ref[...] = (grads_ref[...] + dot_outer(dlogits, router_ref[...])).astype(bf16)
         out_ref[...] = total_ref[...].astype(bf16)
-
-
-def pair_grads(step, slot, mix_ref, cot_ref, gates_ref, w_ref, dgate_ref, total_ref, grads_ref,
+        dgate_t_ref[...] = dgate.T[: dgate_t_ref.shape[0], :]
+
+
+def pair_grads(step, slot, mix_ref, mix_t_ref, cot_ref, gates_ref, w_ref, dgate_ref, total_ref, grads_ref,
                down_ref, hidden_ref, dval_ref, grad_ref, tile):
     rows, depth = mix_ref.shape
     wide = w_ref.shape[2]
@@ -1088,11 +1563,11 @@
             grad_ref[slot, first : first + hid, :] = grad[p * hid : (p + 1) * hid]
     for p in range(2):
         grad_ref[slot, p * deep : p * deep + depth, :] = (
-            dot_inner(mix_ref[...], dval_ref[p]).astype(bf16)
+            dot_rows(mix_t_ref[...], dval_ref[p]).astype(bf16)
         )
 
 
-def experts(mix, cot, gates, weights, router_at, experts_w, out, dmix, ds):
+def experts(mix, mix_t, cot, gates, weights, router_at, experts_w, out, dmix, ds):
     senders, deep, wide = experts_w.shape
     rows, depth = mix.shape
     core = lax.axis_size("core")
@@ -1103,7 +1578,8 @@
     once = lambda a: pl.BlockSpec(
         a.shape, lambda i: (0,) * a.ndim, pipeline_mode=pl.Buffered(1)
     )
-    outs = [shape((rows, depth), bf16), shape((rows, depth), bf16), shape((rows, LANES), f32)]
+    kinds = 2 * senders + -2 * senders % 8
+    outs = [shape((rows, depth), bf16), shape((rows, depth), bf16), shape((kinds, rows), f32)]
     if core == 2:
         steps = senders + 1
         kept_map = lambda i: (jnp.maximum(i - 1, 0) // 2, 0, 0)
@@ -1119,16 +1595,17 @@
         steps, remote, params = senders, [], pltpu.CompilerParams(vmem_limit_bytes=60 << 20)
         kept_map = lambda i: (i, 0, 0)
     return pl.pallas_call(
-        partial(experts_kernel, tile=min(256, rows), senders=senders, core=core),
+        partial(experts_kernel, tile=min(512, rows), senders=senders, core=core),
         grid=(steps,),
-        in_specs=[once(mix), once(cot), once(gates),
+        in_specs=[once(mix), once(mix_t), once(cot), once(gates),
                   pl.BlockSpec((depth, LANES), lambda i: (0, router_at // LANES)),
                   pl.BlockSpec((1, 3 * depth, wide), lambda i: (jnp.minimum(i, senders - 1), 0, 0)),
                   pl.BlockSpec(memory_space=pl.ANY), pl.BlockSpec(memory_space=pl.ANY), once(ds)],
         out_specs=[whole(o) for o in outs] + [pl.BlockSpec((1, deep, wide), kept_map)],
         out_shape=outs + [shape((kept, deep, wide), bf16)],
         scratch_shapes=[
-            pltpu.VMEM((rows, depth), f32), pltpu.VMEM((rows, depth), f32),
+            pltpu.VMEM((rows, LANES), f32), pltpu.VMEM((rows, depth), f32),
+            pltpu.VMEM((rows, depth), f32),
             pltpu.VMEM((wide, depth), bf16), pltpu.VMEM((rows, wide), bf16),
             pltpu.VMEM((2, rows, wide), bf16), pltpu.VMEM((core, 3 * depth, wide), bf16),
             pltpu.SemaphoreType.DMA((2,)),
@@ -1136,7 +1613,7 @@
         compiler_params=params,
         cost_estimate=cost(6 * senders),
         name="experts",
-    )(mix, cot, gates, weights, experts_w, out, dmix, ds)
+    )(mix, mix_t, cot, gates, weights, experts_w, out, dmix, ds)
 
 
 def local(
@@ -1185,28 +1662,12 @@
     experts_w = gather_rows(packed[None])
 
     seg_row = segments[0]
-    last = jnp.concatenate(
-        [block_input[tokens - CONV + 1 :],
-         jnp.pad(seg_row[None, tokens - CONV + 1 :].astype(bf16), ((0, 0), (0, quarter - CONV + 1)))], axis=0
-    )
-    halo = shifted(last, CTX, 1)
-    halo_seg = halo[CONV - 1, : CONV - 1].astype(jnp.int32)
-    extra = jnp.concatenate(
-        [jnp.zeros((HALO - CONV + 1, quarter), bf16), halo[: CONV - 1], gain_input[None],
-         gain_mix[None], jnp.zeros((14, quarter), bf16)], axis=0
-    )
-    wide = lambda got: got.transpose(1, 0, 2).reshape(got.shape[1], depth)
-    got = spread(block_input)
-    cotangent, got = lax.optimization_barrier((cotangent, got))
-    got = wide(got)
-    got_extra = spread_small(extra)
-    cot_raw = spread(cotangent)
-    gain_row = got_extra[HALO].astype(f32)
-    gain_mid = got_extra[HALO + 1].astype(f32)
-    x_ext = jnp.concatenate([got_extra[:HALO], got], axis=0).astype(f32)
-    scale_ext = lax.rsqrt(jnp.mean(x_ext * x_ext, axis=-1, keepdims=True) + epsilon)
-    normed_ext = x_ext * scale_ext
-    mixed_ext = (normed_ext * gain_row).astype(bf16)
+    halo_seg = shifted(seg_row[tokens - CONV + 1 :], CTX, 1)
+    gains = jnp.concatenate(
+        [gain_input[None], gain_mix[None], jnp.zeros((14, quarter), bf16)], axis=0
+    )
+    mixed_ext, mixed_t, got, gain_rows = intake(block_input, gains)
+    gain_row, gain_mid = gain_rows[0:1], gain_rows[1:2]
 
     segments_ext = jnp.concatenate([halo_seg, seg_row], axis=0)
     same = jnp.stack(
@@ -1222,106 +1683,68 @@
     at_end = (seg_row == seg_row[-1]).astype(f32)[:, None]
     seg_col = seg_row[:, None]
     seg_line = seg_row[None]
-    value, act, scaled, step, running, run_exp, state_local = enter(
-        mixed_ext, weights, taps, same, bias, decay, at_end, link, inner, nstate, per
-    )
-    run_t = running[:, :heads].T[:, None, :]
-    far_in = far_states(state_local, False)
-    within = intra(act, scaled, run_t, run_exp, seg_col, seg_line, inner, nstate, per)
     gain_gate_f = gain_gate.astype(f32)[None, :]
-    mixer, part, square, state_in = leave(
-        act, within, value, far_in, run_exp, link, skip, gain_gate_f, weights, inner, nstate, per
-    )
-    part, cot_raw = lax.optimization_barrier((part, cot_raw))
-    cot_full = wide(cot_raw)
-    residual, scale_rows, own_part = residual_step(part, square, got, di_all)
-
-    gain_mid = gain_mid[None]
+    (value, act, scaled, step, running, run_exp, within, mixer, state_in, packed, residual, scale_rows,
+     own_part, cot_full) = front(
+        mixed_ext, taps, same, bias, decay, at_end, link, seg_col, seg_line, skip, gain_gate_f, got,
+        cotangent, weights, inner, nstate, per, heads, di_all
+    )
+
     chosen = jnp.any(
         routes[:, :, None] == jnp.arange(LANES, dtype=jnp.int32)[None, None, :], axis=1
     ).astype(f32)
-    out_part, dmix_part, mixed_two, gates, shared_grad = shared_expert(
+    out_part, dmix_part, mixed_two, mix_t, gates, shared_grad = shared_expert(
         residual, cot_full, gain_mid, weights, router_at, chosen, experts_w
     )
     out_part, dmix_part, dgate, dw = experts(
-        mixed_two, cot_full, gates, weights, router_at, experts_w, out_part, dmix_part, shared_grad
+        mixed_two, mix_t, cot_full, gates, weights, router_at, experts_w, out_part, dmix_part, shared_grad
     )
     expert_rows = scatter_chips(dw.reshape(-1, 2 * hid))
     dmixer, notes, gains_mid = turn_step(
         dmix_part, dgate, residual, cot_full, own_part, gain_mid
     )
 
-    stats = jnp.stack([scale_rows[0], notes[:, LANES - 1]], axis=1)
-    heads_grad, z_grad, gated_out, direct, sums = back(
-        dmixer, weights, mixer, value, act, run_exp, link, gain_gate_f, stats, state_local[inner:],
-        inner, nstate, di_all
-    )
-    out_part, dmixer = lax.optimization_barrier((out_part, dmixer))
-    out_blocks = out_part.reshape(tokens, tensors, quarter).transpose(1, 0, 2)
-    out_raw = exchange(out_blocks)
-    far_out = far_states(direct, True)
-    dscaled, dstate, drun = intra_back(
-        heads_grad, act, scaled, run_t, run_exp, seg_col, seg_line, inner, nstate, per
-    )
-    state_rows, state_taps, leaving, kept = state_back(
-        heads_grad, act, step, running, run_exp, link, at_end, value, taps, same, dstate, state_in,
-        far_out, inner, nstate, per
-    )
-    state_rows, out_raw = lax.optimization_barrier((state_rows, out_raw))
-    state_raw = spread(state_rows)
-    value_grad, dtaps, small_sums = signal_back(
-        heads_grad, act, step, value, taps, same, bias, decay, skip, mixer, within, dscaled, drun,
-        leaving, kept, z_grad, state_rows, inner, nstate, per
+    value_grad, gated_out, dtaps, sums, small_sums, state_all, output = rear(
+        (dmixer, scale_rows, notes, mixer, within, act, scaled, step, running, run_exp, state_in, taps,
+         same, bias, decay, skip, gain_gate_f, at_end, link, seg_col, seg_line, packed[inner:]),
+        out_part, value, weights, residual, inner, nstate, per, heads, di_all
     )
     first = 2 * inner
     last = first + 2 * nstate
-    halo_back = shifted(value_grad[:HALO], CTX, -1)
-    state_taps = jnp.pad(state_taps, ((0, 8 - CONV), (0, 0)))
-    grad_input, gains, state_taps = finish_step(
-        value_grad, halo_back, weights, got, dmixer, gain_row[None], gains_mid, state_taps
-    )
-    block_sum = jnp.sum(out_raw.astype(f32), axis=0)
-    output = (
-        lax.dynamic_slice_in_dim(residual, column, quarter, 1).astype(f32) + block_sum
-    ).astype(bf16)
-
-    grad_main = dot_inner(mixed_ext, value_grad)
-    grad_state = dot_inner(mixed_ext, jnp.sum(state_raw.astype(f32), axis=0).astype(bf16))
-    grad_proj_out = dot_inner(dmixer, gated_out)
-    moved = jnp.where(col_iota(notes.shape) < experts_all, notes, 0.0)
-    dlogits = (gates * (moved - jnp.sum(gates * moved, axis=1, keepdims=True))).astype(bf16)
-    grad_router = dot_inner(mixed_two, dlogits)
-    main_local = jnp.concatenate(
-        [grad_main[:, :first].astype(bf16), grad_state.astype(bf16),
-         grad_main[:, last:].astype(bf16), grad_proj_out.astype(bf16), grad_router.astype(bf16)], axis=1
-    )
-    main_local, expert_rows = lax.optimization_barrier((main_local, expert_rows))
-    main_grad = scatter_rows(main_local).astype(f32)
-    pair_rows = expert_rows[: local_experts * 3 * depth // 2].reshape(local_experts, -1, 2 * hid)
-    down_rows = pair_rows[:, depth:].reshape(local_experts, depth // (2 * hid), hid, 2 * hid)
-    shared_rows = expert_rows[local_experts * 3 * depth // 2 :]
+    main_local = weight_grads(
+        mixed_t, value_grad, state_all, dmixer, gated_out, mix_t, gates, notes, inner, nstate
+    )
+    shared_rows = expert_rows[3 * depth :]
     shared_up = shared_rows[: 2 * wrows].reshape(2, wrows, 2, shared_here // 2)
-    small = lax.psum((dtaps, small_sums[:2], sums[:2], gains[:2], state_taps[:CONV]), ROWS)
+    early = jnp.concatenate(
+        [dtaps[:, :inner], sums[:2], jnp.pad(small_sums[:2], ((0, 0), (0, inner - LANES)))], axis=0
+    )
+    main_local, early, expert_rows = lax.optimization_barrier((main_local, early, expert_rows))
+    main_grad = scatter_chips(main_local).astype(f32)
+    grad_input, early, late, gates_rows, down_rows = finish_step(
+        value_grad, weights, got, dmixer, gain_row, gains_mid,
+        jnp.pad(dtaps[:, inner:], ((0, 8 - CONV), (0, 0))), early, expert_rows[: 3 * depth], hid
+    )
     return (
         output,
         grad_input,
-        small[3][0],
+        late[0, :quarter],
         jnp.stack([main_grad[:, :inner], main_grad[:, inner:first]], axis=1),
         main_grad[:, first:last],
         main_grad[:, last : last + heads],
-        small[0],
-        small[4],
-        small[1][0, :heads],
-        small[1][1, :heads],
-        jnp.sum(small[2][1].reshape(heads, per), axis=1),
-        small[2][0],
+        early[:CONV],
+        late[:CONV, quarter:],
+        early[CONV + 2, :heads],
+        early[CONV + 3, :heads],
+        jnp.sum(early[CONV + 1].reshape(heads, per), axis=1),
+        early[CONV],
         main_grad[:, main_wide:router_at],
-        small[3][1],
+        late[1, :quarter],
         main_grad[:, router_at : router_at + experts_all],
         shared_up.transpose(1, 2, 0, 3).reshape(wrows, 2, shared_here).astype(f32),
         shared_rows[2 * wrows :].astype(f32),
-        pair_rows[:, :depth].reshape(expert_gates.shape).astype(f32),
-        down_rows.transpose(0, 2, 1, 3).reshape(expert_down.shape).astype(f32),
+        gates_rows.reshape(expert_gates.shape),
+        down_rows,
     )
 
 

time: 597 us -> 481 us (0.81)
  starting transfers between devices: 50.2 us -> 2.8 us
  Pallas kernels: 346 us -> 379 us
  blocking collectives: 27.6 us -> 0 us
  waiting for transfers between devices: 45.4 us -> 23.4 us
  local copies, waits for them, and re-layouts: 66.7 us -> 46.6 us
  matrix products: 14.7 us -> 0 us
  other arithmetic: 22.1 us -> 10.2 us
    pallas_call x12 -> x8, Pallas kernels: 346 us -> 379 us  [the longest x1 99 us: front(): pl.pallas_call(partial(front_kernel, inner=inner, nstate=nstate, per=per,...]
    all_to_all x4 -> x0, starting transfers between devices: 30 us -> none  [exchange(): lax.all_to_all(blocks, 'tensor', split_axis=0, concat_axis=0, tiled=True)]
    psum x1 -> x0, blocking collectives: 27.6 us -> none  [local(): lax.psum((dtaps, small_sums[:2], sums[:2], gains[:2], state_taps[:CONV]),...]
    ppermute x3 -> x0, waiting for transfers between devices: 25.6 us -> none  [spread_small(): lax.ppermute(block, 'tensor', [(i, (i + away) % count) for i in range(cou...]
    all_gather x2, waiting for transfers between devices: 0.01 us -> 19 us  [gather_rows(): return lax.all_gather(value, ROWS, axis=0, tiled=True)]
    dot_general x4 -> x0, matrix products: 14.7 us -> none  [dot_inner(): lax.dot_general(left, right, (((0,), (0,)), ((), ())), preferred_element_...]
    all_to_all x4 -> x0, waiting for transfers between devices: 12 us -> none  [exchange(): lax.all_to_all(blocks, 'tensor', split_axis=0, concat_axis=0, tiled=True)]
    ppermute x8 -> x1, starting transfers between devices: 14.1 us -> 2.64 us  [shifted(): lax.ppermute(value, axis, [(source, source + steps) for source in range(l...]
  transfers between devices with their start and end apart: 19 -> 5, of which waited for: 4 -> 2; matrix products, arithmetic and copies ran while one was open for 13% -> 7% of each run, Pallas kernels for 47% -> 66%
where the time goes in v3:
time: 481 us; the launch traced here: 477 us
  Pallas kernels  379 us (79%)
  local copies, waits for them, and re-layouts  46.6 us (10%)
  waiting for transfers between devices  23.4 us (5%)
  between operations  14.5 us (3%)
  other arithmetic  10.2 us (2%)
    pallas_call x1, Pallas kernels, front(): pl.pallas_call(partial(front_kernel, inner=inner, nstate=nstate, per=per,...  99 us
    pallas_call x1, Pallas kernels, turn_step(): pl.pallas_call(partial(turn_kernel, n=n), in_specs=[HBM] + [VMEM] * 5, ou...  65.8 us
    pallas_call x1, Pallas kernels, experts(): pl.pallas_call(partial(experts_kernel, tile=min(512, rows), senders=sende...  54 us
    pallas_call x1, Pallas kernels, rear(): pl.pallas_call(partial(rear_kernel, inner=inner, nstate=nstate, per=per,...  50.9 us
    pallas_call x1, Pallas kernels, finish_step(): pl.pallas_call(partial(finish_kernel, n=n, count=count), in_specs=[VMEM]...  44.4 us
    pallas_call x1, Pallas kernels, intake(): pl.pallas_call(partial(intake_kernel, n=n), in_specs=[VMEM] * 2, out_spec...  39.4 us
    all_gather x2, waiting for transfers between devices, gather_rows(): return lax.all_gather(value, ROWS, axis=0, tiled=True)  19 us
    pallas_call x1, Pallas kernels, weight_grads(): pl.pallas_call(partial(weight_kernel, first=first, last=first + 2 * nstat...  16 us
  transfers between devices with their start and end apart: 5, of which 2 were waited for; matrix products, arithmetic and copies ran while one was open for 7% of the time, Pallas kernels for 66%

profile of v3, /device:TPU:0, one launch (start us, length us, event | category | flops | bytes accessed | tf_op | source)
XLA Modules:
  0.0 476.8 jit_solution(6261552825028689636)
XLA Ops:
  8.9 2.3 fusion.3
  14.2 2.8 reshape.130
  17.9 1.7 pad_maximum_fusion
  20.3 2.6 collective-permute-start
  28.4 39.4 %intake.1 = (bf16[528,1536]{1,0:T(8,128)(2,1)}, bf16[1536,512]{1,0:T(8,128)(2,1)}, bf16[512,1536]{1,0:T(8,128)(2,1)}, f32[16,1536]{1,0:T(8,128)}) custom-call(bf16[512,384]{1,0:T(8,128)(2,1)} %x_ref.1, bf16[16,384]{1,0:T(8,128)(2,1)} %maximum_maximum_fusion.gains_ref), custom_call_target="tpu_custom_call" | custom-call | flops 44999999488 | bytes 1048576 | tf_op jit(solution)/shard_map/intake/pallas_call | solution.py:509
  67.8 1.5 fusion.4
  70.1 2.1 compare_convert_fusion
  73.6 99.0 %front.1 = (f32[528,1920]{1,0:T(8,128)}, bf16[512,1024]{1,0:T(8,128)(2,1)}, bf16[512,768]{1,0:T(8,128)(2,1)}, f32[512,128]{1,0:T(8,128)}, f32[512,128]{1,0:T(8,1...) custom-call(bf16[528,1536]{1,0:T(8,128)(2,1)} %get-tuple-element.65., ...), custom_call_target="tpu_custom_call" | custom-call | flops 89999998976 | bytes 1048576 | tf_op jit(solution)/shard_map/front/pallas_call | solution.py:662
  172.6 19.0 %all-gather.6.cloned.1.call-done = bf16[41472,256]{1,0:T(8,128)(2,1)} async-done(((bf16[5184,256]{1,0:T(8,128)(2,1)}), bf16[41472,256]{1,0:T(8,128)(2,1)}) %all-gather.6.cloned.1.call-update) | async-done | bytes 21233680 | tf_op jit(solution)/shard_map/all_gather | solution.py:65
  191.6 9.8 %shared_expert.1 = (f32[512,1536]{1,0:T(8,128)}, f32[512,1536]{1,0:T(8,128)}, bf16[512,1536]{1,0:T(8,128)(2,1)}, bf16[1536,512]{1,0:T(8,128)(2,1)}, f32[512,128]{1,0:T(8,128)}, /*index=5*/bf16[8,576,256]{2,1,0:T(8,128)(2,1)}) custom-call(bf16[512,1536]{1,0:T(8,128)(2,1)} %get-tuple-element.67.res_ref.res_hbm, bf16[512,1536]{1,0:T(8,128)(2,1)} %get-tuple-element.68.cot_ref, ...), custom_call_target="tpu_custom_call" | custom-call | flops 8999999488 | bytes 1048576 | tf_op jit(solution)/shard_map/shared_expert/pallas_call | solution.py:1410
  201.4 3.2 copy.114
  204.6 54.0 %experts.1 = (bf16[512,1536]{1,0:T(8,128)(2,1)}, bf16[512,1536]{1,0:T(8,128)(2,1)}, f32[16,512]{1,0:T(8,128)}, bf16[4,5184,256]{2,1,0:T(8,128)(2,1)}) custom-call(bf16[512,1536]{1,0:T(8,128)(2,1)} %get-tuple-element.70.mix_ref, bf16[1536,512]{1,0:T(8,128)(2,1)} %get-tuple-element.71.mix_t_ref.mix_ref, bf16[512,1536]{1,0:T(8,128)(2,1)} %get-tuple-element.68.cot_ref, ...), custom_call_target="tpu_custom_call" | custom-call | flops 43200000000 | bytes 1048576 | tf_op jit(solution)/shard_map/experts/pallas_call | solution.py:1597
  260.0 65.8 %turn_step.1 = (bf16[512,1536]{1,0:T(8,128)(2,1)}, f32[24,512]{1,0:T(8,128)}, f32[8,1536]{1,0:T(8,128)}) custom-call(bf16[512,1536]{1,0:T(8,128)(2,1)} %get-tuple-element.76.dmix_hbm, f32[16,512]{1,0:T(8,128)} %get-tuple-element.77.dgate_ref, bf16[512,1536]{1,0:T(8,128)(2,1)} %get-tuple-element.67.res_ref.res_hbm, ...), custom_call_target="tpu_custom_call" | custom-call | flops 54000001024 | bytes 1048576 | tf_op jit(solution)/shard_map/turn_step/pallas_call | solution.py:748
  325.8 50.9 %rear.1 = (bf16[512,1920]{1,0:T(8,128)(2,1)}, bf16[512,768]{1,0:T(8,128)(2,1)}, f32[4,1024]{1,0:T(4,128)}, f32[8,768]{1,0:T(8,128)}, f32[8,128]{1,0:T(8,128)}, /...) custom-call(bf16[512,1536]{1,0:T(8,128)(2,1)} %get-tuple-element.79.dout_ref.dres_ref, ...), custom_call_target="tpu_custom_call" | custom-call | flops 44999999488 | bytes 1048576 | tf_op jit(solution)/shard_map/rear/pallas_call | solution.py:1220
  379.4 16.0 %weight_grads.1 = bf16[768,2816]{1,0:T(8,128)(2,1)} custom-call(bf16[1536,512]{1,0:T(8,128)(2,1)} %get-tuple-element.97.mixed_ref, bf16[512,1920]{1,0:T(8,128)(2,1)} %get-tuple-element.94.value_ref.grad_ref, bf16[512,256]{1,0:T(8,128)(2,1)} %get-tuple-element.98.state_ref, bf16[512,1536]{1,0:T(8,128)(2,1)} %get-tuple-element.79.dout_ref.dres_ref, ...), custom_call_target="tpu_custom_call" | custom-call | flops 10800000000 | bytes 1048576 | tf_op jit(solution)/shard_map/weight_grads/pallas_call | solution.py:1332
  397.4 1.6 slice.119.pair_hbm
  399.0 44.4 %finish_step.1 = (f32[512,384]{1,0:T(8,128)}, f32[8,768]{1,0:T(8,128)}, f32[8,640]{1,0:T(8,128)}, f32[3072,2,128]{2,1,0:T(2,128)}, f32[2,128,1536]{2,1,0:T(8,128)}) custom-call(bf16[512,1920]{1,0:T(8,128)(2,1)} %get-tuple-element.94.value_ref.grad_ref, bf16[512,1536]{1,0:T(8,128)(2,1)} %get-tuple-element.66.x_ref, ...), custom_call_target="tpu_custom_call" | custom-call | flops 40499998720 | bytes 1048576 | tf_op jit(solution)/shard_map/finish_step/pallas_call | solution.py:896
  444.7 1.3 slice.125
  446.0 1.4 slice_reduce_fusion
  448.1 1.4 slice_reduce_fusion.2
  452.4 4.3 reduce-scatter.5.cloned.1.call-done
  459.7 1.4 convert_element_type.68
  461.2 1.9 copy.98
  466.4 1.7 copy.127
  (121 shorter events, 32.9 us)
Async XLA Ops:
  7.2 65.1 %all-gather.4.cloned.1.call-start = ((), (), s32[]{:S(2)}) async-start(), calls=%async_computation.2 | async-start | bytes 9732096 | tf_op jit(solution)/shard_map/all_gather | solution.py:65
  8.9 2.4 copy-start.11
  11.2 2.0 copy-start.10
  11.3 2.2 copy-start.6
  13.2 178.4 %all-gather.6.cloned.1.call-start = ((), (), s32[]{:S(2)}) async-start(), calls=%async_computation.5 | async-start | bytes 23887872 | tf_op jit(solution)/shard_map/all_gather | solution.py:65
  19.6 4.0 copy-start.18
  19.6 4.0 copy-start.19
  19.6 4.0 copy-start.17
  19.6 4.6 copy-start.20
  19.6 5.3 %copy-start.14 = (s32[512,6]{0,1:T(8,128)S(1)}, s32[512,6]{0,1:T(8,128)}, u32[]{:S(2)}) copy-start(s32[512,6]{0,1:T(8,128)} %param.40) | copy-start | bytes 36868
  19.6 7.0 %copy-start.21 = (f32[12]{0:T(128)S(1)}, f32[12]{0:T(128)}, u32[]{:S(2)}) copy-start(f32[12]{0:T(128)} %param.29) | copy-start | bytes 148
  19.6 6.9 %copy-start.22 = (f32[12]{0:T(128)S(1)}, f32[12]{0:T(128)}, u32[]{:S(2)}) copy-start(f32[12]{0:T(128)} %param.28) | copy-start | bytes 148
  19.6 7.5 %copy-start.15 = (bf16[4,768]{1,0:T(4,128)(2,1)S(1)}, bf16[4,768]{1,0:T(4,128)(2,1)}, u32[]{:S(2)}) copy-start(bf16[4,768]{1,0:T(4,128)(2,1)} %param.26) | copy-start | bytes 18436
  19.6 7.4 %copy-start.16 = (bf16[4,256]{1,0:T(4,128)(2,1)S(1)}, bf16[4,256]{1,0:T(4,128)(2,1)}, u32[]{:S(2)}) copy-start(bf16[4,256]{1,0:T(4,128)(2,1)} %param.27) | copy-start | bytes 6148
  19.7 375.7 %reduce-scatter.3.cloned.1.call-start = ((), (), s32[]{:S(2)}) async-start(), calls=%async_computation.3 | async-start | bytes 13271040 | tf_op jit(solution)/shard_map/reduce_scatter | solution.py:74
  20.3 48.9 %collective-permute-start = (s32[3]{0:T(128)S(1)}, s32[3]{0:T(128)S(1)}, u32[]{:S(2)}, u32[]{:S(2)}) collective-permute-start(s32[3]{0:T(128)S(1)} %slice_bitcast_fusion.4), channel_id=1, source_target_pairs={{0,4},{4,8},{8,12},{1,5},{5,9},{9,13},{2,6},{6,10},{10,14},{3,7},{... | collective-permute-start | bytes 44 | tf_op jit(solution)/shard_map/ppermute | solution.py:45
  26.4 43.7 %copy-start.5 = (s32[512,1]{1,0:T(8,128)}, s32[512,1]{1,0:T(8,128)S(1)}, u32[]{:S(2)}) copy-start(s32[512,1]{1,0:T(8,128)S(1)} %copy.83.seg_col_ref) | copy-start | bytes 6148
  258.7 198.0 %reduce-scatter.5.cloned.1.call-start = ((), (), s32[]{:S(2)}) async-start(), calls=%async_computation.4 | async-start | bytes 5406720 | tf_op jit(solution)/shard_map/reduce_scatter | solution.py:74
  395.4 1.8 copy-start.2
  461.2 1.9 copy-start
  461.2 3.5 copy-start.8
  463.2 2.3 copy-start.7
  463.9 2.5 copy-start.1
  466.4 2.5 copy-start.4
  (4 other events, 3.5 us)
Sparse Core Ops, SparseCore 0:
  13.3 58.3 all-gather.3
  74.2 117.3 all-gather.5
  258.8 113.7 reduce-scatter.2
  395.6 61.0 reduce-scatter.4

commit v4 on v3

--- a/solution.py
+++ b/solution.py
@@ -323,6 +323,161 @@
             barrier, inc=1, device_id=ctx_peer(lax.rem(place + d, count)), device_id_type=MESH
         )
     pl.semaphore_wait(barrier, n - 1 + count - 1)
+
+
+def rows_barrier(me, n):
+    barrier = line_barrier(me, n)
+    place, count = row_place(), lax.axis_size(ROWS)
+    for d in range(1, count):
+        pl.semaphore_signal(barrier, inc=1, device_id=row_peer(lax.rem(place + d, count)),
+                            device_id_type=MESH)
+    pl.semaphore_wait(barrier, n - 1 + count - 1)
+
+
+class RowGather:
+    def __init__(self, source, full, sems):
+        self.cy, self.core = lax.axis_size("cy"), lax.axis_size("core")
+        self.chips = lax.axis_size(CHIPS)
+        me = lax.axis_index("core")
+        chip = lax.axis_index("shard") * self.cy + lax.axis_index("cy")
+        slot = lambda c: c * self.core + me
+        self.far, self.near = [], []
+        for d in range(1, self.chips):
+            peer = lax.rem(chip + d, self.chips)
+            self.far.append(push(source, full.at[slot(chip)], sems[0], d - 1,
+                                 {"shard": peer // self.cy, "cy": lax.rem(peer, self.cy)}))
+        if self.core == 2:
+            for d in range(self.chips):
+                origin = lax.rem(chip - d + self.chips, self.chips)
+                self.near.append(push(source if d == 0 else full.at[slot(origin)], full.at[slot(origin)],
+                                      sems[1], d, {"core": 1 - me}))
+
+    def start(self):
+        for copy in self.far + self.near[:1]:
+            copy.start()
+
+    def relay(self):
+        for d, copy in enumerate(self.far):
+            copy.wait_recv()
+            if self.near:
+                self.near[d + 1].start()
+
+    def finish(self):
+        for copy in self.near:
+            copy.wait()
+        for copy in self.far:
+            copy.wait_send()
+
+
+class WeightSum:
+    def __init__(self, stage, boxes):
+        self.stage, self.boxes = stage, boxes
+        self.depth = stage.shape[0]
+        self.core, self.cy = lax.axis_index("core"), lax.axis_size("cy")
+        self.chip = lax.axis_index("shard") * self.cy + lax.axis_index("cy")
+        self.chips = boxes[0].shape[0] if boxes else 0
+        self.paired = boxes[1:3] if len(boxes) == 3 else boxes[3:5]
+        self.owner = boxes[0].shape[1] if boxes else 0
+        self.siblings, self.mains, self.units = [], [], []
+
+    def rows(self, k):
+        return pl.ds(pl.multiple_of(k * self.owner, 16), self.owner)
+
+    def product(self, lhs_ref, rhs, at, transposed=True):
+        span = rhs.shape[1]
+        tall = self.depth // 2
+
+        def part(m, _):
+            here = pl.ds(pl.multiple_of(m * tall, tall), tall)
+            if transposed:
+                value = dot_rows(lhs_ref[here, :], rhs[...])
+            else:
+                value = dot_inner(lhs_ref[:, here], rhs[...])
+            self.stage[here, at : at + span] = value.astype(bf16)
+            return 0
+
+        lax.fori_loop(0, 2, part, 0)
+
+    def to_sibling(self, at, span):
+        unit = len(self.units)
+        self.units.append((at, span))
+        copies = []
+        for j in range(self.chips):
+            copies.append(push(
+                self.stage.at[self.rows(2 * j + 1 - self.core), pl.ds(at, span)],
+                self.boxes[0].at[j, :, pl.ds(at, span)], self.paired, unit * self.chips + j,
+                {"core": 1 - self.core},
+            ))
+            copies[-1].start()
+        self.siblings.append(copies)
+
+    def to_chips(self, unit):
+        if not self.chips:
+            return
+        sib_in, sum_ref, main_in = self.boxes[:3]
+        at, span = self.units[unit]
+        for j, copy in enumerate(self.siblings[unit]):
+            copy.wait_recv()
+            sum_ref[j * self.owner : (j + 1) * self.owner, at : at + span] = (
+                self.stage[self.rows(2 * j + self.core), at : at + span] + sib_in[j, :, at : at + span]
+            )
+        for d in range(1, self.chips):
+            peer = lax.rem(self.chip + d, self.chips)
+            self.mains.append(push(
+                sum_ref.at[self.rows(peer), pl.ds(at, span)], main_in.at[d - 1, :, pl.ds(at, span)],
+                self.boxes[5:7], unit * (self.chips - 1) + d - 1,
+                {"shard": peer // self.cy, "cy": lax.rem(peer, self.cy)},
+            ))
+            self.mains[-1].start()
+
+    def pair(self, unit, out_ref):
+        at, span = self.units[unit]
+        if not self.chips:
+            out_ref[:, at : at + span] = self.stage[:, at : at + span]
+            return
+        for j, copy in enumerate(self.siblings[unit]):
+            copy.wait_recv()
+            out_ref[j * self.owner : (j + 1) * self.owner, at : at + span] = (
+                self.stage[self.rows(2 * j + self.core), at : at + span]
+                + self.boxes[0][j, :, at : at + span]
+            )
+
+    def wait_send(self):
+        for copies in self.siblings:
+            for copy in copies:
+                copy.wait_send()
+
+    def finish(self, out_ref):
+        if not self.chips:
+            out_ref[...] = self.stage[...]
+            return
+        _, sum_ref, main_in = self.boxes[:3]
+        main_in[self.chips - 1] = sum_ref[self.rows(self.chip), :]
+        for copy in self.mains:
+            copy.wait_recv()
+        out_ref[...] = in_order(main_in, self.chip, self.chips)
+        self.wait_send()
+        for copy in self.mains:
+            copy.wait_send()
+
+
+def weight_boxes(depth, width, units, between_chips=True):
+    dma = pltpu.SemaphoreType.DMA
+    if lax.axis_size("core") != 2:
+        return [pltpu.VMEM((depth, width), bf16)], jax.ShapeDtypeStruct((depth, width), bf16)
+    chips = lax.axis_size(CHIPS)
+    owner = depth // (2 * chips)
+    if not between_chips:
+        return [
+            pltpu.VMEM((depth, width), bf16), pltpu.VMEM((chips, owner, width), bf16),
+            dma((units * chips,)), dma((units * chips,)),
+        ], jax.ShapeDtypeStruct((chips * owner, width), bf16)
+    return [
+        pltpu.VMEM((depth, width), bf16), pltpu.VMEM((chips, owner, width), bf16),
+        pltpu.VMEM((chips * owner, width), bf16), pltpu.VMEM((chips, owner, width), bf16),
+        dma((units * chips,)), dma((units * chips,)), dma((units * (chips - 1),)),
+        dma((units * (chips - 1),)),
+    ], jax.ShapeDtypeStruct((owner, width), f32)
 
 
 class StatePush:
@@ -543,6 +698,9 @@
     own = rows // n
     groups = [(sems[2 * i], sems[2 * i + 1]) for i in range(3)]
     block_at = lambda d: pl.ds(pl.multiple_of(d * own, own), own)
+    half = own // 2
+    half_at = lambda d, h: pl.ds(pl.multiple_of(d * own + h * half, half), half)
+    lines_at = lambda k: line_groups(sems[6 + 4 * k : 10 + 4 * k])
     mine = pl.ds(pl.multiple_of(me * own, own), own)
     wide = wm_ref.shape[1]
     loads = [
@@ -558,7 +716,7 @@
     front_barrier(me, n)
     cots = LineGather(
         me, n, lambda d: cot_box.at[:, pl.ds(pl.multiple_of(d * quarter, LANES), quarter)],
-        line_groups(sems[14:18]),
+        lines_at(0),
     )
     cots.step(0)
     loads[0].wait()
@@ -594,37 +752,50 @@
         peer = lax.rem(me + d, n)
         squares.append(push(square_ref.at[:, block_at(peer)], square_box.at[d - 1], groups[1], d - 1, peer))
         squares[-1].start()
-    line = LineReduce(me, n, lambda d: part_ref.at[d], right_box, left_box, line_groups(sems[6:10]))
+    lines = [
+        LineReduce(me, n, lambda d, h=h: part_ref.at[d, pl.ds(h * half, half)], right_box.at[h],
+                   left_box.at[h], lines_at(1 + h)) for h in range(2)
+    ]
+    gathers = [LineGather(me, n, lambda d, h=h: res_box.at[half_at(d, h)], lines_at(3 + h))
+               for h in range(2)]
     for k in range(n):
         d = jnp.where(2 * me < n, n - 1 - k, k)
         part_ref[d] = dot_outer(lifted_ref[block_at(d), :], wo_ref[...]).astype(bf16)
         if k == 0:
-            line.step(0)
-    for t in range(1, n):
-        line.step(t)
-    total = line.total()
+            for line in lines:
+                line.step(0)
     square = square_ref[:, mine]
     for copy in squares:
         copy.wait_recv()
     for d in range(1, n):
         square = square + square_box[d - 1]
-    own_ref[...] = total
     scale = lax.rsqrt(square / di_all + epsilon)
     stat_box[:, mine] = scale
-    res_box[mine, :] = (x_ref[mine, :].astype(f32) + total * as_column(scale[:1])).astype(bf16)
-    gather = LineGather(me, n, lambda d: res_box.at[block_at(d)], line_groups(sems[10:14]))
-    gather.step(0)
     for d in range(1, n):
         stats.append(push(stat_box.at[:, mine], stat_box.at[:, mine], groups[2], d - 1,
                           lax.rem(me + d, n)))
         stats[-1].start()
+    scale = as_column(scale[:1])
+    for t in range(1, n - 1):
+        for line in lines:
+            line.step(t)
+    for h in range(2):
+        lines[h].step(n - 1)
+        total = lines[h].total()
+        own_ref[h * half : (h + 1) * half, :] = total
+        here = half_at(me, h)
+        res_box[here, :] = (
+            x_ref[here, :].astype(f32) + total * scale[h * half : (h + 1) * half]
+        ).astype(bf16)
+        gathers[h].step(0)
     for t in range(1, n):
-        gather.step(t)
+        for gather in gathers:
+            gather.step(t)
     cot_full_ref[...] = cot_box[...]
     states.wait_send()
     cots.wait_send()
-    line.wait_send()
-    gather.wait_send()
+    for line in lines + gathers:
+        line.wait_send()
     for copy in squares:
         copy.wait_send()
     for copy in stats:
@@ -669,11 +840,11 @@
             pltpu.VMEM((heads, 1, tokens), f32), pltpu.VMEM((tokens, tokens), f32),
             pltpu.VMEM((n, own, depth), bf16), pltpu.VMEM((8, tokens), f32),
             pltpu.VMEM((tokens, inner), bf16), pltpu.VMEM((others, inner + 16, nstate), bf16),
-            pltpu.VMEM((n, own, depth), bf16), pltpu.VMEM((n, own, depth), bf16),
+            pltpu.VMEM((2, n, own // 2, depth), bf16), pltpu.VMEM((2, n, own // 2, depth), bf16),
             pltpu.VMEM((n - 1, 8, own), f32),
             pltpu.VMEM((tokens, depth), bf16), pltpu.VMEM((8, tokens), f32),
             pltpu.VMEM((tokens, depth), bf16), dma((2,)), dma((others,)), dma((others,)),
-        ] + pairs(2, n) + line_sems(n) * 3,
+        ] + pairs(2, n) + line_sems(n) * 5,
         compiler_params=pltpu.CompilerParams(
             vmem_limit_bytes=60 << 20, collective_id=1, has_side_effects=True
         ),
@@ -695,10 +866,15 @@
     load.start()
     tensor_barrier(me, n)
     load.wait()
-    line = LineReduce(me, n, lambda d: dmix_ref.at[block_at(d)], right_box, left_box,
-                      line_groups(sems[4:8]))
-    gather = LineGather(me, n, lambda d: dres_box.at[block_at(d)], line_groups(sems[8:12]))
-    line.step(0)
+    half = own // 2
+    half_at = lambda d, h: pl.ds(pl.multiple_of(d * own + h * half, half), half)
+    lines_at = lambda k: line_groups(sems[4 + 4 * k : 8 + 4 * k])
+    lines = [LineReduce(me, n, lambda d, h=h: dmix_ref.at[half_at(d, h)], right_box.at[h],
+                        left_box.at[h], lines_at(h)) for h in range(2)]
+    gathers = [LineGather(me, n, lambda d, h=h: dres_box.at[half_at(d, h)], lines_at(2 + h))
+               for h in range(2)]
+    for line in lines:
+        line.step(0)
     first, second = [], []
     for d in range(1, n):
         peer = lax.rem(me + d, n)
@@ -707,15 +883,24 @@
     res = res_ref[mine, :].astype(f32)
     scale = lax.rsqrt(jnp.mean(res * res, axis=1, keepdims=True) + epsilon)
     normed = res * scale
-    for t in range(1, n):
-        line.step(t)
-    dmix = line.total()
-    lifted = dmix * gain_ref[...]
-    inside = jnp.mean(lifted * normed, axis=1, keepdims=True)
-    dres = (cot_ref[mine, :].astype(f32) + scale * (lifted - normed * inside)).astype(bf16)
-    dres_box[mine, :] = dres
-    gather.step(0)
-    gains_ref[...] = jnp.broadcast_to(jnp.sum(dmix * normed, axis=0, keepdims=True), gains_ref.shape)
+    for t in range(1, n - 1):
+        for line in lines:
+            line.step(t)
+    gain_sum = None
+    for h in range(2):
+        lines[h].step(n - 1)
+        dmix = lines[h].total()
+        part = slice(h * half, (h + 1) * half)
+        here = half_at(me, h)
+        lifted = dmix * gain_ref[...]
+        inside = jnp.mean(lifted * normed[part], axis=1, keepdims=True)
+        dres_box[here, :] = (
+            cot_ref[here, :].astype(f32) + scale[part] * (lifted - normed[part] * inside)
+        ).astype(bf16)
+        gathers[h].step(0)
+        term = jnp.sum(dmix * normed[part], axis=0, keepdims=True)
+        gain_sum = term if gain_sum is None else gain_sum + term
+    gains_ref[...] = jnp.broadcast_to(gain_sum, gains_ref.shape)
     dgate = dgate_ref[:, mine]
     for copy in first:
         copy.wait_recv()
@@ -723,15 +908,16 @@
         dgate = dgate + gate_box[d - 1]
     gates = dgate.shape[0]
     notes_box[:gates, mine] = dgate
-    notes_box[gates:, mine] = row_sums(dres.astype(f32) * own_ref[...])
+    notes_box[gates:, mine] = row_sums(dres_box[mine, :].astype(f32) * own_ref[...])
     for d in range(1, n):
         peer = lax.rem(me + d, n)
         second.append(push(notes_box.at[:, mine], notes_box.at[:, mine], groups[1], d - 1, peer))
         second[-1].start()
     for t in range(1, n):
-        gather.step(t)
-    line.wait_send()
-    gather.wait_send()
+        for gather in gathers:
+            gather.step(t)
+    for line in lines + gathers:
+        line.wait_send()
     for copy in first:
         copy.wait_send()
     for copy in second:
@@ -753,11 +939,11 @@
                    shape((8, depth), f32)],
         scratch_shapes=[
             pltpu.VMEM((tokens, depth), bf16),
-            pltpu.VMEM((n, own, depth), bf16), pltpu.VMEM((n, own, depth), bf16),
+            pltpu.VMEM((2, n, own // 2, depth), bf16), pltpu.VMEM((2, n, own // 2, depth), bf16),
             pltpu.VMEM((n - 1, dgate.shape[0], own), f32),
             pltpu.VMEM((tokens, depth), bf16), pltpu.VMEM((dgate.shape[0] + 8, tokens), f32),
             pltpu.SemaphoreType.DMA,
-        ] + pairs(2, n) + line_sems(n) * 2,
+        ] + pairs(2, n) + line_sems(n) * 4,
         compiler_params=pltpu.CompilerParams(
             vmem_limit_bytes=60 << 20, collective_id=2, has_side_effects=True
         ),
@@ -784,11 +970,13 @@
     return {"shard": place // (cy * core), "cy": lax.rem(place // core, cy), "core": lax.rem(place, core)}
 
 
-def finish_kernel(grad_ref, x_ref, dres_ref, gain_ref, mid_ref, state_ref, early_ref,
-                  w_hbm, pair_hbm,
-                  out_ref, early_out, late_out, gates_out, down_out,
-                  w_ref, pair_ref, blocks_ref, right_box, left_box, cross_box, cross_in, gains_box, gains_in,
-                  state_in, early_in, late_ref, late_in, load_sem, *sems, n, count):
+def last_kernel(grad_ref, x_ref, dres_ref, gain_ref, mid_ref, state_ref, early_ref, mixed_t_ref, mix_t_ref,
+                state_all_ref, gates_ref, notes_ref, w_hbm,
+                out_ref, early_out, late_out, main_out,
+                w_ref, blocks_ref, right_box, left_box, cross_box, cross_in, gains_box, gains_in, state_in,
+                early_in, late_ref, late_in, load_sem, stage_ref, *sems, n, count, boxes, inner, last):
+    weights = WeightSum(stage_ref, sems[:boxes])
+    sems = sems[boxes:]
     me = lax.axis_index("tensor")
     place = row_place()
     rows, depth = x_ref.shape
@@ -796,23 +984,18 @@
     wide = w_ref.shape[1]
     groups = [(sems[2 * i], sems[2 * i + 1]) for i in range(3)]
     row_groups = [(sems[6 + 2 * i], sems[7 + 2 * i]) for i in range(2)]
-    loads = [pltpu.make_async_copy(w_hbm.at[:, pl.ds(0, wide)], w_ref, load_sem.at[0]),
-             pltpu.make_async_copy(pair_hbm, pair_ref, load_sem.at[1])]
-    for copy in loads:
-        copy.start()
-    barrier = line_barrier(me, n)
-    for d in range(1, count):
-        pl.semaphore_signal(barrier, inc=1, device_id=row_peer(lax.rem(place + d, count)),
-                            device_id_type=MESH)
-    pl.semaphore_wait(barrier, n - 1 + count - 1)
+    load = pltpu.make_async_copy(w_hbm.at[:, pl.ds(0, wide)], w_ref, load_sem)
+    load.start()
+    rows_barrier(me, n)
     copies, states, lates = [], [], []
-    for d in range(1, n):
-        states.append(push(state_ref, state_in.at[d - 1], groups[2], d - 1, lax.rem(me + d, n)))
-        states[-1].start()
     x = x_ref[...].astype(f32)
     scale = lax.rsqrt(jnp.mean(x * x, axis=1, keepdims=True) + epsilon)
-    loads[0].wait()
-    line = LineReduce(me, n, lambda d: blocks_ref.at[d], right_box, left_box, line_groups(sems[10:14]))
+    load.wait()
+    half = rows // 2
+    lines = [
+        LineReduce(me, n, lambda d, h=h: blocks_ref.at[d, pl.ds(h * half, half)], right_box.at[h],
+                   left_box.at[h], line_groups(sems[10 + 4 * h : 14 + 4 * h])) for h in range(2)
+    ]
     cross = jnp.zeros((8, rows), f32)
     for k in range(n):
         d = jnp.where(2 * me < n, n - 1 - k, k)
@@ -821,7 +1004,8 @@
         block = dot_outer(grad_ref[...], w)
         blocks_ref[d] = block.astype(bf16)
         if k == 0:
-            line.step(0)
+            for line in lines:
+                line.step(0)
         normed = x_ref[:, theirs].astype(f32) * scale
         cross = cross + row_sums(block * normed * gain_ref[:, theirs])
         gains_box[d] = jnp.where(
@@ -829,63 +1013,75 @@
             mid_ref[:, theirs],
         )
     cross_box[...] = cross
+    sums = []
     for d in range(1, n):
         peer = lax.rem(me + d, n)
-        copies.append(push(gains_box.at[peer], gains_in.at[d - 1], groups[0], d - 1, peer))
-        copies.append(push(cross_box, cross_in.at[d - 1], groups[1], d - 1, peer))
+        sums.append(push(gains_box.at[peer], gains_in.at[d - 1], groups[0], d - 1, peer))
+        sums.append(push(cross_box, cross_in.at[d - 1], groups[1], d - 1, peer))
+        states.append(push(state_ref, state_in.at[d - 1], groups[2], d - 1, peer))
     for d in range(1, count):
         copies.append(push(early_ref, early_in.at[d - 1], row_groups[0], d - 1,
                            row_peer(lax.rem(place + d, count))))
-    for copy in copies:
+    for copy in sums + states + copies:
         copy.start()
-    if n > 1:
+
+    gates = gates_ref[...]
+    kinds = notes_ref.shape[0] - 8
+    moved = jnp.concatenate(
+        [notes_ref[:kinds, :], jnp.zeros((LANES - kinds, gates.shape[0]), f32)], axis=0
+    ).T
+    inside = jnp.sum(gates * moved, axis=1, keepdims=True)
+    first = 2 * inner
+    weights.product(mixed_t_ref, grad_ref.at[:, pl.ds(inner, inner)], 0)
+    weights.to_sibling(0, inner)
+    for line in lines:
         line.step(1)
-    loads[1].wait()
-    hid = down_out.shape[1]
-    wides = 2 * hid
-    deep = pair_ref.shape[0] // 2
-    for p in range(2):
-        top = pair_ref[p * deep : p * deep + depth, :].astype(f32)
-        gates_out[p * depth : (p + 1) * depth, 0, :] = top[:, :hid]
-        gates_out[p * depth : (p + 1) * depth, 1, :] = top[:, hid:]
-        for c in range(depth // wides):
-            at = p * deep + depth + c * hid
-            down_out[p, :, c * wides : (c + 1) * wides] = pair_ref[at : at + hid, :].astype(f32)
-    for copy in copies[: 2 * (n - 1)] + states:
+    weights.product(mixed_t_ref, state_all_ref, inner)
+    weights.product(mixed_t_ref, grad_ref.at[:, pl.ds(last, LANES)], inner + last - first)
+    weights.product(mix_t_ref, (gates * (moved - inside)).astype(bf16), inner + wide - first)
+    weights.to_sibling(inner, wide - first + LANES)
+    weights.to_chips(0)
+    for copy in sums + states:
         copy.wait_recv()
     gains = gains_box[me]
-    state = state_ref[...]
     for d in range(1, n):
         gains = gains + gains_in[d - 1]
         cross = cross + cross_in[d - 1]
-    state_in[n - 1] = state
-    state = in_order(state_in, me, n)
+    state_in[n - 1] = state_ref[...]
     late_ref[:, :quarter] = gains
-    late_ref[:, quarter:] = state
+    late_ref[:, quarter:] = in_order(state_in, me, n)
     for d in range(1, count):
         lates.append(push(late_ref, late_in.at[d - 1], row_groups[1], d - 1,
                           row_peer(lax.rem(place + d, count))))
         lates[-1].start()
-    for t in range(2, n):
-        line.step(t)
-    total = line.total()
+    for t in range(2, n - 1):
+        for line in lines:
+            line.step(t)
+    weights.to_chips(1)
     here = pl.ds(pl.multiple_of(me * quarter, LANES), quarter)
     inside = row_columns(cross[:1]) / depth
-    out_ref[...] = dres_ref[:, here].astype(f32) + scale * (
-        total * gain_ref[:, here] - x_ref[:, here].astype(f32) * scale * inside
-    )
-    for copy in copies[2 * (n - 1) :] + lates:
+    for h in range(2):
+        lines[h].step(n - 1)
+        part = slice(h * half, (h + 1) * half)
+        out_ref[part, :] = dres_ref[part, here].astype(f32) + scale[part] * (
+            lines[h].total() * gain_ref[:, here]
+            - x_ref[part, here].astype(f32) * scale[part] * inside[part]
+        )
+    for copy in copies + lates:
         copy.wait_recv()
     early_in[count - 1] = early_ref[...]
     late_in[count - 1] = late_ref[...]
     early_out[...] = in_order(early_in, place, count)
     late_out[...] = in_order(late_in, place, count)
-    for copy in copies + states + lates:
+    weights.finish(main_out)
+    for copy in copies + states + lates + sums:
         copy.wait_send()
-    line.wait_send()
-
-
-def finish_step(value_grad, weights, x, dres, gain, gains_mid, state, early, pair_rows, hid):
+    for line in lines:
+        line.wait_send()
+
+
+def last_step(vmem_args, weights, inner, last):
+    value_grad, x, early, state = (vmem_args[i] for i in (0, 1, 6, 5))
     n, count = lax.axis_size("tensor"), lax.axis_size(ROWS)
     tokens, depth = x.shape
     quarter = depth // n
@@ -893,27 +1089,98 @@
     late = quarter + state.shape[1]
     shape = jax.ShapeDtypeStruct
     dma = pltpu.SemaphoreType.DMA
+    boxes, main = weight_boxes(depth, wide - inner + LANES, 2)
     return pl.pallas_call(
-        partial(finish_kernel, n=n, count=count),
-        in_specs=[VMEM] * 7 + [HBM] * 2,
-        out_specs=[VMEM] * 5,
-        out_shape=[shape((tokens, quarter), f32), shape(early.shape, f32), shape((8, late), f32),
-                   shape((2 * depth, 2, hid), f32), shape((2, hid, depth), f32)],
+        partial(last_kernel, n=n, count=count, boxes=len(boxes) - 1, inner=inner, last=last),
+        in_specs=[VMEM] * len(vmem_args) + [HBM],
+        out_specs=[VMEM] * 4,
+        out_shape=[shape((tokens, quarter), f32), shape(early.shape, f32), shape((8, late), f32), main],
         scratch_shapes=[
-            pltpu.VMEM((depth, wide), bf16), pltpu.VMEM((3 * depth, 2 * hid), bf16),
-            pltpu.VMEM((n, tokens, quarter), bf16),
-            pltpu.VMEM((n, tokens, quarter), bf16), pltpu.VMEM((n, tokens, quarter), bf16),
+            pltpu.VMEM((depth, wide), bf16), pltpu.VMEM((n, tokens, quarter), bf16),
+            pltpu.VMEM((2, n, tokens // 2, quarter), bf16), pltpu.VMEM((2, n, tokens // 2, quarter), bf16),
             pltpu.VMEM((8, tokens), f32), pltpu.VMEM((n - 1, 8, tokens), f32),
             pltpu.VMEM((n, 8, quarter), f32), pltpu.VMEM((n - 1, 8, quarter), f32),
             pltpu.VMEM((n,) + state.shape, f32), pltpu.VMEM((count,) + early.shape, f32),
-            pltpu.VMEM((8, late), f32), pltpu.VMEM((count, 8, late), f32), dma((2,)),
-        ] + pairs(3, n) + [dma((count - 1,))] * 4 + line_sems(n),
+            pltpu.VMEM((8, late), f32), pltpu.VMEM((count, 8, late), f32), dma,
+        ] + boxes + pairs(3, n) + [dma((count - 1,))] * 4 + line_sems(n) * 2,
         compiler_params=pltpu.CompilerParams(
-            vmem_limit_bytes=60 << 20, collective_id=3, has_side_effects=True
+            vmem_limit_bytes=62 << 20, collective_id=3, has_side_effects=True
         ),
-        cost_estimate=cost(45),
-        name="finish_step",
-    )(value_grad, x, dres, gain, gains_mid, state, early, weights, pair_rows)
+        cost_estimate=cost(60),
+        name="last_step",
+    )(*vmem_args, weights)
+
+
+def emit_kernel(out_ref, grad_ref, early_ref, late_ref, rear_ref, main_ref, pair_ref, *outs, per):
+    (out, grad, gain_in, pair_out, state_out, step_out, conv, conv_state, bias, decay, skip, gate, proj,
+     gain_mid, router, shared_up, shared_down, gates, down) = outs
+    out[...] = out_ref[...]
+    grad[...] = grad_ref[...]
+    taps, inner = conv.shape
+    heads = bias.shape[1]
+    quarter = grad.shape[1]
+    conv[...] = early_ref[:taps]
+    conv_state[...] = late_ref[:taps, quarter:]
+    for i in range(inner // LANES):
+        gate[i : i + 1, :] = early_ref[taps : taps + 1, i * LANES : (i + 1) * LANES]
+    for i in range(quarter // LANES):
+        columns = slice(i * LANES, (i + 1) * LANES)
+        gain_in[i : i + 1, :] = late_ref[0:1, columns]
+        gain_mid[i : i + 1, :] = late_ref[1:2, columns]
+    skips = jnp.broadcast_to(early_ref[taps + 1 : taps + 2], (8, inner))
+    skip[...] = fold_heads(skips, head_fold(inner, LANES, per).astype(bf16))[:1, :heads]
+    bias[...] = early_ref[taps + 2 : taps + 3, :heads]
+    decay[...] = early_ref[taps + 3 : taps + 4, :heads]
+    last = inner + state_out.shape[1]
+    wide = last + LANES
+    proj[...] = rear_ref[:, :inner].astype(f32)
+    pair_out[:, 0, :] = rear_ref[:, inner:].astype(f32)
+    pair_out[:, 1, :] = main_ref[:, :inner].astype(f32)
+    state_out[...] = main_ref[:, inner:last].astype(f32)
+    step_out[...] = main_ref[:, last:wide].astype(f32).T[:heads, :]
+    router[...] = main_ref[:, wide:].astype(f32).T[: router.shape[0], :]
+    hid, depth = down.shape[1:]
+    wides = 2 * hid
+    deep = depth + depth // 2
+    for p in range(2):
+        top = pair_ref[p * deep : p * deep + depth, :].astype(f32)
+        gates[p * depth : (p + 1) * depth, 0, :] = top[:, :hid]
+        gates[p * depth : (p + 1) * depth, 1, :] = top[:, hid:]
+        for c in range(depth // wides):
+            at = p * deep + depth + c * hid
+            down[p, :, c * wides : (c + 1) * wides] = pair_ref[at : at + hid, :].astype(f32)
+    wrows = shared_down.shape[0]
+    part = shared_down.shape[1] // 2
+    for p in range(2):
+        top = pair_ref[2 * deep + p * wrows : 2 * deep + (p + 1) * wrows, :].astype(f32)
+        shared_up[:, 0, p * part : (p + 1) * part] = top[:, :part]
+        shared_up[:, 1, p * part : (p + 1) * part] = top[:, part:]
+    shared_down[...] = pair_ref[2 * deep + 2 * wrows :, :].astype(f32)
+
+
+def emit(args, inner, nstate, per, heads, kinds, hid):
+    out, grad, _, _, _, main, pair = args
+    tokens, quarter = grad.shape
+    wrows = main.shape[0]
+    depth = pair.shape[0] // 3 - wrows
+    wide = pair.shape[1]
+    flat = lambda *size: jax.ShapeDtypeStruct(size, f32)
+    outs = [
+        jax.ShapeDtypeStruct(out.shape, bf16), flat(tokens, quarter), flat(quarter // LANES, LANES),
+        flat(wrows, 2, inner), flat(wrows, 2 * nstate), flat(heads, wrows), flat(CONV, inner),
+        flat(CONV, 2 * nstate), flat(1, heads), flat(1, heads), flat(1, heads),
+        flat(inner // LANES, LANES), flat(wrows, inner), flat(quarter // LANES, LANES), flat(kinds, wrows),
+        flat(wrows, 2, wide), flat(wrows, wide), flat(2 * depth, 2, hid), flat(2, hid, depth),
+    ]
+    return pl.pallas_call(
+        partial(emit_kernel, per=per),
+        in_specs=[VMEM] * 7,
+        out_specs=[VMEM] * len(outs),
+        out_shape=outs,
+        compiler_params=BIG,
+        cost_estimate=cost(8),
+        name="emit",
+    )(*args)
 
 
 def back_part(dout_ref, w_ref, mixer_ref, value_ref, act_ref, run_exp_ref, link_ref, gain_ref,
@@ -1096,15 +1363,17 @@
 
 def rear_kernel(dout_ref, stat_ref, notes_ref, mixer_ref, inner_ref, act_ref, scaled_ref, step_ref,
                 run_ref, run_exp_ref, state_ref, taps_ref, same_ref, bias_ref, decay_ref, skip_ref,
-                gain_ref, end_ref, link_ref, seg_col_ref, seg_row_ref, packed_ref,
+                gain_ref, end_ref, link_ref, seg_col_ref, seg_row_ref, packed_ref, mixed_t_ref,
                 part_hbm, value_hbm, w_hbm, res_hbm,
-                grad_ref, gated_ref, dtaps_ref, sums_ref, small_ref, state_all_ref, out_ref,
-                value_ref, w_ref, res_ref, run_t_ref, heads_ref, zgrad_ref, direct_ref, dscaled_ref,
+                grad_ref, main_ref, dtaps_ref, sums_ref, small_ref, state_all_ref, out_ref,
+                gated_ref, value_ref, w_ref, res_ref, run_t_ref, heads_ref, zgrad_ref, direct_ref, dscaled_ref,
                 dstate_ref, drun_ref, scores_ref, dscores_ref, leaving_ref, kept_ref, rows_ref, dact_ref,
                 far_ref, part_ref, right_box, left_box, rows_box, sum_box, ext_ref, state_halo, signal_halo,
-                local_sem, *sems,
-                inner, nstate, per, heads, di_all, n):
+                local_sem, stage_ref, *sems,
+                inner, nstate, per, heads, di_all, n, boxes):
     me = lax.axis_index("tensor")
+    weights = WeightSum(stage_ref, sems[:boxes])
+    sems = sems[boxes:]
     tokens = act_ref.shape[0]
     quarter = part_ref.shape[1] // n
     own = tokens // n
@@ -1122,7 +1391,7 @@
     far_ref[...] = jnp.zeros_like(far_ref)
     state_halo[...] = jnp.zeros_like(state_halo)
     signal_halo[...] = jnp.zeros_like(signal_halo)
-    front_barrier(me, n)
+    rows_barrier(me, n)
     line = LineReduce(me, n, lambda d: part_ref.at[:, column(d)], right_box, left_box,
                       line_groups(sems[8:12]))
     loads[0].wait()
@@ -1138,6 +1407,10 @@
     states = StatePush(direct_ref, far_ref, groups[0], True)
     states.start()
     line.step(1)
+    weights.product(dout_ref, gated_ref, 0, False)
+    weights.to_sibling(0, inner)
+    weights.product(mixed_t_ref, zgrad_ref, inner)
+    weights.to_sibling(inner, inner)
     run_t = run_ref[...].T
     for h in range(heads):
         run_t_ref[h] = run_t[h : h + 1, :]
@@ -1145,6 +1418,7 @@
                     dscaled_ref, dstate_ref, drun_ref, scores_ref, dscores_ref,
                     inner=inner, nstate=nstate, per=per, block=128)
     line.step(2)
+    weights.pair(0, main_ref)
     states.wait_recv()
     state_back_part(heads_ref, act_ref, step_ref, run_ref, run_exp_ref, link_ref, end_ref, value_ref,
                     taps_ref, same_ref, dstate_ref, state_ref, far_ref, rows_ref, dtaps_ref,
@@ -1158,6 +1432,8 @@
     state_copy = push(rows_ref.at[pl.ds(0, HALO)], state_halo, groups[2], 0, before)
     signal_copy = push(ext_ref.at[pl.ds(0, HALO), pl.ds(inner, inner)], signal_halo, groups[2], 1, before)
     pl.when(sends)(state_copy.start)
+
+    weights.pair(1, main_ref)
 
     def middle():
         pl.when(gets)(state_copy.wait_recv)
@@ -1195,6 +1471,7 @@
     for copy in gathers:
         copy.wait_recv()
     state_all_ref[...] = sum_box[HALO:, :]
+    weights.wait_send()
     states.wait_send()
     line.wait_send()
     pl.when(sends)(state_copy.wait_send)
@@ -1210,19 +1487,22 @@
     tokens = ext - HALO
     depth = residual.shape[1]
     quarter = depth // n
+    boxes, main = weight_boxes(depth, 2 * inner, 2, False)
     shape = jax.ShapeDtypeStruct
     outs = [
-        shape((tokens, wide), bf16), shape((tokens, inner), bf16), shape((CONV, inner + 2 * nstate), f32),
+        shape((tokens, wide), bf16), main, shape((CONV, inner + 2 * nstate), f32),
         shape((8, inner), f32), shape((8, LANES), f32), shape((tokens, 2 * nstate), bf16),
         shape((tokens, quarter), bf16),
     ]
     dma = pltpu.SemaphoreType.DMA
     return pl.pallas_call(
-        partial(rear_kernel, inner=inner, nstate=nstate, per=per, heads=heads, di_all=di_all, n=n),
+        partial(rear_kernel, inner=inner, nstate=nstate, per=per, heads=heads, di_all=di_all, n=n,
+                boxes=len(boxes) - 1),
         in_specs=[VMEM] * len(vmem_args) + [HBM] * 4,
         out_specs=[VMEM] * len(outs),
         out_shape=outs,
         scratch_shapes=[
+            pltpu.VMEM((tokens, inner), bf16),
             pltpu.VMEM((ext, wide), f32), pltpu.VMEM((depth, inner), bf16),
             pltpu.VMEM((tokens, quarter), bf16), pltpu.VMEM((heads, 1, tokens), f32),
             pltpu.VMEM((tokens, inner), f32), pltpu.VMEM((tokens, inner), bf16),
@@ -1237,235 +1517,78 @@
             pltpu.VMEM((n - 1, tokens // n, 2 * nstate), bf16),
             pltpu.VMEM((ext, 2 * nstate), bf16), pltpu.VMEM((ext, wide), bf16),
             pltpu.VMEM((HALO, 2 * nstate), bf16), pltpu.VMEM((HALO, inner), bf16),
-            dma((4,)), dma((others,)), dma((others,)), dma((n - 1,)), dma((n - 1,)), dma((2,)), dma((2,)),
+            dma((4,)),
+        ] + boxes + [
+            dma((others,)), dma((others,)), dma((n - 1,)), dma((n - 1,)), dma((2,)), dma((2,)),
             dma((n - 1,)), dma((n - 1,)),
         ] + line_sems(n),
         compiler_params=pltpu.CompilerParams(
-            vmem_limit_bytes=60 << 20, collective_id=5, has_side_effects=True
+            vmem_limit_bytes=63 << 20, collective_id=5, has_side_effects=True
         ),
         cost_estimate=cost(50),
         name="rear",
     )(*vmem_args, part, value, weights, residual)
 
 
-def weight_kernel(mixed_ref, value_ref, state_ref, dout_ref, gated_ref, mix_ref, gates_ref, notes_ref,
-                  out_ref, stage_ref, *remote, first, last, inner, core):
-    depth, width = stage_ref.shape
-    wide = value_ref.shape[1]
-    block = depth // 2
-    blocks = depth // block
-    me = lax.axis_index("core") if core == 2 else 0
-    count = remote[0].shape[0] if core == 2 else 0
-    owner = depth // (2 * count) if core == 2 else 0
-    copies = []
-    if core == 2:
-        inbox, send, receive = remote
-        other = 1 - me
-        barrier = pltpu.get_barrier_semaphore()
-        pl.semaphore_signal(barrier, inc=1, device_id={"core": other}, device_id_type=MESH)
-        pl.semaphore_wait(barrier, 1)
-
-    def segment(number, lhs_ref, rhs, at, transposed=True):
-        span = rhs.shape[1]
-
-        def rows(m, _):
-            here = pl.ds(pl.multiple_of(m * block, block), block)
-            if transposed:
-                product = dot_rows(lhs_ref[here, :], rhs[...])
-            else:
-                product = dot_inner(lhs_ref[:, here], rhs[...])
-            stage_ref[here, at : at + span] = product.astype(bf16)
-            return 0
-
-        lax.fori_loop(0, blocks, rows, 0)
-        if core == 2:
-            for j in range(count):
-                theirs = pl.ds(pl.multiple_of((2 * j + other) * owner, 64), owner)
-                copy = pltpu.make_async_remote_copy(
-                    src_ref=stage_ref.at[theirs, pl.ds(at, span)],
-                    dst_ref=inbox.at[j, :, pl.ds(at, span)],
-                    send_sem=send.at[number * count + j], recv_sem=receive.at[number * count + j],
-                    device_id={"core": other}, device_id_type=MESH,
-                )
-                copy.start()
-                copies.append(copy)
-
-    gates = gates_ref[...]
-    kinds = notes_ref.shape[0] - 8
-    moved = jnp.concatenate(
-        [notes_ref[:kinds, :], jnp.zeros((LANES - kinds, gates.shape[0]), f32)], axis=0
-    ).T
-    inside = jnp.sum(gates * moved, axis=1, keepdims=True)
-    segment(0, mix_ref, (gates * (moved - inside)).astype(bf16), wide + inner)
-    segment(1, dout_ref, gated_ref, wide, False)
-    segment(2, mixed_ref, value_ref.at[:, pl.ds(0, inner)], 0)
-    segment(3, mixed_ref, value_ref.at[:, pl.ds(inner, inner)], inner)
-    segment(4, mixed_ref, state_ref, first)
-    segment(5, mixed_ref, value_ref.at[:, pl.ds(last, LANES)], last)
-    if core == 2:
-        for copy in copies:
-            copy.wait_recv()
-        for j in range(count):
-            kept = pl.ds(pl.multiple_of((2 * j + me) * owner, 64), owner)
-            out_ref[j * owner : (j + 1) * owner, :] = stage_ref[kept, :] + inbox[j]
-        for copy in copies:
-            copy.wait_send()
-    else:
-        out_ref[...] = stage_ref[...]
-
-
-def weight_grads(mixed_ext, value_grad, state_all, dout, gated_out, mix, gates, notes, inner, nstate):
-    core = lax.axis_size("core")
-    count = lax.axis_size(CHIPS)
-    depth = mix.shape[0]
-    wide = value_grad.shape[1]
-    width = wide + inner + LANES
-    first = 2 * inner
-    remote, params = [], pltpu.CompilerParams(vmem_limit_bytes=60 << 20)
-    if core == 2:
-        owner = depth // (2 * count)
-        remote = [pltpu.VMEM((count, owner, width), bf16), pltpu.SemaphoreType.DMA((6 * count,)),
-                  pltpu.SemaphoreType.DMA((6 * count,))]
-        params = pltpu.CompilerParams(
-            vmem_limit_bytes=60 << 20, collective_id=6, has_side_effects=True
-        )
-    return pl.pallas_call(
-        partial(weight_kernel, first=first, last=first + 2 * nstate, inner=inner, core=core),
-        in_specs=[VMEM] * 8,
-        out_specs=VMEM,
-        out_shape=jax.ShapeDtypeStruct((depth // core, width), bf16),
-        scratch_shapes=[pltpu.VMEM((depth, width), bf16)] + remote,
-        compiler_params=params,
-        cost_estimate=cost(12),
-        name="weight_grads",
-    )(mixed_ext, value_grad, state_all, dout, gated_out, mix, gates, notes)
-
-
 def swiglu(first, second):
     sig = sigmoid(first)
     act = first * sig
     return act, sig * (1.0 + first * (1.0 - sig)), (act * second).astype(bf16)
 
 
-def shared_kernel(res_ref, cot_ref, gain_ref, router_ref, chosen_ref, w_ref,
-                  out_ref, dmix_ref, mix_ref, mix_t_ref, gates_ref, dw_ref, first_ref, down_ref, hidden_ref,
-                  dval_ref, *, tile):
-    rows, depth = res_ref.shape
-    wrows = w_ref.shape[1] // 3
-    wide = w_ref.shape[2]
-    hid = wide // 2
-    for p in range(2):
-        first_ref[p] = w_ref[:, p * wrows : (p + 1) * wrows, :].reshape(depth, wide)
-    down_ref[...] = w_ref[:, 2 * wrows :, :].reshape(depth, wide)
-
-    def part(i, _):
-        at = pl.ds(pl.multiple_of(i * tile, tile), tile)
-        res = res_ref[at, :].astype(f32)
+def experts_kernel(res_ref, cot_ref, gain_ref, chosen_ref, router_ref, w_ref, shared_hbm,
+                   gates_ref, dgate_t_ref, out_hbm, dmix_hbm, mix_t_hbm, dw_hbm,
+                   mix_ref, mix_t_ref, dgate_ref, total_ref, grads_ref, down_ref, hidden_ref, dval_ref,
+                   grad_ref, shared_ref, first_ref, second_ref, result_ref, local_sem, *remote,
+                   tile, senders, core):
+    step = pl.program_id(0)
+    last = step == pl.num_programs(0) - 1
+    rows, depth = mix_ref.shape
+    place = row_place()
+    far_send, far_receive, near_send, near_receive, keep_sem, *remote = remote
+    gather = RowGather(shared_hbm, shared_ref, ((far_send, far_receive), (near_send, near_receive)))
+    own_copy = pltpu.make_async_copy(shared_hbm, shared_ref.at[place], local_sem.at[0])
+    mix_copy = pltpu.make_async_copy(mix_t_ref, mix_t_hbm, local_sem.at[1])
+    if core == 2:
+        inbox, shared_in, send, receive, pair_sem = remote
+        me = lax.axis_index("core")
+        slot = lax.rem(step + me, 2)
+        pair_copy = lambda k: push(grad_ref.at[1], inbox.at[k], (send, receive), k, {"core": 1 - me})
+        keep_copy = lambda k: pltpu.make_async_copy(
+            inbox.at[k], dw_hbm.at[k, pl.ds(0, 3 * depth)], pair_sem.at[k]
+        )
+    else:
+        slot = 0
+
+    @pl.when(step == 0)
+    def _():
+        own_copy.start()
+        barrier = pltpu.get_barrier_semaphore()
+        cy, chips = lax.axis_size("cy"), lax.axis_size(CHIPS)
+        chip = lax.axis_index("shard") * cy + lax.axis_index("cy")
+        for d in range(1, chips):
+            peer = lax.rem(chip + d, chips)
+            pl.semaphore_signal(barrier, inc=1, device_id={"shard": peer // cy, "cy": lax.rem(peer, cy)},
+                                device_id_type=MESH)
+        if core == 2:
+            pl.semaphore_signal(barrier, inc=1, device_id={"core": 1 - me}, device_id_type=MESH)
+        pl.semaphore_wait(barrier, chips - 1 + core - 1)
+        gather.start()
+        res = res_ref[...].astype(f32)
         scale = lax.rsqrt(jnp.mean(res * res, axis=1, keepdims=True) + epsilon)
-        mix_ref[at, :] = (res * scale * gain_ref[...]).astype(bf16)
-        mix = mix_ref[at, :]
-        chosen = chosen_ref[at, :] > 0.0
+        mix = (res * scale * gain_ref[...]).astype(bf16)
+        mix_ref[...] = mix
+        mix_t_ref[...] = mix.T
+        mix_copy.start()
+        chosen = chosen_ref[...] > 0.0
         logits = dot_rows(mix, router_ref[...])
         top = jnp.max(jnp.where(chosen, logits, -1e30), axis=1, keepdims=True)
         weight = jnp.where(chosen, jnp.exp(jnp.where(chosen, logits - top, 0.0)), 0.0)
-        gates_ref[at, :] = weight / jnp.sum(weight, axis=1, keepdims=True)
-        raw = dot_rows(cot_ref[at, :], down_ref[...])
-        dmix = None
-        for p in range(2):
-            value = dot_rows(mix, first_ref[p])
-            act, slope, hidden = swiglu(value[:, :hid], value[:, hid:])
-            here = pl.ds(p * hid, hid)
-            dh = raw[:, p * hid : (p + 1) * hid]
-            dval_ref[p, at, :hid] = (dh * value[:, hid:] * slope).astype(bf16)
-            dval_ref[p, at, hid:] = (dh * act).astype(bf16)
-            hidden_ref[at, here] = hidden
-            term = dot_outer(dval_ref[p, at, :], first_ref[p])
-            dmix = term if dmix is None else dmix + term
-        out_ref[at, :] = dot_outer(hidden_ref[at, :], down_ref[...])
-        dmix_ref[at, :] = dmix
-        return 0
-
-    lax.fori_loop(0, rows // tile, part, 0)
-    mix_t_ref[...] = mix_ref[...].T
-    for p in range(2):
-        dw_ref[:, p * wrows : (p + 1) * wrows, :] = (
-            dot_rows(mix_t_ref[...], dval_ref[p]).astype(bf16).reshape(-1, wrows, wide)
-        )
-    dw_ref[:, 2 * wrows :, :] = (
-        dot_inner(cot_ref[...], hidden_ref[...]).astype(bf16).reshape(-1, wrows, wide)
-    )
-
-
-def shared_expert(residual, cot, gain, weights, router_at, chosen, experts_w):
-    rows, depth = residual.shape
-    senders, deep, wide = experts_w.shape
-    part = 3 * (depth // senders)
-    own = deep - part
-    assert own % part == 0
-    shape = jax.ShapeDtypeStruct
-    block = pl.BlockSpec((senders, part, wide), lambda i: (0, own // part, 0))
-    grads = shape((senders, part, wide), bf16)
-    outs = [shape((rows, depth), f32), shape((rows, depth), f32), shape((rows, depth), bf16),
-            shape((depth, rows), bf16), shape((rows, LANES), f32)]
-    return pl.pallas_call(
-        partial(shared_kernel, tile=min(512, rows)),
-        grid=(1,),
-        in_specs=[whole(residual), whole(cot), whole(gain), columns(weights, LANES, router_at),
-                  whole(chosen), block],
-        out_specs=[whole(o) for o in outs + [grads]],
-        out_shape=outs + [grads],
-        scratch_shapes=[
-            pltpu.VMEM((2, depth, wide), bf16), pltpu.VMEM((depth, wide), bf16),
-            pltpu.VMEM((rows, wide), bf16), pltpu.VMEM((2, rows, wide), bf16),
-        ],
-        compiler_params=BIG,
-        cost_estimate=cost(10),
-        name="shared_expert",
-    )(residual, cot, gain, weights, chosen, experts_w)
-
-
-def experts_kernel(mix_ref, mix_t_ref, cot_ref, gates_ref, router_ref, w_ref, out_in, dmix_in, ds_ref,
-                   out_ref, dmix_ref, dgate_t_ref, dw_ref,
-                   dgate_ref, total_ref, grads_ref, down_ref, hidden_ref, dval_ref, grad_ref, load_sem,
-                   *remote, tile, senders, core):
-    step = pl.program_id(0)
-    last = step == pl.num_programs(0) - 1
-    rows, depth = mix_ref.shape
-    wide = w_ref.shape[2]
-    hid = wide // 2
-    chunks = depth // wide
-    deep = depth + depth // 2
-    if core == 2:
-        inbox, shared_box, send, receive, shared_send, shared_receive = remote
-        me = lax.axis_index("core")
-        other = 1 - me
-        slot = lax.rem(step + me, 2)
-
-        def to_sibling(source, target, send_sem, recv_sem):
-            return pltpu.make_async_remote_copy(
-                src_ref=source, dst_ref=target, send_sem=send_sem, recv_sem=recv_sem,
-                device_id={"core": other}, device_id_type=MESH,
-            )
-
-        shared_copy = to_sibling(ds_ref.at[other], shared_box, shared_send, shared_receive)
-        pair_copy = lambda k: to_sibling(grad_ref.at[1], inbox.at[k], send.at[k], receive.at[k])
-    else:
-        slot = 0
-
-    @pl.when(step == 0)
-    def _():
-        loads = [pltpu.make_async_copy(out_in, total_ref, load_sem.at[0]),
-                 pltpu.make_async_copy(dmix_in, grads_ref, load_sem.at[1])]
-        for copy in loads:
-            copy.start()
+        gates_ref[...] = weight / jnp.sum(weight, axis=1, keepdims=True)
+        total_ref[...] = jnp.zeros_like(total_ref)
+        grads_ref[...] = jnp.zeros_like(grads_ref)
         dgate_ref[...] = jnp.zeros_like(dgate_ref)
-        if core == 2:
-            barrier = pltpu.get_barrier_semaphore()
-            pl.semaphore_signal(barrier, inc=1, device_id={"core": other}, device_id_type=MESH)
-            pl.semaphore_wait(barrier, 1)
-            shared_copy.start()
-        for copy in loads:
-            copy.wait()
+        own_copy.wait()
 
     if core == 2:
         @pl.when((step >= 2) & (step < senders) & (slot == 1))
@@ -1475,9 +1598,18 @@
     @pl.when(step < senders)
     def _():
         pair_grads(
-            step, slot, mix_ref, mix_t_ref, cot_ref, gates_ref, w_ref, dgate_ref, total_ref, grads_ref, down_ref,
-            hidden_ref, dval_ref, grad_ref, tile
+            step, slot, mix_ref, mix_t_ref, cot_ref, gates_ref, w_ref, dgate_ref, total_ref, grads_ref,
+            down_ref, hidden_ref, dval_ref, grad_ref, tile
         )
+
+    @pl.when(step == 1)
+    def _():
+        gather.relay()
+        mix_copy.wait()
+
+    @pl.when(step == 2)
+    def _():
+        gather.finish()
 
     if core == 2:
         @pl.when((step < senders) & (slot == 1))
@@ -1487,31 +1619,88 @@
         @pl.when((step >= 1) & (slot == 1))
         def _():
             at = (step - 1) // 2
-
-            @pl.when(step <= 2)
-            def _():
-                shared_copy.wait()
-
             pair_copy(at).wait_recv()
-            dw_ref[0, : 3 * depth, :] = grad_ref[0] + inbox[at]
-            dw_ref[0, 3 * depth :, :] = ds_ref[me, at] + shared_box[at]
+            inbox[at] = grad_ref[0] + inbox[at]
+            keep_copy(at).start()
 
         @pl.when(last)
         def _():
             pair_copy(senders // 2 - 1).wait_send()
     else:
-        dw_ref[0, : 3 * depth, :] = grad_ref[0]
-        dw_ref[0, 3 * depth :, :] = ds_ref[0, step]
+        @pl.when(step < senders)
+        def _():
+            copy = pltpu.make_async_copy(
+                grad_ref.at[0], dw_hbm.at[step, pl.ds(0, 3 * depth)], local_sem.at[3]
+            )
+            copy.start()
+            copy.wait()
 
     @pl.when(last)
     def _():
+        wide = w_ref.shape[2]
+        hid = wide // 2
+        wrows = depth // senders
+        for p in range(2):
+            first_ref[p] = shared_ref[:, p * wrows : (p + 1) * wrows, :].reshape(depth, wide)
+        second_ref[...] = shared_ref[:, 2 * wrows :, :].reshape(depth, wide)
+        raw = dot_rows(cot_ref[...], second_ref[...])
+        for p in range(2):
+            value = dot_rows(mix_ref[...], first_ref[p])
+            act, slope, hidden = swiglu(value[:, :hid], value[:, hid:])
+            dh = raw[:, p * hid : (p + 1) * hid]
+            dval_ref[p, :, :hid] = (dh * value[:, hid:] * slope).astype(bf16)
+            dval_ref[p, :, hid:] = (dh * act).astype(bf16)
+            hidden_ref[:, p * hid : (p + 1) * hid] = hidden
+        result_ref[...] = (
+            total_ref[...] + dot_outer(hidden_ref[...], second_ref[...])
+        ).astype(bf16)
+        out_copy = pltpu.make_async_copy(result_ref, out_hbm, local_sem.at[2])
+        out_copy.start()
         gates = gates_ref[...]
         dgate = dgate_ref[...]
         inside = jnp.sum(gates * dgate, axis=1, keepdims=True)
         dlogits = (gates * (dgate - inside)).astype(bf16)
-        dmix_ref[...] = (grads_ref[...] + dot_outer(dlogits, router_ref[...])).astype(bf16)
-        out_ref[...] = total_ref[...].astype(bf16)
+        dmix = grads_ref[...] + dot_outer(dlogits, router_ref[...])
+        for p in range(2):
+            dmix = dmix + dot_outer(dval_ref[p], first_ref[p])
         dgate_t_ref[...] = dgate.T[: dgate_t_ref.shape[0], :]
+        for k in range(3):
+            if k < 2:
+                grad = dot_rows(mix_t_ref[...], dval_ref[k]).astype(bf16)
+            else:
+                grad = dot_inner(cot_ref[...], hidden_ref[...]).astype(bf16)
+            for j in range(senders):
+                at = (3 * ((j % core) * (senders // core) + j // core) + k) * wrows
+                grad_ref[0, at : at + wrows, :] = grad[j * wrows : (j + 1) * wrows]
+        span = 3 * depth // core
+        part = 3 * wrows
+        if core == 2:
+            mine = pl.ds(pl.multiple_of(me * span, 16), span)
+            theirs = pl.ds(pl.multiple_of((1 - me) * span, 16), span)
+            shared_copy = push(grad_ref.at[0, theirs], shared_in, (send, receive), senders // 2,
+                               {"core": 1 - me})
+            shared_copy.start()
+        mix_ref[...] = dmix.astype(bf16)
+        dmix_copy = pltpu.make_async_copy(mix_ref, dmix_hbm, local_sem.at[4])
+        dmix_copy.start()
+        copies = [out_copy, dmix_copy]
+        source = grad_ref.at[0]
+        if core == 2:
+            shared_copy.wait_recv()
+            shared_in[...] = shared_in[...] + grad_ref[0, mine, :]
+            source = shared_in
+        kept = senders // core
+        for j in range(kept):
+            copies.append(pltpu.make_async_copy(
+                source.at[pl.ds(j * part, part)], dw_hbm.at[j, pl.ds(3 * depth, part)], keep_sem.at[j]
+            ))
+            copies[-1].start()
+        for copy in copies:
+            copy.wait()
+        if core == 2:
+            for k in range(kept):
+                keep_copy(k).wait()
+            shared_copy.wait_send()
 
 
 def pair_grads(step, slot, mix_ref, mix_t_ref, cot_ref, gates_ref, w_ref, dgate_ref, total_ref, grads_ref,
@@ -1567,53 +1756,47 @@
         )
 
 
-def experts(mix, mix_t, cot, gates, weights, router_at, experts_w, out, dmix, ds):
+def experts(residual, cot, gain, chosen, weights, router_at, experts_w, shared):
     senders, deep, wide = experts_w.shape
-    rows, depth = mix.shape
-    core = lax.axis_size("core")
+    rows, depth = residual.shape
+    core, chips = lax.axis_size("core"), lax.axis_size(CHIPS)
     kept = senders // core
-    part = deep - 3 * depth
-    ds = ds.reshape(kept, core, part, wide).transpose(1, 0, 2, 3)
+    kinds = 2 * senders + -2 * senders % 8
     shape = jax.ShapeDtypeStruct
-    once = lambda a: pl.BlockSpec(
-        a.shape, lambda i: (0,) * a.ndim, pipeline_mode=pl.Buffered(1)
-    )
-    kinds = 2 * senders + -2 * senders % 8
-    outs = [shape((rows, depth), bf16), shape((rows, depth), bf16), shape((kinds, rows), f32)]
+    dma = pltpu.SemaphoreType.DMA
+    once = lambda a: pl.BlockSpec(a.shape, lambda i: (0,) * a.ndim, pipeline_mode=pl.Buffered(1))
+    outs = [shape((rows, LANES), f32), shape((kinds, rows), f32)]
+    remote = []
     if core == 2:
-        steps = senders + 1
-        kept_map = lambda i: (jnp.maximum(i - 1, 0) // 2, 0, 0)
-        remote = [
-            pltpu.VMEM((kept, 3 * depth, wide), bf16), pltpu.VMEM((kept, part, wide), bf16),
-            pltpu.SemaphoreType.DMA((kept,)), pltpu.SemaphoreType.DMA((kept,)),
-            pltpu.SemaphoreType.DMA, pltpu.SemaphoreType.DMA,
-        ]
-        params = pltpu.CompilerParams(
-            vmem_limit_bytes=60 << 20, collective_id=4, has_side_effects=True
-        )
-    else:
-        steps, remote, params = senders, [], pltpu.CompilerParams(vmem_limit_bytes=60 << 20)
-        kept_map = lambda i: (i, 0, 0)
+        remote = [pltpu.VMEM((kept, deep, wide), bf16), pltpu.VMEM((deep // 2, wide), bf16),
+                  dma((kept + 1,)), dma((kept + 1,)), dma((kept,))]
     return pl.pallas_call(
-        partial(experts_kernel, tile=min(512, rows), senders=senders, core=core),
-        grid=(steps,),
-        in_specs=[once(mix), once(mix_t), once(cot), once(gates),
+        partial(experts_kernel, tile=rows, senders=senders, core=core),
+        grid=(senders + 1,),
+        in_specs=[once(residual), once(cot), once(gain), once(chosen),
                   pl.BlockSpec((depth, LANES), lambda i: (0, router_at // LANES)),
-                  pl.BlockSpec((1, 3 * depth, wide), lambda i: (jnp.minimum(i, senders - 1), 0, 0)),
-                  pl.BlockSpec(memory_space=pl.ANY), pl.BlockSpec(memory_space=pl.ANY), once(ds)],
-        out_specs=[whole(o) for o in outs] + [pl.BlockSpec((1, deep, wide), kept_map)],
-        out_shape=outs + [shape((kept, deep, wide), bf16)],
+                  pl.BlockSpec((1, deep, wide), lambda i: (jnp.minimum(i, senders - 1), 0, 0)), HBM],
+        out_specs=[whole(o) for o in outs] + [HBM] * 4,
+        out_shape=outs + [
+            shape((rows, depth), bf16), shape((rows, depth), bf16), shape((depth, rows), bf16),
+            shape((kept, deep + shared.shape[0], wide), bf16),
+        ],
         scratch_shapes=[
-            pltpu.VMEM((rows, LANES), f32), pltpu.VMEM((rows, depth), f32),
-            pltpu.VMEM((rows, depth), f32),
+            pltpu.VMEM((rows, depth), bf16), pltpu.VMEM((depth, rows), bf16), pltpu.VMEM((rows, LANES), f32),
+            pltpu.VMEM((rows, depth), f32), pltpu.VMEM((rows, depth), f32),
             pltpu.VMEM((wide, depth), bf16), pltpu.VMEM((rows, wide), bf16),
-            pltpu.VMEM((2, rows, wide), bf16), pltpu.VMEM((core, 3 * depth, wide), bf16),
-            pltpu.SemaphoreType.DMA((2,)),
+            pltpu.VMEM((2, rows, wide), bf16), pltpu.VMEM((core, deep, wide), bf16),
+            pltpu.VMEM((senders,) + shared.shape, bf16), pltpu.VMEM((2, depth, wide), bf16),
+            pltpu.VMEM((depth, wide), bf16), pltpu.VMEM((rows, depth), bf16), dma((5,)),
+            dma((max(chips - 1, 1),)), dma((max(chips - 1, 1),)), dma((chips,)), dma((chips,)),
+            dma((kept,)),
         ] + remote,
-        compiler_params=params,
-        cost_estimate=cost(6 * senders),
+        compiler_params=pltpu.CompilerParams(
+            vmem_limit_bytes=63 << 20, collective_id=4, has_side_effects=True
+        ),
+        cost_estimate=cost(7 * senders),
         name="experts",
-    )(mix, mix_t, cot, gates, weights, experts_w, out, dmix, ds)
+    )(residual, cot, gain, chosen, weights, experts_w, shared)
 
 
 def local(
@@ -1656,10 +1839,8 @@
          pair_down.transpose(0, 2, 1, 3).reshape(local_experts, -1, 2 * hid)], axis=1
     )
     shared_pair = shared_gates.reshape(wrows, 2, 2, shared_here // 2).transpose(2, 0, 1, 3)
-    packed = jnp.concatenate(
-        [pair.reshape(-1, 2 * hid), shared_pair.reshape(-1, shared_here), shared_down], axis=0
-    )
-    experts_w = gather_rows(packed[None])
+    experts_w = gather_rows(pair.reshape(1, -1, 2 * hid))
+    shared_local = jnp.concatenate([shared_pair.reshape(-1, shared_here), shared_down], axis=0)
 
     seg_row = segments[0]
     halo_seg = shifted(seg_row[tokens - CONV + 1 :], CTX, 1)
@@ -1693,58 +1874,61 @@
     chosen = jnp.any(
         routes[:, :, None] == jnp.arange(LANES, dtype=jnp.int32)[None, None, :], axis=1
     ).astype(f32)
-    out_part, dmix_part, mixed_two, mix_t, gates, shared_grad = shared_expert(
-        residual, cot_full, gain_mid, weights, router_at, chosen, experts_w
-    )
-    out_part, dmix_part, dgate, dw = experts(
-        mixed_two, mix_t, cot_full, gates, weights, router_at, experts_w, out_part, dmix_part, shared_grad
+    gates, dgate, out_part, dmix_part, mix_t, dw = experts(
+        residual, cot_full, gain_mid, chosen, weights, router_at, experts_w, shared_local
     )
     expert_rows = scatter_chips(dw.reshape(-1, 2 * hid))
     dmixer, notes, gains_mid = turn_step(
         dmix_part, dgate, residual, cot_full, own_part, gain_mid
     )
 
-    value_grad, gated_out, dtaps, sums, small_sums, state_all, output = rear(
+    value_grad, rear_main, dtaps, sums, small_sums, state_all, output = rear(
         (dmixer, scale_rows, notes, mixer, within, act, scaled, step, running, run_exp, state_in, taps,
-         same, bias, decay, skip, gain_gate_f, at_end, link, seg_col, seg_line, packed[inner:]),
+         same, bias, decay, skip, gain_gate_f, at_end, link, seg_col, seg_line, packed[inner:],
+         mixed_t),
         out_part, value, weights, residual, inner, nstate, per, heads, di_all
     )
     first = 2 * inner
     last = first + 2 * nstate
-    main_local = weight_grads(
-        mixed_t, value_grad, state_all, dmixer, gated_out, mix_t, gates, notes, inner, nstate
-    )
-    shared_rows = expert_rows[3 * depth :]
-    shared_up = shared_rows[: 2 * wrows].reshape(2, wrows, 2, shared_here // 2)
+    rear_main, expert_rows = lax.optimization_barrier((rear_main, expert_rows))
+    rear_main = scatter_chips(rear_main)
+
     early = jnp.concatenate(
         [dtaps[:, :inner], sums[:2], jnp.pad(small_sums[:2], ((0, 0), (0, inner - LANES)))], axis=0
     )
-    main_local, early, expert_rows = lax.optimization_barrier((main_local, early, expert_rows))
-    main_grad = scatter_chips(main_local).astype(f32)
-    grad_input, early, late, gates_rows, down_rows = finish_step(
-        value_grad, weights, got, dmixer, gain_row, gains_mid,
-        jnp.pad(dtaps[:, inner:], ((0, 8 - CONV), (0, 0))), early, expert_rows[: 3 * depth], hid
+    state_taps = jnp.pad(dtaps[:, inner:], ((0, 8 - CONV), (0, 0)))
+    grad_input, early, late, main = last_step(
+        (value_grad, got, dmixer, gain_row, gains_mid, state_taps, early, mixed_t, mix_t, state_all,
+         gates, notes),
+        weights, inner, last,
+    )
+    if lax.axis_size("core") != 2:
+        main = scatter_chips(main)
+    (output, grad_input, grad_gain_in, grad_main, grad_state, grad_step, grad_conv, grad_conv_state,
+     grad_bias, grad_decay, grad_skip, grad_gate, grad_proj_out, grad_gain_mid, grad_router, grad_shared,
+     grad_shared_down, grad_gates, grad_down) = emit(
+        (output, grad_input, early, late, rear_main, main, expert_rows), inner, nstate, per, heads, experts_all, hid
     )
     return (
         output,
         grad_input,
-        late[0, :quarter],
-        jnp.stack([main_grad[:, :inner], main_grad[:, inner:first]], axis=1),
-        main_grad[:, first:last],
-        main_grad[:, last : last + heads],
-        early[:CONV],
-        late[:CONV, quarter:],
-        early[CONV + 2, :heads],
-        early[CONV + 3, :heads],
-        jnp.sum(early[CONV + 1].reshape(heads, per), axis=1),
-        early[CONV],
-        main_grad[:, main_wide:router_at],
-        late[1, :quarter],
-        main_grad[:, router_at : router_at + experts_all],
-        shared_up.transpose(1, 2, 0, 3).reshape(wrows, 2, shared_here).astype(f32),
-        shared_rows[2 * wrows :].astype(f32),
-        gates_rows.reshape(expert_gates.shape),
-        down_rows,
+        grad_gain_in.reshape(quarter),
+        grad_main,
+        grad_state,
+        grad_step.T,
+        grad_conv,
+        grad_conv_state,
+        grad_bias[0],
+        grad_decay[0],
+        grad_skip[0],
+        grad_gate.reshape(inner),
+        grad_proj_out,
+        grad_gain_mid.reshape(quarter),
+        grad_router.T,
+        grad_shared,
+        grad_shared_down,
+        grad_gates.reshape(expert_gates.shape),
+        grad_down,
     )
 
 

time: 481 us -> 439 us (0.913)
  local copies, waits for them, and re-layouts: 46.6 us -> 20.9 us
  waiting for transfers between devices: 23.4 us -> 16 us
  Pallas kernels: 379 us -> 374 us
    slice x10 -> x1, local copies, waits for them, and re-layouts: 11 us -> 0.68 us  [local(): state_taps = jnp.pad(dtaps[:, inner:], ((0, 8 - CONV), (0, 0)))]
    unnamed x62 -> x45, local copies, waits for them, and re-layouts: 14.1 us -> 4.58 us
    pallas_call x1, Pallas kernels: 65.8 us -> 58.5 us  [turn_step(): pl.pallas_call(partial(turn_kernel, n=n), in_specs=[HBM] + [VMEM] * 5, ou...]
    all_gather x2, waiting for transfers between devices: 19 us -> 12 us  [gather_rows(): return lax.all_gather(value, ROWS, axis=0, tiled=True)]
    pallas_call x1, Pallas kernels: 50.9 us -> 57.8 us  [rear(): pl.pallas_call(partial(rear_kernel, inner=inner, nstate=nstate, per=per,...]
    pallas_call x4 -> x3, Pallas kernels: 124 us -> 122 us  [the longest x1 64.5 us: experts(): pl.pallas_call(partial(experts_kernel, tile=rows, senders=senders, core=c...]
  transfers between devices with their start and end apart: 5 -> 5, of which waited for: 2 -> 2; matrix products, arithmetic and copies ran while one was open for 7% -> 5% of each run, Pallas kernels for 66% -> 69%
where the time goes in v4:
time: 439 us; the launch traced here: 436 us
  Pallas kernels  374 us (85%)
  local copies, waits for them, and re-layouts  20.9 us (5%)
  waiting for transfers between devices  16 us (4%)
  between operations  14.4 us (3%)
  other arithmetic  7.86 us (2%)
    pallas_call x1, Pallas kernels, front(): pl.pallas_call(partial(front_kernel, inner=inner, nstate=nstate, per=per,...  96.4 us
    pallas_call x1, Pallas kernels, experts(): pl.pallas_call(partial(experts_kernel, tile=rows, senders=senders, core=c...  64.5 us
    pallas_call x1, Pallas kernels, turn_step(): pl.pallas_call(partial(turn_kernel, n=n), in_specs=[HBM] + [VMEM] * 5, ou...  58.5 us
    pallas_call x1, Pallas kernels, rear(): pl.pallas_call(partial(rear_kernel, inner=inner, nstate=nstate, per=per,...  57.8 us
    pallas_call x1, Pallas kernels, last_step(): pl.pallas_call(partial(last_kernel, n=n, count=count, boxes=len(boxes) -...  49.1 us
    pallas_call x1, Pallas kernels, intake(): pl.pallas_call(partial(intake_kernel, n=n), in_specs=[VMEM] * 2, out_spec...  39.4 us
    all_gather x2, waiting for transfers between devices, gather_rows(): return lax.all_gather(value, ROWS, axis=0, tiled=True)  12 us
  transfers between devices with their start and end apart: 5, of which 2 were waited for; matrix products, arithmetic and copies ran while one was open for 5% of the time, Pallas kernels for 69%

profile of v4, /device:TPU:0, one launch (start us, length us, event | category | flops | bytes accessed | tf_op | source)
XLA Modules:
  0.0 435.7 jit_solution(8011786879672117254)
XLA Ops:
  7.3 0.9 copy.99
  8.1 0.8 copy.100
  8.9 2.3 fusion.3
  11.4 0.8 copy-done.5
  12.3 1.0 copy-done.2
  14.0 2.8 reshape.130
  16.8 1.6 pad_maximum_fusion
  19.1 2.6 collective-permute-start
  24.3 0.7 convert_element_type.49.chosen_ref
  26.6 0.7 pad_maximum_fusion.1.shared_hbm
  28.0 39.4 %intake.1 = (bf16[528,1536]{1,0:T(8,128)(2,1)}, bf16[1536,512]{1,0:T(8,128)(2,1)}, bf16[512,1536]{1,0:T(8,128)(2,1)}, f32[16,1536]{1,0:T(8,128)}) custom-call(bf16[512,384]{1,0:T(8,128)(2,1)} %x_ref.1, bf16[16,384]{1,0:T(8,128)(2,1)} %maximum_maximum_fusion.gains_ref), custom_call_target="tpu_custom_call" | custom-call | flops 44999999488 | bytes 1048576 | tf_op jit(solution)/shard_map/intake/pallas_call | solution.py:664
  67.4 1.5 fusion.4
  69.8 2.1 compare_convert_fusion
  71.9 1.3 broadcast_in_dim.36.same_ref
  73.2 96.4 %front.1 = (f32[528,1920]{1,0:T(8,128)}, bf16[512,1024]{1,0:T(8,128)(2,1)}, bf16[512,768]{1,0:T(8,128)(2,1)}, f32[512,128]{1,0:T(8,128)}, f32[512,128]{1,0:T(8,1...) custom-call(bf16[528,1536]{1,0:T(8,128)(2,1)} %get-tuple-element.78., ...), custom_call_target="tpu_custom_call" | custom-call | flops 89999998976 | bytes 1048576 | tf_op jit(solution)/shard_map/front/pallas_call | solution.py:833
  169.6 12.0 %all-gather.5.cloned.1.call-done.w_ref = bf16[8,4608,256]{2,1,0:T(8,128)(2,1)} async-done(((bf16[1,4608,256]{2,1,0:T(8,128)(2,1)}), bf16[8,4608,256]{2,1,0:T(8,128)(2,1)}) %all-gather.5.cloned.1.call-update) | async-done | bytes 18874384 | tf_op jit(solution)/shard_map/all_gather | solution.py:65
  181.6 64.5 %experts.1 = (f32[512,128]{1,0:T(8,128)}, f32[16,512]{1,0:T(8,128)}, bf16[512,1536]{1,0:T(8,128)(2,1)}, bf16[512,1536]{1,0:T(8,128)(2,1)}, bf16[1536,512]{1,0:T(8,128)(2,1)}, /*index=5*/bf16[4,5184,256]{2,1,0:T(8,128)(2,1)}) custom-call(bf16[512,1536]{1,0:T(8,128)(2,1)} %get-tuple-element.80.res_ref.res_hbm, bf16[512,1536]{1,0:T(8,128)(2,1)} %get-tuple-element.81.cot_ref, ...), custom_call_target="tpu_custom_call" | custom-call | flops 50400002048 | bytes 1048576 | tf_op jit(solution)/shard_map/experts/pallas_call | solution.py:1773
  246.2 1.3 slice.59.packed_ref
  247.5 58.5 %turn_step.1 = (bf16[512,1536]{1,0:T(8,128)(2,1)}, f32[24,512]{1,0:T(8,128)}, f32[8,1536]{1,0:T(8,128)}) custom-call(bf16[512,1536]{1,0:T(8,128)(2,1)} %get-tuple-element.83.dmix_hbm, f32[16,512]{1,0:T(8,128)} %get-tuple-element.84.dgate_ref, bf16[512,1536]{1,0:T(8,128)(2,1)} %get-tuple-element.80.res_ref.res_hbm, ...), custom_call_target="tpu_custom_call" | custom-call | flops 54000001024 | bytes 1048576 | tf_op jit(solution)/shard_map/turn_step/pallas_call | solution.py:934
  306.0 57.8 %rear.1 = (bf16[512,1920]{1,0:T(8,128)(2,1)}, bf16[768,1536]{1,0:T(8,128)(2,1)}, f32[4,1024]{1,0:T(4,128)}, f32[8,768]{1,0:T(8,128)}, f32[8,128]{1,0:T(8,128)}, ...) custom-call(bf16[512,1536]{1,0:T(8,128)(2,1)} %get-tuple-element.86.dout_ref.dres_ref, ...), custom_call_target="tpu_custom_call" | custom-call | flops 44999999488 | bytes 1048576 | tf_op jit(solution)/shard_map/rear/pallas_call | solution.py:1498
  365.9 0.7 slice.63
  367.9 49.1 %last_step.1 = (f32[512,384]{1,0:T(8,128)}, f32[8,768]{1,0:T(8,128)}, f32[8,640]{1,0:T(8,128)}, f32[192,1280]{1,0:T(8,128)}) custom-call(bf16[512,1920]{1,0:T(8,128)(2,1)} %get-tuple-element.102.grad_ref, bf16[512,1536]{1,0:T(8,128)(2,1)} %get-tuple-element.79.x_ref, bf16[512,1536]{1,0:T(8,128)(2,1)} %get-tuple-element.86.dout_ref.dres_ref, ...), custom_call_target="tpu_custom_call" | custom-call | flops 54000001024 | bytes 1048576 | tf_op jit(solution)/shard_map/last_step/pallas_call | solution.py:1093
  417.0 3.9 reduce-scatter.5.cloned.1.call-done.rear_ref
  420.9 7.9 %emit.1 = (bf16[512,384]{1,0:T(8,128)(2,1)}, f32[512,384]{1,0:T(8,128)}, f32[3,128]{1,0:T(4,128)}, f32[192,2,768]{2,1,0:T(2,128)}, f32[192,256]{1,0:T(8,128)}, /...) custom-call(bf16[512,384]{1,0:T(8,128)(2,1)} %get-tuple-element.101., ...), custom_call_target="tpu_custom_call" | custom-call | flops 7200000000 | bytes 1048576 | tf_op jit(solution)/shard_map/emit/pallas_call | solution.py:1175
  (82 shorter events, 10.6 us)
Async XLA Ops:
  7.2 17.8 %copy-start = (bf16[192,2,256]{2,1,0:T(2,128)(2,1)S(1)}, bf16[192,2,256]{2,1,0:T(2,128)(2,1)}, u32[]{:S(2)}) copy-start(bf16[192,2,256]{2,1,0:T(2,128)(2,1)} %param.35) | copy-start | bytes 589828
  7.2 64.7 %all-gather.3.cloned.1.call-start = ((), (), s32[]{:S(2)}) async-start(), calls=%async_computation.2 | async-start | bytes 9732096 | tf_op jit(solution)/shard_map/all_gather | solution.py:65
  8.9 2.4 copy-start.7
  11.2 1.0 copy-start.5
  11.3 2.0 copy-start.4
  12.2 1.0 copy-start.2
  13.3 168.4 %all-gather.5.cloned.1.call-start = ((), (), s32[]{:S(2)}) async-start(), calls=%async_computation.3 | async-start | bytes 21233664 | tf_op jit(solution)/shard_map/all_gather | solution.py:65
  18.3 0.7 copy-start.8
  18.3 4.0 copy-start.13
  18.3 4.0 copy-start.14
  18.3 4.0 copy-start.12
  18.3 4.6 %copy-start.15 = (f32[12]{0:T(128)S(1)}, f32[12]{0:T(128)}, u32[]{:S(2)}) copy-start(f32[12]{0:T(128)} %param.30) | copy-start | bytes 148
  18.3 5.3 %copy-start.9 = (s32[512,6]{0,1:T(8,128)S(1)}, s32[512,6]{0,1:T(8,128)}, u32[]{:S(2)}) copy-start(s32[512,6]{0,1:T(8,128)} %param.40) | copy-start | bytes 36868
  18.4 7.1 %copy-start.16 = (f32[12]{0:T(128)S(1)}, f32[12]{0:T(128)}, u32[]{:S(2)}) copy-start(f32[12]{0:T(128)} %param.29) | copy-start | bytes 148
  18.4 7.1 %copy-start.17 = (f32[12]{0:T(128)S(1)}, f32[12]{0:T(128)}, u32[]{:S(2)}) copy-start(f32[12]{0:T(128)} %param.28) | copy-start | bytes 148
  18.4 7.6 %copy-start.10 = (bf16[4,768]{1,0:T(4,128)(2,1)S(1)}, bf16[4,768]{1,0:T(4,128)(2,1)}, u32[]{:S(2)}) copy-start(bf16[4,768]{1,0:T(4,128)(2,1)} %param.26) | copy-start | bytes 18436
  18.4 7.6 %copy-start.11 = (bf16[4,256]{1,0:T(4,128)(2,1)S(1)}, bf16[4,256]{1,0:T(4,128)(2,1)}, u32[]{:S(2)}) copy-start(bf16[4,256]{1,0:T(4,128)(2,1)} %param.27) | copy-start | bytes 6148
  18.4 8.2 %copy-start.6 = (bf16[192,256]{1,0:T(8,128)(2,1)S(1)}, bf16[192,256]{1,0:T(8,128)(2,1)}, u32[]{:S(2)}) copy-start(bf16[192,256]{1,0:T(8,128)(2,1)} %param.36) | copy-start | bytes 294916
  18.4 349.4 %reduce-scatter.3.cloned.1.call-start = ((), (), s32[]{:S(2)}) async-start(), calls=%async_computation.4 | async-start | bytes 13271040 | tf_op jit(solution)/shard_map/reduce_scatter | solution.py:74
  19.1 49.9 %collective-permute-start = (s32[3]{0:T(128)S(1)}, s32[3]{0:T(128)S(1)}, u32[]{:S(2)}, u32[]{:S(2)}) collective-permute-start(s32[3]{0:T(128)S(1)} %slice_bitcast_fusion), channel_id=1, source_target_pairs={{0,4},{4,8},{8,12},{1,5},{5,9},{9,13},{2,6},{6,10},{10,14},{3,7},{... | collective-permute-start | bytes 44 | tf_op jit(solution)/shard_map/ppermute | solution.py:45
  25.3 44.5 %copy-start.3 = (s32[512,1]{1,0:T(8,128)}, s32[512,1]{1,0:T(8,128)S(1)}, u32[]{:S(2)}) copy-start(s32[512,1]{1,0:T(8,128)S(1)} %copy.93.seg_col_ref) | copy-start | bytes 6148
  246.2 174.7 %reduce-scatter.5.cloned.1.call-start = ((), (), s32[]{:S(2)}) async-start(), calls=%async_computation.5 | async-start | bytes 2949120 | tf_op jit(solution)/shard_map/reduce_scatter | solution.py:74
  420.9 8.0 %copy-start.1 = (bf16[192,2,256]{2,1,0:T(2,128)(2,1)S(1)}, bf16[192,2,256]{2,1,0:T(2,128)(2,1)}, u32[]{:S(2)}) copy-start(bf16[192,2,256]{2,1,0:T(2,128)(2,1)} %param.35) | copy-start | bytes 589828
Sparse Core Ops, SparseCore 0:
  13.4 58.3 all-gather.2
  74.2 107.4 all-gather.4
  246.3 109.9 reduce-scatter.2
  368.0 52.8 reduce-scatter.4

commit v5 on v4

--- a/solution.py
+++ b/solution.py
@@ -687,11 +687,11 @@
 
 
 def front_kernel(mixed_ref, taps_ref, same_ref, bias_ref, decay_ref, end_ref, link_ref, seg_col_ref,
-                 seg_row_ref, skip_ref, gain_ref, x_ref, cot_ref, w_ref,
+                 seg_row_ref, skip_ref, gain_ref, x_ref, cot_ref, mid_ref, chosen_ref, w_ref,
                  value_ref, act_ref, scaled_ref, step_ref, run_ref, run_exp_ref, inner_ref, mixer_ref,
-                 state_ref, packed_ref, res_ref, stat_ref, own_ref, cot_full_ref,
+                 state_ref, packed_ref, res_ref, stat_ref, own_ref, cot_full_ref, mix_ref, mix_t_ref, gates_ref,
                  wm_ref, wo_ref, run_t_ref, scores_ref, part_ref, square_ref, lifted_ref, far_ref,
-                 right_box, left_box, square_box, res_box, stat_box, cot_box, local_sem, *sems,
+                 right_box, left_box, square_box, res_box, stat_box, cot_box, router_ref, local_sem, *sems,
                  inner, nstate, per, heads, di_all, n):
     me = lax.axis_index("tensor")
     rows, depth = x_ref.shape
@@ -706,6 +706,7 @@
     loads = [
         pltpu.make_async_copy(w_ref.at[:, pl.ds(0, wide)], wm_ref, local_sem.at[0]),
         pltpu.make_async_copy(w_ref.at[:, pl.ds(wide, inner)], wo_ref, local_sem.at[1]),
+        pltpu.make_async_copy(w_ref.at[:, pl.ds(wide + inner, LANES)], router_ref, local_sem.at[2]),
     ]
     for copy in loads:
         copy.start()
@@ -802,6 +803,18 @@
         copy.wait()
     res_ref[...] = res_box[...]
     stat_ref[...] = stat_box[...]
+    res = res_box[...].astype(f32)
+    mix = (
+        res * lax.rsqrt(jnp.mean(res * res, axis=1, keepdims=True) + epsilon) * mid_ref[...]
+    ).astype(bf16)
+    mix_ref[...] = mix
+    mix_t_ref[...] = mix.T
+    loads[2].wait()
+    chosen = chosen_ref[...] > 0.0
+    logits = dot_rows(mix, router_ref[...])
+    top = jnp.max(jnp.where(chosen, logits, -1e30), axis=1, keepdims=True)
+    weight = jnp.where(chosen, jnp.exp(jnp.where(chosen, logits - top, 0.0)), 0.0)
+    gates_ref[...] = weight / jnp.sum(weight, axis=1, keepdims=True)
 
 
 def pairs(count, n):
@@ -812,8 +825,8 @@
 HBM = pl.BlockSpec(memory_space=pl.ANY)
 
 
-def front(mixed_ext, taps, same, bias, decay, at_end, link, seg_col, seg_row, skip, gain, x, cot, weights,
-          inner, nstate, per, heads, di_all):
+def front(mixed_ext, taps, same, bias, decay, at_end, link, seg_col, seg_row, skip, gain, x, cot, mid,
+          chosen, weights, inner, nstate, per, heads, di_all):
     n = lax.axis_size("tensor")
     others = lax.axis_size(CTX) - 1
     tokens, depth = x.shape
@@ -827,13 +840,14 @@
         shape((tokens, inner), f32), shape((tokens, inner), f32), shape((tokens, inner), f32),
         shape((inner, nstate), f32), shape((inner + 16, nstate), bf16),
         shape((tokens, depth), bf16), shape((8, tokens), f32), shape((own, depth), f32),
-        shape((tokens, depth), bf16),
+        shape((tokens, depth), bf16), shape((tokens, depth), bf16), shape((depth, tokens), bf16),
+        shape((tokens, LANES), f32),
     ]
     dma = pltpu.SemaphoreType.DMA
     return pl.pallas_call(
         partial(front_kernel, inner=inner, nstate=nstate, per=per, heads=heads, di_all=di_all, n=n),
-        in_specs=[VMEM] * 13 + [HBM],
-        out_specs=[VMEM] * 14,
+        in_specs=[VMEM] * 15 + [HBM],
+        out_specs=[VMEM] * 17,
         out_shape=outs,
         scratch_shapes=[
             pltpu.VMEM((depth, wide), bf16), pltpu.VMEM((depth, inner), bf16),
@@ -843,14 +857,16 @@
             pltpu.VMEM((2, n, own // 2, depth), bf16), pltpu.VMEM((2, n, own // 2, depth), bf16),
             pltpu.VMEM((n - 1, 8, own), f32),
             pltpu.VMEM((tokens, depth), bf16), pltpu.VMEM((8, tokens), f32),
-            pltpu.VMEM((tokens, depth), bf16), dma((2,)), dma((others,)), dma((others,)),
+            pltpu.VMEM((tokens, depth), bf16), pltpu.VMEM((depth, LANES), bf16), dma((3,)),
+            dma((others,)), dma((others,)),
         ] + pairs(2, n) + line_sems(n) * 5,
         compiler_params=pltpu.CompilerParams(
-            vmem_limit_bytes=60 << 20, collective_id=1, has_side_effects=True
+            vmem_limit_bytes=63 << 20, collective_id=1, has_side_effects=True
         ),
         cost_estimate=cost(100),
         name="front",
-    )(mixed_ext, taps, same, bias, decay, at_end, link, seg_col, seg_row, skip, gain, x, cot, weights)
+    )(mixed_ext, taps, same, bias, decay, at_end, link, seg_col, seg_row, skip, gain, x, cot, mid,
+      chosen, weights)
 
 
 def turn_kernel(dmix_hbm, dgate_ref, res_ref, cot_ref, own_ref, gain_ref,
@@ -1202,7 +1218,7 @@
     sums_ref[2:, :] = jnp.zeros((6, inner), f32)
     carried = (heads * (jnp.exp(run_exp_ref[...]) * link_ref[...])).astype(bf16)
     direct_ref[:inner, :] = dot_inner(carried, act_ref[:, inner + nstate :]).astype(bf16)
-    direct_ref[inner:, :] = through_ref[...]
+    direct_ref[inner:, :] = through_ref[inner:, :]
 
 
 def intra_back_part(heads_ref, act_ref, scaled_ref, run_t_ref, run_exp_ref, seg_col_ref,
@@ -1365,8 +1381,8 @@
                 run_ref, run_exp_ref, state_ref, taps_ref, same_ref, bias_ref, decay_ref, skip_ref,
                 gain_ref, end_ref, link_ref, seg_col_ref, seg_row_ref, packed_ref, mixed_t_ref,
                 part_hbm, value_hbm, w_hbm, res_hbm,
-                grad_ref, main_ref, dtaps_ref, sums_ref, small_ref, state_all_ref, out_ref,
-                gated_ref, value_ref, w_ref, res_ref, run_t_ref, heads_ref, zgrad_ref, direct_ref, dscaled_ref,
+                grad_ref, main_ref, early_ref, taps_out, state_all_ref, out_ref,
+                dtaps_ref, sums_ref, small_ref, gated_ref, value_ref, w_ref, res_ref, run_t_ref, heads_ref, zgrad_ref, direct_ref, dscaled_ref,
                 dstate_ref, drun_ref, scores_ref, dscores_ref, leaving_ref, kept_ref, rows_ref, dact_ref,
                 far_ref, part_ref, right_box, left_box, rows_box, sum_box, ext_ref, state_halo, signal_halo,
                 local_sem, stage_ref, *sems,
@@ -1406,11 +1422,11 @@
               inner=inner, nstate=nstate, di_all=di_all)
     states = StatePush(direct_ref, far_ref, groups[0], True)
     states.start()
-    line.step(1)
     weights.product(dout_ref, gated_ref, 0, False)
     weights.to_sibling(0, inner)
     weights.product(mixed_t_ref, zgrad_ref, inner)
     weights.to_sibling(inner, inner)
+    line.step(1)
     run_t = run_ref[...].T
     for h in range(heads):
         run_t_ref[h] = run_t[h : h + 1, :]
@@ -1460,6 +1476,12 @@
                      skip_ref, mixer_ref, inner_ref, dscaled_ref, drun_ref, leaving_ref, kept_ref,
                      zgrad_ref, rows_ref, ext_ref, dtaps_ref, small_ref, dact_ref, middle, between,
                      inner=inner, nstate=nstate, per=per)
+    early_ref[:CONV, :] = dtaps_ref[:, :inner]
+    early_ref[CONV : CONV + 2, :] = sums_ref[:2, :]
+    early_ref[CONV + 2 :, :] = jnp.zeros((2, inner), f32)
+    early_ref[CONV + 2 :, :LANES] = small_ref[:2, :]
+    taps_out[:CONV, :] = dtaps_ref[:, inner:]
+    taps_out[CONV:, :] = jnp.zeros((8 - CONV, 2 * nstate), f32)
     grad_ref[...] = ext_ref[HALO:, :]
     pl.when(gets)(signal_copy.wait_recv)
     grad_ref[tokens - HALO :, inner : 2 * inner] = (
@@ -1490,8 +1512,8 @@
     boxes, main = weight_boxes(depth, 2 * inner, 2, False)
     shape = jax.ShapeDtypeStruct
     outs = [
-        shape((tokens, wide), bf16), main, shape((CONV, inner + 2 * nstate), f32),
-        shape((8, inner), f32), shape((8, LANES), f32), shape((tokens, 2 * nstate), bf16),
+        shape((tokens, wide), bf16), main, shape((8, inner), f32), shape((8, 2 * nstate), f32),
+        shape((tokens, 2 * nstate), bf16),
         shape((tokens, quarter), bf16),
     ]
     dma = pltpu.SemaphoreType.DMA
@@ -1502,7 +1524,8 @@
         out_specs=[VMEM] * len(outs),
         out_shape=outs,
         scratch_shapes=[
-            pltpu.VMEM((tokens, inner), bf16),
+            pltpu.VMEM((CONV, inner + 2 * nstate), f32), pltpu.VMEM((8, inner), f32),
+            pltpu.VMEM((8, LANES), f32), pltpu.VMEM((tokens, inner), bf16),
             pltpu.VMEM((ext, wide), f32), pltpu.VMEM((depth, inner), bf16),
             pltpu.VMEM((tokens, quarter), bf16), pltpu.VMEM((heads, 1, tokens), f32),
             pltpu.VMEM((tokens, inner), f32), pltpu.VMEM((tokens, inner), bf16),
@@ -1536,10 +1559,9 @@
     return act, sig * (1.0 + first * (1.0 - sig)), (act * second).astype(bf16)
 
 
-def experts_kernel(res_ref, cot_ref, gain_ref, chosen_ref, router_ref, w_ref, shared_hbm,
-                   gates_ref, dgate_t_ref, out_hbm, dmix_hbm, mix_t_hbm, dw_hbm,
-                   mix_ref, mix_t_ref, dgate_ref, total_ref, grads_ref, down_ref, hidden_ref, dval_ref,
-                   grad_ref, shared_ref, first_ref, second_ref, result_ref, local_sem, *remote,
+def experts_kernel(mix_ref, mix_t_ref, cot_ref, gates_ref, router_ref, w_ref, shared_hbm,
+                   dgate_t_ref, out_hbm, dmix_hbm, dw_hbm, dgate_ref, total_ref, grads_ref, down_ref, hidden_ref, dval_ref,
+                   grad_ref, shared_ref, first_ref, second_ref, result_ref, extra_ref, local_sem, *remote,
                    tile, senders, core):
     step = pl.program_id(0)
     last = step == pl.num_programs(0) - 1
@@ -1548,12 +1570,16 @@
     far_send, far_receive, near_send, near_receive, keep_sem, *remote = remote
     gather = RowGather(shared_hbm, shared_ref, ((far_send, far_receive), (near_send, near_receive)))
     own_copy = pltpu.make_async_copy(shared_hbm, shared_ref.at[place], local_sem.at[0])
-    mix_copy = pltpu.make_async_copy(mix_t_ref, mix_t_hbm, local_sem.at[1])
     if core == 2:
         inbox, shared_in, send, receive, pair_sem = remote
         me = lax.axis_index("core")
         slot = lax.rem(step + me, 2)
         pair_copy = lambda k: push(grad_ref.at[1], inbox.at[k], (send, receive), k, {"core": 1 - me})
+        span = 3 * depth // 2
+        mine = pl.ds(pl.multiple_of(me * span, 16), span)
+        theirs = pl.ds(pl.multiple_of((1 - me) * span, 16), span)
+        shared_copy = push(extra_ref.at[theirs], shared_in, (send, receive), senders // 2,
+                           {"core": 1 - me})
         keep_copy = lambda k: pltpu.make_async_copy(
             inbox.at[k], dw_hbm.at[k, pl.ds(0, 3 * depth)], pair_sem.at[k]
         )
@@ -1574,17 +1600,6 @@
             pl.semaphore_signal(barrier, inc=1, device_id={"core": 1 - me}, device_id_type=MESH)
         pl.semaphore_wait(barrier, chips - 1 + core - 1)
         gather.start()
-        res = res_ref[...].astype(f32)
-        scale = lax.rsqrt(jnp.mean(res * res, axis=1, keepdims=True) + epsilon)
-        mix = (res * scale * gain_ref[...]).astype(bf16)
-        mix_ref[...] = mix
-        mix_t_ref[...] = mix.T
-        mix_copy.start()
-        chosen = chosen_ref[...] > 0.0
-        logits = dot_rows(mix, router_ref[...])
-        top = jnp.max(jnp.where(chosen, logits, -1e30), axis=1, keepdims=True)
-        weight = jnp.where(chosen, jnp.exp(jnp.where(chosen, logits - top, 0.0)), 0.0)
-        gates_ref[...] = weight / jnp.sum(weight, axis=1, keepdims=True)
         total_ref[...] = jnp.zeros_like(total_ref)
         grads_ref[...] = jnp.zeros_like(grads_ref)
         dgate_ref[...] = jnp.zeros_like(dgate_ref)
@@ -1595,17 +1610,19 @@
         def _():
             pair_copy((step - 2) // 2).wait_send()
 
+    kept_at = lambda k: 2 * lax.rem(k, 2)
+    buffer = jnp.where(slot == 1, 1, kept_at(step // 2)) if core == 2 else 0
+
     @pl.when(step < senders)
     def _():
         pair_grads(
-            step, slot, mix_ref, mix_t_ref, cot_ref, gates_ref, w_ref, dgate_ref, total_ref, grads_ref,
+            step, buffer, mix_ref, mix_t_ref, cot_ref, gates_ref, w_ref, dgate_ref, total_ref, grads_ref,
             down_ref, hidden_ref, dval_ref, grad_ref, tile
         )
 
     @pl.when(step == 1)
     def _():
         gather.relay()
-        mix_copy.wait()
 
     @pl.when(step == 2)
     def _():
@@ -1616,12 +1633,14 @@
         def _():
             pair_copy(step // 2).start()
 
-        @pl.when((step >= 1) & (slot == 1))
+        def add_sibling(at):
+            pair_copy(at).wait_recv()
+            inbox[at] = grad_ref[kept_at(at)] + inbox[at]
+            keep_copy(at).start()
+
+        @pl.when((step >= 2) & (slot == 0))
         def _():
-            at = (step - 1) // 2
-            pair_copy(at).wait_recv()
-            inbox[at] = grad_ref[0] + inbox[at]
-            keep_copy(at).start()
+            add_sibling((step - 2) // 2)
 
         @pl.when(last)
         def _():
@@ -1635,7 +1654,7 @@
             copy.start()
             copy.wait()
 
-    @pl.when(last)
+    @pl.when(step == 3)
     def _():
         wide = w_ref.shape[2]
         hid = wide // 2
@@ -1651,19 +1670,8 @@
             dval_ref[p, :, :hid] = (dh * value[:, hid:] * slope).astype(bf16)
             dval_ref[p, :, hid:] = (dh * act).astype(bf16)
             hidden_ref[:, p * hid : (p + 1) * hid] = hidden
-        result_ref[...] = (
-            total_ref[...] + dot_outer(hidden_ref[...], second_ref[...])
-        ).astype(bf16)
-        out_copy = pltpu.make_async_copy(result_ref, out_hbm, local_sem.at[2])
-        out_copy.start()
-        gates = gates_ref[...]
-        dgate = dgate_ref[...]
-        inside = jnp.sum(gates * dgate, axis=1, keepdims=True)
-        dlogits = (gates * (dgate - inside)).astype(bf16)
-        dmix = grads_ref[...] + dot_outer(dlogits, router_ref[...])
-        for p in range(2):
-            dmix = dmix + dot_outer(dval_ref[p], first_ref[p])
-        dgate_t_ref[...] = dgate.T[: dgate_t_ref.shape[0], :]
+        total_ref[...] += dot_outer(hidden_ref[...], second_ref[...])
+        grads_ref[...] += dot_outer(dval_ref[0], first_ref[0]) + dot_outer(dval_ref[1], first_ref[1])
         for k in range(3):
             if k < 2:
                 grad = dot_rows(mix_t_ref[...], dval_ref[k]).astype(bf16)
@@ -1671,23 +1679,21 @@
                 grad = dot_inner(cot_ref[...], hidden_ref[...]).astype(bf16)
             for j in range(senders):
                 at = (3 * ((j % core) * (senders // core) + j // core) + k) * wrows
-                grad_ref[0, at : at + wrows, :] = grad[j * wrows : (j + 1) * wrows]
-        span = 3 * depth // core
-        part = 3 * wrows
+                extra_ref[at : at + wrows, :] = grad[j * wrows : (j + 1) * wrows]
         if core == 2:
-            mine = pl.ds(pl.multiple_of(me * span, 16), span)
-            theirs = pl.ds(pl.multiple_of((1 - me) * span, 16), span)
-            shared_copy = push(grad_ref.at[0, theirs], shared_in, (send, receive), senders // 2,
-                               {"core": 1 - me})
             shared_copy.start()
-        mix_ref[...] = dmix.astype(bf16)
-        dmix_copy = pltpu.make_async_copy(mix_ref, dmix_hbm, local_sem.at[4])
-        dmix_copy.start()
-        copies = [out_copy, dmix_copy]
-        source = grad_ref.at[0]
+
+    @pl.when(last)
+    def _():
+        result_ref[...] = total_ref[...].astype(bf16)
+        out_copy = pltpu.make_async_copy(result_ref, out_hbm, local_sem.at[2])
+        out_copy.start()
+        copies = [out_copy]
+        part = 3 * (depth // senders)
+        source = extra_ref
         if core == 2:
             shared_copy.wait_recv()
-            shared_in[...] = shared_in[...] + grad_ref[0, mine, :]
+            shared_in[...] = shared_in[...] + extra_ref[mine, :]
             source = shared_in
         kept = senders // core
         for j in range(kept):
@@ -1695,7 +1701,18 @@
                 source.at[pl.ds(j * part, part)], dw_hbm.at[j, pl.ds(3 * depth, part)], keep_sem.at[j]
             ))
             copies[-1].start()
-        for copy in copies:
+        gates = gates_ref[...]
+        dgate = dgate_ref[...]
+        inside = jnp.sum(gates * dgate, axis=1, keepdims=True)
+        dlogits = (gates * (dgate - inside)).astype(bf16)
+        out_copy.wait()
+        result_ref[...] = (grads_ref[...] + dot_outer(dlogits, router_ref[...])).astype(bf16)
+        dmix_copy = pltpu.make_async_copy(result_ref, dmix_hbm, local_sem.at[4])
+        dmix_copy.start()
+        dgate_t_ref[...] = dgate.T[: dgate_t_ref.shape[0], :]
+        if core == 2:
+            pl.when(slot == 1)(lambda: add_sibling(senders // 2 - 1))
+        for copy in copies[1:] + [dmix_copy]:
             copy.wait()
         if core == 2:
             for k in range(kept):
@@ -1745,8 +1762,9 @@
         return 0
 
     lax.fori_loop(0, rows // tile, part, 0)
+    hidden_t = hidden_ref[...].T
     for c in range(chunks):
-        grad = dot_inner(hidden_ref[...], cot_ref[:, c * wide : (c + 1) * wide]).astype(bf16)
+        grad = dot_rows(hidden_t, cot_ref[:, c * wide : (c + 1) * wide]).astype(bf16)
         for p in range(2):
             first = p * deep + depth + c * hid
             grad_ref[slot, first : first + hid, :] = grad[p * hid : (p + 1) * hid]
@@ -1756,16 +1774,16 @@
         )
 
 
-def experts(residual, cot, gain, chosen, weights, router_at, experts_w, shared):
+def experts(mix, mix_t, cot, gates, weights, router_at, experts_w, shared):
     senders, deep, wide = experts_w.shape
-    rows, depth = residual.shape
+    rows, depth = mix.shape
     core, chips = lax.axis_size("core"), lax.axis_size(CHIPS)
     kept = senders // core
     kinds = 2 * senders + -2 * senders % 8
     shape = jax.ShapeDtypeStruct
     dma = pltpu.SemaphoreType.DMA
     once = lambda a: pl.BlockSpec(a.shape, lambda i: (0,) * a.ndim, pipeline_mode=pl.Buffered(1))
-    outs = [shape((rows, LANES), f32), shape((kinds, rows), f32)]
+    outs = [shape((kinds, rows), f32)]
     remote = []
     if core == 2:
         remote = [pltpu.VMEM((kept, deep, wide), bf16), pltpu.VMEM((deep // 2, wide), bf16),
@@ -1773,21 +1791,21 @@
     return pl.pallas_call(
         partial(experts_kernel, tile=rows, senders=senders, core=core),
         grid=(senders + 1,),
-        in_specs=[once(residual), once(cot), once(gain), once(chosen),
+        in_specs=[once(mix), once(mix_t), once(cot), once(gates),
                   pl.BlockSpec((depth, LANES), lambda i: (0, router_at // LANES)),
                   pl.BlockSpec((1, deep, wide), lambda i: (jnp.minimum(i, senders - 1), 0, 0)), HBM],
-        out_specs=[whole(o) for o in outs] + [HBM] * 4,
+        out_specs=[whole(o) for o in outs] + [HBM] * 3,
         out_shape=outs + [
-            shape((rows, depth), bf16), shape((rows, depth), bf16), shape((depth, rows), bf16),
+            shape((rows, depth), bf16), shape((rows, depth), bf16),
             shape((kept, deep + shared.shape[0], wide), bf16),
         ],
         scratch_shapes=[
-            pltpu.VMEM((rows, depth), bf16), pltpu.VMEM((depth, rows), bf16), pltpu.VMEM((rows, LANES), f32),
+            pltpu.VMEM((rows, LANES), f32),
             pltpu.VMEM((rows, depth), f32), pltpu.VMEM((rows, depth), f32),
             pltpu.VMEM((wide, depth), bf16), pltpu.VMEM((rows, wide), bf16),
-            pltpu.VMEM((2, rows, wide), bf16), pltpu.VMEM((core, deep, wide), bf16),
+            pltpu.VMEM((2, rows, wide), bf16), pltpu.VMEM((2 * core - 1, deep, wide), bf16),
             pltpu.VMEM((senders,) + shared.shape, bf16), pltpu.VMEM((2, depth, wide), bf16),
-            pltpu.VMEM((depth, wide), bf16), pltpu.VMEM((rows, depth), bf16), dma((5,)),
+            pltpu.VMEM((depth, wide), bf16), pltpu.VMEM((rows, depth), bf16), pltpu.VMEM((deep, wide), bf16), dma((5,)),
             dma((max(chips - 1, 1),)), dma((max(chips - 1, 1),)), dma((chips,)), dma((chips,)),
             dma((kept,)),
         ] + remote,
@@ -1796,7 +1814,7 @@
         ),
         cost_estimate=cost(7 * senders),
         name="experts",
-    )(residual, cot, gain, chosen, weights, experts_w, shared)
+    )(mix, mix_t, cot, gates, weights, experts_w, shared)
 
 
 def local(
@@ -1864,27 +1882,27 @@
     at_end = (seg_row == seg_row[-1]).astype(f32)[:, None]
     seg_col = seg_row[:, None]
     seg_line = seg_row[None]
-    gain_gate_f = gain_gate.astype(f32)[None, :]
-    (value, act, scaled, step, running, run_exp, within, mixer, state_in, packed, residual, scale_rows,
-     own_part, cot_full) = front(
-        mixed_ext, taps, same, bias, decay, at_end, link, seg_col, seg_line, skip, gain_gate_f, got,
-        cotangent, weights, inner, nstate, per, heads, di_all
-    )
-
     chosen = jnp.any(
         routes[:, :, None] == jnp.arange(LANES, dtype=jnp.int32)[None, None, :], axis=1
     ).astype(f32)
-    gates, dgate, out_part, dmix_part, mix_t, dw = experts(
-        residual, cot_full, gain_mid, chosen, weights, router_at, experts_w, shared_local
+    gain_gate_f = gain_gate.astype(f32)[None, :]
+    (value, act, scaled, step, running, run_exp, within, mixer, state_in, packed, residual, scale_rows,
+     own_part, cot_full, mix, mix_t, gates) = front(
+        mixed_ext, taps, same, bias, decay, at_end, link, seg_col, seg_line, skip, gain_gate_f, got,
+        cotangent, gain_mid, chosen, weights, inner, nstate, per, heads, di_all
+    )
+
+    dgate, out_part, dmix_part, dw = experts(
+        mix, mix_t, cot_full, gates, weights, router_at, experts_w, shared_local
     )
     expert_rows = scatter_chips(dw.reshape(-1, 2 * hid))
     dmixer, notes, gains_mid = turn_step(
         dmix_part, dgate, residual, cot_full, own_part, gain_mid
     )
 
-    value_grad, rear_main, dtaps, sums, small_sums, state_all, output = rear(
+    value_grad, rear_main, early, state_taps, state_all, output = rear(
         (dmixer, scale_rows, notes, mixer, within, act, scaled, step, running, run_exp, state_in, taps,
-         same, bias, decay, skip, gain_gate_f, at_end, link, seg_col, seg_line, packed[inner:],
+         same, bias, decay, skip, gain_gate_f, at_end, link, seg_col, seg_line, packed,
          mixed_t),
         out_part, value, weights, residual, inner, nstate, per, heads, di_all
     )
@@ -1893,10 +1911,6 @@
     rear_main, expert_rows = lax.optimization_barrier((rear_main, expert_rows))
     rear_main = scatter_chips(rear_main)
 
-    early = jnp.concatenate(
-        [dtaps[:, :inner], sums[:2], jnp.pad(small_sums[:2], ((0, 0), (0, inner - LANES)))], axis=0
-    )
-    state_taps = jnp.pad(dtaps[:, inner:], ((0, 8 - CONV), (0, 0)))
     grad_input, early, late, main = last_step(
         (value_grad, got, dmixer, gain_row, gains_mid, state_taps, early, mixed_t, mix_t, state_all,
          gates, notes),

time: 439 us -> 427 us (0.973)
  local copies, waits for them, and re-layouts: 20.9 us -> 16.3 us
  transfers between devices with their start and end apart: 5 -> 5, of which waited for: 2 -> 2; matrix products, arithmetic and copies ran while one was open for 5% -> 4% of each run, Pallas kernels for 69% -> 71%
where the time goes in v5:
time: 427 us; the launch traced here: 424 us
  Pallas kernels  370 us (87%)
  local copies, waits for them, and re-layouts  16.3 us (4%)
  between operations  14.4 us (3%)
  waiting for transfers between devices  13.3 us (3%)
  other arithmetic  7.25 us (2%)
    pallas_call x1, Pallas kernels, front(): pl.pallas_call(partial(front_kernel, inner=inner, nstate=nstate, per=per,...  98.3 us
    pallas_call x1, Pallas kernels, experts(): pl.pallas_call(partial(experts_kernel, tile=rows, senders=senders, core=c...  62.6 us
    pallas_call x1, Pallas kernels, turn_step(): pl.pallas_call(partial(turn_kernel, n=n), in_specs=[HBM] + [VMEM] * 5, ou...  58.1 us
    pallas_call x1, Pallas kernels, rear(): pl.pallas_call(partial(rear_kernel, inner=inner, nstate=nstate, per=per,...  53.8 us
    pallas_call x1, Pallas kernels, last_step(): pl.pallas_call(partial(last_kernel, n=n, count=count, boxes=len(boxes) -...  49.5 us
    pallas_call x1, Pallas kernels, intake(): pl.pallas_call(partial(intake_kernel, n=n), in_specs=[VMEM] * 2, out_spec...  39.4 us
    all_gather x2, waiting for transfers between devices, gather_rows(): return lax.all_gather(value, ROWS, axis=0, tiled=True)  10.1 us
  transfers between devices with their start and end apart: 5, of which 2 were waited for; matrix products, arithmetic and copies ran while one was open for 4% of the time, Pallas kernels for 71%

profile of v5, /device:TPU:0, one launch (start us, length us, event | category | flops | bytes accessed | tf_op | source)
XLA Modules:
  0.0 423.6 jit_solution(7175018765605270432)
XLA Ops:
  7.3 0.9 copy.99
  8.1 0.8 copy.100
  8.9 2.3 fusion.3
  11.4 0.8 copy-done.5
  12.3 1.0 copy-done.2
  14.0 2.8 reshape.130
  16.8 1.6 pad_maximum_fusion
  19.1 2.5 collective-permute-start
  22.9 0.7 broadcast_in_dim_reshape.3.skip_ref
  24.1 0.7 convert_element_type.45.chosen_ref
  26.5 0.7 pad_maximum_fusion.1.shared_hbm
  27.2 0.7 maximum_maximum_fusion.gains_ref
  27.9 39.4 %intake.1 = (bf16[528,1536]{1,0:T(8,128)(2,1)}, bf16[1536,512]{1,0:T(8,128)(2,1)}, bf16[512,1536]{1,0:T(8,128)(2,1)}, f32[16,1536]{1,0:T(8,128)}) custom-call(bf16[512,384]{1,0:T(8,128)(2,1)} %x_ref.1, bf16[16,384]{1,0:T(8,128)(2,1)} %maximum_maximum_fusion.gains_ref), custom_call_target="tpu_custom_call" | custom-call | flops 44999999488 | bytes 1048576 | tf_op jit(solution)/shard_map/intake/pallas_call | solution.py:664
  67.3 1.5 fusion.4
  69.7 2.1 compare_convert_fusion
  71.8 1.3 broadcast_in_dim.36.same_ref
  73.1 98.3 %front.1 = (f32[528,1920]{1,0:T(8,128)}, bf16[512,1024]{1,0:T(8,128)(2,1)}, bf16[512,768]{1,0:T(8,128)(2,1)}, f32[512,128]{1,0:T(8,128)}, f32[512,128]{1,0:T(8,1...) custom-call(bf16[528,1536]{1,0:T(8,128)(2,1)} %get-tuple-element.78., ...), custom_call_target="tpu_custom_call" | custom-call | flops 89999998976 | bytes 1048576 | tf_op jit(solution)/shard_map/front/pallas_call | solution.py:847
  171.4 10.1 %all-gather.5.cloned.1.call-done.w_ref = bf16[8,4608,256]{2,1,0:T(8,128)(2,1)} async-done(((bf16[1,4608,256]{2,1,0:T(8,128)(2,1)}), bf16[8,4608,256]{2,1,0:T(8,128)(2,1)}) %all-gather.5.cloned.1.call-update) | async-done | bytes 18874384 | tf_op jit(solution)/shard_map/all_gather | solution.py:65
  181.6 62.6 %experts.1 = (f32[16,512]{1,0:T(8,128)}, bf16[512,1536]{1,0:T(8,128)(2,1)}, bf16[512,1536]{1,0:T(8,128)(2,1)}, bf16[4,5184,256]{2,1,0:T(8,128)(2,1)}) custom-call(bf16[512,1536]{1,0:T(8,128)(2,1)} %get-tuple-element.81.mix_ref, bf16[1536,512]{1,0:T(8,128)(2,1)} %get-tuple-element.82.mix_t_ref, bf16[512,1536]{1,0:T(8,128)(2,1)} %get-tuple-element.83.cot_ref, ...), custom_call_target="tpu_custom_call" | custom-call | flops 50400002048 | bytes 1048576 | tf_op jit(solution)/shard_map/experts/pallas_call | solution.py:1791
  244.3 58.1 %turn_step.1 = (bf16[512,1536]{1,0:T(8,128)(2,1)}, f32[24,512]{1,0:T(8,128)}, f32[8,1536]{1,0:T(8,128)}) custom-call(bf16[512,1536]{1,0:T(8,128)(2,1)} %get-tuple-element.85.dmix_hbm, f32[16,512]{1,0:T(8,128)} %get-tuple-element.86.dgate_ref, bf16[512,1536]{1,0:T(8,128)(2,1)} %get-tuple-element.87.res_ref.res_hbm, ...), custom_call_target="tpu_custom_call" | custom-call | flops 54000001024 | bytes 1048576 | tf_op jit(solution)/shard_map/turn_step/pallas_call | solution.py:950
  302.4 53.8 %rear.1 = (bf16[512,1920]{1,0:T(8,128)(2,1)}, bf16[768,1536]{1,0:T(8,128)(2,1)}, f32[8,768]{1,0:T(8,128)}, f32[8,256]{1,0:T(8,128)}, bf16[512,256]{1,0:T(8,128)(2,1)}, /*index=5*/bf16[512,384]{1,0:T(8,128)(2,1)}) custom-call(bf16[512,1536]{1,0:T(8,128)(2,1)} %get-tuple-element.89.dout_ref.dres_ref, f32[8,512]{1,0:T(8,128)} %get-tuple-element.90.stat_ref, ...), custom_call_target="tpu_custom_call" | custom-call | flops 44999999488 | bytes 1048576 | tf_op jit(solution)/shard_map/rear/pallas_call | solution.py:1520
  356.3 49.5 %last_step.1 = (f32[512,384]{1,0:T(8,128)}, f32[8,768]{1,0:T(8,128)}, f32[8,640]{1,0:T(8,128)}, f32[192,1280]{1,0:T(8,128)}) custom-call(bf16[512,1920]{1,0:T(8,128)(2,1)} %get-tuple-element.105.grad_ref, bf16[512,1536]{1,0:T(8,128)(2,1)} %get-tuple-element.79.x_ref, bf16[512,1536]{1,0:T(8,128)(2,1)} %get-tuple-element.89.dout_ref.dres_ref, ...), custom_call_target="tpu_custom_call" | custom-call | flops 54000001024 | bytes 1048576 | tf_op jit(solution)/shard_map/last_step/pallas_call | solution.py:1109
  405.8 3.1 reduce-scatter.5.cloned.1.call-done.rear_ref
  408.9 7.9 %emit.1 = (bf16[512,384]{1,0:T(8,128)(2,1)}, f32[512,384]{1,0:T(8,128)}, f32[3,128]{1,0:T(4,128)}, f32[192,2,768]{2,1,0:T(2,128)}, f32[192,256]{1,0:T(8,128)}, /...) custom-call(bf16[512,384]{1,0:T(8,128)(2,1)} %get-tuple-element.104., ...), custom_call_target="tpu_custom_call" | custom-call | flops 7200000000 | bytes 1048576 | tf_op jit(solution)/shard_map/emit/pallas_call | solution.py:1191
  (75 shorter events, 6.0 us)
Async XLA Ops:
  7.2 17.7 %copy-start = (bf16[192,2,256]{2,1,0:T(2,128)(2,1)S(1)}, bf16[192,2,256]{2,1,0:T(2,128)(2,1)}, u32[]{:S(2)}) copy-start(bf16[192,2,256]{2,1,0:T(2,128)(2,1)} %param.35) | copy-start | bytes 589828
  7.2 64.6 %all-gather.3.cloned.1.call-start = ((), (), s32[]{:S(2)}) async-start(), calls=%async_computation.2 | async-start | bytes 9732096 | tf_op jit(solution)/shard_map/all_gather | solution.py:65
  8.9 2.4 copy-start.7
  11.2 1.0 copy-start.5
  11.3 2.0 copy-start.4
  12.2 1.0 copy-start.2
  13.3 168.3 %all-gather.5.cloned.1.call-start = ((), (), s32[]{:S(2)}) async-start(), calls=%async_computation.3 | async-start | bytes 21233664 | tf_op jit(solution)/shard_map/all_gather | solution.py:65
  18.3 0.7 copy-start.8
  18.3 3.9 copy-start.13
  18.3 3.9 copy-start.14
  18.3 3.9 copy-start.12
  18.3 4.5 %copy-start.15 = (f32[12]{0:T(128)S(1)}, f32[12]{0:T(128)}, u32[]{:S(2)}) copy-start(f32[12]{0:T(128)} %param.30) | copy-start | bytes 148
  18.3 5.2 %copy-start.9 = (s32[512,6]{0,1:T(8,128)S(1)}, s32[512,6]{0,1:T(8,128)}, u32[]{:S(2)}) copy-start(s32[512,6]{0,1:T(8,128)} %param.40) | copy-start | bytes 36868
  18.4 7.0 %copy-start.16 = (f32[12]{0:T(128)S(1)}, f32[12]{0:T(128)}, u32[]{:S(2)}) copy-start(f32[12]{0:T(128)} %param.29) | copy-start | bytes 148
  18.4 7.0 %copy-start.17 = (f32[12]{0:T(128)S(1)}, f32[12]{0:T(128)}, u32[]{:S(2)}) copy-start(f32[12]{0:T(128)} %param.28) | copy-start | bytes 148
  18.4 7.5 %copy-start.10 = (bf16[4,768]{1,0:T(4,128)(2,1)S(1)}, bf16[4,768]{1,0:T(4,128)(2,1)}, u32[]{:S(2)}) copy-start(bf16[4,768]{1,0:T(4,128)(2,1)} %param.26) | copy-start | bytes 18436
  18.4 7.5 %copy-start.11 = (bf16[4,256]{1,0:T(4,128)(2,1)S(1)}, bf16[4,256]{1,0:T(4,128)(2,1)}, u32[]{:S(2)}) copy-start(bf16[4,256]{1,0:T(4,128)(2,1)} %param.27) | copy-start | bytes 6148
  18.4 8.1 %copy-start.6 = (bf16[192,256]{1,0:T(8,128)(2,1)S(1)}, bf16[192,256]{1,0:T(8,128)(2,1)}, u32[]{:S(2)}) copy-start(bf16[192,256]{1,0:T(8,128)(2,1)} %param.36) | copy-start | bytes 294916
  18.4 337.8 %reduce-scatter.3.cloned.1.call-start = ((), (), s32[]{:S(2)}) async-start(), calls=%async_computation.4 | async-start | bytes 13271040 | tf_op jit(solution)/shard_map/reduce_scatter | solution.py:74
  19.1 49.7 %collective-permute-start = (s32[3]{0:T(128)S(1)}, s32[3]{0:T(128)S(1)}, u32[]{:S(2)}, u32[]{:S(2)}) collective-permute-start(s32[3]{0:T(128)S(1)} %slice_bitcast_fusion), channel_id=1, source_target_pairs={{0,4},{4,8},{8,12},{1,5},{5,9},{9,13},{2,6},{6,10},{10,14},{3,7},{... | collective-permute-start | bytes 44 | tf_op jit(solution)/shard_map/ppermute | solution.py:45
  25.2 44.5 %copy-start.3 = (s32[512,1]{1,0:T(8,128)}, s32[512,1]{1,0:T(8,128)S(1)}, u32[]{:S(2)}) copy-start(s32[512,1]{1,0:T(8,128)S(1)} %copy.93.seg_col_ref) | copy-start | bytes 6148
  244.2 164.6 %reduce-scatter.5.cloned.1.call-start = ((), (), s32[]{:S(2)}) async-start(), calls=%async_computation.5 | async-start | bytes 2949120 | tf_op jit(solution)/shard_map/reduce_scatter | solution.py:74
  408.8 8.0 %copy-start.1 = (bf16[192,2,256]{2,1,0:T(2,128)(2,1)S(1)}, bf16[192,2,256]{2,1,0:T(2,128)(2,1)}, u32[]{:S(2)}) copy-start(bf16[192,2,256]{2,1,0:T(2,128)(2,1)} %param.35) | copy-start | bytes 589828
Sparse Core Ops, SparseCore 0:
  13.4 58.3 all-gather.2
  74.2 107.3 all-gather.4
  244.3 108.1 reduce-scatter.2
  356.4 52.3 reduce-scatter.4

commit v6 on v5

--- a/solution.py
+++ b/solution.py
@@ -1022,12 +1022,15 @@
         if k == 0:
             for line in lines:
                 line.step(0)
+            weights.product(mixed_t_ref, grad_ref.at[:, pl.ds(inner, inner)], 0)
+            weights.to_sibling(0, inner)
         normed = x_ref[:, theirs].astype(f32) * scale
         cross = cross + row_sums(block * normed * gain_ref[:, theirs])
         gains_box[d] = jnp.where(
             row_iota((8, quarter)) == 0, jnp.sum(block * normed, axis=0, keepdims=True),
             mid_ref[:, theirs],
         )
+    weights.to_chips(0)
     cross_box[...] = cross
     sums = []
     for d in range(1, n):
@@ -1048,15 +1051,12 @@
     ).T
     inside = jnp.sum(gates * moved, axis=1, keepdims=True)
     first = 2 * inner
-    weights.product(mixed_t_ref, grad_ref.at[:, pl.ds(inner, inner)], 0)
-    weights.to_sibling(0, inner)
     for line in lines:
         line.step(1)
     weights.product(mixed_t_ref, state_all_ref, inner)
     weights.product(mixed_t_ref, grad_ref.at[:, pl.ds(last, LANES)], inner + last - first)
     weights.product(mix_t_ref, (gates * (moved - inside)).astype(bf16), inner + wide - first)
     weights.to_sibling(inner, wide - first + LANES)
-    weights.to_chips(0)
     for copy in sums + states:
         copy.wait_recv()
     gains = gains_box[me]
@@ -1127,9 +1127,9 @@
     )(*vmem_args, weights)
 
 
-def emit_kernel(out_ref, grad_ref, early_ref, late_ref, rear_ref, main_ref, pair_ref, *outs, per):
+def emit_kernel(out_ref, grad_ref, early_ref, late_ref, rear_ref, main_ref, *outs, per):
     (out, grad, gain_in, pair_out, state_out, step_out, conv, conv_state, bias, decay, skip, gate, proj,
-     gain_mid, router, shared_up, shared_down, gates, down) = outs
+     gain_mid, router) = outs
     out[...] = out_ref[...]
     grad[...] = grad_ref[...]
     taps, inner = conv.shape
@@ -1155,6 +1155,9 @@
     state_out[...] = main_ref[:, inner:last].astype(f32)
     step_out[...] = main_ref[:, last:wide].astype(f32).T[:heads, :]
     router[...] = main_ref[:, wide:].astype(f32).T[: router.shape[0], :]
+
+
+def emit_experts_kernel(pair_ref, shared_up, shared_down, gates, down):
     hid, depth = down.shape[1:]
     wides = 2 * hid
     deep = depth + depth // 2
@@ -1174,29 +1177,42 @@
     shared_down[...] = pair_ref[2 * deep + 2 * wrows :, :].astype(f32)
 
 
-def emit(args, inner, nstate, per, heads, kinds, hid):
-    out, grad, _, _, _, main, pair = args
+def emit(args, inner, nstate, per, heads, kinds):
+    out, grad, _, _, _, main = args
     tokens, quarter = grad.shape
     wrows = main.shape[0]
-    depth = pair.shape[0] // 3 - wrows
-    wide = pair.shape[1]
     flat = lambda *size: jax.ShapeDtypeStruct(size, f32)
     outs = [
         jax.ShapeDtypeStruct(out.shape, bf16), flat(tokens, quarter), flat(quarter // LANES, LANES),
         flat(wrows, 2, inner), flat(wrows, 2 * nstate), flat(heads, wrows), flat(CONV, inner),
         flat(CONV, 2 * nstate), flat(1, heads), flat(1, heads), flat(1, heads),
         flat(inner // LANES, LANES), flat(wrows, inner), flat(quarter // LANES, LANES), flat(kinds, wrows),
-        flat(wrows, 2, wide), flat(wrows, wide), flat(2 * depth, 2, hid), flat(2, hid, depth),
     ]
     return pl.pallas_call(
         partial(emit_kernel, per=per),
-        in_specs=[VMEM] * 7,
+        in_specs=[VMEM] * 6,
         out_specs=[VMEM] * len(outs),
         out_shape=outs,
         compiler_params=BIG,
-        cost_estimate=cost(8),
+        cost_estimate=cost(4),
         name="emit",
     )(*args)
+
+
+def emit_experts(pair, wrows, hid):
+    depth = pair.shape[0] // 3 - wrows
+    wide = pair.shape[1]
+    flat = lambda *size: jax.ShapeDtypeStruct(size, f32)
+    outs = [flat(wrows, 2, wide), flat(wrows, wide), flat(2 * depth, 2, hid), flat(2, hid, depth)]
+    return pl.pallas_call(
+        emit_experts_kernel,
+        in_specs=[VMEM],
+        out_specs=[VMEM] * len(outs),
+        out_shape=outs,
+        compiler_params=BIG,
+        cost_estimate=cost(5),
+        name="emit_experts",
+    )(pair)
 
 
 def back_part(dout_ref, w_ref, mixer_ref, value_ref, act_ref, run_exp_ref, link_ref, gain_ref,
@@ -1918,10 +1934,11 @@
     )
     if lax.axis_size("core") != 2:
         main = scatter_chips(main)
+    expert_rows, main = lax.optimization_barrier((expert_rows, main))
+    grad_shared, grad_shared_down, grad_gates, grad_down = emit_experts(expert_rows, wrows, hid)
     (output, grad_input, grad_gain_in, grad_main, grad_state, grad_step, grad_conv, grad_conv_state,
-     grad_bias, grad_decay, grad_skip, grad_gate, grad_proj_out, grad_gain_mid, grad_router, grad_shared,
-     grad_shared_down, grad_gates, grad_down) = emit(
-        (output, grad_input, early, late, rear_main, main, expert_rows), inner, nstate, per, heads, experts_all, hid
+     grad_bias, grad_decay, grad_skip, grad_gate, grad_proj_out, grad_gain_mid, grad_router) = emit(
+        (output, grad_input, early, late, rear_main, main), inner, nstate, per, heads, experts_all
     )
     return (
         output,

time: 427 us -> 426 us (level)
    pallas_call x1 -> x2, Pallas kernels: 7.95 us -> 9.59 us  [the longest x1 5.88 us: emit_experts(): pl.pallas_call(emit_experts_kernel, in_specs=[VMEM], out_specs=[VMEM] * l...]
  transfers between devices with their start and end apart: 5 -> 5, of which waited for: 2 -> 1; matrix products, arithmetic and copies ran while one was open for 4% -> 4% of each run, Pallas kernels for 71% -> 72%
where the time goes in v6:
time: 426 us; the launch traced here: 422 us
  Pallas kernels  372 us (87%)
  local copies, waits for them, and re-layouts  16.3 us (4%)
  between operations  14.4 us (3%)
  waiting for transfers between devices  10.2 us (2%)
  other arithmetic  7.25 us (2%)
    pallas_call x1, Pallas kernels, front(): pl.pallas_call(partial(front_kernel, inner=inner, nstate=nstate, per=per,...  98.3 us
    pallas_call x1, Pallas kernels, experts(): pl.pallas_call(partial(experts_kernel, tile=rows, senders=senders, core=c...  62.6 us
    pallas_call x1, Pallas kernels, turn_step(): pl.pallas_call(partial(turn_kernel, n=n), in_specs=[HBM] + [VMEM] * 5, ou...  58.1 us
    pallas_call x1, Pallas kernels, rear(): pl.pallas_call(partial(rear_kernel, inner=inner, nstate=nstate, per=per,...  53.7 us
    pallas_call x1, Pallas kernels, last_step(): pl.pallas_call(partial(last_kernel, n=n, count=count, boxes=len(boxes) -...  49.8 us
    pallas_call x1, Pallas kernels, intake(): pl.pallas_call(partial(intake_kernel, n=n), in_specs=[VMEM] * 2, out_spec...  39.4 us
    all_gather x2, waiting for transfers between devices, gather_rows(): return lax.all_gather(value, ROWS, axis=0, tiled=True)  10.1 us
  transfers between devices with their start and end apart: 5, of which 1 were waited for; matrix products, arithmetic and copies ran while one was open for 4% of the time, Pallas kernels for 72%

profile of v6, /device:TPU:0, one launch (start us, length us, event | category | flops | bytes accessed | tf_op | source)
XLA Modules:
  0.0 422.4 jit_solution(7999914762541402447)
XLA Ops:
  7.3 0.9 copy.99
  8.1 0.8 copy.100
  8.9 2.3 fusion.3
  11.4 0.8 copy-done.5
  12.3 1.0 copy-done.2
  14.0 2.8 reshape.130
  16.8 1.6 pad_maximum_fusion
  19.1 2.5 collective-permute-start
  22.9 0.7 broadcast_in_dim_reshape.3.skip_ref
  24.1 0.7 convert_element_type.45.chosen_ref
  26.5 0.7 pad_maximum_fusion.1.shared_hbm
  27.2 0.7 maximum_maximum_fusion.gains_ref
  27.9 39.4 %intake.1 = (bf16[528,1536]{1,0:T(8,128)(2,1)}, bf16[1536,512]{1,0:T(8,128)(2,1)}, bf16[512,1536]{1,0:T(8,128)(2,1)}, f32[16,1536]{1,0:T(8,128)}) custom-call(bf16[512,384]{1,0:T(8,128)(2,1)} %x_ref.1, bf16[16,384]{1,0:T(8,128)(2,1)} %maximum_maximum_fusion.gains_ref), custom_call_target="tpu_custom_call" | custom-call | flops 44999999488 | bytes 1048576 | tf_op jit(solution)/shard_map/intake/pallas_call | solution.py:664
  67.3 1.5 fusion.4
  69.6 2.1 compare_convert_fusion
  71.8 1.3 broadcast_in_dim.36.same_ref
  73.1 98.3 %front.1 = (f32[528,1920]{1,0:T(8,128)}, bf16[512,1024]{1,0:T(8,128)(2,1)}, bf16[512,768]{1,0:T(8,128)(2,1)}, f32[512,128]{1,0:T(8,128)}, f32[512,128]{1,0:T(8,1...) custom-call(bf16[528,1536]{1,0:T(8,128)(2,1)} %get-tuple-element.80., ...), custom_call_target="tpu_custom_call" | custom-call | flops 89999998976 | bytes 1048576 | tf_op jit(solution)/shard_map/front/pallas_call | solution.py:847
  171.4 10.1 %all-gather.5.cloned.1.call-done.w_ref = bf16[8,4608,256]{2,1,0:T(8,128)(2,1)} async-done(((bf16[1,4608,256]{2,1,0:T(8,128)(2,1)}), bf16[8,4608,256]{2,1,0:T(8,128)(2,1)}) %all-gather.5.cloned.1.call-update) | async-done | bytes 18874384 | tf_op jit(solution)/shard_map/all_gather | solution.py:65
  181.6 62.6 %experts.1 = (f32[16,512]{1,0:T(8,128)}, bf16[512,1536]{1,0:T(8,128)(2,1)}, bf16[512,1536]{1,0:T(8,128)(2,1)}, bf16[4,5184,256]{2,1,0:T(8,128)(2,1)}) custom-call(bf16[512,1536]{1,0:T(8,128)(2,1)} %get-tuple-element.83.mix_ref, bf16[1536,512]{1,0:T(8,128)(2,1)} %get-tuple-element.84.mix_t_ref, bf16[512,1536]{1,0:T(8,128)(2,1)} %get-tuple-element.85.cot_ref, ...), custom_call_target="tpu_custom_call" | custom-call | flops 50400002048 | bytes 1048576 | tf_op jit(solution)/shard_map/experts/pallas_call | solution.py:1807
  244.3 58.1 %turn_step.1 = (bf16[512,1536]{1,0:T(8,128)(2,1)}, f32[24,512]{1,0:T(8,128)}, f32[8,1536]{1,0:T(8,128)}) custom-call(bf16[512,1536]{1,0:T(8,128)(2,1)} %get-tuple-element.87.dmix_hbm, f32[16,512]{1,0:T(8,128)} %get-tuple-element.88.dgate_ref, bf16[512,1536]{1,0:T(8,128)(2,1)} %get-tuple-element.89.res_ref.res_hbm, ...), custom_call_target="tpu_custom_call" | custom-call | flops 54000001024 | bytes 1048576 | tf_op jit(solution)/shard_map/turn_step/pallas_call | solution.py:950
  302.4 53.7 %rear.1 = (bf16[512,1920]{1,0:T(8,128)(2,1)}, bf16[768,1536]{1,0:T(8,128)(2,1)}, f32[8,768]{1,0:T(8,128)}, f32[8,256]{1,0:T(8,128)}, bf16[512,256]{1,0:T(8,128)(2,1)}, /*index=5*/bf16[512,384]{1,0:T(8,128)(2,1)}) custom-call(bf16[512,1536]{1,0:T(8,128)(2,1)} %get-tuple-element.91.dout_ref.dres_ref, f32[8,512]{1,0:T(8,128)} %get-tuple-element.92.stat_ref, ...), custom_call_target="tpu_custom_call" | custom-call | flops 44999999488 | bytes 1048576 | tf_op jit(solution)/shard_map/rear/pallas_call | solution.py:1536
  356.2 49.8 %last_step.1 = (f32[512,384]{1,0:T(8,128)}, f32[8,768]{1,0:T(8,128)}, f32[8,640]{1,0:T(8,128)}, f32[192,1280]{1,0:T(8,128)}) custom-call(bf16[512,1920]{1,0:T(8,128)(2,1)} %get-tuple-element.107.grad_ref, bf16[512,1536]{1,0:T(8,128)(2,1)} %get-tuple-element.81.x_ref, bf16[512,1536]{1,0:T(8,128)(2,1)} %get-tuple-element.91.dout_ref.dres_ref, ...), custom_call_target="tpu_custom_call" | custom-call | flops 54000001024 | bytes 1048576 | tf_op jit(solution)/shard_map/last_step/pallas_call | solution.py:1109
  406.0 5.9 %emit_experts.1 = (f32[192,2,256]{2,1,0:T(2,128)}, f32[192,256]{1,0:T(8,128)}, f32[3072,2,128]{2,1,0:T(2,128)}, f32[2,128,1536]{2,1,0:T(8,128)}) custom-call(bf16[5184,256]{1,0:T(8,128)(2,1)} %reduce-scatter.3.cloned.1.call-done.pair_ref), custom_call_target="tpu_custom_call" | custom-call | flops 4499999744 | bytes 1048576 | tf_op jit(solution)/shard_map/emit_experts/pallas_call | solution.py:1207
  411.9 3.7 emit.1
  (76 shorter events, 6.0 us)
Async XLA Ops:
  7.2 17.7 %copy-start = (bf16[192,2,256]{2,1,0:T(2,128)(2,1)S(1)}, bf16[192,2,256]{2,1,0:T(2,128)(2,1)}, u32[]{:S(2)}) copy-start(bf16[192,2,256]{2,1,0:T(2,128)(2,1)} %param.35) | copy-start | bytes 589828
  7.2 64.6 %all-gather.3.cloned.1.call-start = ((), (), s32[]{:S(2)}) async-start(), calls=%async_computation.2 | async-start | bytes 9732096 | tf_op jit(solution)/shard_map/all_gather | solution.py:65
  8.9 2.4 copy-start.7
  11.2 1.0 copy-start.5
  11.3 2.0 copy-start.4
  12.2 1.0 copy-start.2
  13.3 168.3 %all-gather.5.cloned.1.call-start = ((), (), s32[]{:S(2)}) async-start(), calls=%async_computation.3 | async-start | bytes 21233664 | tf_op jit(solution)/shard_map/all_gather | solution.py:65
  18.3 0.7 copy-start.8
  18.3 3.9 copy-start.13
  18.3 3.9 copy-start.14
  18.3 3.9 copy-start.12
  18.3 4.5 %copy-start.15 = (f32[12]{0:T(128)S(1)}, f32[12]{0:T(128)}, u32[]{:S(2)}) copy-start(f32[12]{0:T(128)} %param.30) | copy-start | bytes 148
  18.3 5.2 %copy-start.9 = (s32[512,6]{0,1:T(8,128)S(1)}, s32[512,6]{0,1:T(8,128)}, u32[]{:S(2)}) copy-start(s32[512,6]{0,1:T(8,128)} %param.40) | copy-start | bytes 36868
  18.4 7.0 %copy-start.16 = (f32[12]{0:T(128)S(1)}, f32[12]{0:T(128)}, u32[]{:S(2)}) copy-start(f32[12]{0:T(128)} %param.29) | copy-start | bytes 148
  18.4 7.0 %copy-start.17 = (f32[12]{0:T(128)S(1)}, f32[12]{0:T(128)}, u32[]{:S(2)}) copy-start(f32[12]{0:T(128)} %param.28) | copy-start | bytes 148
  18.4 7.5 %copy-start.10 = (bf16[4,768]{1,0:T(4,128)(2,1)S(1)}, bf16[4,768]{1,0:T(4,128)(2,1)}, u32[]{:S(2)}) copy-start(bf16[4,768]{1,0:T(4,128)(2,1)} %param.26) | copy-start | bytes 18436
  18.4 7.5 %copy-start.11 = (bf16[4,256]{1,0:T(4,128)(2,1)S(1)}, bf16[4,256]{1,0:T(4,128)(2,1)}, u32[]{:S(2)}) copy-start(bf16[4,256]{1,0:T(4,128)(2,1)} %param.27) | copy-start | bytes 6148
  18.4 8.1 %copy-start.6 = (bf16[192,256]{1,0:T(8,128)(2,1)S(1)}, bf16[192,256]{1,0:T(8,128)(2,1)}, u32[]{:S(2)}) copy-start(bf16[192,256]{1,0:T(8,128)(2,1)} %param.36) | copy-start | bytes 294916
  18.4 337.7 %reduce-scatter.3.cloned.1.call-start = ((), (), s32[]{:S(2)}) async-start(), calls=%async_computation.4 | async-start | bytes 13271040 | tf_op jit(solution)/shard_map/reduce_scatter | solution.py:74
  19.1 49.7 %collective-permute-start = (s32[3]{0:T(128)S(1)}, s32[3]{0:T(128)S(1)}, u32[]{:S(2)}, u32[]{:S(2)}) collective-permute-start(s32[3]{0:T(128)S(1)} %slice_bitcast_fusion), channel_id=1, source_target_pairs={{0,4},{4,8},{8,12},{1,5},{5,9},{9,13},{2,6},{6,10},{10,14},{3,7},{... | collective-permute-start | bytes 44 | tf_op jit(solution)/shard_map/ppermute | solution.py:45
  25.2 44.5 %copy-start.3 = (s32[512,1]{1,0:T(8,128)}, s32[512,1]{1,0:T(8,128)S(1)}, u32[]{:S(2)}) copy-start(s32[512,1]{1,0:T(8,128)S(1)} %copy.93.seg_col_ref) | copy-start | bytes 6148
  244.2 167.7 %reduce-scatter.5.cloned.1.call-start = ((), (), s32[]{:S(2)}) async-start(), calls=%async_computation.5 | async-start | bytes 2949120 | tf_op jit(solution)/shard_map/reduce_scatter | solution.py:74
  411.9 3.7 copy-start.1
Sparse Core Ops, SparseCore 0:
  13.4 58.3 all-gather.2
  74.2 107.3 all-gather.4
  244.3 108.1 reduce-scatter.2
  356.3 52.4 reduce-scatter.4

commit v7 on v6

--- a/solution.py
+++ b/solution.py
@@ -325,13 +325,15 @@
     pl.semaphore_wait(barrier, n - 1 + count - 1)
 
 
-def rows_barrier(me, n):
+def rows_barrier(me, n, meanwhile=lambda: None):
     barrier = line_barrier(me, n)
     place, count = row_place(), lax.axis_size(ROWS)
     for d in range(1, count):
         pl.semaphore_signal(barrier, inc=1, device_id=row_peer(lax.rem(place + d, count)),
                             device_id_type=MESH)
+    result = meanwhile()
     pl.semaphore_wait(barrier, n - 1 + count - 1)
+    return result
 
 
 class RowGather:
@@ -1002,10 +1004,13 @@
     row_groups = [(sems[6 + 2 * i], sems[7 + 2 * i]) for i in range(2)]
     load = pltpu.make_async_copy(w_hbm.at[:, pl.ds(0, wide)], w_ref, load_sem)
     load.start()
-    rows_barrier(me, n)
+
+    def row_scale():
+        x = x_ref[...].astype(f32)
+        return lax.rsqrt(jnp.mean(x * x, axis=1, keepdims=True) + epsilon)
+
+    scale = rows_barrier(me, n, row_scale)
     copies, states, lates = [], [], []
-    x = x_ref[...].astype(f32)
-    scale = lax.rsqrt(jnp.mean(x * x, axis=1, keepdims=True) + epsilon)
     load.wait()
     half = rows // 2
     lines = [
@@ -1423,16 +1428,21 @@
     far_ref[...] = jnp.zeros_like(far_ref)
     state_halo[...] = jnp.zeros_like(state_halo)
     signal_halo[...] = jnp.zeros_like(signal_halo)
-    rows_barrier(me, n)
+
+    def prepare():
+        run_t = run_ref[...].T
+        for h in range(heads):
+            run_t_ref[h] = run_t[h : h + 1, :]
+        gates = notes_ref.shape[0] - 8
+        return row_columns(stat_ref[0:1, :]), row_columns(notes_ref[gates : gates + 1, :])
+
+    scale, cross = rows_barrier(me, n, prepare)
     line = LineReduce(me, n, lambda d: part_ref.at[:, column(d)], right_box, left_box,
                       line_groups(sems[8:12]))
     loads[0].wait()
     line.step(0)
     for copy in loads[1:]:
         copy.wait()
-    scale = row_columns(stat_ref[0:1, :])
-    gates = notes_ref.shape[0] - 8
-    cross = row_columns(notes_ref[gates : gates + 1, :])
     back_part(dout_ref, w_ref, mixer_ref, value_ref, act_ref, run_exp_ref, link_ref, gain_ref,
               scale, cross, packed_ref, heads_ref, zgrad_ref, gated_ref, direct_ref, sums_ref,
               inner=inner, nstate=nstate, di_all=di_all)
@@ -1443,9 +1453,6 @@
     weights.product(mixed_t_ref, zgrad_ref, inner)
     weights.to_sibling(inner, inner)
     line.step(1)
-    run_t = run_ref[...].T
-    for h in range(heads):
-        run_t_ref[h] = run_t[h : h + 1, :]
     intra_back_part(heads_ref, act_ref, scaled_ref, run_t_ref, run_exp_ref, seg_col_ref, seg_row_ref,
                     dscaled_ref, dstate_ref, drun_ref, scores_ref, dscores_ref,
                     inner=inner, nstate=nstate, per=per, block=128)

time: 426 us -> 425 us (level)
  no operation moved by 1% of the time
where the time goes in v7:
time: 425 us; the launch traced here: 422 us
  Pallas kernels  371 us (87%)
  local copies, waits for them, and re-layouts  16.3 us (4%)
  between operations  14.4 us (3%)
  waiting for transfers between devices  10.2 us (2%)
  other arithmetic  7.24 us (2%)
    pallas_call x1, Pallas kernels, front(): pl.pallas_call(partial(front_kernel, inner=inner, nstate=nstate, per=per,...  98.3 us
    pallas_call x1, Pallas kernels, experts(): pl.pallas_call(partial(experts_kernel, tile=rows, senders=senders, core=c...  62.6 us
    pallas_call x1, Pallas kernels, turn_step(): pl.pallas_call(partial(turn_kernel, n=n), in_specs=[HBM] + [VMEM] * 5, ou...  58.1 us
    pallas_call x1, Pallas kernels, rear(): pl.pallas_call(partial(rear_kernel, inner=inner, nstate=nstate, per=per,...  53.4 us
    pallas_call x1, Pallas kernels, last_step(): pl.pallas_call(partial(last_kernel, n=n, count=count, boxes=len(boxes) -...  49.6 us
    pallas_call x1, Pallas kernels, intake(): pl.pallas_call(partial(intake_kernel, n=n), in_specs=[VMEM] * 2, out_spec...  39.4 us
    all_gather x2, waiting for transfers between devices, gather_rows(): return lax.all_gather(value, ROWS, axis=0, tiled=True)  10.1 us
  transfers between devices with their start and end apart: 5, of which 1 were waited for; matrix products, arithmetic and copies ran while one was open for 4% of the time, Pallas kernels for 72%

profile of v7, /device:TPU:0, one launch (start us, length us, event | category | flops | bytes accessed | tf_op | source)
XLA Modules:
  0.0 421.9 jit_solution(18147866627758302610)
XLA Ops:
  7.3 0.9 copy.99
  8.1 0.8 copy.100
  8.9 2.3 fusion.3
  11.4 0.8 copy-done.5
  12.3 1.0 copy-done.2
  14.0 2.8 reshape.130
  16.8 1.6 pad_maximum_fusion
  19.1 2.6 collective-permute-start
  23.0 0.7 broadcast_in_dim_reshape.3.skip_ref
  24.3 0.7 convert_element_type.45.chosen_ref
  26.6 0.7 pad_maximum_fusion.1.shared_hbm
  27.4 0.7 maximum_maximum_fusion.gains_ref
  28.0 39.4 %intake.1 = (bf16[528,1536]{1,0:T(8,128)(2,1)}, bf16[1536,512]{1,0:T(8,128)(2,1)}, bf16[512,1536]{1,0:T(8,128)(2,1)}, f32[16,1536]{1,0:T(8,128)}) custom-call(bf16[512,384]{1,0:T(8,128)(2,1)} %x_ref.1, bf16[16,384]{1,0:T(8,128)(2,1)} %maximum_maximum_fusion.gains_ref), custom_call_target="tpu_custom_call" | custom-call | flops 44999999488 | bytes 1048576 | tf_op jit(solution)/shard_map/intake/pallas_call | solution.py:666
  67.4 1.5 fusion.4
  69.8 2.1 compare_convert_fusion
  71.9 1.3 broadcast_in_dim.36.same_ref
  73.2 98.3 %front.1 = (f32[528,1920]{1,0:T(8,128)}, bf16[512,1024]{1,0:T(8,128)(2,1)}, bf16[512,768]{1,0:T(8,128)(2,1)}, f32[512,128]{1,0:T(8,128)}, f32[512,128]{1,0:T(8,1...) custom-call(bf16[528,1536]{1,0:T(8,128)(2,1)} %get-tuple-element.80., ...), custom_call_target="tpu_custom_call" | custom-call | flops 89999998976 | bytes 1048576 | tf_op jit(solution)/shard_map/front/pallas_call | solution.py:849
  171.5 10.1 %all-gather.5.cloned.1.call-done.w_ref = bf16[8,4608,256]{2,1,0:T(8,128)(2,1)} async-done(((bf16[1,4608,256]{2,1,0:T(8,128)(2,1)}), bf16[8,4608,256]{2,1,0:T(8,128)(2,1)}) %all-gather.5.cloned.1.call-update) | async-done | bytes 18874384 | tf_op jit(solution)/shard_map/all_gather | solution.py:65
  181.6 62.6 %experts.1 = (f32[16,512]{1,0:T(8,128)}, bf16[512,1536]{1,0:T(8,128)(2,1)}, bf16[512,1536]{1,0:T(8,128)(2,1)}, bf16[4,5184,256]{2,1,0:T(8,128)(2,1)}) custom-call(bf16[512,1536]{1,0:T(8,128)(2,1)} %get-tuple-element.83.mix_ref, bf16[1536,512]{1,0:T(8,128)(2,1)} %get-tuple-element.84.mix_t_ref, bf16[512,1536]{1,0:T(8,128)(2,1)} %get-tuple-element.85.cot_ref, ...), custom_call_target="tpu_custom_call" | custom-call | flops 50400002048 | bytes 1048576 | tf_op jit(solution)/shard_map/experts/pallas_call | solution.py:1814
  244.3 58.1 %turn_step.1 = (bf16[512,1536]{1,0:T(8,128)(2,1)}, f32[24,512]{1,0:T(8,128)}, f32[8,1536]{1,0:T(8,128)}) custom-call(bf16[512,1536]{1,0:T(8,128)(2,1)} %get-tuple-element.87.dmix_hbm, f32[16,512]{1,0:T(8,128)} %get-tuple-element.88.dgate_ref, bf16[512,1536]{1,0:T(8,128)(2,1)} %get-tuple-element.89.res_ref.res_hbm, ...), custom_call_target="tpu_custom_call" | custom-call | flops 54000001024 | bytes 1048576 | tf_op jit(solution)/shard_map/turn_step/pallas_call | solution.py:952
  302.5 53.4 %rear.1 = (bf16[512,1920]{1,0:T(8,128)(2,1)}, bf16[768,1536]{1,0:T(8,128)(2,1)}, f32[8,768]{1,0:T(8,128)}, f32[8,256]{1,0:T(8,128)}, bf16[512,256]{1,0:T(8,128)(2,1)}, /*index=5*/bf16[512,384]{1,0:T(8,128)(2,1)}) custom-call(bf16[512,1536]{1,0:T(8,128)(2,1)} %get-tuple-element.91.dout_ref.dres_ref, f32[8,512]{1,0:T(8,128)} %get-tuple-element.92.stat_ref, ...), custom_call_target="tpu_custom_call" | custom-call | flops 44999999488 | bytes 1048576 | tf_op jit(solution)/shard_map/rear/pallas_call | solution.py:1543
  356.0 49.6 %last_step.1 = (f32[512,384]{1,0:T(8,128)}, f32[8,768]{1,0:T(8,128)}, f32[8,640]{1,0:T(8,128)}, f32[192,1280]{1,0:T(8,128)}) custom-call(bf16[512,1920]{1,0:T(8,128)(2,1)} %get-tuple-element.107.grad_ref, bf16[512,1536]{1,0:T(8,128)(2,1)} %get-tuple-element.81.x_ref, bf16[512,1536]{1,0:T(8,128)(2,1)} %get-tuple-element.91.dout_ref.dres_ref, ...), custom_call_target="tpu_custom_call" | custom-call | flops 54000001024 | bytes 1048576 | tf_op jit(solution)/shard_map/last_step/pallas_call | solution.py:1114
  405.5 5.8 %emit_experts.1 = (f32[192,2,256]{2,1,0:T(2,128)}, f32[192,256]{1,0:T(8,128)}, f32[3072,2,128]{2,1,0:T(2,128)}, f32[2,128,1536]{2,1,0:T(8,128)}) custom-call(bf16[5184,256]{1,0:T(8,128)(2,1)} %reduce-scatter.3.cloned.1.call-done.pair_ref), custom_call_target="tpu_custom_call" | custom-call | flops 4499999744 | bytes 1048576 | tf_op jit(solution)/shard_map/emit_experts/pallas_call | solution.py:1212
  411.4 3.7 emit.1
  (76 shorter events, 6.0 us)
Async XLA Ops:
  7.2 17.8 %copy-start = (bf16[192,2,256]{2,1,0:T(2,128)(2,1)S(1)}, bf16[192,2,256]{2,1,0:T(2,128)(2,1)}, u32[]{:S(2)}) copy-start(bf16[192,2,256]{2,1,0:T(2,128)(2,1)} %param.35) | copy-start | bytes 589828
  7.2 64.7 %all-gather.3.cloned.1.call-start = ((), (), s32[]{:S(2)}) async-start(), calls=%async_computation.2 | async-start | bytes 9732096 | tf_op jit(solution)/shard_map/all_gather | solution.py:65
  8.9 2.4 copy-start.7
  11.2 1.0 copy-start.5
  11.3 2.0 copy-start.4
  12.2 1.0 copy-start.2
  13.3 168.4 %all-gather.5.cloned.1.call-start = ((), (), s32[]{:S(2)}) async-start(), calls=%async_computation.3 | async-start | bytes 21233664 | tf_op jit(solution)/shard_map/all_gather | solution.py:65
  18.3 0.7 copy-start.8
  18.3 4.0 copy-start.13
  18.3 4.0 copy-start.14
  18.3 4.0 copy-start.12
  18.3 4.6 %copy-start.15 = (f32[12]{0:T(128)S(1)}, f32[12]{0:T(128)}, u32[]{:S(2)}) copy-start(f32[12]{0:T(128)} %param.30) | copy-start | bytes 148
  18.3 5.3 %copy-start.9 = (s32[512,6]{0,1:T(8,128)S(1)}, s32[512,6]{0,1:T(8,128)}, u32[]{:S(2)}) copy-start(s32[512,6]{0,1:T(8,128)} %param.40) | copy-start | bytes 36868
  18.4 7.1 %copy-start.16 = (f32[12]{0:T(128)S(1)}, f32[12]{0:T(128)}, u32[]{:S(2)}) copy-start(f32[12]{0:T(128)} %param.29) | copy-start | bytes 148
  18.4 7.1 %copy-start.17 = (f32[12]{0:T(128)S(1)}, f32[12]{0:T(128)}, u32[]{:S(2)}) copy-start(f32[12]{0:T(128)} %param.28) | copy-start | bytes 148
  18.4 7.6 %copy-start.10 = (bf16[4,768]{1,0:T(4,128)(2,1)S(1)}, bf16[4,768]{1,0:T(4,128)(2,1)}, u32[]{:S(2)}) copy-start(bf16[4,768]{1,0:T(4,128)(2,1)} %param.26) | copy-start | bytes 18436
  18.4 7.6 %copy-start.11 = (bf16[4,256]{1,0:T(4,128)(2,1)S(1)}, bf16[4,256]{1,0:T(4,128)(2,1)}, u32[]{:S(2)}) copy-start(bf16[4,256]{1,0:T(4,128)(2,1)} %param.27) | copy-start | bytes 6148
  18.4 8.2 %copy-start.6 = (bf16[192,256]{1,0:T(8,128)(2,1)S(1)}, bf16[192,256]{1,0:T(8,128)(2,1)}, u32[]{:S(2)}) copy-start(bf16[192,256]{1,0:T(8,128)(2,1)} %param.36) | copy-start | bytes 294916
  18.4 337.5 %reduce-scatter.3.cloned.1.call-start = ((), (), s32[]{:S(2)}) async-start(), calls=%async_computation.4 | async-start | bytes 13271040 | tf_op jit(solution)/shard_map/reduce_scatter | solution.py:74
  19.1 49.8 %collective-permute-start = (s32[3]{0:T(128)S(1)}, s32[3]{0:T(128)S(1)}, u32[]{:S(2)}, u32[]{:S(2)}) collective-permute-start(s32[3]{0:T(128)S(1)} %slice_bitcast_fusion), channel_id=1, source_target_pairs={{0,4},{4,8},{8,12},{1,5},{5,9},{9,13},{2,6},{6,10},{10,14},{3,7},{... | collective-permute-start | bytes 44 | tf_op jit(solution)/shard_map/ppermute | solution.py:45
  25.3 44.5 %copy-start.3 = (s32[512,1]{1,0:T(8,128)}, s32[512,1]{1,0:T(8,128)S(1)}, u32[]{:S(2)}) copy-start(s32[512,1]{1,0:T(8,128)S(1)} %copy.93.seg_col_ref) | copy-start | bytes 6148
  244.3 167.1 %reduce-scatter.5.cloned.1.call-start = ((), (), s32[]{:S(2)}) async-start(), calls=%async_computation.5 | async-start | bytes 2949120 | tf_op jit(solution)/shard_map/reduce_scatter | solution.py:74
  411.4 3.7 copy-start.1
Sparse Core Ops, SparseCore 0:
  13.4 58.3 all-gather.2
  74.2 107.3 all-gather.4
  244.4 107.9 reduce-scatter.2
  356.1 52.6 reduce-scatter.4
